TPU v7x, 32 devices: a whole 2x2x4 slice. The times are simulated.
32 devices in a mesh: dp: 4 (over y, core), hid: 8 (over z, x).
Axes of the slice: x: 2, y: 2, z: 4, core: 2. Of those that a mesh axis runs over, the one named last changes fastest.
Arguments:
- history: bfloat16 [8, 4096, 2048], P(None, None, ('dp', 'hid')), may hold values from -24 to 24
- mix: float32 [4096, 32], P(('dp', 'hid')), may hold values from -1.5 to 1.5
- segment_ids: int32 [4096], P(('dp', 'hid')), may hold values from 0 to 7, never falling along the last dimension, each value on 1 to 1024 neighbouring positions
- norm_gains: bfloat16 [2048, 4], P('dp'), may hold values from 0.099609375 to 1.8984375
- w_query: bfloat16 [2048, 2048], P('dp'), may hold values from -0.125 to 0.125
- w_key: bfloat16 [2048, 2048], P('dp'), may hold values from -0.125 to 0.125
- w_value: bfloat16 [2048, 2048], P('dp'), may hold values from -0.125 to 0.125
- w_out: bfloat16 [2048, 2048], P('dp'), may hold values from -1 to 1
- w_up: bfloat16 [2048, 8192], P('dp'), may hold values from -0.125 to 0.125
- w_down: bfloat16 [8192, 2048], P('dp'), may hold values from -0.0625 to 0.0625
- w_mixer: bfloat16 [2048, 36], P('dp'), may hold values from -0.125 to 0.125
- mixer_out: float32 [36, 36], replicated, may hold values from -1 to 1
- mix_static: float32 [36], replicated, may hold values from -3 to 3
- out_cotangent: bfloat16 [4096, 2048], P(None, ('dp', 'hid')), may hold values from -6 to 6
- mix_cotangent: float32 [4096, 36], P(('dp', 'hid')), may hold values from -16 to 16
Outputs:
- block_output: bfloat16 [4096, 2048], P(None, ('dp', 'hid'))
- mix_next: float32 [4096, 36], P(('dp', 'hid'))
- history_grad: float32 [8, 4096, 2048], P(None, None, ('dp', 'hid'))
- mix_grad: float32 [4096, 32], P(('dp', 'hid'))
- norm_gains_grad: float32 [2048, 4], P('dp')
- w_query_grad: float32 [2048, 2048], P('dp')
- w_key_grad: float32 [2048, 2048], P('dp')
- w_value_grad: float32 [2048, 2048], P('dp')
- w_out_grad: float32 [2048, 2048], P('dp')
- w_up_grad: float32 [2048, 8192], P('dp')
- w_down_grad: float32 [8192, 2048], P('dp')
- w_mixer_grad: float32 [2048, 36], P('dp')
- mixer_out_grad: float32 [36, 36], replicated
- mix_static_grad: float32 [36], replicated
Inputs may be any that keep to these rules, and one draw needn't show every extreme that they name: `segment_ids`: segment ids never fall along the tokens; each id names 1 to 1024 consecutive tokens, and one names exactly 1024.
All inputs are finite; a program needn't handle non-finite values.
Results may differ from a plain program's by a relative error of at most 0.02.
Values may be sent and summed in bfloat16 or wider, within the bound.
A program may use at most 512 MiB of HBM per device.

v0:
```python
import math

import jax
import jax.numpy as jnp
from jax import lax
from jax.sharding import PartitionSpec as P

D = 2048
HEADS = 16
HEAD = 128
ROT = 32
HIST = 8
STREAMS = 4


highest = lax.Precision.HIGHEST
rope_base = 10000.0


def product(left, right):
    return jnp.dot(left, right, preferred_element_type=jnp.float32)


def product_left(left, right):
    return lax.dot_general(
        left, right, (((0,), (0,)), ((), ())), preferred_element_type=jnp.float32
    )


def product_right(left, right):
    return lax.dot_general(
        left, right, (((1,), (1,)), ((), ())), preferred_element_type=jnp.float32
    )


def product_left_high(left, right):
    return lax.dot_general(
        left, right, (((0,), (0,)), ((), ())), precision=highest, preferred_element_type=jnp.float32
    )


def gelu_exact(values_in):
    return jax.nn.gelu(values_in, approximate=False)


def layer_norm(values_in, gain):
    average = jnp.mean(values_in, axis=-1, keepdims=True)
    centred = values_in - average
    variance = jnp.mean(centred * centred, axis=-1, keepdims=True)
    inv_scale = lax.rsqrt(variance + 1e-05)
    unit_part = centred * inv_scale
    return (unit_part * gain, unit_part, inv_scale)


def norm_back(gradient, gain, unit_part, inv_scale):
    weighted = gradient * gain
    centred = weighted - jnp.mean(weighted, axis=-1, keepdims=True)
    centred = centred - unit_part * jnp.mean(weighted * unit_part, axis=-1, keepdims=True)
    return (centred * inv_scale, jnp.sum(gradient * unit_part, axis=0))


def rotate(values_in, cosine, sine_table, direction):
    half_rot = cosine.shape[1]
    front_half = values_in[..., :half_rot]
    back_half = values_in[..., half_rot : 2 * half_rot]
    cos_heads = cosine[:, None, :]
    sin_heads = sine_table[:, None, :] * direction
    return jnp.concatenate(
        [
            front_half * cos_heads - back_half * sin_heads,
            back_half * cos_heads + front_half * sin_heads,
            values_in[..., 2 * half_rot :],
        ],
        axis=-1,
    )


def reduce_rows(lefts, rights, small):
    parts = (
        product_left(lefts[0], rights[0]),
        product_left(lefts[1], rights[1]),
        product_left(lefts[2], rights[2]),
        small,
    )
    shares = (
        lax.psum_scatter(
            parts[0].astype(jnp.bfloat16), "dp", scatter_dimension=0, tiled=True
        ).astype(jnp.float32),
        lax.psum_scatter(
            parts[1].astype(jnp.bfloat16), "dp", scatter_dimension=0, tiled=True
        ).astype(jnp.float32),
        lax.psum_scatter(
            parts[2].astype(jnp.bfloat16), "dp", scatter_dimension=0, tiled=True
        ).astype(jnp.float32),
        lax.psum_scatter(
            parts[3].astype(jnp.bfloat16), "dp", scatter_dimension=0, tiled=True
        ).astype(jnp.float32),
    )
    return (
        lax.psum(shares[0].astype(jnp.bfloat16), "hid").astype(jnp.float32),
        lax.psum(shares[1].astype(jnp.bfloat16), "hid").astype(jnp.float32),
        lax.psum(shares[2].astype(jnp.bfloat16), "hid").astype(jnp.float32),
        lax.psum(shares[3].astype(jnp.bfloat16), "hid").astype(jnp.float32),
    )


def local(
    history,
    mix,
    segment_ids,
    norm_gains,
    w_query,
    w_key,
    w_value,
    w_out,
    w_up,
    w_down,
    w_mixer,
    mixer_out,
    mix_static,
    out_cotangent,
    mix_cotangent,
):
    local_tokens = segment_ids.shape[0]
    total_tokens = local_tokens * lax.axis_size("dp") * lax.axis_size("hid")
    by_token = lax.all_to_all(history, ("dp", "hid"), split_axis=1, concat_axis=2, tiled=True)
    row_ids = lax.all_gather(segment_ids, "hid", axis=0, tiled=True)
    gathered = (
        lax.all_gather(norm_gains, "dp", axis=0, tiled=True),
        lax.all_gather(w_query, "dp", axis=0, tiled=True),
        lax.all_gather(w_key, "dp", axis=0, tiled=True),
        lax.all_gather(w_value, "dp", axis=0, tiled=True),
        lax.all_gather(w_out, "dp", axis=0, tiled=True),
        lax.all_gather(w_up, "dp", axis=0, tiled=True),
        lax.all_gather(w_down, "dp", axis=0, tiled=True),
        lax.all_gather(w_mixer, "dp", axis=0, tiled=True),
    )
    gains_all, query_w, key_w, value_w, out_w, up_w, down_w, mixer_w = gathered
    row_length = row_ids.shape[0]
    here = lax.axis_index("hid") * local_tokens + jnp.arange(local_tokens, dtype=jnp.int32)
    positions_in_row = jnp.arange(row_length, dtype=jnp.int32)
    same_doc = segment_ids[:, None] == row_ids[None, :]
    doc_start = jnp.min(jnp.where(same_doc, positions_in_row[None, :], row_length), axis=1)
    position = (here - doc_start).astype(jnp.float32)
    visible = same_doc & (positions_in_row[None, :] <= here[:, None])
    frequency = rope_base ** (-jnp.arange(ROT // 2, dtype=jnp.float32) * 2.0 / ROT)
    angle = position[:, None] * frequency[None, :]
    cosine = jnp.cos(angle)
    sine_table = jnp.sin(angle)
    mix_table = mix.reshape(local_tokens, STREAMS, HIST)
    streams = []
    for stream in range(STREAMS):
        stream_sum = jnp.zeros((local_tokens, D), jnp.float32)
        for layer in range(HIST):
            stream_sum = stream_sum + mix_table[:, stream, layer][:, None] * by_token[layer]
        streams.append(stream_sum)
    normed, units, inv_scales, gain_list = ([], [], [], [])
    for stream in range(STREAMS):
        gain = gains_all[:, stream].astype(jnp.float32)
        normed_value, unit_part, inv_scale = layer_norm(streams[stream], gain)
        normed.append(normed_value.astype(jnp.bfloat16))
        units.append(unit_part)
        inv_scales.append(inv_scale)
        gain_list.append(gain)
    queries = rotate(
        product(normed[0], query_w).reshape(local_tokens, HEADS, HEAD), cosine, sine_table, 1.0
    ).astype(jnp.bfloat16)
    key_mine = rotate(
        product(normed[1], key_w).reshape(local_tokens, HEADS, HEAD), cosine, sine_table, 1.0
    ).astype(jnp.bfloat16)
    value_mine = product(normed[2], value_w).astype(jnp.bfloat16).reshape(local_tokens, HEADS, HEAD)
    key_row, value_row = (
        lax.all_gather(key_mine, "hid", axis=0, tiled=True),
        lax.all_gather(value_mine, "hid", axis=0, tiled=True),
    )
    score_scale = 1.0 / math.sqrt(HEAD)
    scores = (
        jnp.einsum("qhd,khd->hqk", queries, key_row, preferred_element_type=jnp.float32)
        * score_scale
    )
    scores = jnp.where(visible[None], scores, -1e30)
    probs = jax.nn.softmax(scores, axis=-1)
    probs_low = probs.astype(jnp.bfloat16)
    attended = jnp.einsum("hqk,khd->qhd", probs_low, value_row, preferred_element_type=jnp.float32)
    attended = attended.reshape(local_tokens, D).astype(jnp.bfloat16)
    branch = product(attended, out_w)
    hidden = product(normed[3], up_w)
    active = gelu_exact(hidden).astype(jnp.bfloat16)
    feed_out = product(active, down_w)
    output = streams[3] + branch + feed_out
    inv_rms = lax.rsqrt(jnp.mean(output * output, axis=-1, keepdims=True) + 1e-06)
    scaled = (output * inv_rms).astype(jnp.bfloat16)
    inner_pre = product(scaled, mixer_w)
    inner_act = gelu_exact(inner_pre)
    raw_mix = jnp.dot(inner_act, mixer_out, precision=highest, preferred_element_type=jnp.float32)
    sum_raw, sum_square = lax.psum(
        (jnp.sum(raw_mix, axis=0), jnp.sum(raw_mix * raw_mix, axis=0)), ("dp", "hid")
    )
    average = sum_raw / total_tokens
    variance = sum_square / total_tokens - average * average
    inv_spread = lax.rsqrt(variance + 1e-05)
    unit_mix = (raw_mix - average) * inv_spread
    mix_next = mix_static + unit_mix
    block_output = lax.all_to_all(
        output.astype(jnp.bfloat16), ("dp", "hid"), split_axis=1, concat_axis=0, tiled=True
    )
    upstream = lax.all_to_all(
        out_cotangent, ("dp", "hid"), split_axis=0, concat_axis=1, tiled=True
    ).astype(jnp.float32)
    sum_grad, sum_grad_unit, inner_grad_sum, inner_unit_sum, inner_total = lax.psum(
        (
            jnp.sum(mix_cotangent, axis=0),
            jnp.sum(mix_cotangent * unit_mix, axis=0),
            product_left_high(inner_act, mix_cotangent),
            product_left_high(inner_act, unit_mix),
            jnp.sum(inner_act, axis=0),
        ),
        ("dp", "hid"),
    )
    mean_grad = sum_grad / total_tokens
    mean_grad_unit = sum_grad_unit / total_tokens
    raw_grad = inv_spread * (mix_cotangent - mean_grad - unit_mix * mean_grad_unit)
    mixer_out_grad = inv_spread * (
        inner_grad_sum
        - inner_total[:, None] * mean_grad[None, :]
        - inner_unit_sum * mean_grad_unit[None, :]
    )
    act_grad = lax.dot_general(
        raw_grad,
        mixer_out,
        (((1,), (1,)), ((), ())),
        precision=highest,
        preferred_element_type=jnp.float32,
    )
    ignored_value, inner_pull = jax.vjp(gelu_exact, inner_pre)
    inner_low = inner_pull(act_grad)[0].astype(jnp.bfloat16)
    mixer_part = product_left(scaled, inner_low)
    scaled_grad = product_right(inner_low, mixer_w)
    output_grad = (
        upstream
        + inv_rms * scaled_grad
        - output
        * (inv_rms * inv_rms * inv_rms)
        * jnp.mean(scaled_grad * output, axis=-1, keepdims=True)
    )
    output_low = output_grad.astype(jnp.bfloat16)
    active_grad = product_right(output_low, down_w)
    ignored_other, hidden_pull = jax.vjp(gelu_exact, hidden)
    hidden_low = hidden_pull(active_grad)[0].astype(jnp.bfloat16)
    residual_norm_grad = product_right(hidden_low, up_w)
    attended_grad = (
        product_right(output_low, out_w).astype(jnp.bfloat16).reshape(local_tokens, HEADS, HEAD)
    )
    late_grads = reduce_rows(
        (normed[3], active, attended), (hidden_low, output_low, output_low), mixer_part
    )
    prob_grad = jnp.einsum(
        "qhd,khd->hqk", attended_grad, value_row, preferred_element_type=jnp.float32
    )
    row_total = jnp.sum(probs * prob_grad, axis=-1, keepdims=True)
    score_grad = (probs * (prob_grad - row_total)).astype(jnp.bfloat16)
    query_grad = (
        jnp.einsum("hqk,khd->qhd", score_grad, key_row, preferred_element_type=jnp.float32)
        * score_scale
    )
    key_row_grad = (
        jnp.einsum("hqk,qhd->khd", score_grad, queries, preferred_element_type=jnp.float32)
        * score_scale
    )
    value_row_grad = jnp.einsum(
        "hqk,qhd->khd", probs_low, attended_grad, preferred_element_type=jnp.float32
    )
    key_grad, value_grad = (
        lax.psum_scatter(
            key_row_grad.astype(jnp.bfloat16), "hid", scatter_dimension=0, tiled=True
        ).astype(jnp.float32),
        lax.psum_scatter(
            value_row_grad.astype(jnp.bfloat16), "hid", scatter_dimension=0, tiled=True
        ).astype(jnp.float32),
    )
    query_low = (
        rotate(query_grad, cosine, sine_table, -1.0).astype(jnp.bfloat16).reshape(local_tokens, D)
    )
    key_low = (
        rotate(key_grad, cosine, sine_table, -1.0).astype(jnp.bfloat16).reshape(local_tokens, D)
    )
    value_low = value_grad.astype(jnp.bfloat16).reshape(local_tokens, D)
    normed_grads = [
        product_right(query_low, query_w),
        product_right(key_low, key_w),
        product_right(value_low, value_w),
        residual_norm_grad,
    ]
    stream_grads, gain_grads = ([], [])
    for stream in range(STREAMS):
        stream_grad, gain_grad = norm_back(
            normed_grads[stream], gain_list[stream], units[stream], inv_scales[stream]
        )
        if stream == STREAMS - 1:
            stream_grad = stream_grad + output_grad
        stream_grads.append(stream_grad)
        gain_grads.append(gain_grad)
    gains_part = jnp.stack(gain_grads, axis=1)
    early_grads = reduce_rows(
        (normed[0], normed[1], normed[2]), (query_low, key_low, value_low), gains_part
    )
    history_part = []
    for layer in range(HIST):
        layer_sum = jnp.zeros((local_tokens, D), jnp.float32)
        for stream in range(STREAMS):
            layer_sum = layer_sum + mix_table[:, stream, layer][:, None] * stream_grads[stream]
        history_part.append(layer_sum)
    history_part = jnp.stack(history_part, axis=0)
    mix_grad = jnp.stack(
        [
            jnp.einsum(
                "td,jtd->tj",
                stream_grads[stream],
                by_token,
                precision=highest,
                preferred_element_type=jnp.float32,
            )
            for stream in range(STREAMS)
        ],
        axis=1,
    ).reshape(local_tokens, STREAMS * HIST)
    history_grad = lax.all_to_all(
        history_part.astype(jnp.bfloat16), ("dp", "hid"), split_axis=2, concat_axis=1, tiled=True
    ).astype(history_part.dtype)
    return (
        block_output,
        mix_next,
        history_grad,
        mix_grad,
        early_grads[3],
        early_grads[0],
        early_grads[1],
        early_grads[2],
        late_grads[2],
        late_grads[0],
        late_grads[1],
        late_grads[3],
        mixer_out_grad,
        sum_grad,
    )


def solution(mesh):
    placed = (
        P(None, None, ("dp", "hid")),
        P(("dp", "hid"), None),
        P(("dp", "hid")),
        P("dp", None),
        P("dp", None),
        P("dp", None),
        P("dp", None),
        P("dp", None),
        P("dp", None),
        P("dp", None),
        P("dp", None),
        P(),
        P(),
        P(None, ("dp", "hid")),
        P(("dp", "hid"), None),
    )
    return jax.shard_map(
        local,
        mesh=mesh,
        in_specs=placed,
        out_specs=(
            P(None, ("dp", "hid")),
            P(("dp", "hid"), None),
            P(None, None, ("dp", "hid")),
            P(("dp", "hid"), None),
            P("dp", None),
            P("dp", None),
            P("dp", None),
            P("dp", None),
            P("dp", None),
            P("dp", None),
            P("dp", None),
            P("dp", None),
            P(),
            P(),
        ),
        check_vma=False,
    )
```

profile of v0, /device:TPU:0, one launch (start us, length us, event | category | flops | bytes accessed | tf_op | source)
XLA Modules:
  0.0 2863.3 jit_solution(5909885468711126501)
XLA Ops:
  41.1 45.8 %all_gather.33 = bf16[2048,4]{0,1:T(4,128)(2,1)S(1)} all-gather(bf16[512,4]{0,1:T(4,128)(2,1)S(1)} %copy-done.153), channel_id=1, replica_groups=mesh['dp'=4,'hid'=8] {'dp'}, dimensions={0}, use_global_device_ids=true | all-gather | bytes 20480 | tf_op jit(solution)/shard_map/all_gather | solution.py:129
  87.9 40.3 %all-gather = s32[8,1,128]{2,1,0:T(1,128)S(1)} all-gather(s32[1,1,128]{2,1,0:T(1,128)S(1)} %bitcast.312), channel_id=1, replica_groups=mesh['dp'=4,'hid'=8] {'hid'}, dimensions={0}, use_global_device_ids=true | all-gather | bytes 4608 | tf_op jit(solution)/shard_map/all_gather | solution.py:127
  281.6 24.1 all-to-all-done.2
  331.5 66.9 %all-gather.12.cloned.1.call-done = bf16[1024,16,128]{0,2,1:T(8,128)(2,1)} async-done(((bf16[128,16,128]{0,2,1:T(8,128)(2,1)}), bf16[1024,16,128]{0,2,1:T(8,128)(2,1)}) %all-gather.12.cloned.1.call-update) | async-done | bytes 4194320 | tf_op jit(solution)/shard_map/all_gather | solution.py:174
  404.5 51.8 %all-gather.20.cloned.1.call-done = bf16[2048,2048]{1,0:T(8,128)(2,1)} async-done(((bf16[512,2048]{1,0:T(8,128)(2,1)}), bf16[2048,2048]{1,0:T(8,128)(2,1)}) %all-gather.20.cloned.1.call-update) | async-done | bytes 8388624 | tf_op jit(solution)/shard_map/all_gather | solution.py:133
  462.0 197.5 %all-gather.22.cloned.1.call-done = bf16[2048,8192]{1,0:T(8,128)(2,1)} async-done(((bf16[512,8192]{1,0:T(8,128)(2,1)}), bf16[2048,8192]{1,0:T(8,128)(2,1)}) %all-gather.22.cloned.1.call-update) | async-done | bytes 33554448 | tf_op jit(solution)/shard_map/all_gather | solution.py:134
  659.5 24.6 multiply_convert_fusion.2
  684.0 178.6 %all-gather.24.cloned.1.call-done = bf16[8192,2048]{1,0:T(8,128)(2,1)} async-done(((bf16[2048,2048]{1,0:T(8,128)(2,1)}), bf16[8192,2048]{1,0:T(8,128)(2,1)}) %all-gather.24.cloned.1.call-update) | async-done | bytes 33554448 | tf_op jit(solution)/shard_map/all_gather | solution.py:135
  862.6 16.0 multiply_reduce_fusion.10
  880.2 39.4 %all-reduce.3 = (f32[36]{0:T(128)S(1)}, f32[36]{0:T(128)S(1)}) all-reduce(f32[36]{0:T(128)S(1)} %get-tuple-element.33, f32[36]{0:T(128)S(1)} %get-tuple-element.32), channel_id=1, replica_groups=mesh['dp'=4,'hid'=8] {'dp','hid'}, use_global_device_ids=true, to_apply=%region_15.16 | all-reduce | flops 72 | bytes 576 | tf_op jit(solution)/shard_map/psum | solution.py:196
  920.6 42.3 %all-reduce.2 = (f32[36]{0:T(128)S(1)}, f32[36]{0:T(128)S(1)}, f32[36,36]{1,0:T(8,128)}, f32[36,36]{1,0:T(8,128)}, f32[36]{0:T(128)}) all-reduce(f32[36]{0:T(128)S(1)} %get-tuple-element.31, f32[36]{0:T(128)S(1)} %get-tuple-element.30, f32[36,36]{1,0:T(8,128)S(1)} %fusion.83, ...), channel_id=1, replica_groups=mesh['dp'=4,'hid'=8] {'dp','hid'}, use_global_device_ids=true, to_apply=%region_19.20 | all-reduce | flops 2700 | bytes 21600 | tf_op jit(solution)/shard_map/psum | solution.py:210
  1020.3 62.2 %reduce-scatter.31.cloned.1.call-done = bf16[128,2048]{1,0:T(8,128)(2,1)} async-done(((bf16[1024,2048]{1,0:T(8,128)(2,1)}), bf16[128,2048]{1,0:T(8,128)(2,1)}) %reduce-scatter.31.cloned.1.call-update) | async-done | bytes 524304
  1104.5 69.6 %reduce-scatter.33.cloned.1.call-done = bf16[128,2048]{1,0:T(8,128)(2,1)} async-done(((bf16[1024,2048]{1,0:T(8,128)(2,1)}), bf16[128,2048]{1,0:T(8,128)(2,1)}) %reduce-scatter.33.cloned.1.call-update) | async-done | bytes 524304 | tf_op jit(solution)/shard_map/reshape | solution.py:287
  1181.1 22.7 add_convert_fusion
  1203.9 15.6 convolution_convert_fusion
  1219.5 15.7 convolution_convert_fusion.1
  1235.6 19.2 multiply_reduce_fusion.1
  1281.3 41.9 %reduce-scatter.21.cloned.1.call-done = bf16[512,2048]{1,0:T(8,128)(2,1)} async-done(((bf16[2048,2048]{1,0:T(8,128)(2,1)}), bf16[512,2048]{1,0:T(8,128)(2,1)}) %reduce-scatter.21.cloned.1.call-update) | async-done | bytes 2097168 | tf_op jit(solution)/shard_map/reduce_scatter | solution.py:86
  1323.2 74.9 %reduce-scatter.23.cloned.1.call-done = bf16[512,2048]{1,0:T(8,128)(2,1)} async-done(((bf16[2048,2048]{1,0:T(8,128)(2,1)}), bf16[512,2048]{1,0:T(8,128)(2,1)}) %reduce-scatter.23.cloned.1.call-update) | async-done | bytes 2097168 | tf_op jit(solution)/shard_map/reduce_scatter | solution.py:89
  1398.1 74.4 %reduce-scatter.25.cloned.1.call-done = bf16[512,2048]{1,0:T(8,128)(2,1)} async-done(((bf16[2048,2048]{1,0:T(8,128)(2,1)}), bf16[512,2048]{1,0:T(8,128)(2,1)}) %reduce-scatter.25.cloned.1.call-update) | async-done | bytes 2097168 | tf_op jit(solution)/shard_map/reduce_scatter | solution.py:92
  1472.5 237.3 %reduce-scatter.37.cloned.1.call-done = bf16[512,8192]{1,0:T(8,128)(2,1)} async-done(((bf16[2048,8192]{1,0:T(8,128)(2,1)}), bf16[512,8192]{1,0:T(8,128)(2,1)}) %reduce-scatter.37.cloned.1.call-update) | async-done | bytes 8388624
  1709.8 237.3 %reduce-scatter.39.cloned.1.call-done = bf16[2048,2048]{1,0:T(8,128)(2,1)} async-done(((bf16[8192,2048]{1,0:T(8,128)(2,1)}), bf16[2048,2048]{1,0:T(8,128)(2,1)}) %reduce-scatter.39.cloned.1.call-update) | async-done | bytes 8388624
  2004.9 165.4 %all-reduce.4 = (bf16[512,4]{0,1:T(4,128)(2,1)S(1)}, bf16[512,36]{0,1:T(8,128)(2,1)S(1)}) all-reduce(bf16[512,4]{0,1:T(4,128)(2,1)S(1)} %copy.258, bf16[512,36]{0,1:T(8,128)(2,1)} %reduce-scatter.29.cloned.1.call-done), channel_id=1, replica_groups=mesh['dp'=4,'hid'=8] {'hid'}, use_global_device_ids=true, to_apply=%region_37.38 | all-reduce | flops 20480 | bytes 81920 | tf_op jit(solution)/shard_map/psum | solution.py:103
  2178.8 642.1 %all-reduce.8.cloned.1.call-done = (bf16[512,2048]{1,0:T(8,128)(2,1)}, bf16[512,2048]{1,0:T(8,128)(2,1)}, bf16[512,2048]{1,0:T(8,128)(2,1)}, bf16[512,2048]{1,0:...) async-done(((bf16[512,2048]{1,0:T(8,128)(2,1)}, bf16[512,2048]{1,0:T(8,128)(2,1)}, bf16[512,2048]{1,0:T(8,128)(2,1)}, bf16[512,2048]{1,0:T(8,128)(2,1)}, ...) | async-done | bytes 25165840 | tf_op jit(solution)/shard_map/psum | solution.py:100
  (542 shorter events, 440.9 us)
Async XLA Ops:
  7.2 158.9 %all-gather.16.cloned.1.call-start = ((), (), s32[]{:S(2)}) async-start(), calls=%async_computation.17 | async-start | bytes 10485760 | tf_op jit(solution)/shard_map/all_gather | solution.py:131
  7.9 170.6 %all-gather.14.cloned.1.call-start = ((), (), s32[]{:S(2)}) async-start(), calls=%async_computation.16 | async-start | bytes 10485760 | tf_op jit(solution)/shard_map/all_gather | solution.py:130
  8.7 244.6 %all-gather.10.cloned.1.call-start = ((), (), s32[]{:S(2)}) async-start(), calls=%async_computation.14 | async-start | bytes 10485760 | tf_op jit(solution)/shard_map/all_gather | solution.py:132
  33.6 102.7 %all-to-all-start = ((bf16[32,2,32768]{2,1,0:T(2,128)(2,1)}), bf16[32,2,32768]{2,1,0:T(2,128)(2,1)}, u32[]{:S(2)}, u32[]{:S(2)}) async-start(bf16[32,2,32768]{2,1,0:T(2,128)(2,1)} %reshape.1344), calls=%async_computation | async-start | bytes 8388608 | tf_op jit(solution)/shard_map/all_to_all | solution.py:126
  41.1 281.4 %all-gather.18.cloned.1.call-start = ((), (), s32[]{:S(2)}) async-start(), calls=%async_computation.18 | async-start | bytes 4718592 | tf_op jit(solution)/shard_map/all_gather | solution.py:173
  201.9 196.5 %all-gather.12.cloned.1.call-start = ((), (), s32[]{:S(2)}) async-start(), calls=%async_computation.15 | async-start | bytes 4718592 | tf_op jit(solution)/shard_map/all_gather | solution.py:174
  259.4 196.9 %all-gather.20.cloned.1.call-start = ((), (), s32[]{:S(2)}) async-start(), calls=%async_computation.19 | async-start | bytes 10485760 | tf_op jit(solution)/shard_map/all_gather | solution.py:133
  260.0 399.4 %all-gather.22.cloned.1.call-start = ((), (), s32[]{:S(2)}) async-start(), calls=%async_computation.20 | async-start | bytes 41943040 | tf_op jit(solution)/shard_map/all_gather | solution.py:134
  260.8 601.8 %all-gather.24.cloned.1.call-start = ((), (), s32[]{:S(2)}) async-start(), calls=%async_computation.21 | async-start | bytes 41943040 | tf_op jit(solution)/shard_map/all_gather | solution.py:135
  262.5 43.3 %all-to-all-start.2 = ((bf16[32,128,64]{1,2,0:T(8,128)(2,1)}), bf16[32,128,64]{1,2,0:T(8,128)(2,1)S(1)}, u32[]{:S(2)}, u32[]{:S(2)}) async-start(bf16[32,128,64]{1,2,0:T(8,128)(2,1)} %copy_bitcast_fusion.2), calls=%async_computation.2 | async-start | bytes 1048576 | tf_op jit(solution)/shard_map/all_to_all | solution.py:207
  274.3 808.3 %reduce-scatter.31.cloned.1.call-start = ((), (), s32[]{:S(2)}) async-start(), calls=%async_computation.27 | async-start | bytes 4718592
  312.6 346.9 %copy-start.64 = (f32[128]{0:T(128)}, f32[128]{0:T(128)S(1)}, u32[]{:S(2)}) copy-start(f32[128]{0:T(128)S(1)} %broadcast_multiply_fusion.13) | copy-start | bytes 1540
  994.7 179.4 %reduce-scatter.33.cloned.1.call-start = ((), (), s32[]{:S(2)}) async-start(), calls=%async_computation.28 | async-start | bytes 4718592 | tf_op jit(solution)/shard_map/reshape | solution.py:287
  1008.3 273.0 %reduce-scatter.27.cloned.1.call-start = ((), (), s32[]{:S(2)}) async-start(), calls=%async_computation.25 | async-start | bytes 10485760 | tf_op jit(solution)/shard_map/reduce_scatter | solution.py:92
  1014.0 309.2 %reduce-scatter.21.cloned.1.call-start = ((), (), s32[]{:S(2)}) async-start(), calls=%async_computation.22 | async-start | bytes 10485760 | tf_op jit(solution)/shard_map/reduce_scatter | solution.py:86
  1094.1 304.0 %reduce-scatter.23.cloned.1.call-start = ((), (), s32[]{:S(2)}) async-start(), calls=%async_computation.23 | async-start | bytes 10485760 | tf_op jit(solution)/shard_map/reduce_scatter | solution.py:89
  1101.9 370.6 %reduce-scatter.25.cloned.1.call-start = ((), (), s32[]{:S(2)}) async-start(), calls=%async_computation.24 | async-start | bytes 10485760 | tf_op jit(solution)/shard_map/reduce_scatter | solution.py:92
  1180.9 528.9 %reduce-scatter.37.cloned.1.call-start = ((), (), s32[]{:S(2)}) async-start(), calls=%async_computation.30 | async-start | bytes 41943040
  1219.5 727.6 %reduce-scatter.39.cloned.1.call-start = ((), (), s32[]{:S(2)}) async-start(), calls=%async_computation.31 | async-start | bytes 41943040
  1235.3 768.6 %reduce-scatter.35.cloned.1.call-start = ((), (), s32[]{:S(2)}) async-start(), calls=%async_computation.29 | async-start | bytes 655360
  1280.2 724.8 %reduce-scatter.29.cloned.1.call-start = ((), (), s32[]{:S(2)}) async-start(), calls=%async_computation.26 | async-start | bytes 204800 | tf_op jit(solution)/shard_map/reduce_scatter | solution.py:95
  1281.2 1539.6 %all-reduce.8.cloned.1.call-start = ((), (), s32[]{:S(2)}) async-start(), calls=%async_computation.32 | async-start | bytes 50331648 | tf_op jit(solution)/shard_map/psum | solution.py:100
  1949.1 25.5 all-to-all-start.1
  1974.6 197.0 %all-to-all-start.3 = ((bf16[8,128,2048]{1,0,2:T(8,128)(2,1)}), bf16[8,128,2048]{1,0,2:T(8,128)(2,1)}, u32[]{:S(2)}, u32[]{:S(2)}) async-start(bf16[8,128,2048]{1,0,2:T(8,128)(2,1)} %copy.209), calls=%async_computation.3 | async-start | bytes 8388608 | tf_op jit(solution)/shard_map/all_to_all | solution.py:327
  (164 other events, 4212.8 us)
Sparse Core Ops, SparseCore 0:
  9.6 104.6 all-gather.15
  115.8 56.0 all-gather.13
  173.4 61.0 all-gather.9
  236.4 85.9 all-gather.17
  324.9 73.4 all-gather.11
  399.8 56.4 all-gather.19
  457.9 201.5 all-gather.21
  661.0 201.5 all-gather.23
  994.8 87.6 reduce-scatter.30
  1086.5 87.6 reduce-scatter.32
  1176.7 71.4 reduce-scatter.26
  1251.4 71.7 reduce-scatter.20
  1326.4 71.7 reduce-scatter.22
  1400.7 71.7 reduce-scatter.24
  1474.9 234.8 reduce-scatter.36
  1712.2 234.8 reduce-scatter.38
  1949.4 21.8 reduce-scatter.34
  1973.7 30.5 reduce-scatter.28
  2010.8 809.9 all-reduce.7
where the time goes:
time: 2880 us; the launch traced here: 2860 us
  waiting for transfers between devices  1980 us (69%)
  blocking collectives  340 us (12%)
  matrix products  227 us (8%)
  local copies, waits for them, and re-layouts  175 us (6%)
  other arithmetic  96.7 us (3%)
  starting transfers between devices  31.6 us (1%)
    psum x1, waiting for transfers between devices, reduce_rows(): lax.psum(shares[0].astype(jnp.bfloat16), 'hid').astype(jnp.float32)  642 us
    unnamed x23, waiting for transfers between devices  541 us
    all_gather x1, waiting for transfers between devices, local(): lax.all_gather(w_up, 'dp', axis=0, tiled=True)  197 us
    all_gather x1, waiting for transfers between devices, local(): lax.all_gather(w_down, 'dp', axis=0, tiled=True)  179 us
    psum x1, blocking collectives, reduce_rows(): lax.psum(shares[3].astype(jnp.bfloat16), 'hid').astype(jnp.float32)  165 us
    unnamed x343, local copies, waits for them, and re-layouts  80.8 us
    reduce_scatter x1, waiting for transfers between devices, reduce_rows(): lax.psum_scatter(parts[1].astype(jnp.bfloat16), 'dp', scatter_dimension=0...  74.9 us
    reduce_scatter x2, waiting for transfers between devices, reduce_rows(): lax.psum_scatter(parts[2].astype(jnp.bfloat16), 'dp', scatter_dimension=0...  74.4 us
  transfers between devices with their start and end apart: 23, of which 15 were waited for; matrix products, arithmetic and copies ran while one was open for 14% of the time, Pallas kernels for 0%

commit v1 on v0

v1 whole, which is shorter than its diff:
```python
import functools
import math

import jax
import jax.numpy as jnp
from jax import lax
from jax.experimental import pallas as pl
from jax.experimental.pallas import tpu as pltpu
from jax.sharding import PartitionSpec as P

HEADS = 16
HEAD = 128
ROT = 32
HIST = 8
STREAMS = 4
CORES = 2
CHUNK = 1 << 16
SLACK = 5

highest = lax.Precision.HIGHEST
rope_base = 10000.0
low = jnp.bfloat16
full = jnp.float32


def contract(left, right, left_dim, right_dim):
    return lax.dot_general(
        left, right, (((left_dim,), (right_dim,)), ((), ())), preferred_element_type=full
    )


def contract_high(left, right, left_dim, right_dim):
    return lax.dot_general(
        left,
        right,
        (((left_dim,), (right_dim,)), ((), ())),
        precision=highest,
        preferred_element_type=full,
    )


def batched(left, right, left_dim, right_dim):
    return lax.dot_general(
        left, right, (((left_dim,), (right_dim,)), ((0,), (0,))), preferred_element_type=full
    )


def gelu_exact(values_in):
    return jax.nn.gelu(values_in, approximate=False)


def core_swap(values_in):
    size = lax.axis_size("dp")
    return lax.ppermute(values_in, "dp", [(i, i ^ 1) for i in range(size)])


def outer_shift(values_in, step):
    size = lax.axis_size("dp")
    outer = size // CORES
    pairs = [
        (o * CORES + c, ((o + step) % outer) * CORES + c) for o in range(outer) for c in range(CORES)
    ]
    return lax.ppermute(values_in, "dp", pairs)


def hid_swap(values_in, bit):
    size = lax.axis_size("hid")
    return lax.ppermute(values_in, "hid", [(i, i ^ bit) for i in range(size)])


def ordered(first, values_in, other, axis):
    return jnp.stack(
        [jnp.where(first, values_in, other), jnp.where(first, other, values_in)], axis=axis
    )


def take(values_in, index):
    return lax.dynamic_index_in_dim(values_in, index, 0, keepdims=False)


def put(target, values_in, index):
    return lax.dynamic_update_index_in_dim(target, values_in, index, 0)


def split_ways():
    return 2 if HEADS // lax.axis_size("dp") >= 2 else 1


def gather_ways(values_in, axis):
    if split_ways() == 1:
        return jnp.expand_dims(values_in, axis)
    return ordered(lax.axis_index("hid") % 2 == 0, values_in, hid_swap(values_in, 1), axis)


def gather_dp(values_in):
    size = lax.axis_size("dp")
    outer = size // CORES
    me = lax.axis_index("dp")
    mine, core = me // CORES, me % CORES
    if outer == 2:
        held = ordered(mine == 0, values_in, outer_shift(values_in, 1), 0)
    else:
        held = jnp.zeros((outer,) + values_in.shape, values_in.dtype)
        held = put(held, values_in, mine)
        for step in range(1, outer):
            held = put(held, outer_shift(values_in, step), (mine - step) % outer)
    pair = ordered(core == 0, held, core_swap(held), 1)
    return pair.reshape((size,) + values_in.shape)


def sum_features(values_in):
    if split_ways() == 2:
        values_in = values_in + hid_swap(values_in, 1)
    parts = gather_dp(values_in)
    total = parts[0]
    for i in range(1, parts.shape[0]):
        total = total + parts[i]
    return total


def sum_tokens(values_in):
    size = lax.axis_size("hid")
    bit = split_ways()
    while bit < size:
        values_in = values_in + hid_swap(values_in, bit)
        bit *= 2
    return values_in


def gather_all(values_in):
    for axis in ("hid", "dp"):
        size, me = lax.axis_size(axis), lax.axis_index(axis)
        bit = 1
        while bit < size:
            other = lax.ppermute(values_in, axis, [(i, i ^ bit) for i in range(size)])
            both = ordered(me // bit % 2 == 0, values_in, other, 0)
            values_in = both.reshape((2 * values_in.shape[0],) + values_in.shape[1:])
            bit *= 2
    return values_in


def scatter_dp(make):
    size = lax.axis_size("dp")
    outer = size // CORES
    me = lax.axis_index("dp")
    mine, core = me // CORES, me % CORES
    total = None
    for step in list(range(1, outer)) + [0]:
        there = (mine + step) % outer
        away = core_swap(make(there * CORES + 1 - core).astype(low))
        block = make(there * CORES + core) + away.astype(full)
        if step:
            block = outer_shift(block.astype(low), step).astype(full)
        total = block if total is None else total + block
    return total


def exchange(values_in):
    ways, size = split_ways(), lax.axis_size("hid")
    groups = None
    if ways > 1:
        groups = [[t * ways + w for t in range(size // ways)] for w in range(ways)]
    return lax.all_to_all(
        values_in, "hid", split_axis=0, concat_axis=0, tiled=True, axis_index_groups=groups
    )


def chain_kernel(
    ways,
    places,
    part_ref,
    out_ref,
    landed,
    sums,
    up_send,
    up_recv,
    down_send,
    down_recv,
    side_send,
    side_recv,
    kept,
):
    count = part_ref.shape[0]
    last = places - 1
    me = lax.axis_index("hid")
    if ways == 2:
        place, way = me // 2, me % 2
        above, below, beside = me + 2, me - 2, me + 1 - 2 * way
    else:
        odd, half = me % 2, places // 2
        place, way = (1 - odd) * (me // 2) + odd * (last - me // 2), 0
        turn_up = (place + 1) // half
        turn_down = (place - 1 + places) // half - 2
        above = (1 - turn_up) * 2 * (place + 1) + turn_up * (2 * (last - place - 1) + 1)
        below = (1 - turn_down) * 2 * (place - 1) + turn_down * (2 * (last - place + 1) + 1)
        beside = me

    def remote(source, target, send, recv, device):
        return pltpu.make_async_remote_copy(
            src_ref=source,
            dst_ref=target,
            send_sem=send,
            recv_sem=recv,
            device_id={"hid": device},
            device_id_type=pl.DeviceIdType.MESH,
        )

    def up_copy(i):
        return remote(sums.at[i], landed.at[i], up_send, up_recv.at[i], above)

    def down_copy(source, i):
        return remote(source, out_ref.at[way, i], down_send, down_recv.at[i], below)

    def side_copy(source, i):
        return remote(source, out_ref.at[way, i], side_send, side_recv, beside)

    barrier = pltpu.get_barrier_semaphore()

    def greet(device):
        pl.semaphore_signal(
            barrier, inc=1, device_id={"hid": device}, device_id_type=pl.DeviceIdType.MESH
        )

    @pl.when(place > 0)
    def _():
        greet(below)

    @pl.when(place < last)
    def _():
        greet(above)

    if ways == 2:
        greet(beside)
    met = jnp.where(place > 0, 1, 0) + jnp.where(place < last, 1, 0) + (ways - 1)
    pl.semaphore_wait(barrier, met)

    def upward(i):
        @pl.when(place == 0)
        def _():
            remote(part_ref.at[i], landed.at[i], up_send, up_recv.at[i], above).start()

        @pl.when(place > 0)
        def _():
            up_copy(i).wait_recv()
            sums[i] = (landed[i].astype(full) + part_ref[i].astype(full)).astype(low)

            @pl.when(place < last)
            def _():
                up_copy(i).start()

            @pl.when(place == last)
            def _():
                down_copy(sums.at[i], i).start()
                if ways == 2:
                    side_copy(sums.at[i], i).start()
                pltpu.make_async_copy(sums.at[i], out_ref.at[way, i], kept).start()

    def downward(i):
        down_copy(sums.at[i], i).wait_recv()

        @pl.when(place > 0)
        def _():
            down_copy(out_ref.at[way, i], i).start()

        if ways == 2:
            side_copy(out_ref.at[way, i], i).start()

    lag = SLACK * (last - place) + 2

    def step(i, carry):
        @pl.when(i < count)
        def _():
            upward(i)

        behind = i - lag

        @pl.when((behind >= 0) & (behind < count) & (place < last))
        def _():
            downward(behind)

        return carry

    lax.fori_loop(0, count + SLACK * last + 2, step, 0)

    @pl.when(place < last)
    def _():
        remote(sums, landed, up_send, kept, above).wait_send()

    @pl.when(place > 0)
    def _():
        remote(sums, out_ref.at[way], down_send, kept, below).wait_send()

    @pl.when(place == last)
    def _():
        pltpu.make_async_copy(sums, out_ref.at[way], kept).wait()

    if ways == 2:
        remote(sums, out_ref.at[way], side_send, kept, beside).wait_send()
        remote(sums, out_ref.at[1 - way], kept, side_recv, beside).wait_recv()


def chain_sum(part, collective_id):
    ways, size = split_ways(), lax.axis_size("hid")
    rows, columns = part.shape
    depth = max(16, CHUNK // columns)
    count = rows // depth
    return pl.pallas_call(
        functools.partial(chain_kernel, ways, size // ways),
        out_shape=jax.ShapeDtypeStruct((ways, count, depth, columns), low),
        in_specs=[pl.BlockSpec(memory_space=pltpu.VMEM)],
        out_specs=pl.BlockSpec(memory_space=pl.ANY),
        scratch_shapes=[
            pltpu.VMEM((count, depth, columns), low),
            pltpu.VMEM((count, depth, columns), low),
            pltpu.SemaphoreType.DMA,
            pltpu.SemaphoreType.DMA((count,)),
            pltpu.SemaphoreType.DMA,
            pltpu.SemaphoreType.DMA((count,)),
            pltpu.SemaphoreType.DMA,
            pltpu.SemaphoreType.DMA,
            pltpu.SemaphoreType.DMA,
        ],
        compiler_params=pltpu.CompilerParams(
            collective_id=collective_id, has_side_effects=True, vmem_limit_bytes=48 << 20
        ),
        cost_estimate=pl.CostEstimate(
            flops=rows * columns, bytes_accessed=300 * rows * columns, transcendentals=0
        ),
    )(part.reshape(count, depth, columns))


def to_owner(values_in):
    dp, hid, ways = lax.axis_size("dp"), lax.axis_size("hid"), split_ways()
    index = lax.axis_index("dp") * ways + lax.axis_index("hid") % ways
    mine = lax.dynamic_index_in_dim(values_in, index, 1, keepdims=False)
    pairs = [
        (d * hid + t * ways + w, (t * dp + d) * ways + w)
        for d in range(dp)
        for t in range(hid // ways)
        for w in range(ways)
    ]
    return lax.ppermute(mine, ("dp", "hid"), pairs)


def rotate(values_in, cosine, sine):
    half = cosine.shape[1]
    front, back = values_in[:, :half], values_in[:, half : 2 * half]
    return jnp.concatenate(
        [
            front * cosine - back * sine,
            back * cosine + front * sine,
            values_in[:, 2 * half :],
        ],
        axis=1,
    )


def local(
    history,
    mix,
    segment_ids,
    norm_gains,
    w_query,
    w_key,
    w_value,
    w_out,
    w_up,
    w_down,
    w_mixer,
    mixer_out,
    mix_static,
    out_cotangent,
    mix_cotangent,
):
    dp, hid, ways = lax.axis_size("dp"), lax.axis_size("hid"), split_ways()
    places = hid // ways
    my_hid = lax.axis_index("hid")
    place, way = my_hid // ways, my_hid % ways
    block = segment_ids.shape[0]
    total_tokens = block * dp * hid
    row = total_tokens // dp
    group = total_tokens // places
    rows = group // row
    piece = history.shape[2]
    mine = piece * places
    feats = piece * hid
    width = feats * dp
    heads = HEADS // dp // ways
    n_mix = mix.shape[1]
    n_cot = mix_cotangent.shape[1]

    def by_place(values_in):
        return jnp.stack(
            [values_in[..., p * group : (p + 1) * group] for p in range(places)], axis=0
        )

    stored = exchange(by_place(history.swapaxes(1, 2)))
    upstream = exchange(by_place(out_cotangent.T))
    upstream = upstream.reshape(mine, group).astype(full)

    table = jnp.concatenate(
        [mix.T, mix_cotangent.T, segment_ids.astype(full)[None]], axis=0
    )
    table = gather_all(table[None])
    table = lax.dynamic_slice_in_dim(table, place * dp * ways, dp * ways, 0)
    table = table.transpose(1, 0, 2).reshape(table.shape[1], group)
    mix_t = table[:n_mix]
    cot_t = table[n_mix : n_mix + n_cot]
    ids = table[-1].reshape(rows, row)

    there = jnp.arange(row, dtype=jnp.int32)
    same_doc = ids[:, :, None] == ids[:, None, :]
    doc_start = jnp.min(jnp.where(same_doc, there[None, None], row), axis=2)
    position = (there[None] - doc_start).astype(full).reshape(group)
    visible = same_doc & (there[None, None] <= there[None, :, None])
    frequency = rope_base ** (-jnp.arange(ROT // 2, dtype=full) * 2.0 / ROT)
    angle = frequency[:, None] * position[None, :]
    cosine, sine = jnp.cos(angle)[None], jnp.sin(angle)[None]

    streams = []
    for s in range(STREAMS):
        total = mix_t[s * HIST] * stored[:, 0].astype(full)
        for j in range(1, HIST):
            total = total + mix_t[s * HIST + j] * stored[:, j].astype(full)
        streams.append(total.reshape(mine, group))
    local_means = [jnp.mean(v, axis=0) for v in streams]
    local_devs = [jnp.sum(jnp.square(v - m), axis=0) for v, m in zip(streams, local_means)]
    moments = gather_dp(gather_ways(jnp.stack(local_means + local_devs, axis=0), 0))
    moments = moments.reshape((dp * ways,) + moments.shape[2:])
    mean_parts, dev_parts = moments[:, :STREAMS], moments[:, STREAMS:]
    means = jnp.sum(mean_parts, axis=0) / (dp * ways)
    variance = (
        jnp.sum(dev_parts, axis=0) + mine * jnp.sum(jnp.square(mean_parts - means), axis=0)
    ) / width
    inv_scales = lax.rsqrt(variance + 1e-05)

    def own_rows(values_in):
        parts = values_in.reshape((places, ways, piece) + values_in.shape[1:])
        part = lax.dynamic_index_in_dim(parts, way, 1, keepdims=False)
        return part.reshape((mine,) + values_in.shape[1:])

    def all_rows(values_in):
        parts = values_in.reshape((places, piece) + values_in.shape[1:])
        return gather_ways(parts, 1).reshape((feats,) + values_in.shape[1:])

    own_gains = own_rows(norm_gains).astype(full)
    gains = [own_gains[:, s][:, None] for s in range(STREAMS)]
    units = [(streams[s] - means[s]) * inv_scales[s] for s in range(STREAMS)]
    normed = [all_rows((units[s] * gains[s]).astype(low)) for s in range(STREAMS)]

    def project(weight, left):
        columns = weight.shape[1] // dp // ways

        def make(index):
            start = (index * ways + way) * columns
            part = lax.dynamic_slice_in_dim(weight, start, columns, 1)
            return contract(part, left, 0, 0)

        return scatter_dp(make)

    def way_columns(weight):
        if ways == 1:
            return weight
        size = weight.shape[1] // dp // ways
        parts = [weight[:, i * size : (i + 1) * size] for i in range(dp * ways)]
        pairs = zip(parts[::2], parts[1::2])
        return jnp.concatenate([jnp.where(way == 0, a, b) for a, b in pairs], axis=1)

    def way_rows(weight):
        size = weight.shape[0] // ways
        return lax.dynamic_slice_in_dim(weight, way * size, size, 0)

    def by_head(values_in):
        return values_in.reshape(heads, HEAD, group)

    queries = rotate(by_head(project(w_query, normed[0])), cosine, sine).astype(low)
    keys = rotate(by_head(project(w_key, normed[1])), cosine, sine).astype(low)
    values = by_head(project(w_value, normed[2])).astype(low)
    hidden = project(w_up, normed[3])

    def by_row(values_in):
        if rows == 1:
            return values_in
        return (
            values_in.reshape(heads, HEAD, rows, row)
            .transpose(0, 2, 1, 3)
            .reshape(heads * rows, HEAD, row)
        )

    def from_row(values_in):
        if rows == 1:
            return values_in
        return (
            values_in.reshape(heads, rows, HEAD, row)
            .transpose(0, 2, 1, 3)
            .reshape(heads, HEAD, group)
        )

    q_rows, k_rows, v_rows = by_row(queries), by_row(keys), by_row(values)
    score_scale = 1.0 / math.sqrt(HEAD)
    scores = batched(q_rows, k_rows, 1, 1) * score_scale
    mask = jnp.broadcast_to(visible[None], (heads, rows, row, row)).reshape(scores.shape)
    scores = jnp.where(mask, scores, -1e30)
    probs = jax.nn.softmax(scores, axis=-1)
    probs_low = probs.astype(low)
    attended = from_row(batched(v_rows, probs_low, 2, 2).astype(low)).reshape(heads * HEAD, group)

    active, hidden_pull = jax.vjp(gelu_exact, hidden)
    active = active.astype(low)
    (slope,) = hidden_pull(jnp.ones_like(hidden))
    out_rows, down_rows = way_rows(w_out), way_rows(w_down)

    def make_out(index):
        start = index * feats
        left = lax.dynamic_slice_in_dim(out_rows, start, feats, 1)
        other = lax.dynamic_slice_in_dim(down_rows, start, feats, 1)
        return contract(left, attended, 0, 0) + contract(other, active, 0, 0)

    branches = scatter_dp(make_out).reshape(places, ways, piece, group)
    kept = lax.dynamic_index_in_dim(branches, way, 1, keepdims=False)
    if ways == 2:
        given = lax.dynamic_index_in_dim(branches, 1 - way, 1, keepdims=False).astype(low)
        kept = kept + hid_swap(given, 1).astype(full)
    output = streams[3] + kept.reshape(mine, group)
    output_rounded = output.astype(low)

    block_output = exchange(output_rounded.reshape(places, piece, group))
    block_output = block_output.transpose(1, 0, 2).reshape(piece, total_tokens).T

    square = jnp.sum(output * output, axis=0, keepdims=True)
    mixer_rows = own_rows(w_mixer)
    mixer_part = contract(mixer_rows, output_rounded, 0, 0)
    sums = sum_features(jnp.concatenate([mixer_part, square], axis=0))
    inv_rms = lax.rsqrt(sums[-1] / width + 1e-06)
    inner_raw = sums[:-1]
    inner_pre = inner_raw * inv_rms
    inner_act, inner_pull = jax.vjp(gelu_exact, inner_pre)
    raw_mix = contract_high(mixer_out, inner_act, 0, 0)
    column = jnp.stack(
        [
            jnp.sum(raw_mix, axis=1),
            jnp.sum(raw_mix * raw_mix, axis=1),
            jnp.sum(cot_t, axis=1),
            jnp.sum(cot_t * raw_mix, axis=1),
        ],
        axis=0,
    )
    act_total = jnp.sum(inner_act, axis=1)
    act_cot = contract_high(inner_act, cot_t, 1, 1)
    act_raw = contract_high(inner_act, raw_mix, 1, 1)
    n_inner = act_total.shape[0]
    flat = sum_tokens(
        jnp.concatenate([column.reshape(-1), act_total, act_cot.reshape(-1), act_raw.reshape(-1)])
    )
    sum_raw, sum_square, sum_grad, sum_grad_raw = flat[: 4 * n_cot].reshape(4, n_cot)
    start = 4 * n_cot
    act_total = flat[start : start + n_inner]
    start += n_inner
    act_cot = flat[start : start + n_inner * n_cot].reshape(n_inner, n_cot)
    start += n_inner * n_cot
    act_raw = flat[start:].reshape(n_inner, n_cot)
    average = sum_raw / total_tokens
    variance_mix = sum_square / total_tokens - average * average
    inv_spread = lax.rsqrt(variance_mix + 1e-05)
    unit_mix = (raw_mix - average[:, None]) * inv_spread[:, None]
    mix_next = mix_static[:, None] + unit_mix
    mix_next = to_owner(mix_next.reshape(n_cot, dp * ways, block)).T
    mean_grad = sum_grad / total_tokens
    sum_grad_unit = inv_spread * (sum_grad_raw - average * sum_grad)
    mean_grad_unit = sum_grad_unit / total_tokens
    raw_grad = inv_spread[:, None] * (
        cot_t - mean_grad[:, None] - unit_mix * mean_grad_unit[:, None]
    )
    act_unit = inv_spread[None, :] * (act_raw - act_total[:, None] * average[None, :])
    mixer_out_grad = inv_spread[None, :] * (
        act_cot - act_total[:, None] * mean_grad[None, :] - act_unit * mean_grad_unit[None, :]
    )
    act_grad = contract_high(mixer_out, raw_grad, 1, 0)
    inner_low = inner_pull(act_grad)[0].astype(low)
    scaled = (output * inv_rms).astype(low)
    mixer_grad_part = contract(inner_low, scaled, 1, 1)
    scaled_grad = contract(mixer_rows, inner_low, 1, 0)
    along = jnp.sum(inner_low.astype(full) * inner_raw, axis=0) / width
    output_grad = upstream + inv_rms * scaled_grad - output * (inv_rms * inv_rms * inv_rms) * along
    output_low = gather_dp(all_rows(output_grad.astype(low))).reshape(width, group)

    branch_part = jnp.concatenate(
        [
            contract(attended, output_low, 1, 1).astype(low),
            contract(active, output_low, 1, 1).astype(low),
        ],
        axis=0,
    )
    hidden_low = (contract(down_rows, output_low, 1, 0) * slope).astype(low)

    attended_grad = contract(out_rows, output_low, 1, 0).astype(low)
    a_rows = by_row(by_head(attended_grad))
    prob_grad = batched(a_rows, v_rows, 1, 1)
    row_total = jnp.sum(probs * prob_grad, axis=-1, keepdims=True)
    score_grad = (probs * (prob_grad - row_total)).astype(low)
    query_grad = from_row(batched(k_rows, score_grad, 2, 2) * score_scale)
    key_grad = from_row(batched(q_rows, score_grad, 2, 1) * score_scale)
    value_grad = from_row(batched(a_rows, probs_low, 2, 1))
    query_low = rotate(query_grad, cosine, -sine).astype(low).reshape(heads * HEAD, group)
    key_low = rotate(key_grad, cosine, -sine).astype(low).reshape(heads * HEAD, group)
    value_low = value_grad.astype(low).reshape(heads * HEAD, group)

    lows_mine, hidden_mine = (query_low, key_low, value_low), hidden_low
    branch_part, hidden_mine, lows_mine = lax.optimization_barrier(
        (branch_part, hidden_mine, lows_mine)
    )
    hidden_all = gather_dp(hidden_mine).reshape(-1, group)
    lows = [gather_dp(v).reshape(-1, group) for v in lows_mine]
    branch_sum = chain_sum(branch_part, 0)
    n_out = out_rows.shape[0] // branch_sum.shape[2]
    w_out_grad = branch_sum[:, :n_out].astype(full).reshape(w_out.shape)
    w_down_grad = branch_sum[:, n_out:].astype(full).reshape(w_down.shape)

    def unsplit(total, weight):
        total = total.reshape(ways, weight.shape[0], -1)
        size = total.shape[2] // dp
        parts = [total[w, :, d * size : (d + 1) * size] for d in range(dp) for w in range(ways)]
        return jnp.concatenate([v.astype(full) for v in parts], axis=1)

    up_part = contract(normed[3], hidden_all, 1, 1).astype(low)
    w_up_grad = unsplit(chain_sum(up_part, 1), w_up)
    parts = [contract(normed[s], lows[s], 1, 1).astype(low) for s in range(3)]
    head_sum = chain_sum(jnp.concatenate(parts, axis=0), 2)
    head_sum = head_sum.reshape(ways, 3, -1, head_sum.shape[2], head_sum.shape[3])
    w_query_grad, w_key_grad, w_value_grad = [
        unsplit(head_sum[:, s], w) for s, w in enumerate((w_query, w_key, w_value))
    ]

    normed_grads = []
    for s, weight in enumerate((w_query, w_key, w_value, w_up)):
        right = lows[s] if s < 3 else hidden_all
        part = contract(way_columns(weight), right, 1, 0).reshape(places, ways, piece, group)
        kept = lax.dynamic_index_in_dim(part, way, 1, keepdims=False)
        if ways == 2:
            given = lax.dynamic_index_in_dim(part, 1 - way, 1, keepdims=False).astype(low)
            kept = kept + hid_swap(given, 1).astype(full)
        normed_grads.append(kept.reshape(mine, group))
    weighted = [normed_grads[s] * gains[s] for s in range(STREAMS)]
    means_back = sum_features(
        jnp.stack(
            [jnp.sum(e, axis=0) for e in weighted]
            + [jnp.sum(e * u, axis=0) for e, u in zip(weighted, units)],
            axis=0,
        )
    ) / width
    gain_parts = [jnp.sum(g * u, axis=1) for g, u in zip(normed_grads, units)]
    stream_grads = [
        (weighted[s] - means_back[s] - units[s] * means_back[STREAMS + s]) * inv_scales[s]
        for s in range(STREAMS)
    ]
    stream_grads[3] = stream_grads[3] + output_grad
    smalls = sum_tokens(jnp.concatenate([mixer_grad_part, jnp.stack(gain_parts, axis=0)], axis=0))
    smalls = gather_ways(smalls.reshape(-1, places, piece), 2).reshape(-1, feats)
    w_mixer_grad = smalls[:n_inner].T
    norm_gains_grad = smalls[n_inner:].T

    split = [v.reshape(places, piece, group) for v in stream_grads]
    layers = []
    for j in range(HIST):
        total = mix_t[j] * split[0]
        for s in range(1, STREAMS):
            total = total + mix_t[s * HIST + j] * split[s]
        layers.append(total.astype(low))
    history_grad = exchange(jnp.stack(layers, axis=1))
    history_grad = (
        history_grad.transpose(1, 2, 0, 3)
        .reshape(HIST, piece, total_tokens)
        .astype(full)
        .swapaxes(1, 2)
    )
    mix_parts = jnp.stack(
        [
            jnp.sum(split[s] * stored[:, j].astype(full), axis=(0, 1))
            for s in range(STREAMS)
            for j in range(HIST)
        ],
        axis=0,
    )
    mix_grad = to_owner(sum_features(mix_parts).reshape(n_mix, dp * ways, block)).T

    return (
        block_output,
        mix_next,
        history_grad,
        mix_grad,
        norm_gains_grad,
        w_query_grad,
        w_key_grad,
        w_value_grad,
        w_out_grad,
        w_up_grad,
        w_down_grad,
        w_mixer_grad,
        mixer_out_grad,
        sum_grad,
    )


def solution(mesh):
    everywhere = ("dp", "hid")
    placed = (
        P(None, None, everywhere),
        P(everywhere, None),
        P(everywhere),
        P("dp", None),
        P("dp", None),
        P("dp", None),
        P("dp", None),
        P("dp", None),
        P("dp", None),
        P("dp", None),
        P("dp", None),
        P(),
        P(),
        P(None, everywhere),
        P(everywhere, None),
    )
    return jax.shard_map(
        local,
        mesh=mesh,
        in_specs=placed,
        out_specs=(
            P(None, everywhere),
            P(everywhere, None),
            P(None, None, everywhere),
            P(everywhere, None),
            P("dp", None),
            P("dp", None),
            P("dp", None),
            P("dp", None),
            P("dp", None),
            P("dp", None),
            P("dp", None),
            P("dp", None),
            P(),
            P(),
        ),
        check_vma=False,
    )
```

time: 2880 us -> 1240 us (0.43)
  waiting for transfers between devices: 1980 us -> 278 us
  Pallas kernels: 0 us -> 475 us
  blocking collectives: 340 us -> 0 us
  matrix products: 227 us -> 131 us
  local copies, waits for them, and re-layouts: 175 us -> 106 us
  other arithmetic: 96.7 us -> 152 us
  starting transfers between devices: 31.6 us -> 77 us
    psum x1 -> x0, waiting for transfers between devices: 642 us -> none  [reduce_rows(): lax.psum(shares[0].astype(jnp.bfloat16), 'hid').astype(jnp.float32)]
    unnamed x23 -> x0, waiting for transfers between devices: 541 us -> none
    all_gather x8 -> x0, waiting for transfers between devices: 501 us -> none  [the longest x1 197 us: local(): lax.all_gather(w_up, 'dp', axis=0, tiled=True)]
    pallas_call x0 -> x3, Pallas kernels: none -> 475 us  [chain_sum(): pl.pallas_call(functools.partial(chain_kernel, ways, size // ways), out_s...]
    ppermute x0 -> x59, waiting for transfers between devices: none -> 265 us  [the longest x5 102 us: gather_all(): other = lax.ppermute(values_in, axis, [(i, i ^ bit) for i in range(size)])]
    psum x3 -> x0, blocking collectives: 247 us -> none  [the longest x1 165 us: reduce_rows(): lax.psum(shares[3].astype(jnp.bfloat16), 'hid').astype(jnp.float32)]
    reduce_scatter x5 -> x0, waiting for transfers between devices: 191 us -> none  [the longest x1 74.9 us: reduce_rows(): lax.psum_scatter(parts[1].astype(jnp.bfloat16), 'dp', scatter_dimension=0...]
    dot_general x30 -> x48, matrix products: 218 us -> 122 us  [the longest x39 109 us: contract(): lax.dot_general(left, right, (((left_dim,), (right_dim,)), ((), ())), pre...]
  transfers between devices with their start and end apart: 23 -> 63, of which waited for: 15 -> 30; matrix products, arithmetic and copies ran while one was open for 14% -> 21% of each run, Pallas kernels for 0% -> 39%
where the time goes in v1:
time: 1240 us; the launch traced here: 1220 us
  Pallas kernels  475 us (38%)
  waiting for transfers between devices  278 us (22%)
  other arithmetic  152 us (12%)
  matrix products  131 us (11%)
  local copies, waits for them, and re-layouts  106 us (9%)
  starting transfers between devices  77 us (6%)
    pallas_call x3, Pallas kernels, chain_sum(): pl.pallas_call(functools.partial(chain_kernel, ways, size // ways), out_s...  475 us
    dot_general x39, matrix products, contract(): lax.dot_general(left, right, (((left_dim,), (right_dim,)), ((), ())), pre...  109 us
    ppermute x5, waiting for transfers between devices, gather_all(): other = lax.ppermute(values_in, axis, [(i, i ^ bit) for i in range(size)])  102 us
    ppermute x14, waiting for transfers between devices, outer_shift(): return lax.ppermute(values_in, 'dp', pairs)  84.3 us
    ppermute x19, waiting for transfers between devices, hid_swap(): return lax.ppermute(values_in, 'hid', [(i, i ^ bit) for i in range(size)])  76.3 us
    unnamed x440, local copies, waits for them, and re-layouts  45.1 us
  transfers between devices with their start and end apart: 63, of which 30 were waited for; matrix products, arithmetic and copies ran while one was open for 21% of the time, Pallas kernels for 39%

profile of v1, /device:TPU:0, one launch (start us, length us, event | category | flops | bytes accessed | tf_op | source)
XLA Modules:
  0.0 1224.3 jit_solution(14436976633909237894)
XLA Ops:
  18.6 63.0 %collective-permute-done.1 = f32[2,69,128]{2,1,0:T(8,128)S(1)} collective-permute-done((f32[2,69,128]{2,1,0:T(8,128)S(1)}, f32[2,69,128]{2,1,0:T(8,128)S(1)}, u32[]{:S(2)}, u32[]{:S(2)}) %collective-permute-start.1) | collective-permute-done | bytes 70688 | tf_op jit(solution)/shard_map/ppermute | solution.py:135
  86.6 25.5 %collective-permute-done.2 = f32[4,69,128]{2,1,0:T(8,128)S(1)} collective-permute-done((f32[4,69,128]{2,1,0:T(8,128)S(1)}, f32[4,69,128]{2,1,0:T(8,128)S(1)}, u32[]{:S(2)}, u32[]{:S(2)}) %collective-permute-start.2) | collective-permute-done | bytes 141344 | tf_op jit(solution)/shard_map/ppermute | solution.py:135
  120.3 9.5 collective-permute-done.4
  178.6 8.8 collective-permute-done.8
  198.6 10.8 collective-permute-done.20
  280.0 8.8 fusion.376
  293.8 19.7 %collective-permute-done.22 = bf16[1024,1024]{1,0:T(8,128)(2,1)} collective-permute-done((bf16[1024,1024]{1,0:T(8,128)(2,1)}, bf16[1024,1024]{1,0:T(8,128)(2,1)}, u32[]{:S(2)}, u32[]{:S(2)}) %collective-permute-start.22) | collective-permute-done | bytes 2097184 | tf_op jit(solution)/shard_map/ppermute | solution.py:63
  313.5 13.7 %multiply_convert_fusion.2 = (bf16[1024,1024]{1,0:T(8,128)(2,1)S(1)}, f32[1024,1024]{1,0:T(8,128)}, f32[1024,1024]{1,0:T(8,128)}) fusion(bf16[1024,1024]{1,0:T(8,128)(2,1)} %collective-permute-done.23, bf16[512,1024]{1,0:T(8,128)(2,1)S(1)} %bitcast.1563, bf16[512,8192]{1,0:T(8,128)(2,1)} %param.23, s32[]{:T(128)S(6)} %select_n.682, ...), kind=kOutput, calls=%fused_computation.22 | convolution fusion | flops 1146093568 | bytes 16777220 | tf_op jit(solution)/shard_map/dot_general | solution.py:27
  345.8 19.5 %collective-permute-done.25 = bf16[512,1024]{1,0:T(8,128)(2,1)} collective-permute-done((bf16[512,1024]{1,0:T(8,128)(2,1)}, bf16[512,1024]{1,0:T(8,128)(2,1)}, u32[]{:S(2)}, u32[]{:S(2)}) %collective-permute-start.25) | collective-permute-done | bytes 1048608 | tf_op jit(solution)/shard_map/ppermute | solution.py:63
  372.7 10.4 collective-permute-done.27
  414.2 8.0 collective-permute-done.32
  427.7 12.0 collective-permute-done.34
  445.7 19.2 %collective-permute-done.35 = bf16[512,1024]{1,0:T(8,128)(2,1)S(1)} collective-permute-done((bf16[512,1024]{1,0:T(8,128)(2,1)S(1)}, bf16[512,1024]{1,0:T(8,128)(2,1)S(1)}, u32[]{:S(2)}, u32[]{:S(2)}) %collective-permute-start.35) | collective-permute-done | bytes 1048608 | tf_op jit(solution)/shard_map/ppermute | solution.py:63
  480.1 12.8 %all-to-all-done.1 = bf16[4,64,1024]{2,1,0:T(8,128)(2,1)} async-done(((bf16[4,64,1024]{2,1,0:T(8,128)(2,1)}), bf16[4,64,1024]{2,1,0:T(8,128)(2,1)}, u32[]{:S(2)}, u32[]{:S(2)}) %all-to-all-start.1) | async-done | bytes 524320 | tf_op jit(solution)/shard_map/all_to_all | solution.py:163
  523.4 11.2 multiply_convert_fusion.1
  538.9 158.2 %shard_map.255 = bf16[2,40,32,2048]{3,2,1,0:T(8,128)(2,1)} custom-call(bf16[40,32,2048]{2,1,0:T(8,128)(2,1)S(1)} %bitcast.1456), custom_call_target="tpu_custom_call" | custom-call | flops 2621440 | bytes 786432000 | tf_op jit(solution)/shard_map/pallas_call | solution.py:307
  697.0 8.4 slice.899
  705.5 11.7 bitcast_convert_fusion
  748.0 114.0 %shard_map.254 = bf16[2,24,64,1024]{3,2,1,0:T(8,128)(2,1)} custom-call(bf16[24,64,1024]{2,1,0:T(8,128)(2,1)S(1)} %bitcast.1457), custom_call_target="tpu_custom_call" | custom-call | flops 1572864 | bytes 471859200 | tf_op jit(solution)/shard_map/pallas_call | solution.py:307
  880.3 7.9 copy.251
  901.1 8.4 collective-permute-done.48
  962.2 8.1 convolution_convert_fusion
  970.3 202.7 %shard_map.256 = bf16[2,32,16,4096]{3,2,1,0:T(8,128)(2,1)} custom-call(bf16[32,16,4096]{2,1,0:T(8,128)(2,1)S(1)} %bitcast.1458), custom_call_target="tpu_custom_call" | custom-call | flops 2097152 | bytes 629145600 | tf_op jit(solution)/shard_map/pallas_call | solution.py:307
  1196.1 11.7 concatenate.91
  (831 shorter events, 435.2 us)
Async XLA Ops:
  6.0 126.1 %all-to-all-start = ((bf16[4,8,64,1024]{3,2,1,0:T(8,128)(2,1)}), bf16[4,8,64,1024]{3,2,1,0:T(8,128)(2,1)}, u32[]{:S(2)}, u32[]{:S(2)}) async-start(bf16[4,8,64,1024]{3,2,1,0:T(8,128)(2,1)} %pad_maximum_fusion.2), calls=%async_computation | async-start | bytes 8388608 | tf_op jit(solution)/shard_map/all_to_all | solution.py:163
  16.6 65.1 %collective-permute-start.1 = (f32[2,69,128]{2,1,0:T(8,128)S(1)}, f32[2,69,128]{2,1,0:T(8,128)S(1)}, u32[]{:S(2)}, u32[]{:S(2)}) collective-permute-start(f32[2,69,128]{2,1,0:T(8,128)S(1)} %maximum_bitcast_fusion), channel_id=1, source_target_pairs={{0,2},{1,3},{2,0},{3,1},{4,6},{5,7},{6,4},{7,5},{8,10},{9,11},{10,... | collective-permute-start | bytes 211976 | tf_op jit(solution)/shard_map/ppermute | solution.py:135
  81.7 30.4 %collective-permute-start.2 = (f32[4,69,128]{2,1,0:T(8,128)S(1)}, f32[4,69,128]{2,1,0:T(8,128)S(1)}, u32[]{:S(2)}, u32[]{:S(2)}) collective-permute-start(f32[4,69,128]{2,1,0:T(8,128)S(1)} %bitcast.1571), channel_id=1, source_target_pairs={{0,4},{1,5},{2,6},{3,7},{4,0},{5,1},{6,2},{7,3},{8,12},{9,13},{10,... | collective-permute-start | bytes 423944 | tf_op jit(solution)/shard_map/ppermute | solution.py:135
  172.3 26.3 %collective-permute-start.16 = (bf16[4,64,1024]{2,1,0:T(8,128)(2,1)S(1)}, bf16[4,64,1024]{2,1,0:T(8,128)(2,1)S(1)}, u32[]{:S(2)}, u32[]{:S(2)}) collective-permute-start(bf16[4,64,1024]{2,1,0:T(8,128)(2,1)S(1)} %get-tuple-element.108), channel_id=1, source_target_pairs={{0,1},{1,0},{2,3},{3,2},{4,5},{5,4},{6,7},{7,6},{8,9},{9,8},{10,11... | collective-permute-start | bytes 1572872 | tf_op jit(solution)/shard_map/ppermute | solution.py:68
  178.2 31.3 %collective-permute-start.20 = (bf16[4,64,1024]{2,1,0:T(8,128)(2,1)S(1)}, bf16[4,64,1024]{2,1,0:T(8,128)(2,1)S(1)}, u32[]{:S(2)}, u32[]{:S(2)}) collective-permute-start(bf16[4,64,1024]{2,1,0:T(8,128)(2,1)S(1)} %get-tuple-element.104), channel_id=1, source_target_pairs={{0,1},{1,0},{2,3},{3,2},{4,5},{5,4},{6,7},{7,6},{8,9},{9,8},{10,11... | collective-permute-start | bytes 1572872 | tf_op jit(solution)/shard_map/ppermute | solution.py:68
  188.7 32.9 %collective-permute-start.13 = (bf16[256,1024]{1,0:T(8,128)(2,1)S(1)}, bf16[256,1024]{1,0:T(8,128)(2,1)S(1)}, u32[]{:S(2)}, u32[]{:S(2)}) collective-permute-start(bf16[256,1024]{1,0:T(8,128)(2,1)S(1)} %convolution_convert_fusion.11), channel_id=1, source_target_pairs={{0,8},{8,0},{16,24},{24,16},{1,9},{9,1},{17,25},{25,17},{2,10},{10... | collective-permute-start | bytes 1572872 | tf_op jit(solution)/shard_map/ppermute | solution.py:54
  188.7 40.0 %collective-permute-start.15 = (bf16[256,1024]{1,0:T(8,128)(2,1)S(1)}, bf16[256,1024]{1,0:T(8,128)(2,1)S(1)}, u32[]{:S(2)}, u32[]{:S(2)}) collective-permute-start(bf16[256,1024]{1,0:T(8,128)(2,1)S(1)} %convolution_convert_fusion.10), channel_id=1, source_target_pairs={{0,8},{8,0},{16,24},{24,16},{1,9},{9,1},{17,25},{25,17},{2,10},{10... | collective-permute-start | bytes 1572872 | tf_op jit(solution)/shard_map/ppermute | solution.py:54
  191.1 31.5 %collective-permute-start.9 = (bf16[256,1024]{1,0:T(8,128)(2,1)S(1)}, bf16[256,1024]{1,0:T(8,128)(2,1)S(1)}, u32[]{:S(2)}, u32[]{:S(2)}) collective-permute-start(bf16[256,1024]{1,0:T(8,128)(2,1)S(1)} %convolution_convert_fusion.13), channel_id=1, source_target_pairs={{0,8},{8,0},{16,24},{24,16},{1,9},{9,1},{17,25},{25,17},{2,10},{10... | collective-permute-start | bytes 1572872 | tf_op jit(solution)/shard_map/ppermute | solution.py:54
  198.6 72.3 %collective-permute-start.11 = (bf16[256,1024]{1,0:T(8,128)(2,1)}, bf16[256,1024]{1,0:T(8,128)(2,1)}, u32[]{:S(2)}, u32[]{:S(2)}) collective-permute-start(bf16[256,1024]{1,0:T(8,128)(2,1)} %convolution_convert_fusion.12), channel_id=1, source_target_pairs={{0,8},{8,0},{16,24},{24,16},{1,9},{9,1},{17,25},{25,17},{2,10},{10... | collective-permute-start | bytes 1572872 | tf_op jit(solution)/shard_map/ppermute | solution.py:54
  221.6 42.9 %collective-permute-start.21 = (bf16[1024,1024]{1,0:T(8,128)(2,1)}, bf16[1024,1024]{1,0:T(8,128)(2,1)}, u32[]{:S(2)}, u32[]{:S(2)}) collective-permute-start(bf16[1024,1024]{1,0:T(8,128)(2,1)} %convolution_convert_fusion.4), channel_id=1, source_target_pairs={{0,8},{8,0},{16,24},{24,16},{1,9},{9,1},{17,25},{25,17},{2,10},{10... | collective-permute-start | bytes 6291464 | tf_op jit(solution)/shard_map/ppermute | solution.py:54
  228.7 65.0 %collective-permute-start.23 = (bf16[1024,1024]{1,0:T(8,128)(2,1)}, bf16[1024,1024]{1,0:T(8,128)(2,1)}, u32[]{:S(2)}, u32[]{:S(2)}) collective-permute-start(bf16[1024,1024]{1,0:T(8,128)(2,1)} %convolution_convert_fusion.3), channel_id=1, source_target_pairs={{0,8},{8,0},{16,24},{24,16},{1,9},{9,1},{17,25},{25,17},{2,10},{10... | collective-permute-start | bytes 6291464 | tf_op jit(solution)/shard_map/ppermute | solution.py:54
  244.7 26.2 %collective-permute-start.10 = (bf16[256,1024]{1,0:T(8,128)(2,1)}, bf16[256,1024]{1,0:T(8,128)(2,1)}, u32[]{:S(2)}, u32[]{:S(2)}) collective-permute-start(bf16[256,1024]{1,0:T(8,128)(2,1)} %add_convert_fusion.18), channel_id=1, source_target_pairs={{0,16},{8,24},{16,0},{24,8},{1,17},{9,25},{17,1},{25,9},{2,18},{10... | collective-permute-start | bytes 1572872 | tf_op jit(solution)/shard_map/ppermute | solution.py:63
  269.3 44.2 %collective-permute-start.22 = (bf16[1024,1024]{1,0:T(8,128)(2,1)}, bf16[1024,1024]{1,0:T(8,128)(2,1)}, u32[]{:S(2)}, u32[]{:S(2)}) collective-permute-start(bf16[1024,1024]{1,0:T(8,128)(2,1)} %add_convert_fusion), channel_id=1, source_target_pairs={{0,16},{8,24},{16,0},{24,8},{1,17},{9,25},{17,1},{25,9},{2,18},{10... | collective-permute-start | bytes 6291464 | tf_op jit(solution)/shard_map/ppermute | solution.py:63
  340.0 25.3 %collective-permute-start.25 = (bf16[512,1024]{1,0:T(8,128)(2,1)}, bf16[512,1024]{1,0:T(8,128)(2,1)}, u32[]{:S(2)}, u32[]{:S(2)}) collective-permute-start(bf16[512,1024]{1,0:T(8,128)(2,1)} %add_convert_fusion.2), channel_id=1, source_target_pairs={{0,16},{8,24},{16,0},{24,8},{1,17},{9,25},{17,1},{25,9},{2,18},{10... | collective-permute-start | bytes 3145736 | tf_op jit(solution)/shard_map/ppermute | solution.py:63
  402.4 21.2 %all-to-all-start.2 = ((bf16[4,64,1024]{2,1,0:T(8,128)(2,1)}), bf16[4,64,1024]{2,1,0:T(8,128)(2,1)}, u32[]{:S(2)}, u32[]{:S(2)}) async-start(bf16[4,64,1024]{2,1,0:T(8,128)(2,1)} %pad_maximum_fusion.27), calls=%async_computation.2 | async-start | bytes 1048576 | tf_op jit(solution)/shard_map/all_to_all | solution.py:163
  441.2 23.7 %collective-permute-start.35 = (bf16[512,1024]{1,0:T(8,128)(2,1)S(1)}, bf16[512,1024]{1,0:T(8,128)(2,1)S(1)}, u32[]{:S(2)}, u32[]{:S(2)}) collective-permute-start(bf16[512,1024]{1,0:T(8,128)(2,1)S(1)} %bitcast.1532), channel_id=1, source_target_pairs={{0,16},{8,24},{16,0},{24,8},{1,17},{9,25},{17,1},{25,9},{2,18},{10... | collective-permute-start | bytes 3145736 | tf_op jit(solution)/shard_map/ppermute | solution.py:63
  467.6 27.1 %collective-permute-start.36 = (bf16[2,512,1024]{2,1,0:T(8,128)(2,1)}, bf16[2,512,1024]{2,1,0:T(8,128)(2,1)}, u32[]{:S(2)}, u32[]{:S(2)}) collective-permute-start(bf16[2,512,1024]{2,1,0:T(8,128)(2,1)} %pad_maximum_fusion.7), channel_id=1, source_target_pairs={{0,8},{8,0},{16,24},{24,16},{1,9},{9,1},{17,25},{25,17},{2,10},{10... | collective-permute-start | bytes 6291464 | tf_op jit(solution)/shard_map/ppermute | solution.py:54
  535.2 184.0 %collective-permute-start.37 = (bf16[256,1024]{1,0:T(8,128)(2,1)}, bf16[256,1024]{1,0:T(8,128)(2,1)S(1)}, u32[]{:S(2)}, u32[]{:S(2)}) collective-permute-start(bf16[256,1024]{1,0:T(8,128)(2,1)} %bitcast.156), channel_id=1, source_target_pairs={{0,16},{8,24},{16,0},{24,8},{1,17},{9,25},{17,1},{25,9},{2,18},{10... | collective-permute-start | bytes 1572872 | tf_op jit(solution)/shard_map/ppermute | solution.py:63
  536.8 186.3 %collective-permute-start.40 = (bf16[256,1024]{1,0:T(8,128)(2,1)S(1)}, bf16[256,1024]{1,0:T(8,128)(2,1)S(1)}, u32[]{:S(2)}, u32[]{:S(2)}) collective-permute-start(bf16[256,1024]{1,0:T(8,128)(2,1)S(1)} %bitcast.1544), channel_id=1, source_target_pairs={{0,16},{8,24},{16,0},{24,8},{1,17},{9,25},{17,1},{25,9},{2,18},{10... | collective-permute-start | bytes 1572872 | tf_op jit(solution)/shard_map/ppermute | solution.py:63
  537.3 324.7 %collective-permute-start.46 = (bf16[1024,1024]{1,0:T(8,128)(2,1)S(1)}, bf16[1024,1024]{1,0:T(8,128)(2,1)}, u32[]{:S(2)}, u32[]{:S(2)}) collective-permute-start(bf16[1024,1024]{1,0:T(8,128)(2,1)S(1)} %multiply_convert_fusion.1), channel_id=1, source_target_pairs={{0,16},{8,24},{16,0},{24,8},{1,17},{9,25},{17,1},{25,9},{2,18},{10... | collective-permute-start | bytes 6291464 | tf_op jit(solution)/shard_map/ppermute | solution.py:63
  732.6 164.4 %collective-permute-start.39 = (bf16[4,64,1024]{2,1,0:T(8,128)(2,1)}, bf16[4,64,1024]{2,1,0:T(8,128)(2,1)}, u32[]{:S(2)}, u32[]{:S(2)}) collective-permute-start(bf16[4,64,1024]{2,1,0:T(8,128)(2,1)} %fusion.214), channel_id=1, source_target_pairs={{0,1},{1,0},{2,3},{3,2},{4,5},{5,4},{6,7},{7,6},{8,9},{9,8},{10,11... | collective-permute-start | bytes 1572872 | tf_op jit(solution)/shard_map/ppermute | solution.py:68
  737.8 160.5 %collective-permute-start.42 = (bf16[4,64,1024]{2,1,0:T(8,128)(2,1)}, bf16[4,64,1024]{2,1,0:T(8,128)(2,1)}, u32[]{:S(2)}, u32[]{:S(2)}) collective-permute-start(bf16[4,64,1024]{2,1,0:T(8,128)(2,1)} %fusion.233), channel_id=1, source_target_pairs={{0,1},{1,0},{2,3},{3,2},{4,5},{5,4},{6,7},{7,6},{8,9},{9,8},{10,11... | collective-permute-start | bytes 1572872 | tf_op jit(solution)/shard_map/ppermute | solution.py:68
  741.9 157.8 %collective-permute-start.45 = (bf16[4,64,1024]{2,1,0:T(8,128)(2,1)}, bf16[4,64,1024]{2,1,0:T(8,128)(2,1)}, u32[]{:S(2)}, u32[]{:S(2)}) collective-permute-start(bf16[4,64,1024]{2,1,0:T(8,128)(2,1)} %fusion.234), channel_id=1, source_target_pairs={{0,1},{1,0},{2,3},{3,2},{4,5},{5,4},{6,7},{7,6},{8,9},{9,8},{10,11... | collective-permute-start | bytes 1572872 | tf_op jit(solution)/shard_map/ppermute | solution.py:68
  949.1 266.0 %all-to-all-start.3 = ((bf16[4,8,64,1024]{3,2,1,0:T(8,128)(2,1)}), bf16[4,8,64,1024]{3,2,1,0:T(8,128)(2,1)}, u32[]{:S(2)}, u32[]{:S(2)}) async-start(bf16[4,8,64,1024]{3,2,1,0:T(8,128)(2,1)} %copy.254), calls=%async_computation.3 | async-start | bytes 8388608 | tf_op jit(solution)/shard_map/all_to_all | solution.py:163
  (240 other events, 3997.2 us)

commit v2 on v1

--- a/solution.py
+++ b/solution.py
@@ -14,8 +14,8 @@
 HIST = 8
 STREAMS = 4
 CORES = 2
-CHUNK = 1 << 16
-SLACK = 5
+CHUNK = 1 << 15
+SLACK = 4
 
 highest = lax.Precision.HIGHEST
 rope_base = 10000.0
@@ -128,15 +128,10 @@
 
 
 def gather_all(values_in):
-    for axis in ("hid", "dp"):
-        size, me = lax.axis_size(axis), lax.axis_index(axis)
-        bit = 1
-        while bit < size:
-            other = lax.ppermute(values_in, axis, [(i, i ^ bit) for i in range(size)])
-            both = ordered(me // bit % 2 == 0, values_in, other, 0)
-            values_in = both.reshape((2 * values_in.shape[0],) + values_in.shape[1:])
-            bit *= 2
-    return values_in
+    count = lax.axis_size("dp") * lax.axis_size("hid")
+    copies = jnp.broadcast_to(values_in[None], (count,) + values_in.shape)
+    held = lax.all_to_all(copies, ("dp", "hid"), split_axis=0, concat_axis=0, tiled=True)
+    return held.transpose(1, 0, 2).reshape(values_in.shape[0], -1)
 
 
 def scatter_dp(make):
@@ -327,6 +322,51 @@
             flops=rows * columns, bytes_accessed=300 * rows * columns, transcendentals=0
         ),
     )(part.reshape(count, depth, columns))
+
+
+def assemble_kernel(ways, dp, own_ref, *refs):
+    halves, (up_ref, *head_refs, out_ref) = refs[:ways], refs[ways:]
+    wide = own_ref.shape[3]
+    size = up_ref.shape[1] // dp // ways
+    blocks = dp * size // wide
+    for w in range(ways):
+        for d in range(dp):
+            start = d * size
+            part = own_ref[w, start // wide, :, start % wide : start % wide + size]
+            place = (d * ways + w) * size
+            up_ref[:, place : place + size] = part.astype(full)
+        for s, ref in enumerate(head_refs):
+            own = wide // dp
+            for d in range(dp):
+                place = (d * ways + w) * own
+                part = own_ref[w, blocks + s, :, d * own : (d + 1) * own]
+                ref[:, place : place + own] = part.astype(full)
+    for w in range(ways):
+        out_ref[:, w * wide : (w + 1) * wide] = halves[w][0, 0].astype(full)
+
+
+def assemble(total, w_up):
+    ways, dp = split_ways(), lax.axis_size("dp")
+    blocks, rows, wide = total.shape[1:]
+    depth = min(64, rows // ways)
+    share = rows // ways // depth
+
+    def half_map(half):
+        return lambda i: (i // share, blocks - 1, half * share + i % share, 0)
+
+    widths = [w_up.shape[1]] + [ways * wide] * 4
+    return pl.pallas_call(
+        functools.partial(assemble_kernel, ways, dp),
+        grid=(rows // depth,),
+        out_shape=[jax.ShapeDtypeStruct((rows, n), full) for n in widths],
+        in_specs=[pl.BlockSpec((ways, blocks, depth, wide), lambda i: (0, 0, i, 0))]
+        + [pl.BlockSpec((1, 1, depth, wide), half_map(half)) for half in range(ways)],
+        out_specs=[pl.BlockSpec((depth, n), lambda i: (i, 0)) for n in widths],
+        compiler_params=pltpu.CompilerParams(vmem_limit_bytes=48 << 20),
+        cost_estimate=pl.CostEstimate(
+            flops=0, bytes_accessed=6 * total.size, transcendentals=0
+        ),
+    )(total, *[total] * ways)
 
 
 def to_owner(values_in):
@@ -394,18 +434,40 @@
             [values_in[..., p * group : (p + 1) * group] for p in range(places)], axis=0
         )
 
-    stored = exchange(by_place(history.swapaxes(1, 2)))
+    stored = history.swapaxes(1, 2)
+    mix_all = gather_all(mix.T)
+    own_means, own_devs, deviations = [], [], []
+    for s in range(STREAMS):
+        total = mix_all[s * HIST] * stored[0].astype(full)
+        for j in range(1, HIST):
+            total = total + mix_all[s * HIST + j] * stored[j].astype(full)
+        own_means.append(jnp.mean(total, axis=0))
+        off = total - own_means[s]
+        own_devs.append(jnp.sum(off * off, axis=0))
+        deviations.append(off.astype(low))
+    moments = exchange(by_place(jnp.stack(own_means + own_devs, axis=0)))
+    deviations[3] = exchange(by_place(deviations[3]))
+    for s in range(3):
+        deviations[s] = exchange(by_place(deviations[s]))
     upstream = exchange(by_place(out_cotangent.T))
     upstream = upstream.reshape(mine, group).astype(full)
 
-    table = jnp.concatenate(
-        [mix.T, mix_cotangent.T, segment_ids.astype(full)[None]], axis=0
-    )
-    table = gather_all(table[None])
-    table = lax.dynamic_slice_in_dim(table, place * dp * ways, dp * ways, 0)
-    table = table.transpose(1, 0, 2).reshape(table.shape[1], group)
-    mix_t = table[:n_mix]
-    cot_t = table[n_mix : n_mix + n_cot]
+    def join_moments(mean_parts, dev_parts, size):
+        mean = jnp.mean(mean_parts, axis=0)
+        spread = size * jnp.sum(jnp.square(mean_parts - mean), axis=0)
+        return mean, jnp.sum(dev_parts, axis=0) + spread
+
+    block_means = moments[:, :STREAMS]
+    joined = join_moments(block_means, moments[:, STREAMS:], piece)
+    joined = gather_dp(gather_ways(jnp.concatenate(joined, axis=0), 0))
+    joined = joined.reshape((dp * ways,) + joined.shape[2:])
+    means, variance = join_moments(joined[:, :STREAMS], joined[:, STREAMS:], mine)
+    inv_scales = lax.rsqrt(variance / width + 1e-05)
+    all_means = gather_ways(block_means, 1)
+
+    table = jnp.concatenate([mix_cotangent.T, segment_ids.astype(full)[None]], axis=0)
+    table = lax.dynamic_slice_in_dim(gather_all(table), place * group, group, 1)
+    cot_t = table[:n_cot]
     ids = table[-1].reshape(rows, row)
 
     there = jnp.arange(row, dtype=jnp.int32)
@@ -417,23 +479,6 @@
     angle = frequency[:, None] * position[None, :]
     cosine, sine = jnp.cos(angle)[None], jnp.sin(angle)[None]
 
-    streams = []
-    for s in range(STREAMS):
-        total = mix_t[s * HIST] * stored[:, 0].astype(full)
-        for j in range(1, HIST):
-            total = total + mix_t[s * HIST + j] * stored[:, j].astype(full)
-        streams.append(total.reshape(mine, group))
-    local_means = [jnp.mean(v, axis=0) for v in streams]
-    local_devs = [jnp.sum(jnp.square(v - m), axis=0) for v, m in zip(streams, local_means)]
-    moments = gather_dp(gather_ways(jnp.stack(local_means + local_devs, axis=0), 0))
-    moments = moments.reshape((dp * ways,) + moments.shape[2:])
-    mean_parts, dev_parts = moments[:, :STREAMS], moments[:, STREAMS:]
-    means = jnp.sum(mean_parts, axis=0) / (dp * ways)
-    variance = (
-        jnp.sum(dev_parts, axis=0) + mine * jnp.sum(jnp.square(mean_parts - means), axis=0)
-    ) / width
-    inv_scales = lax.rsqrt(variance + 1e-05)
-
     def own_rows(values_in):
         parts = values_in.reshape((places, ways, piece) + values_in.shape[1:])
         part = lax.dynamic_index_in_dim(parts, way, 1, keepdims=False)
@@ -443,10 +488,20 @@
         parts = values_in.reshape((places, piece) + values_in.shape[1:])
         return gather_ways(parts, 1).reshape((feats,) + values_in.shape[1:])
 
+    def unit(values_in, block_mean, s):
+        return (values_in.astype(full) + (block_mean - means[s])[..., None, :]) * inv_scales[s]
+
     own_gains = own_rows(norm_gains).astype(full)
     gains = [own_gains[:, s][:, None] for s in range(STREAMS)]
-    units = [(streams[s] - means[s]) * inv_scales[s] for s in range(STREAMS)]
-    normed = [all_rows((units[s] * gains[s]).astype(low)) for s in range(STREAMS)]
+    all_gains = norm_gains.astype(full)
+    units = [
+        unit(deviations[s], block_means[:, s], s).reshape(mine, group) for s in range(STREAMS)
+    ]
+    normed = []
+    for s in range(STREAMS):
+        both = unit(gather_ways(deviations[s], 1), all_means[:, :, s], s).reshape(feats, group)
+        normed.append((both * all_gains[:, s][:, None]).astype(low))
+    residual = (deviations[3].astype(full) + block_means[:, 3][:, None]).reshape(mine, group)
 
     def project(weight, left):
         columns = weight.shape[1] // dp // ways
@@ -473,10 +528,11 @@
     def by_head(values_in):
         return values_in.reshape(heads, HEAD, group)
 
+    hidden = project(w_up, normed[3])
     queries = rotate(by_head(project(w_query, normed[0])), cosine, sine).astype(low)
     keys = rotate(by_head(project(w_key, normed[1])), cosine, sine).astype(low)
     values = by_head(project(w_value, normed[2])).astype(low)
-    hidden = project(w_up, normed[3])
+    queries, upstream = lax.optimization_barrier((queries, upstream))
 
     def by_row(values_in):
         if rows == 1:
@@ -521,7 +577,7 @@
     if ways == 2:
         given = lax.dynamic_index_in_dim(branches, 1 - way, 1, keepdims=False).astype(low)
         kept = kept + hid_swap(given, 1).astype(full)
-    output = streams[3] + kept.reshape(mine, group)
+    output = residual + kept.reshape(mine, group)
     output_rounded = output.astype(low)
 
     block_output = exchange(output_rounded.reshape(places, piece, group))
@@ -584,13 +640,7 @@
     output_grad = upstream + inv_rms * scaled_grad - output * (inv_rms * inv_rms * inv_rms) * along
     output_low = gather_dp(all_rows(output_grad.astype(low))).reshape(width, group)
 
-    branch_part = jnp.concatenate(
-        [
-            contract(attended, output_low, 1, 1).astype(low),
-            contract(active, output_low, 1, 1).astype(low),
-        ],
-        axis=0,
-    )
+    branch_part = contract(active, output_low, 1, 1).astype(low)
     hidden_low = (contract(down_rows, output_low, 1, 0) * slope).astype(low)
 
     attended_grad = contract(out_rows, output_low, 1, 0).astype(low)
@@ -612,76 +662,55 @@
     hidden_all = gather_dp(hidden_mine).reshape(-1, group)
     lows = [gather_dp(v).reshape(-1, group) for v in lows_mine]
     branch_sum = chain_sum(branch_part, 0)
-    n_out = out_rows.shape[0] // branch_sum.shape[2]
-    w_out_grad = branch_sum[:, :n_out].astype(full).reshape(w_out.shape)
-    w_down_grad = branch_sum[:, n_out:].astype(full).reshape(w_down.shape)
-
-    def unsplit(total, weight):
-        total = total.reshape(ways, weight.shape[0], -1)
-        size = total.shape[2] // dp
-        parts = [total[w, :, d * size : (d + 1) * size] for d in range(dp) for w in range(ways)]
-        return jnp.concatenate([v.astype(full) for v in parts], axis=1)
-
-    up_part = contract(normed[3], hidden_all, 1, 1).astype(low)
-    w_up_grad = unsplit(chain_sum(up_part, 1), w_up)
-    parts = [contract(normed[s], lows[s], 1, 1).astype(low) for s in range(3)]
-    head_sum = chain_sum(jnp.concatenate(parts, axis=0), 2)
-    head_sum = head_sum.reshape(ways, 3, -1, head_sum.shape[2], head_sum.shape[3])
-    w_query_grad, w_key_grad, w_value_grad = [
-        unsplit(head_sum[:, s], w) for s, w in enumerate((w_query, w_key, w_value))
-    ]
-
-    normed_grads = []
+    w_down_grad = branch_sum.astype(full).reshape(w_down.shape)
+
+    normed_grads, alongs = [], []
     for s, weight in enumerate((w_query, w_key, w_value, w_up)):
         right = lows[s] if s < 3 else hidden_all
-        part = contract(way_columns(weight), right, 1, 0).reshape(places, ways, piece, group)
+        part = contract(way_columns(weight), right, 1, 0)
+        alongs.append(jnp.sum(part * all_gains[:, s][:, None], axis=0))
+        alongs.append(jnp.sum(part * normed[s].astype(full), axis=0))
+        part = part.reshape(places, ways, piece, group)
         kept = lax.dynamic_index_in_dim(part, way, 1, keepdims=False)
         if ways == 2:
             given = lax.dynamic_index_in_dim(part, 1 - way, 1, keepdims=False).astype(low)
             kept = kept + hid_swap(given, 1).astype(full)
         normed_grads.append(kept.reshape(mine, group))
     weighted = [normed_grads[s] * gains[s] for s in range(STREAMS)]
-    means_back = sum_features(
-        jnp.stack(
-            [jnp.sum(e, axis=0) for e in weighted]
-            + [jnp.sum(e * u, axis=0) for e, u in zip(weighted, units)],
-            axis=0,
-        )
-    ) / width
+    means_back = sum_features(jnp.stack(alongs, axis=0)) / width
     gain_parts = [jnp.sum(g * u, axis=1) for g, u in zip(normed_grads, units)]
     stream_grads = [
-        (weighted[s] - means_back[s] - units[s] * means_back[STREAMS + s]) * inv_scales[s]
+        (weighted[s] - means_back[2 * s] - units[s] * means_back[2 * s + 1]) * inv_scales[s]
         for s in range(STREAMS)
     ]
     stream_grads[3] = stream_grads[3] + output_grad
     smalls = sum_tokens(jnp.concatenate([mixer_grad_part, jnp.stack(gain_parts, axis=0)], axis=0))
     smalls = gather_ways(smalls.reshape(-1, places, piece), 2).reshape(-1, feats)
+
+    split = jnp.stack([v.astype(low).reshape(places, piece, group) for v in stream_grads], axis=1)
+    split = exchange(split)
+    split = jnp.concatenate([split[p] for p in range(places)], axis=-1).astype(full)
+    mix_layers = mix_all.reshape(STREAMS, HIST, total_tokens)
+    history_grad = sum(mix_layers[s][:, None] * split[s][None] for s in range(STREAMS))
+    history_grad = history_grad.swapaxes(1, 2)
+    mix_parts = jnp.concatenate(
+        [jnp.sum(split[s][None] * stored.astype(full), axis=1) for s in range(STREAMS)], axis=0
+    )
+    mix_parts = mix_parts.reshape(n_mix, dp * hid, block).transpose(1, 0, 2)
+
+    wide = w_query.shape[1] // ways
+    pairs = [(normed[3], hidden_all[i : i + wide]) for i in range(0, hidden_all.shape[0], wide)]
+    pairs += [(normed[s], lows[s]) for s in range(3)]
+    pairs += [(attended, output_low[i : i + wide]) for i in range(0, width, wide)]
+    parts = [contract(left, right, 1, 1).astype(low) for left, right in pairs]
+    late_part = jnp.concatenate(parts, axis=0)
+    late_part, mix_parts, smalls = lax.optimization_barrier((late_part, mix_parts, smalls))
+    mix_parts = lax.all_to_all(mix_parts, ("dp", "hid"), split_axis=0, concat_axis=0, tiled=True)
+    mix_grad = jnp.sum(mix_parts, axis=0).T
     w_mixer_grad = smalls[:n_inner].T
     norm_gains_grad = smalls[n_inner:].T
-
-    split = [v.reshape(places, piece, group) for v in stream_grads]
-    layers = []
-    for j in range(HIST):
-        total = mix_t[j] * split[0]
-        for s in range(1, STREAMS):
-            total = total + mix_t[s * HIST + j] * split[s]
-        layers.append(total.astype(low))
-    history_grad = exchange(jnp.stack(layers, axis=1))
-    history_grad = (
-        history_grad.transpose(1, 2, 0, 3)
-        .reshape(HIST, piece, total_tokens)
-        .astype(full)
-        .swapaxes(1, 2)
-    )
-    mix_parts = jnp.stack(
-        [
-            jnp.sum(split[s] * stored[:, j].astype(full), axis=(0, 1))
-            for s in range(STREAMS)
-            for j in range(HIST)
-        ],
-        axis=0,
-    )
-    mix_grad = to_owner(sum_features(mix_parts).reshape(n_mix, dp * ways, block)).T
+    late_sum = chain_sum(late_part, 1).reshape(ways, -1, feats, wide)
+    w_up_grad, w_query_grad, w_key_grad, w_value_grad, w_out_grad = assemble(late_sum, w_up)
 
     return (
         block_output,

time: 1240 us -> 1090 us (0.88)
  Pallas kernels: 475 us -> 399 us
  waiting for transfers between devices: 278 us -> 234 us
  other arithmetic: 152 us -> 114 us
  local copies, waits for them, and re-layouts: 106 us -> 75.7 us
  starting transfers between devices: 77 us -> 105 us
  matrix products: 131 us -> 149 us
    ppermute x5 -> x0, waiting for transfers between devices: 102 us -> none  [gather_all(): other = lax.ppermute(values_in, axis, [(i, i ^ bit) for i in range(size)])]
    pallas_call x3 -> x2, Pallas kernels: 475 us -> 380 us  [chain_sum(): pl.pallas_call(functools.partial(chain_kernel, ways, size // ways), out_s...]
    all_to_all x4 -> x8, waiting for transfers between devices: 12.8 us -> 49.6 us  [exchange(): lax.all_to_all(values_in, 'hid', split_axis=0, concat_axis=0, tiled=True,...]
    concatenate x10 -> x2, other arithmetic: 30.8 us -> 0.02 us  [the longest x1 0.01 us: local(): joined = gather_dp(gather_ways(jnp.concatenate(joined, axis=0), 0))]
    unnamed x440 -> x320, local copies, waits for them, and re-layouts: 45.1 us -> 23.1 us
    pallas_call x0 -> x1, Pallas kernels: none -> 19.5 us  [assemble(): pl.pallas_call(functools.partial(assemble_kernel, ways, dp), grid=(rows /...]
    dot_general x39 -> x43, matrix products: 109 us -> 125 us  [contract(): lax.dot_general(left, right, (((left_dim,), (right_dim,)), ((), ())), pre...]
    all_to_all x0 -> x3, waiting for transfers between devices: none -> 15.5 us  [the longest x2 15.5 us: gather_all(): lax.all_to_all(copies, ('dp', 'hid'), split_axis=0, concat_axis=0, tiled=...]
  transfers between devices with their start and end apart: 63 -> 62, of which waited for: 30 -> 35; matrix products, arithmetic and copies ran while one was open for 21% -> 25% of each run, Pallas kernels for 39% -> 37%
where the time goes in v2:
time: 1090 us; the launch traced here: 1080 us
  Pallas kernels  399 us (37%)
  waiting for transfers between devices  234 us (21%)
  matrix products  149 us (14%)
  other arithmetic  114 us (10%)
  starting transfers between devices  105 us (10%)
  local copies, waits for them, and re-layouts  75.7 us (7%)
    pallas_call x2, Pallas kernels, chain_sum(): pl.pallas_call(functools.partial(chain_kernel, ways, size // ways), out_s...  380 us
    dot_general x43, matrix products, contract(): lax.dot_general(left, right, (((left_dim,), (right_dim,)), ((), ())), pre...  125 us
    ppermute x19, waiting for transfers between devices, hid_swap(): return lax.ppermute(values_in, 'hid', [(i, i ^ bit) for i in range(size)])  83.3 us
    ppermute x13, waiting for transfers between devices, outer_shift(): return lax.ppermute(values_in, 'dp', pairs)  78.7 us
    all_to_all x8, waiting for transfers between devices, exchange(): lax.all_to_all(values_in, 'hid', split_axis=0, concat_axis=0, tiled=True,...  49.6 us
    all_to_all x8, starting transfers between devices, exchange(): lax.all_to_all(values_in, 'hid', split_axis=0, concat_axis=0, tiled=True,...  33.9 us
    ppermute x19, starting transfers between devices, hid_swap(): return lax.ppermute(values_in, 'hid', [(i, i ^ bit) for i in range(size)])  32 us
    another operation x41, other arithmetic, ordered(): jnp.stack([jnp.where(first, values_in, other), jnp.where(first, other, va...  26.9 us
  transfers between devices with their start and end apart: 62, of which 35 were waited for; matrix products, arithmetic and copies ran while one was open for 25% of the time, Pallas kernels for 37%

profile of v2, /device:TPU:0, one launch (start us, length us, event | category | flops | bytes accessed | tf_op | source)
XLA Modules:
  0.0 1080.4 jit_solution(1256113388808119194)
XLA Ops:
  9.8 13.8 %all-to-all-done.6 = bf16[4,64,1024]{2,1,0:T(8,128)(2,1)S(1)} async-done(((bf16[4,64,1024]{2,1,0:T(8,128)(2,1)}), bf16[4,64,1024]{2,1,0:T(8,128)(2,1)S(1)}, u32[]{:S(2)}, u32[]{:S(2)}) %all-to-all-start.6) | async-done | bytes 524320 | tf_op jit(solution)/shard_map/all_to_all | solution.py:158
  32.9 12.4 %all-to-all-done = f32[32,32,128]{2,1,0:T(8,128)S(1)} async-done(((f32[32,32,128]{2,1,0:T(8,128)}), f32[32,32,128]{2,1,0:T(8,128)S(1)}, u32[]{:S(2)}, u32[]{:S(2)}) %all-to-all-start) | async-done | bytes 524320 | tf_op jit(solution)/shard_map/all_to_all | solution.py:133
  101.1 9.6 all-to-all-done.3
  115.9 12.7 %all-to-all-done.1 = bf16[4,64,1024]{2,1,0:T(8,128)(2,1)} async-done(((bf16[4,64,1024]{2,1,0:T(8,128)(2,1)}), bf16[4,64,1024]{2,1,0:T(8,128)(2,1)}, u32[]{:S(2)}, u32[]{:S(2)}) %all-to-all-start.1) | async-done | bytes 524320 | tf_op jit(solution)/shard_map/all_to_all | solution.py:158
  150.0 11.2 %collective-permute-done = bf16[4,64,1024]{2,1,0:T(8,128)(2,1)} collective-permute-done((bf16[4,64,1024]{2,1,0:T(8,128)(2,1)S(1)}, bf16[4,64,1024]{2,1,0:T(8,128)(2,1)}, u32[]{:S(2)}, u32[]{:S(2)}) %collective-permute-start) | collective-permute-done | bytes 524320 | tf_op jit(solution)/shard_map/ppermute | solution.py:68
  174.2 7.7 collective-permute-done.12
  219.2 9.0 collective-permute-done.14
  257.9 8.9 fusion.298
  271.7 26.2 %collective-permute-done.18 = bf16[1024,1024]{1,0:T(8,128)(2,1)} collective-permute-done((bf16[1024,1024]{1,0:T(8,128)(2,1)}, bf16[1024,1024]{1,0:T(8,128)(2,1)}, u32[]{:S(2)}, u32[]{:S(2)}) %collective-permute-start.18) | collective-permute-done | bytes 2097184 | tf_op jit(solution)/shard_map/ppermute | solution.py:63
  297.9 13.5 %multiply_convert_fusion.2 = (bf16[1024,1024]{1,0:T(8,128)(2,1)S(1)}, f32[1024,1024]{1,0:T(8,128)}, f32[1024,1024]{1,0:T(8,128)}) fusion(bf16[1024,1024]{1,0:T(8,128)(2,1)} %collective-permute-done.19, bf16[512,1024]{1,0:T(8,128)(2,1)S(1)} %copy-done.72, bf16[512,8192]{1,0:T(8,128)(2,1)} %param.23, s32[]{:T(128)S(6)} %select_n.568, ...), kind=kOutput, calls=%fused_computation.38 | convolution fusion | flops 1146093568 | bytes 16777220 | tf_op jit(solution)/shard_map/dot_general | solution.py:27
  330.1 19.5 %collective-permute-done.21 = bf16[512,1024]{1,0:T(8,128)(2,1)} collective-permute-done((bf16[512,1024]{1,0:T(8,128)(2,1)}, bf16[512,1024]{1,0:T(8,128)(2,1)}, u32[]{:S(2)}, u32[]{:S(2)}) %collective-permute-start.21) | collective-permute-done | bytes 1048608 | tf_op jit(solution)/shard_map/ppermute | solution.py:63
  356.2 10.2 collective-permute-done.23
  403.7 10.2 collective-permute-done.30
  423.1 13.1 %collective-permute-done.31 = bf16[512,1024]{1,0:T(8,128)(2,1)} collective-permute-done((bf16[512,1024]{1,0:T(8,128)(2,1)S(1)}, bf16[512,1024]{1,0:T(8,128)(2,1)}, u32[]{:S(2)}, u32[]{:S(2)}) %collective-permute-start.31) | collective-permute-done | bytes 1048608 | tf_op jit(solution)/shard_map/ppermute | solution.py:63
  482.2 8.9 multiply_convert_fusion.1
  506.6 130.8 %shard_map.256 = bf16[2,64,16,2048]{3,2,1,0:T(8,128)(2,1)} custom-call(bf16[64,16,2048]{2,1,0:T(8,128)(2,1)S(1)} %bitcast.715), custom_call_target="tpu_custom_call" | custom-call | flops 2097152 | bytes 629145600 | tf_op jit(solution)/shard_map/pallas_call | solution.py:302
  637.4 11.8 %bitcast_convert_fusion = f32[2048,2048]{1,0:T(8,128)} fusion(bf16[2,64,16,2048]{3,2,1,0:T(8,128)(2,1)} %shard_map.256), kind=kLoop, calls=%fused_computation.10 | loop fusion | flops 4194304 | bytes 25165824 | tf_op jit(solution)/shard_map/reshape | solution.py:665
  683.9 8.0 copy.341
  691.9 9.3 multiply_reduce_fusion.1
  719.6 9.3 collective-permute-done.47
  759.5 11.0 %collective-permute-done.48 = f32[40,256]{1,0:T(8,128)S(1)} collective-permute-done((f32[40,256]{1,0:T(8,128)S(1)}, f32[40,256]{1,0:T(8,128)S(1)}, u32[]{:S(2)}, u32[]{:S(2)}) %collective-permute-start.48) | collective-permute-done | bytes 40992 | tf_op jit(solution)/shard_map/ppermute | solution.py:68
  777.0 8.7 collective-permute-done.49
  805.0 249.0 %shard_map.254 = bf16[2,128,32,1024]{3,2,1,0:T(8,128)(2,1)} custom-call(bf16[128,32,1024]{2,1,0:T(8,128)(2,1)} %bitcast.723), custom_call_target="tpu_custom_call" | custom-call | flops 4194304 | bytes 1258291200 | tf_op jit(solution)/shard_map/pallas_call | solution.py:302
  1054.0 19.5 %shard_map.255 = (f32[512,8192]{1,0:T(8,128)}, f32[512,2048]{1,0:T(8,128)}, f32[512,2048]{1,0:T(8,128)}, f32[512,2048]{1,0:T(8,128)}, f32[512,2048]{1,0:T(8,128)}) custom-call(bf16[2,8,512,1024]{3,2,1,0:T(8,128)(2,1)} %bitcast.716, bf16[2,8,512,1024]{3,2,1,0:T(8,128)(2,1)} %bitcast.717, bf16[2,8,512,1024]{3,2,1,0:T(8,128)(2,1)} %bitcast.718), custom_call_target="tpu_custom_call" | custom-call | bytes 50331648 | tf_op jit(solution)/shard_map/pallas_call | solution.py:358
  (702 shorter events, 432.5 us)
Async XLA Ops:
  137.1 24.2 %collective-permute-start = (bf16[4,64,1024]{2,1,0:T(8,128)(2,1)S(1)}, bf16[4,64,1024]{2,1,0:T(8,128)(2,1)}, u32[]{:S(2)}, u32[]{:S(2)}) collective-permute-start(bf16[4,64,1024]{2,1,0:T(8,128)(2,1)S(1)} %all-to-all-done.3), channel_id=1, source_target_pairs={{0,1},{1,0},{2,3},{3,2},{4,5},{5,4},{6,7},{7,6},{8,9},{9,8},{10,11... | collective-permute-start | bytes 1572872 | tf_op jit(solution)/shard_map/ppermute | solution.py:68
  137.3 36.3 %collective-permute-start.16 = (bf16[4,64,1024]{2,1,0:T(8,128)(2,1)}, bf16[4,64,1024]{2,1,0:T(8,128)(2,1)}, u32[]{:S(2)}, u32[]{:S(2)}) collective-permute-start(bf16[4,64,1024]{2,1,0:T(8,128)(2,1)} %all-to-all-done.1), channel_id=1, source_target_pairs={{0,1},{1,0},{2,3},{3,2},{4,5},{5,4},{6,7},{7,6},{8,9},{9,8},{10,11... | collective-permute-start | bytes 1572872 | tf_op jit(solution)/shard_map/ppermute | solution.py:68
  146.9 35.1 %collective-permute-start.12 = (bf16[4,64,1024]{2,1,0:T(8,128)(2,1)}, bf16[4,64,1024]{2,1,0:T(8,128)(2,1)S(1)}, u32[]{:S(2)}, u32[]{:S(2)}) collective-permute-start(bf16[4,64,1024]{2,1,0:T(8,128)(2,1)} %all-to-all-done.7), channel_id=1, source_target_pairs={{0,1},{1,0},{2,3},{3,2},{4,5},{5,4},{6,7},{7,6},{8,9},{9,8},{10,11... | collective-permute-start | bytes 1572872 | tf_op jit(solution)/shard_map/ppermute | solution.py:68
  167.6 87.7 %collective-permute-start.7 = (bf16[256,1024]{1,0:T(8,128)(2,1)}, bf16[256,1024]{1,0:T(8,128)(2,1)}, u32[]{:S(2)}, u32[]{:S(2)}) collective-permute-start(bf16[256,1024]{1,0:T(8,128)(2,1)} %convolution_convert_fusion.10), channel_id=1, source_target_pairs={{0,8},{8,0},{16,24},{24,16},{1,9},{9,1},{17,25},{25,17},{2,10},{10... | collective-permute-start | bytes 1572872 | tf_op jit(solution)/shard_map/ppermute | solution.py:54
  169.0 30.1 %collective-permute-start.5 = (bf16[256,1024]{1,0:T(8,128)(2,1)S(1)}, bf16[256,1024]{1,0:T(8,128)(2,1)S(1)}, u32[]{:S(2)}, u32[]{:S(2)}) collective-permute-start(bf16[256,1024]{1,0:T(8,128)(2,1)S(1)} %convolution_convert_fusion.11), channel_id=1, source_target_pairs={{0,8},{8,0},{16,24},{24,16},{1,9},{9,1},{17,25},{25,17},{2,10},{10... | collective-permute-start | bytes 1572872 | tf_op jit(solution)/shard_map/ppermute | solution.py:54
  173.0 32.3 %collective-permute-start.11 = (bf16[256,1024]{1,0:T(8,128)(2,1)S(1)}, bf16[256,1024]{1,0:T(8,128)(2,1)S(1)}, u32[]{:S(2)}, u32[]{:S(2)}) collective-permute-start(bf16[256,1024]{1,0:T(8,128)(2,1)S(1)} %convolution_convert_fusion.8), channel_id=1, source_target_pairs={{0,8},{8,0},{16,24},{24,16},{1,9},{9,1},{17,25},{25,17},{2,10},{10... | collective-permute-start | bytes 1572872 | tf_op jit(solution)/shard_map/ppermute | solution.py:54
  173.6 24.4 %collective-permute-start.9 = (bf16[256,1024]{1,0:T(8,128)(2,1)S(1)}, bf16[256,1024]{1,0:T(8,128)(2,1)S(1)}, u32[]{:S(2)}, u32[]{:S(2)}) collective-permute-start(bf16[256,1024]{1,0:T(8,128)(2,1)S(1)} %convolution_convert_fusion.9), channel_id=1, source_target_pairs={{0,8},{8,0},{16,24},{24,16},{1,9},{9,1},{17,25},{25,17},{2,10},{10... | collective-permute-start | bytes 1572872 | tf_op jit(solution)/shard_map/ppermute | solution.py:54
  187.8 31.1 %collective-permute-start.15 = (bf16[256,1024]{1,0:T(8,128)(2,1)}, bf16[256,1024]{1,0:T(8,128)(2,1)}, u32[]{:S(2)}, u32[]{:S(2)}) collective-permute-start(bf16[256,1024]{1,0:T(8,128)(2,1)} %convolution_convert_fusion.6), channel_id=1, source_target_pairs={{0,8},{8,0},{16,24},{24,16},{1,9},{9,1},{17,25},{25,17},{2,10},{10... | collective-permute-start | bytes 1572872 | tf_op jit(solution)/shard_map/ppermute | solution.py:54
  203.1 45.7 %collective-permute-start.17 = (bf16[1024,1024]{1,0:T(8,128)(2,1)}, bf16[1024,1024]{1,0:T(8,128)(2,1)}, u32[]{:S(2)}, u32[]{:S(2)}) collective-permute-start(bf16[1024,1024]{1,0:T(8,128)(2,1)} %convolution_convert_fusion.2), channel_id=1, source_target_pairs={{0,8},{8,0},{16,24},{24,16},{1,9},{9,1},{17,25},{25,17},{2,10},{10... | collective-permute-start | bytes 6291464 | tf_op jit(solution)/shard_map/ppermute | solution.py:54
  205.3 66.3 %collective-permute-start.19 = (bf16[1024,1024]{1,0:T(8,128)(2,1)}, bf16[1024,1024]{1,0:T(8,128)(2,1)}, u32[]{:S(2)}, u32[]{:S(2)}) collective-permute-start(bf16[1024,1024]{1,0:T(8,128)(2,1)} %convolution_convert_fusion.1), channel_id=1, source_target_pairs={{0,8},{8,0},{16,24},{24,16},{1,9},{9,1},{17,25},{25,17},{2,10},{10... | collective-permute-start | bytes 6291464 | tf_op jit(solution)/shard_map/ppermute | solution.py:54
  218.9 36.4 %collective-permute-start.6 = (bf16[256,1024]{1,0:T(8,128)(2,1)}, bf16[256,1024]{1,0:T(8,128)(2,1)}, u32[]{:S(2)}, u32[]{:S(2)}) collective-permute-start(bf16[256,1024]{1,0:T(8,128)(2,1)} %add_convert_fusion.10), channel_id=1, source_target_pairs={{0,16},{8,24},{16,0},{24,8},{1,17},{9,25},{17,1},{25,9},{2,18},{10... | collective-permute-start | bytes 1572872 | tf_op jit(solution)/shard_map/ppermute | solution.py:63
  253.6 44.2 %collective-permute-start.18 = (bf16[1024,1024]{1,0:T(8,128)(2,1)}, bf16[1024,1024]{1,0:T(8,128)(2,1)}, u32[]{:S(2)}, u32[]{:S(2)}) collective-permute-start(bf16[1024,1024]{1,0:T(8,128)(2,1)} %add_convert_fusion), channel_id=1, source_target_pairs={{0,16},{8,24},{16,0},{24,8},{1,17},{9,25},{17,1},{25,9},{2,18},{10... | collective-permute-start | bytes 6291464 | tf_op jit(solution)/shard_map/ppermute | solution.py:63
  324.2 25.4 %collective-permute-start.21 = (bf16[512,1024]{1,0:T(8,128)(2,1)}, bf16[512,1024]{1,0:T(8,128)(2,1)}, u32[]{:S(2)}, u32[]{:S(2)}) collective-permute-start(bf16[512,1024]{1,0:T(8,128)(2,1)} %add_convert_fusion.2), channel_id=1, source_target_pairs={{0,16},{8,24},{16,0},{24,8},{1,17},{9,25},{17,1},{25,9},{2,18},{10... | collective-permute-start | bytes 3145736 | tf_op jit(solution)/shard_map/ppermute | solution.py:63
  451.4 49.1 %all-to-all-start.8 = ((bf16[4,64,1024]{2,1,0:T(8,128)(2,1)}), bf16[4,64,1024]{2,1,0:T(8,128)(2,1)}, u32[]{:S(2)}, u32[]{:S(2)}) async-start(bf16[4,64,1024]{2,1,0:T(8,128)(2,1)} %copy-done.26), calls=%async_computation.8 | async-start | bytes 1048576 | tf_op jit(solution)/shard_map/all_to_all | solution.py:158
  456.3 44.1 %collective-permute-start.29 = (f32[36,128]{1,0:T(8,128)S(1)}, f32[36,128]{1,0:T(8,128)S(1)}, u32[]{:S(2)}, u32[]{:S(2)}) collective-permute-start(f32[36,128]{1,0:T(8,128)S(1)} %bitcast.876), channel_id=1, source_target_pairs={{0,0},{1,1},{2,8},{3,9},{4,16},{5,17},{6,24},{7,25},{8,2},{9,3},{1... | collective-permute-start | bytes 55304 | tf_op jit(solution)/shard_map/ppermute | solution.py:382
  493.8 155.6 %collective-permute-start.40 = (bf16[1024,1024]{1,0:T(8,128)(2,1)}, bf16[1024,1024]{1,0:T(8,128)(2,1)}, u32[]{:S(2)}, u32[]{:S(2)}) collective-permute-start(bf16[1024,1024]{1,0:T(8,128)(2,1)} %multiply_convert_fusion.1), channel_id=1, source_target_pairs={{0,16},{8,24},{16,0},{24,8},{1,17},{9,25},{17,1},{25,9},{2,18},{10... | collective-permute-start | bytes 6291464 | tf_op jit(solution)/shard_map/ppermute | solution.py:63
  502.3 146.9 %collective-permute-start.33 = (bf16[256,1024]{1,0:T(8,128)(2,1)S(1)}, bf16[256,1024]{1,0:T(8,128)(2,1)S(1)}, u32[]{:S(2)}, u32[]{:S(2)}) collective-permute-start(bf16[256,1024]{1,0:T(8,128)(2,1)S(1)} %bitcast.760), channel_id=1, source_target_pairs={{0,16},{8,24},{16,0},{24,8},{1,17},{9,25},{17,1},{25,9},{2,18},{10... | collective-permute-start | bytes 1572872 | tf_op jit(solution)/shard_map/ppermute | solution.py:63
  502.4 150.0 %collective-permute-start.36 = (bf16[256,1024]{1,0:T(8,128)(2,1)S(1)}, bf16[256,1024]{1,0:T(8,128)(2,1)S(1)}, u32[]{:S(2)}, u32[]{:S(2)}) collective-permute-start(bf16[256,1024]{1,0:T(8,128)(2,1)S(1)} %bitcast.758), channel_id=1, source_target_pairs={{0,16},{8,24},{16,0},{24,8},{1,17},{9,25},{17,1},{25,9},{2,18},{10... | collective-permute-start | bytes 1572872 | tf_op jit(solution)/shard_map/ppermute | solution.py:63
  504.4 148.3 %collective-permute-start.38 = (bf16[256,1024]{1,0:T(8,128)(2,1)}, bf16[256,1024]{1,0:T(8,128)(2,1)S(1)}, u32[]{:S(2)}, u32[]{:S(2)}) collective-permute-start(bf16[256,1024]{1,0:T(8,128)(2,1)} %bitcast.165), channel_id=1, source_target_pairs={{0,16},{8,24},{16,0},{24,8},{1,17},{9,25},{17,1},{25,9},{2,18},{10... | collective-permute-start | bytes 1572872 | tf_op jit(solution)/shard_map/ppermute | solution.py:63
  651.6 23.4 %collective-permute-start.41 = (bf16[2,1024,1024]{2,1,0:T(8,128)(2,1)S(1)}, bf16[2,1024,1024]{2,1,0:T(8,128)(2,1)S(1)}, u32[]{:S(2)}, u32[]{:S(2)}) collective-permute-start(bf16[2,1024,1024]{2,1,0:T(8,128)(2,1)S(1)} %pad_maximum_fusion.2), channel_id=1, source_target_pairs={{0,8},{8,0},{16,24},{24,16},{1,9},{9,1},{17,25},{25,17},{2,10},{10... | collective-permute-start | bytes 12582920 | tf_op jit(solution)/shard_map/ppermute | solution.py:54
  667.8 46.6 %collective-permute-start.46 = (bf16[4,64,1024]{2,1,0:T(8,128)(2,1)}, bf16[4,64,1024]{2,1,0:T(8,128)(2,1)}, u32[]{:S(2)}, u32[]{:S(2)}) collective-permute-start(bf16[4,64,1024]{2,1,0:T(8,128)(2,1)} %fusion.168), channel_id=1, source_target_pairs={{0,1},{1,0},{2,3},{3,2},{4,5},{5,4},{6,7},{7,6},{8,9},{9,8},{10,11... | collective-permute-start | bytes 1572872 | tf_op jit(solution)/shard_map/ppermute | solution.py:68
  672.2 44.1 %collective-permute-start.45 = (bf16[4,64,1024]{2,1,0:T(8,128)(2,1)}, bf16[4,64,1024]{2,1,0:T(8,128)(2,1)}, u32[]{:S(2)}, u32[]{:S(2)}) collective-permute-start(bf16[4,64,1024]{2,1,0:T(8,128)(2,1)} %fusion.167), channel_id=1, source_target_pairs={{0,1},{1,0},{2,3},{3,2},{4,5},{5,4},{6,7},{7,6},{8,9},{9,8},{10,11... | collective-permute-start | bytes 1572872 | tf_op jit(solution)/shard_map/ppermute | solution.py:68
  732.5 58.2 %all-to-all-start.9 = ((bf16[4,4,64,1024]{3,2,1,0:T(8,128)(2,1)}), bf16[4,4,64,1024]{3,2,1,0:T(8,128)(2,1)S(1)}, u32[]{:S(2)}, u32[]{:S(2)}) async-start(bf16[4,4,64,1024]{3,2,1,0:T(8,128)(2,1)} %copy.346), calls=%async_computation.9 | async-start | bytes 4194304 | tf_op jit(solution)/shard_map/all_to_all | solution.py:158
  800.7 277.2 %all-to-all-start.10 = ((f32[32,32,128]{2,1,0:T(8,128)}), f32[32,32,128]{2,1,0:T(8,128)}, u32[]{:S(2)}, u32[]{:S(2)}) async-start(f32[32,32,128]{2,1,0:T(8,128)} %copy.354), calls=%async_computation.10 | async-start | bytes 1048576 | tf_op jit(solution)/shard_map/all_to_all | solution.py:708
  (188 other events, 2403.5 us)

commit v3 on v2

--- a/solution.py
+++ b/solution.py
@@ -15,7 +15,9 @@
 STREAMS = 4
 CORES = 2
 CHUNK = 1 << 15
-SLACK = 4
+SLACK = 6
+TILE = 128
+VMEM = 52 << 20
 
 highest = lax.Precision.HIGHEST
 rope_base = 10000.0
@@ -108,6 +110,31 @@
     return pair.reshape((size,) + values_in.shape)
 
 
+def gather_outer(values_in):
+    steps = range(1, lax.axis_size("dp") // CORES)
+    return [values_in] + [outer_shift(values_in, step) for step in steps]
+
+
+def gather_cores(held):
+    return [v for h in held for v in (h, core_swap(h))]
+
+
+def gather_turns(values_in):
+    return gather_cores(gather_outer(values_in))
+
+
+def turn_source(turn):
+    outer, me = lax.axis_size("dp") // CORES, lax.axis_index("dp")
+    there = (me // CORES + outer - turn // CORES) % outer
+    return there * CORES + (me + turn) % CORES
+
+
+def turn_of(index):
+    outer, me = lax.axis_size("dp") // CORES, lax.axis_index("dp")
+    step = (me // CORES + outer - index // CORES) % outer
+    return step * CORES + (me + index) % CORES
+
+
 def sum_features(values_in):
     if split_ways() == 2:
         values_in = values_in + hid_swap(values_in, 1)
@@ -160,22 +187,25 @@
     )
 
 
-def chain_kernel(
-    ways,
-    places,
-    part_ref,
-    out_ref,
-    landed,
-    sums,
-    up_send,
-    up_recv,
-    down_send,
-    down_recv,
-    side_send,
-    side_recv,
-    kept,
-):
-    count = part_ref.shape[0]
+def chain_kernel(ways, places, blocks, n_operands, depth, *refs):
+    operand_refs, refs = refs[:n_operands], refs[n_operands:]
+    out_ref, refs = refs[0], refs[1:]
+    operands, refs = refs[:n_operands], refs[n_operands:]
+    (
+        own,
+        landed,
+        sums,
+        fetched,
+        up_send,
+        up_recv,
+        down_send,
+        down_recv,
+        side_send,
+        side_recv,
+        kept,
+    ) = refs
+    count = sums.shape[0]
+    per_tile = TILE // depth
     last = places - 1
     me = lax.axis_index("hid")
     if ways == 2:
@@ -209,6 +239,12 @@
     def side_copy(source, i):
         return remote(source, out_ref.at[way, i], side_send, side_recv, beside)
 
+    def fetch(n):
+        return pltpu.make_async_copy(operand_refs[n], operands[n], fetched.at[n])
+
+    for n in range(n_operands):
+        fetch(n).start()
+
     barrier = pltpu.get_barrier_semaphore()
 
     def greet(device):
@@ -229,15 +265,49 @@
     met = jnp.where(place > 0, 1, 0) + jnp.where(place < last, 1, 0) + (ways - 1)
     pl.semaphore_wait(barrier, met)
 
+    def compute(tile):
+        seen, first = set(), 0
+        for rows, segments in blocks:
+            start = first
+            first = first + rows // TILE
+            fresh = [n for seg in segments for n in (seg[0], seg[2])]
+            fresh = [n for n in dict.fromkeys(fresh) if n not in seen]
+            seen.update(fresh)
+
+            @pl.when(tile == start)
+            def _(fresh=fresh):
+                for n in fresh:
+                    fetch(n).wait()
+
+            @pl.when((tile >= start) & (tile < first))
+            def _(start=start, segments=segments):
+                column = 0
+                for left, left_row, right, right_row, size in segments:
+                    row = pl.multiple_of(left_row + (tile - start) * TILE, TILE)
+                    own[:, column : column + size] = lax.dot_general(
+                        operands[left][pl.ds(row, TILE), :],
+                        operands[right][right_row : right_row + size, :],
+                        (((1,), (1,)), ((), ())),
+                        preferred_element_type=full,
+                    )
+                    column += size
+
     def upward(i):
+        @pl.when(i % per_tile == 0)
+        def _():
+            compute(i // per_tile)
+
+        mine = own[pl.ds(pl.multiple_of(i % per_tile * depth, depth), depth), :]
+
         @pl.when(place == 0)
         def _():
-            remote(part_ref.at[i], landed.at[i], up_send, up_recv.at[i], above).start()
+            sums[i] = mine.astype(low)
+            up_copy(i).start()
 
         @pl.when(place > 0)
         def _():
             up_copy(i).wait_recv()
-            sums[i] = (landed[i].astype(full) + part_ref[i].astype(full)).astype(low)
+            sums[i] = (landed[i].astype(full) + mine).astype(low)
 
             @pl.when(place < last)
             def _():
@@ -294,19 +364,24 @@
         remote(sums, out_ref.at[1 - way], kept, side_recv, beside).wait_recv()
 
 
-def chain_sum(part, collective_id):
+def chain_sum(operands, blocks, collective_id):
     ways, size = split_ways(), lax.axis_size("hid")
-    rows, columns = part.shape
+    columns = sum(seg[4] for seg in blocks[0][1])
+    rows = sum(block[0] for block in blocks)
     depth = max(16, CHUNK // columns)
     count = rows // depth
+    tokens = operands[0].shape[1]
     return pl.pallas_call(
-        functools.partial(chain_kernel, ways, size // ways),
+        functools.partial(chain_kernel, ways, size // ways, blocks, len(operands), depth),
         out_shape=jax.ShapeDtypeStruct((ways, count, depth, columns), low),
-        in_specs=[pl.BlockSpec(memory_space=pltpu.VMEM)],
+        in_specs=[pl.BlockSpec(memory_space=pl.ANY)] * len(operands),
         out_specs=pl.BlockSpec(memory_space=pl.ANY),
-        scratch_shapes=[
+        scratch_shapes=[pltpu.VMEM(v.shape, low) for v in operands]
+        + [
+            pltpu.VMEM((TILE, columns), full),
             pltpu.VMEM((count, depth, columns), low),
             pltpu.VMEM((count, depth, columns), low),
+            pltpu.SemaphoreType.DMA((len(operands),)),
             pltpu.SemaphoreType.DMA,
             pltpu.SemaphoreType.DMA((count,)),
             pltpu.SemaphoreType.DMA,
@@ -316,33 +391,68 @@
             pltpu.SemaphoreType.DMA,
         ],
         compiler_params=pltpu.CompilerParams(
-            collective_id=collective_id, has_side_effects=True, vmem_limit_bytes=48 << 20
+            collective_id=collective_id, has_side_effects=True, vmem_limit_bytes=60 << 20
         ),
         cost_estimate=pl.CostEstimate(
-            flops=rows * columns, bytes_accessed=300 * rows * columns, transcendentals=0
+            flops=2 * rows * columns * tokens,
+            bytes_accessed=300 * rows * columns,
+            transcendentals=0,
         ),
-    )(part.reshape(count, depth, columns))
+    )(*operands)
+
+
+def chain_sums(operands, blocks, collective_id):
+    groups, held, size = [[]], set(), 0
+    for rows, segments in blocks:
+        used = {n for seg in segments for n in (seg[0], seg[2])}
+        more = sum(2 * operands[n].size for n in used - held)
+        more += 4 * rows * sum(seg[4] for seg in segments)
+        if groups[-1] and size + more > VMEM:
+            groups.append([])
+            held, size = set(), 0
+            more = sum(2 * operands[n].size for n in used)
+            more += 4 * rows * sum(seg[4] for seg in segments)
+        groups[-1].append((rows, segments))
+        held |= used
+        size += more
+    totals = []
+    for i, group in enumerate(groups):
+        used = sorted({n for _, segments in group for seg in segments for n in (seg[0], seg[2])})
+        place = {n: k for k, n in enumerate(used)}
+        own = [
+            (rows, [(place[a], b, place[c], d, e) for a, b, c, d, e in segments])
+            for rows, segments in group
+        ]
+        total = chain_sum([operands[n] for n in used], own, collective_id + i)
+        totals.append(total.reshape(total.shape[0], -1, total.shape[3]))
+    return totals[0] if len(totals) == 1 else jnp.concatenate(totals, axis=1)
 
 
 def assemble_kernel(ways, dp, own_ref, *refs):
     halves, (up_ref, *head_refs, out_ref) = refs[:ways], refs[ways:]
-    wide = own_ref.shape[3]
+    rows, wide = own_ref.shape[2:]
     size = up_ref.shape[1] // dp // ways
     blocks = dp * size // wide
-    for w in range(ways):
-        for d in range(dp):
-            start = d * size
-            part = own_ref[w, start // wide, :, start % wide : start % wide + size]
+    own = wide // dp
+    feats = out_ref.shape[1] // dp
+    for d in range(dp):
+        turn = turn_of(d)
+        for w in range(ways):
+            start = turn * size
+            lanes = pl.ds(pl.multiple_of(start % wide, size), size)
             place = (d * ways + w) * size
-            up_ref[:, place : place + size] = part.astype(full)
-        for s, ref in enumerate(head_refs):
-            own = wide // dp
-            for d in range(dp):
+            up_ref[:, place : place + size] = own_ref[w, start // wide, :, lanes].astype(full)
+            for s, ref in enumerate(head_refs):
+                lanes = pl.ds(pl.multiple_of(turn * own, own), own)
                 place = (d * ways + w) * own
-                part = own_ref[w, blocks + s, :, d * own : (d + 1) * own]
-                ref[:, place : place + own] = part.astype(full)
-    for w in range(ways):
-        out_ref[:, w * wide : (w + 1) * wide] = halves[w][0, 0].astype(full)
+                ref[:, place : place + own] = own_ref[w, blocks + s, :, lanes].astype(full)
+        start = turn * feats
+        lanes = pl.ds(pl.multiple_of(start % wide, feats), feats)
+        for w in range(ways):
+
+            @pl.when(start // wide == w)
+            def _(w=w, d=d, lanes=lanes):
+                out_ref[:, d * feats : (d + 1) * feats] = halves[w][0, 0, :, lanes].astype(full)
 
 
 def assemble(total, w_up):
@@ -367,6 +477,28 @@
             flops=0, bytes_accessed=6 * total.size, transcendentals=0
         ),
     )(total, *[total] * ways)
+
+
+def unturn_kernel(dp, own_ref, out_ref):
+    size = out_ref.shape[1] // dp
+    for d in range(dp):
+        lanes = pl.ds(pl.multiple_of(turn_of(d) * size, size), size)
+        out_ref[:, d * size : (d + 1) * size] = own_ref[:, lanes].astype(full)
+
+
+def unturn(total):
+    rows, columns = total.shape
+    depth = 256
+    return pl.pallas_call(
+        functools.partial(unturn_kernel, lax.axis_size("dp")),
+        grid=(rows // depth,),
+        out_shape=jax.ShapeDtypeStruct((rows, columns), full),
+        in_specs=[pl.BlockSpec((depth, columns), lambda i: (i, 0))],
+        out_specs=pl.BlockSpec((depth, columns), lambda i: (i, 0)),
+        cost_estimate=pl.CostEstimate(
+            flops=0, bytes_accessed=6 * total.size, transcendentals=0
+        ),
+    )(total)
 
 
 def to_owner(values_in):
@@ -449,9 +581,6 @@
     deviations[3] = exchange(by_place(deviations[3]))
     for s in range(3):
         deviations[s] = exchange(by_place(deviations[s]))
-    upstream = exchange(by_place(out_cotangent.T))
-    upstream = upstream.reshape(mine, group).astype(full)
-
     def join_moments(mean_parts, dev_parts, size):
         mean = jnp.mean(mean_parts, axis=0)
         spread = size * jnp.sum(jnp.square(mean_parts - mean), axis=0)
@@ -532,7 +661,26 @@
     queries = rotate(by_head(project(w_query, normed[0])), cosine, sine).astype(low)
     keys = rotate(by_head(project(w_key, normed[1])), cosine, sine).astype(low)
     values = by_head(project(w_value, normed[2])).astype(low)
-    queries, upstream = lax.optimization_barrier((queries, upstream))
+    cotangent, queries = lax.optimization_barrier((out_cotangent, queries))
+    upstream = exchange(by_place(cotangent.T)).reshape(mine, group)
+
+    def turned(weight, stride, offset, size):
+        starts = [turn_source(turn) * stride + offset for turn in range(dp)]
+        parts = [lax.dynamic_slice_in_dim(weight, start, size, 1) for start in starts]
+        return jnp.concatenate(parts, axis=1)
+
+    n_head = heads * HEAD
+    n_units = hidden.shape[0]
+    out_rows, down_rows = way_rows(w_out), way_rows(w_down)
+    turned_weights = (
+        turned(w_query, ways * n_head, way * n_head, n_head),
+        turned(w_key, ways * n_head, way * n_head, n_head),
+        turned(w_value, ways * n_head, way * n_head, n_head),
+        turned(w_up, ways * n_units, way * n_units, n_units),
+        turned(out_rows, feats, 0, feats),
+        turned(down_rows, feats, 0, feats),
+    )
+    hidden, turned_weights = lax.optimization_barrier((hidden, turned_weights))
 
     def by_row(values_in):
         if rows == 1:
@@ -564,7 +712,6 @@
     active, hidden_pull = jax.vjp(gelu_exact, hidden)
     active = active.astype(low)
     (slope,) = hidden_pull(jnp.ones_like(hidden))
-    out_rows, down_rows = way_rows(w_out), way_rows(w_down)
 
     def make_out(index):
         start = index * feats
@@ -578,10 +725,11 @@
         given = lax.dynamic_index_in_dim(branches, 1 - way, 1, keepdims=False).astype(low)
         kept = kept + hid_swap(given, 1).astype(full)
     output = residual + kept.reshape(mine, group)
+    output, upstream = lax.optimization_barrier((output, upstream))
+    upstream = upstream.astype(full)
     output_rounded = output.astype(low)
 
     block_output = exchange(output_rounded.reshape(places, piece, group))
-    block_output = block_output.transpose(1, 0, 2).reshape(piece, total_tokens).T
 
     square = jnp.sum(output * output, axis=0, keepdims=True)
     mixer_rows = own_rows(w_mixer)
@@ -638,12 +786,13 @@
     scaled_grad = contract(mixer_rows, inner_low, 1, 0)
     along = jnp.sum(inner_low.astype(full) * inner_raw, axis=0) / width
     output_grad = upstream + inv_rms * scaled_grad - output * (inv_rms * inv_rms * inv_rms) * along
-    output_low = gather_dp(all_rows(output_grad.astype(low))).reshape(width, group)
-
-    branch_part = contract(active, output_low, 1, 1).astype(low)
-    hidden_low = (contract(down_rows, output_low, 1, 0) * slope).astype(low)
-
-    attended_grad = contract(out_rows, output_low, 1, 0).astype(low)
+    output_lows = gather_turns(all_rows(output_grad.astype(low)))
+
+    output_low = jnp.concatenate(output_lows, axis=0)
+
+    hidden_low = (contract(turned_weights[5], output_low, 1, 0) * slope).astype(low)
+
+    attended_grad = contract(turned_weights[4], output_low, 1, 0).astype(low)
     a_rows = by_row(by_head(attended_grad))
     prob_grad = batched(a_rows, v_rows, 1, 1)
     row_total = jnp.sum(probs * prob_grad, axis=-1, keepdims=True)
@@ -655,19 +804,25 @@
     key_low = rotate(key_grad, cosine, -sine).astype(low).reshape(heads * HEAD, group)
     value_low = value_grad.astype(low).reshape(heads * HEAD, group)
 
-    lows_mine, hidden_mine = (query_low, key_low, value_low), hidden_low
-    branch_part, hidden_mine, lows_mine = lax.optimization_barrier(
-        (branch_part, hidden_mine, lows_mine)
-    )
-    hidden_all = gather_dp(hidden_mine).reshape(-1, group)
-    lows = [gather_dp(v).reshape(-1, group) for v in lows_mine]
-    branch_sum = chain_sum(branch_part, 0)
-    w_down_grad = branch_sum.astype(full).reshape(w_down.shape)
-
-    normed_grads, alongs = [], []
-    for s, weight in enumerate((w_query, w_key, w_value, w_up)):
-        right = lows[s] if s < 3 else hidden_all
-        part = contract(way_columns(weight), right, 1, 0)
+    lows_mine = jnp.concatenate([query_low, key_low, value_low], axis=0)
+    active_kept, hidden_low, lows_mine = lax.optimization_barrier((active, hidden_low, lows_mine))
+    hidden_lows, lows = gather_outer(hidden_low), gather_outer(lows_mine)
+    blocks = [(active.shape[0], [(0, 0, 1, 0, width)])]
+    branch_sum = chain_sum([active_kept, output_low], blocks, 0)
+    branch_sum, block_output, hidden_lows, lows = lax.optimization_barrier(
+        (branch_sum, block_output, hidden_lows, lows)
+    )
+    block_output = block_output.transpose(1, 0, 2).reshape(piece, total_tokens).T
+    hidden_lows, lows = gather_cores(hidden_lows), gather_cores(lows)
+
+    normed_grads, alongs, rights = [], [], []
+    for s in range(STREAMS):
+        if s < 3:
+            right = jnp.concatenate([v[s * n_head : (s + 1) * n_head] for v in lows], axis=0)
+        else:
+            right = jnp.concatenate(hidden_lows, axis=0)
+        rights.append(right)
+        part = contract(turned_weights[s], right, 1, 0)
         alongs.append(jnp.sum(part * all_gains[:, s][:, None], axis=0))
         alongs.append(jnp.sum(part * normed[s].astype(full), axis=0))
         part = part.reshape(places, ways, piece, group)
@@ -684,10 +839,10 @@
         for s in range(STREAMS)
     ]
     stream_grads[3] = stream_grads[3] + output_grad
-    smalls = sum_tokens(jnp.concatenate([mixer_grad_part, jnp.stack(gain_parts, axis=0)], axis=0))
-    smalls = gather_ways(smalls.reshape(-1, places, piece), 2).reshape(-1, feats)
+    smalls = jnp.concatenate([mixer_grad_part, jnp.stack(gain_parts, axis=0)], axis=0)
 
     split = jnp.stack([v.astype(low).reshape(places, piece, group) for v in stream_grads], axis=1)
+    attended, split, smalls = lax.optimization_barrier((attended, split, smalls))
     split = exchange(split)
     split = jnp.concatenate([split[p] for p in range(places)], axis=-1).astype(full)
     mix_layers = mix_all.reshape(STREAMS, HIST, total_tokens)
@@ -699,17 +854,20 @@
     mix_parts = mix_parts.reshape(n_mix, dp * hid, block).transpose(1, 0, 2)
 
     wide = w_query.shape[1] // ways
-    pairs = [(normed[3], hidden_all[i : i + wide]) for i in range(0, hidden_all.shape[0], wide)]
-    pairs += [(normed[s], lows[s]) for s in range(3)]
-    pairs += [(attended, output_low[i : i + wide]) for i in range(0, width, wide)]
-    parts = [contract(left, right, 1, 1).astype(low) for left, right in pairs]
-    late_part = jnp.concatenate(parts, axis=0)
-    late_part, mix_parts, smalls = lax.optimization_barrier((late_part, mix_parts, smalls))
+    operands = [rights[3]] + rights[:3] + [output_low, normed[3]] + normed[:3] + [attended]
+    blocks = [(feats, [(5, 0, 0, i, wide)]) for i in range(0, rights[3].shape[0], wide)]
+    blocks += [(feats, [(6 + s, 0, 1 + s, 0, wide)]) for s in range(3)]
+    blocks += [(n_head, [(9, 0, 4, i, wide)]) for i in range(0, width, wide)]
+    late_sum = chain_sums(operands, blocks, 1)
+    late_sum, mix_parts, smalls = lax.optimization_barrier((late_sum, mix_parts, smalls))
+    smalls = sum_tokens(smalls)
+    smalls = gather_ways(smalls.reshape(-1, places, piece), 2).reshape(-1, feats)
+    w_mixer_grad = smalls[:n_inner].T
+    norm_gains_grad = smalls[n_inner:].T
     mix_parts = lax.all_to_all(mix_parts, ("dp", "hid"), split_axis=0, concat_axis=0, tiled=True)
     mix_grad = jnp.sum(mix_parts, axis=0).T
-    w_mixer_grad = smalls[:n_inner].T
-    norm_gains_grad = smalls[n_inner:].T
-    late_sum = chain_sum(late_part, 1).reshape(ways, -1, feats, wide)
+    w_down_grad = unturn(branch_sum.reshape(w_down.shape))
+    late_sum = late_sum.reshape(ways, -1, feats, wide)
     w_up_grad, w_query_grad, w_key_grad, w_value_grad, w_out_grad = assemble(late_sum, w_up)
 
     return (

time: 1090 us -> 1030 us (0.945)
  matrix products: 149 us -> 112 us
  starting transfers between devices: 105 us -> 87.2 us
  other arithmetic: 114 us -> 97.5 us
  local copies, waits for them, and re-layouts: 75.7 us -> 88.6 us
    dot_general x43 -> x33, matrix products: 125 us -> 86.1 us  [contract(): lax.dot_general(left, right, (((left_dim,), (right_dim,)), ((), ())), pre...]
    another operation x41 -> x20, other arithmetic: 26.9 us -> 3.13 us  [ordered(): jnp.stack([jnp.where(first, values_in, other), jnp.where(first, other, va...]
    dynamic_slice x0 -> x6, local copies, waits for them, and re-layouts: none -> 16.5 us  [turned(): lax.dynamic_slice_in_dim(weight, start, size, 1)]
    concatenate x0 -> x10, other arithmetic: none -> 15.1 us  [the longest x5 10.8 us: turned(): return jnp.concatenate(parts, axis=1)]
    reshape x1 -> x0, other arithmetic: 11.8 us -> none  [local(): w_down_grad = branch_sum.astype(full).reshape(w_down.shape)]
    ppermute x13 -> x11, starting transfers between devices: 23.3 us -> 12.9 us  [outer_shift(): return lax.ppermute(values_in, 'dp', pairs)]
    pallas_call x2 -> x3, Pallas kernels: 380 us -> 389 us  [the longest x2 378 us: chain_sum(): pl.pallas_call(functools.partial(chain_kernel, ways, size // ways, blocks...]
    ppermute x13 -> x11, waiting for transfers between devices: 78.7 us -> 86.5 us  [outer_shift(): return lax.ppermute(values_in, 'dp', pairs)]
  transfers between devices with their start and end apart: 62 -> 61, of which waited for: 35 -> 31; matrix products, arithmetic and copies ran while one was open for 25% -> 18% of each run, Pallas kernels for 37% -> 40%
where the time goes in v3:
time: 1030 us; the launch traced here: 1020 us
  Pallas kernels  407 us (40%)
  waiting for transfers between devices  225 us (22%)
  matrix products  112 us (11%)
  other arithmetic  97.5 us (9%)
  local copies, waits for them, and re-layouts  88.6 us (9%)
  starting transfers between devices  87.2 us (8%)
    pallas_call x2, Pallas kernels, chain_sum(): pl.pallas_call(functools.partial(chain_kernel, ways, size // ways, blocks...  378 us
    ppermute x11, waiting for transfers between devices, outer_shift(): return lax.ppermute(values_in, 'dp', pairs)  86.5 us
    dot_general x33, matrix products, contract(): lax.dot_general(left, right, (((left_dim,), (right_dim,)), ((), ())), pre...  86.1 us
    ppermute x19, waiting for transfers between devices, hid_swap(): return lax.ppermute(values_in, 'hid', [(i, i ^ bit) for i in range(size)])  82.4 us
    all_to_all x8, waiting for transfers between devices, exchange(): lax.all_to_all(values_in, 'hid', split_axis=0, concat_axis=0, tiled=True,...  43.5 us
    all_to_all x8, starting transfers between devices, exchange(): lax.all_to_all(values_in, 'hid', split_axis=0, concat_axis=0, tiled=True,...  30 us
    unnamed x263, local copies, waits for them, and re-layouts  24.5 us
    ppermute x19, starting transfers between devices, hid_swap(): return lax.ppermute(values_in, 'hid', [(i, i ^ bit) for i in range(size)])  23.2 us
  transfers between devices with their start and end apart: 61, of which 31 were waited for; matrix products, arithmetic and copies ran while one was open for 18% of the time, Pallas kernels for 40%

profile of v3, /device:TPU:0, one launch (start us, length us, event | category | flops | bytes accessed | tf_op | source)
XLA Modules:
  0.0 1020.7 jit_solution(4797837181339373681)
XLA Ops:
  2.4 7.3 all-to-all-start
  18.5 6.7 fusion.207
  40.1 6.2 all-to-all-start.4
  57.9 7.7 all-to-all-done.4
  95.8 12.4 %all-to-all-done.1 = bf16[4,64,1024]{2,1,0:T(8,128)(2,1)S(1)} async-done(((bf16[4,64,1024]{2,1,0:T(8,128)(2,1)}), bf16[4,64,1024]{2,1,0:T(8,128)(2,1)S(1)}, u32[]{:S(2)}, u32[]{:S(2)}) %all-to-all-start.1) | async-done | bytes 524320 | tf_op jit(solution)/shard_map/all_to_all | solution.py:185
  111.9 13.6 %all-to-all-done.6 = bf16[4,64,1024]{2,1,0:T(8,128)(2,1)S(1)} async-done(((bf16[4,64,1024]{2,1,0:T(8,128)(2,1)}), bf16[4,64,1024]{2,1,0:T(8,128)(2,1)S(1)}, u32[]{:S(2)}, u32[]{:S(2)}) %all-to-all-start.6) | async-done | bytes 524320 | tf_op jit(solution)/shard_map/all_to_all | solution.py:185
  147.8 11.2 %collective-permute-done = bf16[4,64,1024]{2,1,0:T(8,128)(2,1)} collective-permute-done((bf16[4,64,1024]{2,1,0:T(8,128)(2,1)S(1)}, bf16[4,64,1024]{2,1,0:T(8,128)(2,1)}, u32[]{:S(2)}, u32[]{:S(2)}) %collective-permute-start) | collective-permute-done | bytes 524320 | tf_op jit(solution)/shard_map/ppermute | solution.py:70
  170.2 9.4 collective-permute-done.12
  206.4 7.5 collective-permute-done.14
  230.2 9.3 collective-permute-done.10
  254.9 8.6 fusion.223
  267.8 25.2 %collective-permute-done.6 = bf16[1024,1024]{1,0:T(8,128)(2,1)} collective-permute-done((bf16[1024,1024]{1,0:T(8,128)(2,1)}, bf16[1024,1024]{1,0:T(8,128)(2,1)}, u32[]{:S(2)}, u32[]{:S(2)}) %collective-permute-start.6) | collective-permute-done | bytes 2097184 | tf_op jit(solution)/shard_map/ppermute | solution.py:65
  297.0 10.4 %multiply_convert_fusion.2 = (bf16[1024,1024]{1,0:T(8,128)(2,1)S(1)}, f32[1024,1024]{1,0:T(8,128)}) fusion(f32[1024,1024]{1,0:T(8,128)S(1)} %add_add_fusion), kind=kLoop, calls=%fused_computation.26 | loop fusion | flops 68157440 | bytes 10485760 | tf_op jit(solution)/shard_map/convert_element_type | solution.py:713
  332.7 17.8 %collective-permute-done.21 = bf16[512,1024]{1,0:T(8,128)(2,1)} collective-permute-done((bf16[512,1024]{1,0:T(8,128)(2,1)}, bf16[512,1024]{1,0:T(8,128)(2,1)}, u32[]{:S(2)}, u32[]{:S(2)}) %collective-permute-start.21) | collective-permute-done | bytes 1048608 | tf_op jit(solution)/shard_map/ppermute | solution.py:65
  404.9 10.9 %collective-permute-done.29 = bf16[4,64,1024]{2,1,0:T(8,128)(2,1)S(1)} collective-permute-done((bf16[4,64,1024]{2,1,0:T(8,128)(2,1)S(1)}, bf16[4,64,1024]{2,1,0:T(8,128)(2,1)S(1)}, u32[]{:S(2)}, u32[]{:S(2)}) %collective-permute-start.29) | collective-permute-done | bytes 524320 | tf_op jit(solution)/shard_map/ppermute | solution.py:70
  418.0 21.2 %collective-permute-done.31 = bf16[512,1024]{1,0:T(8,128)(2,1)} collective-permute-done((bf16[512,1024]{1,0:T(8,128)(2,1)}, bf16[512,1024]{1,0:T(8,128)(2,1)}, u32[]{:S(2)}, u32[]{:S(2)}) %collective-permute-start.31) | collective-permute-done | bytes 1048608 | tf_op jit(solution)/shard_map/ppermute | solution.py:65
  448.1 5.9 fusion.33
  472.8 12.5 %multiply_convert_fusion.1 = bf16[1024,1024]{1,0:T(8,128)(2,1)} fusion(f32[1024,1024]{1,0:T(8,128)} %get-tuple-element.110, f32[1024,1024]{1,0:T(8,128)} %copy-done.38, bf16[1024,2048]{1,0:T(8,128)(2,1)} %pad_maximum_fusion.1, bf16[2048,1024]{1,0:T(8,128)(2,1)} %copy-done.10), kind=kOutput, calls=%fused_computation.20 | convolution fusion | flops 4307550208 | bytes 18874368 | tf_op jit(solution)/shard_map/dot_general | solution.py:29
  492.8 128.8 %shard_map.254 = bf16[2,64,16,2048]{3,2,1,0:T(8,128)(2,1)} custom-call(bf16[1024,1024]{1,0:T(8,128)(2,1)} %copy-done.4, bf16[2048,1024]{1,0:T(8,128)(2,1)} %copy-done.10), custom_call_target="tpu_custom_call" | custom-call | flops 4294967296 | bytes 629145600 | tf_op jit(solution)/shard_map/pallas_call | solution.py:374
  647.6 5.9 multiply_reduce_fusion.1
  665.2 18.0 %collective-permute-done.38 = bf16[4,64,1024]{2,1,0:T(8,128)(2,1)S(1)} collective-permute-done((bf16[4,64,1024]{2,1,0:T(8,128)(2,1)S(1)}, bf16[4,64,1024]{2,1,0:T(8,128)(2,1)S(1)}, u32[]{:S(2)}, u32[]{:S(2)}) %collective-permute-start.38) | collective-permute-done | bytes 524320 | tf_op jit(solution)/shard_map/ppermute | solution.py:70
  705.6 249.5 %shard_map.255 = bf16[2,128,32,1024]{3,2,1,0:T(8,128)(2,1)} custom-call(bf16[4096,1024]{1,0:T(8,128)(2,1)} %copy-done.13, bf16[1024,1024]{1,0:T(8,128)(2,1)} %copy-done.15, bf16[1024,1024]{1,0:T(8,128)(2,1)} %copy-done.16, bf16[1024,1024]{1,0:T(8,128)(2,1)} %copy-done.14, bf16[2048,1024]{1,0:T(8,128)(2,1)} %copy-done.10, bf16[512,1024]{1,0:T(8,128)(2,1)} %copy-done.33, ...), custom_call_target="tpu_custom_call" | custom-call | flops 8589934592 | bytes 1258291200 | tf_op jit(solution)/shard_map/pallas_call | solution.py:374
  973.4 10.3 %shard_map.257 = f32[2048,2048]{1,0:T(8,128)} custom-call(bf16[2048,2048]{1,0:T(8,128)(2,1)} %bitcast.657), custom_call_target="tpu_custom_call" | custom-call | bytes 25165824 | tf_op jit(solution)/shard_map/pallas_call | solution.py:492
  997.8 18.7 %shard_map.256 = (f32[512,8192]{1,0:T(8,128)}, f32[512,2048]{1,0:T(8,128)}, f32[512,2048]{1,0:T(8,128)}, f32[512,2048]{1,0:T(8,128)}, f32[512,2048]{1,0:T(8,128)}) custom-call(bf16[2,8,512,1024]{3,2,1,0:T(8,128)(2,1)} %bitcast.642, bf16[2,8,512,1024]{3,2,1,0:T(8,128)(2,1)} %bitcast.643, bf16[2,8,512,1024]{3,2,1,0:T(8,128)(2,1)} %bitcast.644), custom_call_target="tpu_custom_call" | custom-call | bytes 50331648 | tf_op jit(solution)/shard_map/pallas_call | solution.py:468
  (611 shorter events, 382.3 us)
Async XLA Ops:
  2.4 36.8 %all-to-all-start = ((f32[32,32,128]{2,1,0:T(8,128)}), f32[32,32,128]{2,1,0:T(8,128)S(1)}, u32[]{:S(2)}, u32[]{:S(2)}) async-start(f32[32,32,128]{2,1,0:T(8,128)} %broadcast_in_dim.17), calls=%async_computation | async-start | bytes 1048576 | tf_op jit(solution)/shard_map/all_to_all | solution.py:160
  40.1 25.4 %all-to-all-start.4 = ((f32[32,37,128]{2,1,0:T(8,128)}), f32[32,37,128]{2,1,0:T(8,128)S(1)}, u32[]{:S(2)}, u32[]{:S(2)}) async-start(f32[32,37,128]{2,1,0:T(8,128)} %broadcast_in_dim.19), calls=%async_computation.4 | async-start | bytes 1310720 | tf_op jit(solution)/shard_map/all_to_all | solution.py:160
  134.8 24.2 %collective-permute-start = (bf16[4,64,1024]{2,1,0:T(8,128)(2,1)S(1)}, bf16[4,64,1024]{2,1,0:T(8,128)(2,1)}, u32[]{:S(2)}, u32[]{:S(2)}) collective-permute-start(bf16[4,64,1024]{2,1,0:T(8,128)(2,1)S(1)} %all-to-all-done.1), channel_id=1, source_target_pairs={{0,1},{1,0},{2,3},{3,2},{4,5},{5,4},{6,7},{7,6},{8,9},{9,8},{10,11... | collective-permute-start | bytes 1572872 | tf_op jit(solution)/shard_map/ppermute | solution.py:70
  135.1 35.2 %collective-permute-start.16 = (bf16[4,64,1024]{2,1,0:T(8,128)(2,1)S(1)}, bf16[4,64,1024]{2,1,0:T(8,128)(2,1)}, u32[]{:S(2)}, u32[]{:S(2)}) collective-permute-start(bf16[4,64,1024]{2,1,0:T(8,128)(2,1)S(1)} %all-to-all-done.6), channel_id=1, source_target_pairs={{0,1},{1,0},{2,3},{3,2},{4,5},{5,4},{6,7},{7,6},{8,9},{9,8},{10,11... | collective-permute-start | bytes 1572872 | tf_op jit(solution)/shard_map/ppermute | solution.py:70
  142.9 36.8 %collective-permute-start.12 = (bf16[4,64,1024]{2,1,0:T(8,128)(2,1)S(1)}, bf16[4,64,1024]{2,1,0:T(8,128)(2,1)S(1)}, u32[]{:S(2)}, u32[]{:S(2)}) collective-permute-start(bf16[4,64,1024]{2,1,0:T(8,128)(2,1)S(1)} %all-to-all-done.5), channel_id=1, source_target_pairs={{0,1},{1,0},{2,3},{3,2},{4,5},{5,4},{6,7},{7,6},{8,9},{9,8},{10,11... | collective-permute-start | bytes 1572872 | tf_op jit(solution)/shard_map/ppermute | solution.py:70
  188.8 79.0 %collective-permute-start.7 = (bf16[1024,1024]{1,0:T(8,128)(2,1)}, bf16[1024,1024]{1,0:T(8,128)(2,1)}, u32[]{:S(2)}, u32[]{:S(2)}) collective-permute-start(bf16[1024,1024]{1,0:T(8,128)(2,1)} %convolution_convert_fusion), channel_id=1, source_target_pairs={{0,8},{8,0},{16,24},{24,16},{1,9},{9,1},{17,25},{25,17},{2,10},{10... | collective-permute-start | bytes 6291464 | tf_op jit(solution)/shard_map/ppermute | solution.py:56
  192.6 49.3 %collective-permute-start.5 = (bf16[1024,1024]{1,0:T(8,128)(2,1)}, bf16[1024,1024]{1,0:T(8,128)(2,1)}, u32[]{:S(2)}, u32[]{:S(2)}) collective-permute-start(bf16[1024,1024]{1,0:T(8,128)(2,1)} %convolution_convert_fusion.1), channel_id=1, source_target_pairs={{0,8},{8,0},{16,24},{24,16},{1,9},{9,1},{17,25},{25,17},{2,10},{10... | collective-permute-start | bytes 6291464 | tf_op jit(solution)/shard_map/ppermute | solution.py:56
  203.7 26.6 %collective-permute-start.11 = (bf16[256,1024]{1,0:T(8,128)(2,1)}, bf16[256,1024]{1,0:T(8,128)(2,1)}, u32[]{:S(2)}, u32[]{:S(2)}) collective-permute-start(bf16[256,1024]{1,0:T(8,128)(2,1)} %convolution_convert_fusion.6), channel_id=1, source_target_pairs={{0,8},{8,0},{16,24},{24,16},{1,9},{9,1},{17,25},{25,17},{2,10},{10... | collective-permute-start | bytes 1572872 | tf_op jit(solution)/shard_map/ppermute | solution.py:56
  246.8 46.2 %collective-permute-start.6 = (bf16[1024,1024]{1,0:T(8,128)(2,1)}, bf16[1024,1024]{1,0:T(8,128)(2,1)}, u32[]{:S(2)}, u32[]{:S(2)}) collective-permute-start(bf16[1024,1024]{1,0:T(8,128)(2,1)} %add_convert_fusion), channel_id=1, source_target_pairs={{0,16},{8,24},{16,0},{24,8},{1,17},{9,25},{17,1},{25,9},{2,18},{10... | collective-permute-start | bytes 6291464 | tf_op jit(solution)/shard_map/ppermute | solution.py:65
  325.2 25.3 %collective-permute-start.21 = (bf16[512,1024]{1,0:T(8,128)(2,1)}, bf16[512,1024]{1,0:T(8,128)(2,1)}, u32[]{:S(2)}, u32[]{:S(2)}) collective-permute-start(bf16[512,1024]{1,0:T(8,128)(2,1)} %add_convert_fusion.2), channel_id=1, source_target_pairs={{0,16},{8,24},{16,0},{24,8},{1,17},{9,25},{17,1},{25,9},{2,18},{10... | collective-permute-start | bytes 3145736 | tf_op jit(solution)/shard_map/ppermute | solution.py:65
  417.0 22.3 %collective-permute-start.31 = (bf16[512,1024]{1,0:T(8,128)(2,1)}, bf16[512,1024]{1,0:T(8,128)(2,1)}, u32[]{:S(2)}, u32[]{:S(2)}) collective-permute-start(bf16[512,1024]{1,0:T(8,128)(2,1)} %bitcast.150), channel_id=1, source_target_pairs={{0,16},{8,24},{16,0},{24,8},{1,17},{9,25},{17,1},{25,9},{2,18},{10... | collective-permute-start | bytes 3145736 | tf_op jit(solution)/shard_map/ppermute | solution.py:65
  418.0 22.3 %collective-permute-start.30 = (bf16[512,1024]{1,0:T(8,128)(2,1)}, bf16[512,1024]{1,0:T(8,128)(2,1)}, u32[]{:S(2)}, u32[]{:S(2)}) collective-permute-start(bf16[512,1024]{1,0:T(8,128)(2,1)} %bitcast.150), channel_id=1, source_target_pairs={{0,8},{8,0},{16,24},{24,16},{1,9},{9,1},{17,25},{25,17},{2,10},{10... | collective-permute-start | bytes 3145736 | tf_op jit(solution)/shard_map/ppermute | solution.py:56
  486.6 135.0 %collective-permute-start.33 = (bf16[1024,1024]{1,0:T(8,128)(2,1)}, bf16[1024,1024]{1,0:T(8,128)(2,1)}, u32[]{:S(2)}, u32[]{:S(2)}) collective-permute-start(bf16[1024,1024]{1,0:T(8,128)(2,1)} %multiply_convert_fusion.1), channel_id=1, source_target_pairs={{0,16},{8,24},{16,0},{24,8},{1,17},{9,25},{17,1},{25,9},{2,18},{10... | collective-permute-start | bytes 6291464 | tf_op jit(solution)/shard_map/ppermute | solution.py:65
  487.6 134.0 %collective-permute-start.34 = (bf16[768,1024]{1,0:T(8,128)(2,1)}, bf16[768,1024]{1,0:T(8,128)(2,1)}, u32[]{:S(2)}, u32[]{:S(2)}) collective-permute-start(bf16[768,1024]{1,0:T(8,128)(2,1)} %pad_maximum_fusion.7), channel_id=1, source_target_pairs={{0,16},{8,24},{16,0},{24,8},{1,17},{9,25},{17,1},{25,9},{2,18},{10... | collective-permute-start | bytes 4718600 | tf_op jit(solution)/shard_map/ppermute | solution.py:65
  488.6 133.0 %all-to-all-start.8 = ((bf16[4,64,1024]{2,1,0:T(8,128)(2,1)}), bf16[4,64,1024]{2,1,0:T(8,128)(2,1)}, u32[]{:S(2)}, u32[]{:S(2)}) async-start(bf16[4,64,1024]{2,1,0:T(8,128)(2,1)} %bitcast.155), calls=%async_computation.8 | async-start | bytes 1048576 | tf_op jit(solution)/shard_map/all_to_all | solution.py:185
  624.9 21.6 %collective-permute-start.40 = (bf16[1024,1024]{1,0:T(8,128)(2,1)}, bf16[1024,1024]{1,0:T(8,128)(2,1)S(1)}, u32[]{:S(2)}, u32[]{:S(2)}) collective-permute-start(bf16[1024,1024]{1,0:T(8,128)(2,1)} %collective-permute-done.33), channel_id=1, source_target_pairs={{0,8},{8,0},{16,24},{24,16},{1,9},{9,1},{17,25},{25,17},{2,10},{10... | collective-permute-start | bytes 6291464 | tf_op jit(solution)/shard_map/ppermute | solution.py:56
  635.7 53.1 %collective-permute-start.45 = (bf16[4,64,1024]{2,1,0:T(8,128)(2,1)}, bf16[4,64,1024]{2,1,0:T(8,128)(2,1)}, u32[]{:S(2)}, u32[]{:S(2)}) collective-permute-start(bf16[4,64,1024]{2,1,0:T(8,128)(2,1)} %fusion.93), channel_id=1, source_target_pairs={{0,1},{1,0},{2,3},{3,2},{4,5},{5,4},{6,7},{7,6},{8,9},{9,8},{10,11... | collective-permute-start | bytes 1572872 | tf_op jit(solution)/shard_map/ppermute | solution.py:70
  656.8 28.4 %collective-permute-start.44 = (bf16[4,64,1024]{2,1,0:T(8,128)(2,1)}, bf16[4,64,1024]{2,1,0:T(8,128)(2,1)}, u32[]{:S(2)}, u32[]{:S(2)}) collective-permute-start(bf16[4,64,1024]{2,1,0:T(8,128)(2,1)} %fusion.92), channel_id=1, source_target_pairs={{0,1},{1,0},{2,3},{3,2},{4,5},{5,4},{6,7},{7,6},{8,9},{9,8},{10,11... | collective-permute-start | bytes 1572872 | tf_op jit(solution)/shard_map/ppermute | solution.py:70
  660.5 22.7 %collective-permute-start.38 = (bf16[4,64,1024]{2,1,0:T(8,128)(2,1)S(1)}, bf16[4,64,1024]{2,1,0:T(8,128)(2,1)S(1)}, u32[]{:S(2)}, u32[]{:S(2)}) collective-permute-start(bf16[4,64,1024]{2,1,0:T(8,128)(2,1)S(1)} %fusion.91), channel_id=1, source_target_pairs={{0,1},{1,0},{2,3},{3,2},{4,5},{5,4},{6,7},{7,6},{8,9},{9,8},{10,11... | collective-permute-start | bytes 1572872 | tf_op jit(solution)/shard_map/ppermute | solution.py:70
  664.1 28.9 %collective-permute-start.46 = (bf16[4,64,1024]{2,1,0:T(8,128)(2,1)}, bf16[4,64,1024]{2,1,0:T(8,128)(2,1)}, u32[]{:S(2)}, u32[]{:S(2)}) collective-permute-start(bf16[4,64,1024]{2,1,0:T(8,128)(2,1)} %fusion.94), channel_id=1, source_target_pairs={{0,1},{1,0},{2,3},{3,2},{4,5},{5,4},{6,7},{7,6},{8,9},{9,8},{10,11... | collective-permute-start | bytes 1572872 | tf_op jit(solution)/shard_map/ppermute | solution.py:70
  700.3 254.9 %all-to-all-start.9 = ((bf16[4,4,64,1024]{3,2,1,0:T(8,128)(2,1)}), bf16[4,4,64,1024]{3,2,1,0:T(8,128)(2,1)S(1)}, u32[]{:S(2)}, u32[]{:S(2)}) async-start(bf16[4,4,64,1024]{3,2,1,0:T(8,128)(2,1)} %pad_maximum_fusion.6), calls=%async_computation.9 | async-start | bytes 4194304 | tf_op jit(solution)/shard_map/all_to_all | solution.py:185
  966.8 22.3 %collective-permute-start.48 = (f32[40,256]{1,0:T(8,128)S(1)}, f32[40,256]{1,0:T(8,128)S(1)}, u32[]{:S(2)}, u32[]{:S(2)}) collective-permute-start(f32[40,256]{1,0:T(8,128)S(1)} %add.987), channel_id=1, source_target_pairs={{0,4},{1,5},{2,6},{3,7},{4,0},{5,1},{6,2},{7,3},{8,12},{9,13},{10,... | collective-permute-start | bytes 122888 | tf_op jit(solution)/shard_map/ppermute | solution.py:70
  985.8 32.4 %all-to-all-start.10 = ((f32[32,32,128]{2,1,0:T(8,128)}), f32[32,32,128]{2,1,0:T(8,128)}, u32[]{:S(2)}, u32[]{:S(2)}) async-start(f32[32,32,128]{2,1,0:T(8,128)} %copy.260), calls=%async_computation.10 | async-start | bytes 1048576 | tf_op jit(solution)/shard_map/all_to_all | solution.py:867
  990.7 25.8 %collective-permute-start.49 = (f32[40,4,64]{2,1,0:T(4,128)S(1)}, f32[40,4,64]{2,1,0:T(4,128)S(1)}, u32[]{:S(2)}, u32[]{:S(2)}) collective-permute-start(f32[40,4,64]{2,1,0:T(4,128)S(1)} %reshape.776), channel_id=1, source_target_pairs={{0,1},{1,0},{2,3},{3,2},{4,5},{5,4},{6,7},{7,6},{8,9},{9,8},{10,11... | collective-permute-start | bytes 122888 | tf_op jit(solution)/shard_map/ppermute | solution.py:70
  (157 other events, 3316.1 us)

commit v4 on v3

--- a/solution.py
+++ b/solution.py
@@ -184,6 +184,378 @@
         groups = [[t * ways + w for t in range(size // ways)] for w in range(ways)]
     return lax.all_to_all(
         values_in, "hid", split_axis=0, concat_axis=0, tiled=True, axis_index_groups=groups
+    )
+
+
+def forward_kernel(dims, *refs):
+    places, piece, group, n_head, n_units = dims
+    (send_ref, mom_ref, gains_ref, query_ref, key_ref, value_ref, up_ref), refs = refs[:7], refs[7:]
+    (
+        normed_ref,
+        own_ref,
+        shift_ref,
+        active_ref,
+        slope_ref,
+        heads_ref,
+        turned_ref,
+        turned_up_ref,
+    ), refs = refs[:8], refs[8:]
+    (
+        devs,
+        moms,
+        joins,
+        weights,
+        core_out,
+        core_in,
+        outer_out,
+        outer_in,
+        mom_send,
+        mom_recv,
+        dev_send,
+        dev_recv,
+        way_send,
+        way_recv,
+        pair_send,
+        pair_recv,
+        join_send,
+        join_recv,
+        weight_sem,
+        turned_sem,
+        core_send,
+        core_recv,
+        outer_send,
+        outer_recv,
+    ) = refs
+    count = weights.shape[0]
+    ups = n_units // n_head
+    index, hid = lax.axis_index("dp"), lax.axis_index("hid")
+    outer, core = index // 2, index % 2
+    place, way = hid // 2, hid % 2
+    me = index * 2 + way
+    partner = {"hid": hid + 1 - 2 * way}
+    core_peer = {"dp": index + 1 - 2 * core}
+    outer_peer = {"dp": (index + 2) % 4}
+
+    def remote(source, target, send, recv, device):
+        return pltpu.make_async_remote_copy(
+            src_ref=source,
+            dst_ref=target,
+            send_sem=send,
+            recv_sem=recv,
+            device_id=device,
+            device_id_type=pl.DeviceIdType.MESH,
+        )
+
+    def peer(k):
+        return (place + k) % places
+
+    def z_device(k):
+        return {"hid": peer(k) * 2 + way}
+
+    others = [(i, j) for i in range(4) for j in range(2) if i or j]
+
+    def join_device(i, j):
+        return {"dp": (index + i) % 4, "hid": place * 2 + (way + j) % 2}
+
+    def weight_copy(unit, t):
+        there = (1 - outer if t < 2 else outer) * 2 + (core if t % 2 else 1 - core)
+        block = there * 2 + way
+        if unit < ups:
+            source, start = up_ref, block * n_units + unit * n_head
+        else:
+            source, start = (query_ref, key_ref, value_ref)[unit - ups], block * n_head
+        start = pl.multiple_of(start, n_head)
+        return pltpu.make_async_copy(
+            source.at[:, pl.ds(start, n_head)], weights.at[unit, t], weight_sem.at[unit]
+        )
+
+    for unit in range(count):
+        for t in range(4):
+            weight_copy(unit, t).start()
+
+    barrier = pltpu.get_barrier_semaphore()
+
+    def greet(device):
+        pl.semaphore_signal(barrier, inc=1, device_id=device, device_id_type=pl.DeviceIdType.MESH)
+
+    for k in range(1, places):
+        greet(z_device(k))
+    for i, j in others:
+        greet(join_device(i, j))
+    pl.semaphore_wait(barrier, places - 1 + len(others))
+
+    def mom_copy(k, sender, target):
+        return remote(
+            mom_ref.at[target], moms.at[way, sender], mom_send, mom_recv.at[sender], z_device(k)
+        )
+
+    def dev_copy(s, k, sender, target):
+        return remote(
+            send_ref.at[target, s],
+            devs.at[s, way, sender],
+            dev_send,
+            dev_recv.at[s, sender],
+            z_device(k),
+        )
+
+    for k in range(1, places):
+        mom_copy(k, place, peer(k)).start()
+    for s in (3, 0, 1, 2):
+        for k in range(1, places):
+            dev_copy(s, k, place, peer(k)).start()
+    moms[way, place] = mom_ref[place]
+    for s in range(STREAMS):
+        devs[s, way, place] = send_ref[place, s]
+
+    def way_copy(source, s, q):
+        return remote(source, devs.at[s, way, q], way_send, way_recv.at[s], partner)
+
+    def forward(s):
+        way_copy(send_ref.at[place, s], s, place).start()
+        for k in range(1, places):
+            q = peer(k)
+            dev_copy(s, k, q, q).wait_recv()
+            way_copy(devs.at[s, way, q], s, q).start()
+
+    def join_parts(means, parts, size):
+        mean = means[0]
+        for m in means[1:]:
+            mean = mean + m
+        mean = mean / len(means)
+        total = parts[0]
+        for v in parts[1:]:
+            total = total + v
+        for m in means:
+            total = total + size * (m - mean) * (m - mean)
+        return mean, total
+
+    for k in range(1, places):
+        mom_copy(k, peer(k), place).wait_recv()
+    remote(moms.at[way], moms.at[way], pair_send, pair_recv, partner).start()
+    mean, total = join_parts(
+        [moms[way, q, :STREAMS, :] for q in range(places)],
+        [moms[way, q, STREAMS:, :] for q in range(places)],
+        piece,
+    )
+    joins[me, :STREAMS, :] = mean
+    joins[me, STREAMS:, :] = total
+    for i, j in others:
+        remote(joins.at[me], joins.at[me], join_send, join_recv, join_device(i, j)).start()
+    forward(3)
+    n_others = len(others)
+    remote(
+        joins.at[pl.ds(0, n_others)], joins.at[pl.ds(0, n_others)], join_send, join_recv, partner
+    ).wait_recv()
+    remote(moms.at[way], moms.at[1 - way], pair_send, pair_recv, partner).wait_recv()
+    mean, total = join_parts(
+        [joins[i, :STREAMS, :] for i in range(n_others + 1)],
+        [joins[i, STREAMS:, :] for i in range(n_others + 1)],
+        piece * places,
+    )
+    scale = lax.rsqrt(total / (piece * places * (n_others + 1)) + 1e-05)
+    for s in range(STREAMS):
+        for q in range(places):
+            for w in range(2):
+                off = moms[w, q, s : s + 1, :] - mean[s : s + 1]
+                shift_ref[s, 2 * q + w : 2 * q + w + 1, :] = off * scale[s : s + 1]
+        shift_ref[s, 2 * places : 2 * places + 1, :] = scale[s : s + 1]
+        shift_ref[s, 2 * places + 1 : 2 * places + 2, :] = mean[s : s + 1]
+
+    def normalize(s):
+        remote(devs.at[s, 1 - way], devs.at[s, 1 - way], way_send, way_recv.at[s], partner).wait_recv()
+        size = shift_ref[s, 2 * places : 2 * places + 1, :]
+        for q in range(places):
+            for w in range(2):
+                block = 2 * q + w
+                rows = slice(block * piece, (block + 1) * piece)
+                unit = devs[s, w, q].astype(full) * size + shift_ref[s, block : block + 1, :]
+                normed_ref[s, rows, :] = (unit * gains_ref[s, rows, :]).astype(low)
+
+    def core_copy(unit, half):
+        return remote(
+            core_out.at[unit, half],
+            core_in.at[unit, half],
+            core_send,
+            core_recv.at[unit, half],
+            core_peer,
+        )
+
+    def outer_copy(unit):
+        return remote(
+            outer_out.at[unit], outer_in.at[unit], outer_send, outer_recv.at[unit], outer_peer
+        )
+
+    def project(unit, carry):
+        @pl.when(unit == 0)
+        def _():
+            normalize(3)
+            forward(0)
+
+        for s in (1, 2):
+
+            @pl.when(unit == s)
+            def _(s=s):
+                forward(s)
+
+        @pl.when(unit >= ups)
+        def _():
+            normalize(unit - ups)
+
+        stream = jnp.where(unit < ups, 3, unit - ups)
+        pltpu.make_async_copy(weights.at[unit], weights.at[unit], weight_sem.at[unit]).wait()
+
+        def product(t):
+            return lax.dot_general(
+                weights[unit, t],
+                normed_ref[stream],
+                (((0,), (0,)), ((), ())),
+                preferred_element_type=full,
+            )
+
+        core_out[unit, 0] = product(0).astype(low)
+        core_copy(unit, 0).start()
+        passing = product(1)
+        core_out[unit, 1] = product(2).astype(low)
+        core_copy(unit, 1).start()
+        core_copy(unit, 0).wait_recv()
+        outer_out[unit] = (passing + core_in[unit, 0].astype(full)).astype(low)
+        outer_copy(unit).start()
+        kept = product(3)
+        core_copy(unit, 1).wait_recv()
+        kept = kept + core_in[unit, 1].astype(full)
+
+        @pl.when(unit < ups)
+        def _():
+            slope_ref[pl.ds(pl.multiple_of(unit * n_head, n_head), n_head), :] = kept
+
+        @pl.when(unit >= ups)
+        def _():
+            heads_ref[unit - ups] = kept
+
+        return carry
+
+    lax.fori_loop(0, count, project, 0)
+
+    def turned_copies():
+        for unit in range(count):
+            for t in range(4):
+                turn = 3 - t
+                if unit < ups:
+                    start = turn * n_units + unit * n_head
+                    target = turned_up_ref.at[:, start : start + n_head]
+                else:
+                    target = turned_ref.at[unit - ups, :, turn * n_head : (turn + 1) * n_head]
+                yield pltpu.make_async_copy(weights.at[unit, t], target, turned_sem)
+
+    for copy in turned_copies():
+        copy.start()
+    for s in range(STREAMS):
+        own_ref[s] = devs[s, way]
+
+    step = 32
+
+    def finish_up(unit, carry):
+        outer_copy(unit).wait_recv()
+
+        def part(i, carry):
+            inner = pl.ds(pl.multiple_of(i * step, step), step)
+            rows = pl.ds(pl.multiple_of(unit * n_head + i * step, step), step)
+            hidden = slope_ref[rows, :] + outer_in[unit, inner, :].astype(full)
+            half = 0.5 + 0.5 * lax.erf(hidden * math.sqrt(0.5))
+            active_ref[rows, :] = (hidden * half).astype(low)
+            bell = jnp.exp(-0.5 * hidden * hidden) * (1.0 / math.sqrt(2.0 * math.pi))
+            slope_ref[rows, :] = half + hidden * bell
+            return carry
+
+        return lax.fori_loop(0, n_head // step, part, carry)
+
+    lax.fori_loop(0, ups, finish_up, 0)
+
+    def finish_head(unit, carry):
+        outer_copy(unit).wait_recv()
+        heads_ref[unit - ups] = heads_ref[unit - ups] + outer_in[unit].astype(full)
+        return carry
+
+    lax.fori_loop(ups, count, finish_head, 0)
+
+    def sent(ref, sem):
+        remote(ref, ref, sem, join_recv, partner).wait_send()
+
+    sent(moms.at[0, pl.ds(0, places - 1)], mom_send)
+    sent(send_ref.at[pl.ds(0, places - 1)], dev_send)
+    sent(send_ref, way_send)
+    sent(moms.at[0], pair_send)
+    sent(joins.at[pl.ds(0, n_others)], join_send)
+    sent(core_out, core_send)
+    sent(outer_out, outer_send)
+    pltpu.make_async_copy(weights, weights, turned_sem).wait()
+
+
+def forward_projections(deviations, moments, norm_gains, w_query, w_key, w_value, w_up):
+    places, _, piece, group = deviations.shape
+    feats = norm_gains.shape[0]
+    n_head = w_query.shape[1] // 8
+    n_units = w_up.shape[1] // 8
+    count = n_units // n_head + 3
+    vmem, dma = pltpu.VMEM, pltpu.SemaphoreType.DMA
+    out_types = [
+        ((STREAMS, feats, group), low),
+        ((STREAMS, places, piece, group), low),
+        ((STREAMS, 2 * places + 8, group), full),
+        ((n_units, group), low),
+        ((n_units, group), full),
+        ((3, n_head, group), full),
+        ((3, feats, 4 * n_head), low),
+        ((feats, 4 * n_units), low),
+    ]
+    spaces = [vmem] * 6 + [pl.ANY] * 2
+    return pl.pallas_call(
+        functools.partial(forward_kernel, (places, piece, group, n_head, n_units)),
+        out_shape=[jax.ShapeDtypeStruct(*t) for t in out_types],
+        in_specs=[pl.BlockSpec(memory_space=vmem)] * 3 + [pl.BlockSpec(memory_space=pl.ANY)] * 4,
+        out_specs=[pl.BlockSpec(memory_space=m) for m in spaces],
+        scratch_shapes=[
+            vmem((STREAMS, 2, places, piece, group), low),
+            vmem((2, places, 2 * STREAMS, group), full),
+            vmem((8, 2 * STREAMS, group), full),
+            vmem((count, 4, feats, n_head), low),
+            vmem((count, 2, n_head, group), low),
+            vmem((count, 2, n_head, group), low),
+            vmem((count, n_head, group), low),
+            vmem((count, n_head, group), low),
+            dma,
+            dma((places,)),
+            dma,
+            dma((STREAMS, places)),
+            dma,
+            dma((STREAMS,)),
+            dma,
+            dma,
+            dma,
+            dma,
+            dma((count,)),
+            dma,
+            dma,
+            dma((count, 2)),
+            dma,
+            dma((count,)),
+        ],
+        compiler_params=pltpu.CompilerParams(
+            collective_id=7, has_side_effects=True, vmem_limit_bytes=62 << 20
+        ),
+        cost_estimate=pl.CostEstimate(
+            flops=8 * count * n_head * feats * group,
+            bytes_accessed=300 << 20,
+            transcendentals=2 * n_units * group,
+        ),
+    )(
+        deviations,
+        moments,
+        norm_gains.T.astype(full)[:, :, None],
+        w_query,
+        w_key,
+        w_value,
+        w_up,
     )
 
 
@@ -577,22 +949,9 @@
         off = total - own_means[s]
         own_devs.append(jnp.sum(off * off, axis=0))
         deviations.append(off.astype(low))
-    moments = exchange(by_place(jnp.stack(own_means + own_devs, axis=0)))
-    deviations[3] = exchange(by_place(deviations[3]))
-    for s in range(3):
-        deviations[s] = exchange(by_place(deviations[s]))
-    def join_moments(mean_parts, dev_parts, size):
-        mean = jnp.mean(mean_parts, axis=0)
-        spread = size * jnp.sum(jnp.square(mean_parts - mean), axis=0)
-        return mean, jnp.sum(dev_parts, axis=0) + spread
-
-    block_means = moments[:, :STREAMS]
-    joined = join_moments(block_means, moments[:, STREAMS:], piece)
-    joined = gather_dp(gather_ways(jnp.concatenate(joined, axis=0), 0))
-    joined = joined.reshape((dp * ways,) + joined.shape[2:])
-    means, variance = join_moments(joined[:, :STREAMS], joined[:, STREAMS:], mine)
-    inv_scales = lax.rsqrt(variance / width + 1e-05)
-    all_means = gather_ways(block_means, 1)
+    moments = by_place(jnp.stack(own_means + own_devs, axis=0))
+    deviations = by_place(jnp.stack(deviations, axis=0))
+    fused = dp == 4 and ways == 2 and rows == 1
 
     table = jnp.concatenate([mix_cotangent.T, segment_ids.astype(full)[None]], axis=0)
     table = lax.dynamic_slice_in_dim(gather_all(table), place * group, group, 1)
@@ -617,20 +976,9 @@
         parts = values_in.reshape((places, piece) + values_in.shape[1:])
         return gather_ways(parts, 1).reshape((feats,) + values_in.shape[1:])
 
-    def unit(values_in, block_mean, s):
-        return (values_in.astype(full) + (block_mean - means[s])[..., None, :]) * inv_scales[s]
-
     own_gains = own_rows(norm_gains).astype(full)
     gains = [own_gains[:, s][:, None] for s in range(STREAMS)]
     all_gains = norm_gains.astype(full)
-    units = [
-        unit(deviations[s], block_means[:, s], s).reshape(mine, group) for s in range(STREAMS)
-    ]
-    normed = []
-    for s in range(STREAMS):
-        both = unit(gather_ways(deviations[s], 1), all_means[:, :, s], s).reshape(feats, group)
-        normed.append((both * all_gains[:, s][:, None]).astype(low))
-    residual = (deviations[3].astype(full) + block_means[:, 3][:, None]).reshape(mine, group)
 
     def project(weight, left):
         columns = weight.shape[1] // dp // ways
@@ -657,30 +1005,75 @@
     def by_head(values_in):
         return values_in.reshape(heads, HEAD, group)
 
-    hidden = project(w_up, normed[3])
-    queries = rotate(by_head(project(w_query, normed[0])), cosine, sine).astype(low)
-    keys = rotate(by_head(project(w_key, normed[1])), cosine, sine).astype(low)
-    values = by_head(project(w_value, normed[2])).astype(low)
-    cotangent, queries = lax.optimization_barrier((out_cotangent, queries))
-    upstream = exchange(by_place(cotangent.T)).reshape(mine, group)
-
     def turned(weight, stride, offset, size):
         starts = [turn_source(turn) * stride + offset for turn in range(dp)]
         parts = [lax.dynamic_slice_in_dim(weight, start, size, 1) for start in starts]
         return jnp.concatenate(parts, axis=1)
 
     n_head = heads * HEAD
-    n_units = hidden.shape[0]
+    n_units = w_up.shape[1] // dp // ways
+    if fused:
+        normed, deviations, shifts, active, slope, products, turned_heads, turned_up = (
+            forward_projections(deviations, moments, norm_gains, w_query, w_key, w_value, w_up)
+        )
+        inv_scales = shifts[:, 2 * places]
+        own_shifts = shifts[:, : 2 * places].reshape(STREAMS, places, ways, group)
+        own_shifts = lax.dynamic_index_in_dim(own_shifts, way, 2, keepdims=False)
+        offset = own_shifts[3] / inv_scales[3] + shifts[3, 2 * places + 1]
+        residual = (deviations[3].astype(full) + offset[:, None]).reshape(mine, group)
+        units = [
+            (deviations[s].astype(full) * inv_scales[s] + own_shifts[s][:, None]).reshape(mine, group)
+            for s in range(STREAMS)
+        ]
+        normed = [normed[s] for s in range(STREAMS)]
+        products = [by_head(v) for v in products]
+        turned_weights = [turned_heads[s] for s in range(3)] + [turned_up]
+    else:
+        moments = exchange(moments)
+        deviations = exchange(deviations)
+        deviations = [deviations[:, s] for s in range(STREAMS)]
+        def join_moments(mean_parts, dev_parts, size):
+            mean = jnp.mean(mean_parts, axis=0)
+            spread = size * jnp.sum(jnp.square(mean_parts - mean), axis=0)
+            return mean, jnp.sum(dev_parts, axis=0) + spread
+
+        block_means = moments[:, :STREAMS]
+        joined = join_moments(block_means, moments[:, STREAMS:], piece)
+        joined = gather_dp(gather_ways(jnp.concatenate(joined, axis=0), 0))
+        joined = joined.reshape((dp * ways,) + joined.shape[2:])
+        means, variance = join_moments(joined[:, :STREAMS], joined[:, STREAMS:], mine)
+        inv_scales = lax.rsqrt(variance / width + 1e-05)
+        all_means = gather_ways(block_means, 1)
+
+        def unit(values_in, block_mean, s):
+            return (values_in.astype(full) + (block_mean - means[s])[..., None, :]) * inv_scales[s]
+
+        units = [
+            unit(deviations[s], block_means[:, s], s).reshape(mine, group) for s in range(STREAMS)
+        ]
+        normed = []
+        for s in range(STREAMS):
+            both = unit(gather_ways(deviations[s], 1), all_means[:, :, s], s).reshape(feats, group)
+            normed.append((both * all_gains[:, s][:, None]).astype(low))
+        residual = (deviations[3].astype(full) + block_means[:, 3][:, None]).reshape(mine, group)
+        products = [
+            by_head(project(w, normed[s])) for s, w in enumerate((w_query, w_key, w_value))
+        ]
+        hidden = project(w_up, normed[3])
+        active, hidden_pull = jax.vjp(gelu_exact, hidden)
+        active = active.astype(low)
+        (slope,) = hidden_pull(jnp.ones_like(hidden))
+        turned_weights = [
+            turned(w, ways * n_head, way * n_head, n_head) for w in (w_query, w_key, w_value)
+        ] + [turned(w_up, ways * n_units, way * n_units, n_units)]
+    queries = rotate(products[0], cosine, sine).astype(low)
+    keys = rotate(products[1], cosine, sine).astype(low)
+    values = products[2].astype(low)
+    cotangent, queries = lax.optimization_barrier((out_cotangent, queries))
+    upstream = exchange(by_place(cotangent.T)).reshape(mine, group)
+
     out_rows, down_rows = way_rows(w_out), way_rows(w_down)
-    turned_weights = (
-        turned(w_query, ways * n_head, way * n_head, n_head),
-        turned(w_key, ways * n_head, way * n_head, n_head),
-        turned(w_value, ways * n_head, way * n_head, n_head),
-        turned(w_up, ways * n_units, way * n_units, n_units),
-        turned(out_rows, feats, 0, feats),
-        turned(down_rows, feats, 0, feats),
-    )
-    hidden, turned_weights = lax.optimization_barrier((hidden, turned_weights))
+    turned_weights += [turned(out_rows, feats, 0, feats), turned(down_rows, feats, 0, feats)]
 
     def by_row(values_in):
         if rows == 1:
@@ -709,10 +1102,6 @@
     probs_low = probs.astype(low)
     attended = from_row(batched(v_rows, probs_low, 2, 2).astype(low)).reshape(heads * HEAD, group)
 
-    active, hidden_pull = jax.vjp(gelu_exact, hidden)
-    active = active.astype(low)
-    (slope,) = hidden_pull(jnp.ones_like(hidden))
-
     def make_out(index):
         start = index * feats
         left = lax.dynamic_slice_in_dim(out_rows, start, feats, 1)
@@ -725,7 +1114,9 @@
         given = lax.dynamic_index_in_dim(branches, 1 - way, 1, keepdims=False).astype(low)
         kept = kept + hid_swap(given, 1).astype(full)
     output = residual + kept.reshape(mine, group)
-    output, upstream = lax.optimization_barrier((output, upstream))
+    output, upstream, turned_weights = lax.optimization_barrier(
+        (output, upstream, turned_weights)
+    )
     upstream = upstream.astype(full)
     output_rounded = output.astype(low)
 

time: 1030 us -> 941 us (0.914)
  waiting for transfers between devices: 225 us -> 95.6 us
  Pallas kernels: 407 us -> 533 us
  matrix products: 112 us -> 80.2 us
  starting transfers between devices: 87.2 us -> 60 us
  other arithmetic: 97.5 us -> 76.2 us
    pallas_call x0 -> x1, Pallas kernels: none -> 130 us  [forward_projections(): pl.pallas_call(functools.partial(forward_kernel, (places, piece, group, n...]
    ppermute x11 -> x6, waiting for transfers between devices: 86.5 us -> 37.5 us  [outer_shift(): return lax.ppermute(values_in, 'dp', pairs)]
    all_to_all x8 -> x3, waiting for transfers between devices: 43.5 us -> 0.01 us  [exchange(): lax.all_to_all(values_in, 'hid', split_axis=0, concat_axis=0, tiled=True,...]
    dot_general x33 -> x17, matrix products: 86.1 us -> 52.4 us  [contract(): lax.dot_general(left, right, (((left_dim,), (right_dim,)), ((), ())), pre...]
    ppermute x19 -> x13, waiting for transfers between devices: 82.4 us -> 53.4 us  [hid_swap(): return lax.ppermute(values_in, 'hid', [(i, i ^ bit) for i in range(size)])]
    all_to_all x8 -> x3, starting transfers between devices: 30 us -> 14.1 us  [exchange(): lax.all_to_all(values_in, 'hid', split_axis=0, concat_axis=0, tiled=True,...]
    convert_element_type x5 -> x0, other arithmetic: 11.3 us -> none  [the longest x1 10.4 us: local(): active = active.astype(low)]
    ppermute x19 -> x13, starting transfers between devices: 23.2 us -> 20.1 us  [hid_swap(): return lax.ppermute(values_in, 'hid', [(i, i ^ bit) for i in range(size)])]
  transfers between devices with their start and end apart: 61 -> 36, of which waited for: 31 -> 17; matrix products, arithmetic and copies ran while one was open for 18% -> 14% of each run, Pallas kernels for 40% -> 57%
where the time goes in v4:
time: 941 us; the launch traced here: 934 us
  Pallas kernels  533 us (57%)
  waiting for transfers between devices  95.6 us (10%)
  local copies, waits for them, and re-layouts  86.5 us (9%)
  matrix products  80.2 us (9%)
  other arithmetic  76.2 us (8%)
  starting transfers between devices  60 us (6%)
    pallas_call x2, Pallas kernels, chain_sum(): pl.pallas_call(functools.partial(chain_kernel, ways, size // ways, blocks...  373 us
    pallas_call x1, Pallas kernels, forward_projections(): pl.pallas_call(functools.partial(forward_kernel, (places, piece, group, n...  130 us
    ppermute x13, waiting for transfers between devices, hid_swap(): return lax.ppermute(values_in, 'hid', [(i, i ^ bit) for i in range(size)])  53.4 us
    dot_general x17, matrix products, contract(): lax.dot_general(left, right, (((left_dim,), (right_dim,)), ((), ())), pre...  52.4 us
    ppermute x6, waiting for transfers between devices, outer_shift(): return lax.ppermute(values_in, 'dp', pairs)  37.5 us
    unnamed x176, local copies, waits for them, and re-layouts  21.8 us
    ppermute x13, starting transfers between devices, hid_swap(): return lax.ppermute(values_in, 'hid', [(i, i ^ bit) for i in range(size)])  20.1 us
  transfers between devices with their start and end apart: 36, of which 17 were waited for; matrix products, arithmetic and copies ran while one was open for 14% of the time, Pallas kernels for 57%

profile of v4, /device:TPU:0, one launch (start us, length us, event | category | flops | bytes accessed | tf_op | source)
XLA Modules:
  0.0 933.8 jit_solution(13101662015453917238)
XLA Ops:
  2.2 7.3 all-to-all-start
  16.4 5.4 fusion.218
  26.8 5.4 all-to-all-start.1
  45.6 130.3 %shard_map.254 = (bf16[4,512,1024]{2,1,0:T(8,128)(2,1)}, bf16[4,4,64,1024]{3,2,1,0:T(8,128)(2,1)}, f32[4,16,1024]{2,1,0:T(8,128)}, bf16[1024,1024]{1,0:T(8,128)(...) custom-call(bf16[4,4,64,1024]{3,2,1,0:T(8,128)(2,1)} %pad_maximum_fu, ...), custom_call_target="tpu_custom_call" | custom-call | flops 7516192768 | bytes 314572800 | tf_op jit(solution)/shard_map/pallas_call | solution.py:512
  208.6 8.7 fusion.234
  217.4 4.4 fusion.48
  244.4 5.9 all-to-all-start.2
  251.9 11.2 %collective-permute-done.1 = bf16[512,1024]{1,0:T(8,128)(2,1)} collective-permute-done((bf16[512,1024]{1,0:T(8,128)(2,1)}, bf16[512,1024]{1,0:T(8,128)(2,1)}, u32[]{:S(2)}, u32[]{:S(2)}) %collective-permute-start.1) | collective-permute-done | bytes 1048608 | tf_op jit(solution)/shard_map/ppermute | solution.py:65
  268.8 10.3 %collective-permute-done.3 = bf16[4,64,1024]{2,1,0:T(8,128)(2,1)S(1)} collective-permute-done((bf16[4,64,1024]{2,1,0:T(8,128)(2,1)S(1)}, bf16[4,64,1024]{2,1,0:T(8,128)(2,1)S(1)}, u32[]{:S(2)}, u32[]{:S(2)}) %collective-permute-start.3) | collective-permute-done | bytes 524320 | tf_op jit(solution)/shard_map/ppermute | solution.py:70
  320.5 11.1 %collective-permute-done.9 = bf16[4,64,1024]{2,1,0:T(8,128)(2,1)} collective-permute-done((bf16[4,64,1024]{2,1,0:T(8,128)(2,1)}, bf16[4,64,1024]{2,1,0:T(8,128)(2,1)}, u32[]{:S(2)}, u32[]{:S(2)}) %collective-permute-start.9) | collective-permute-done | bytes 524320 | tf_op jit(solution)/shard_map/ppermute | solution.py:70
  335.2 21.3 %collective-permute-done.11 = bf16[512,1024]{1,0:T(8,128)(2,1)} collective-permute-done((bf16[512,1024]{1,0:T(8,128)(2,1)}, bf16[512,1024]{1,0:T(8,128)(2,1)}, u32[]{:S(2)}, u32[]{:S(2)}) %collective-permute-start.11) | collective-permute-done | bytes 1048608 | tf_op jit(solution)/shard_map/ppermute | solution.py:65
  365.3 5.9 fusion.51
  386.5 10.6 %multiply_convert_fusion.1 = bf16[1024,1024]{1,0:T(8,128)(2,1)} fusion(f32[1024,1024]{1,0:T(8,128)} %get-tuple-element.63, bf16[1024,2048]{1,0:T(8,128)(2,1)} %pad_maximum_fusion, bf16[2048,1024]{1,0:T(8,128)(2,1)} %copy-done.5), kind=kOutput, calls=%fused_computation.17 | convolution fusion | flops 4297064448 | bytes 14680064 | tf_op jit(solution)/shard_map/dot_general | solution.py:29
  400.4 4.5 all-to-all-start.3
  404.9 128.8 %shard_map.255 = bf16[2,64,16,2048]{3,2,1,0:T(8,128)(2,1)} custom-call(bf16[1024,1024]{1,0:T(8,128)(2,1)} %get-tuple-element.65.refs_0_, bf16[2048,1024]{1,0:T(8,128)(2,1)} %copy-done.5), custom_call_target="tpu_custom_call" | custom-call | flops 4294967296 | bytes 629145600 | tf_op jit(solution)/shard_map/pallas_call | solution.py:746
  556.8 10.0 %multiply_reduce_fusion.1 = (f32[1024]{0:T(1024)S(1)}, f32[1024]{0:T(1024)S(1)}, f32[1024]{0:T(1024)S(1)}, f32[1024]{0:T(1024)S(1)}, f32[1024]{0:T(1024)S(1)}, /...) fusion(bf16[4,512,1024]{2,1,0:T(8,128)(2,1)} %get-tuple-element.72, ...), kind=kOutput, calls=%fused_computation.32 | convolution fusion | flops 4305444864 | bytes 25206784 | tf_op jit(solution)/shard_map/dot_general | solution.py:29
  578.6 6.1 collective-permute-done.24
  584.6 11.2 %collective-permute-done.25 = bf16[4,64,1024]{2,1,0:T(8,128)(2,1)S(1)} collective-permute-done((bf16[4,64,1024]{2,1,0:T(8,128)(2,1)S(1)}, bf16[4,64,1024]{2,1,0:T(8,128)(2,1)S(1)}, u32[]{:S(2)}, u32[]{:S(2)}) %collective-permute-start.25) | collective-permute-done | bytes 524320 | tf_op jit(solution)/shard_map/ppermute | solution.py:70
  601.1 4.6 collective-permute-done.26
  618.6 4.3 slice_bitcast_fusion.1
  624.5 244.6 %shard_map.256 = bf16[2,128,32,1024]{3,2,1,0:T(8,128)(2,1)} custom-call(bf16[4096,1024]{1,0:T(8,128)(2,1)} %copy-done.7, bf16[1024,1024]{1,0:T(8,128)(2,1)} %copy-done.8, bf16[1024,1024]{1,0:T(8,128)(2,1)} %copy-done.9, bf16[1024,1024]{1,0:T(8,128)(2,1)} %copy-done.10, bf16[2048,1024]{1,0:T(8,128)(2,1)} %copy-done.5, ...), custom_call_target="tpu_custom_call" | custom-call | flops 8589934592 | bytes 1258291200 | tf_op jit(solution)/shard_map/pallas_call | solution.py:746
  886.4 10.3 %shard_map.258 = f32[2048,2048]{1,0:T(8,128)} custom-call(bf16[2048,2048]{1,0:T(8,128)(2,1)} %bitcast.701), custom_call_target="tpu_custom_call" | custom-call | bytes 25165824 | tf_op jit(solution)/shard_map/pallas_call | solution.py:864
  905.3 5.5 multiply_add_fusion
  910.9 18.7 %shard_map.257 = (f32[512,8192]{1,0:T(8,128)}, f32[512,2048]{1,0:T(8,128)}, f32[512,2048]{1,0:T(8,128)}, f32[512,2048]{1,0:T(8,128)}, f32[512,2048]{1,0:T(8,128)}) custom-call(bf16[2,8,512,1024]{3,2,1,0:T(8,128)(2,1)} %bitcast.693, bf16[2,8,512,1024]{3,2,1,0:T(8,128)(2,1)} %bitcast.694, bf16[2,8,512,1024]{3,2,1,0:T(8,128)(2,1)} %bitcast.695), custom_call_target="tpu_custom_call" | custom-call | bytes 50331648 | tf_op jit(solution)/shard_map/pallas_call | solution.py:840
  (427 shorter events, 245.0 us)
Async XLA Ops:
  2.2 23.7 %all-to-all-start = ((f32[32,32,128]{2,1,0:T(8,128)}), f32[32,32,128]{2,1,0:T(8,128)S(1)}, u32[]{:S(2)}, u32[]{:S(2)}) async-start(f32[32,32,128]{2,1,0:T(8,128)} %broadcast_in_dim.25), calls=%async_computation | async-start | bytes 1048576 | tf_op jit(solution)/shard_map/all_to_all | solution.py:160
  26.8 165.7 %all-to-all-start.1 = ((f32[32,37,128]{2,1,0:T(8,128)}), f32[32,37,128]{2,1,0:T(8,128)}, u32[]{:S(2)}, u32[]{:S(2)}) async-start(f32[32,37,128]{2,1,0:T(8,128)} %broadcast_in_dim.29), calls=%async_computation.1 | async-start | bytes 1310720 | tf_op jit(solution)/shard_map/all_to_all | solution.py:160
  224.6 9.7 %collective-permute-start = (bf16[512,1024]{1,0:T(8,128)(2,1)}, bf16[512,1024]{1,0:T(8,128)(2,1)}, u32[]{:S(2)}, u32[]{:S(2)}) collective-permute-start(bf16[512,1024]{1,0:T(8,128)(2,1)} %add_convert_fusion.2), channel_id=1, source_target_pairs={{0,8},{8,0},{16,24},{24,16},{1,9},{9,1},{17,25},{25,17},{2,10},{10... | collective-permute-start | bytes 3145736 | tf_op jit(solution)/shard_map/ppermute | solution.py:56
  234.2 17.6 %collective-permute-start.2 = (bf16[512,1024]{1,0:T(8,128)(2,1)}, bf16[512,1024]{1,0:T(8,128)(2,1)}, u32[]{:S(2)}, u32[]{:S(2)}) collective-permute-start(bf16[512,1024]{1,0:T(8,128)(2,1)} %add_convert_fusion), channel_id=1, source_target_pairs={{0,8},{8,0},{16,24},{24,16},{1,9},{9,1},{17,25},{25,17},{2,10},{10... | collective-permute-start | bytes 3145736 | tf_op jit(solution)/shard_map/ppermute | solution.py:56
  237.3 25.8 %collective-permute-start.1 = (bf16[512,1024]{1,0:T(8,128)(2,1)}, bf16[512,1024]{1,0:T(8,128)(2,1)}, u32[]{:S(2)}, u32[]{:S(2)}) collective-permute-start(bf16[512,1024]{1,0:T(8,128)(2,1)} %add_convert_fusion.1), channel_id=1, source_target_pairs={{0,16},{8,24},{16,0},{24,8},{1,17},{9,25},{17,1},{25,9},{2,18},{10... | collective-permute-start | bytes 3145736 | tf_op jit(solution)/shard_map/ppermute | solution.py:65
  244.4 35.2 %all-to-all-start.2 = ((bf16[4,64,1024]{2,1,0:T(8,128)(2,1)}), bf16[4,64,1024]{2,1,0:T(8,128)(2,1)}, u32[]{:S(2)}, u32[]{:S(2)}) async-start(bf16[4,64,1024]{2,1,0:T(8,128)(2,1)} %pad_maximum_fusion.14), calls=%async_computation.2 | async-start | bytes 1048576 | tf_op jit(solution)/shard_map/all_to_all | solution.py:185
  265.6 13.5 %collective-permute-start.3 = (bf16[4,64,1024]{2,1,0:T(8,128)(2,1)S(1)}, bf16[4,64,1024]{2,1,0:T(8,128)(2,1)S(1)}, u32[]{:S(2)}, u32[]{:S(2)}) collective-permute-start(bf16[4,64,1024]{2,1,0:T(8,128)(2,1)S(1)} %fusion.158), channel_id=1, source_target_pairs={{0,1},{1,0},{2,3},{3,2},{4,5},{5,4},{6,7},{7,6},{8,9},{9,8},{10,11... | collective-permute-start | bytes 1572872 | tf_op jit(solution)/shard_map/ppermute | solution.py:70
  319.3 12.3 %collective-permute-start.9 = (bf16[4,64,1024]{2,1,0:T(8,128)(2,1)}, bf16[4,64,1024]{2,1,0:T(8,128)(2,1)}, u32[]{:S(2)}, u32[]{:S(2)}) collective-permute-start(bf16[4,64,1024]{2,1,0:T(8,128)(2,1)} %bitcast.102), channel_id=1, source_target_pairs={{0,1},{1,0},{2,3},{3,2},{4,5},{5,4},{6,7},{7,6},{8,9},{9,8},{10,11... | collective-permute-start | bytes 1572872 | tf_op jit(solution)/shard_map/ppermute | solution.py:70
  333.9 22.6 %collective-permute-start.11 = (bf16[512,1024]{1,0:T(8,128)(2,1)}, bf16[512,1024]{1,0:T(8,128)(2,1)}, u32[]{:S(2)}, u32[]{:S(2)}) collective-permute-start(bf16[512,1024]{1,0:T(8,128)(2,1)} %bitcast.106), channel_id=1, source_target_pairs={{0,16},{8,24},{16,0},{24,8},{1,17},{9,25},{17,1},{25,9},{2,18},{10... | collective-permute-start | bytes 3145736 | tf_op jit(solution)/shard_map/ppermute | solution.py:65
  335.2 22.3 %collective-permute-start.10 = (bf16[512,1024]{1,0:T(8,128)(2,1)}, bf16[512,1024]{1,0:T(8,128)(2,1)}, u32[]{:S(2)}, u32[]{:S(2)}) collective-permute-start(bf16[512,1024]{1,0:T(8,128)(2,1)} %bitcast.106), channel_id=1, source_target_pairs={{0,8},{8,0},{16,24},{24,16},{1,9},{9,1},{17,25},{25,17},{2,10},{10... | collective-permute-start | bytes 3145736 | tf_op jit(solution)/shard_map/ppermute | solution.py:56
  398.4 135.5 %collective-permute-start.13 = (bf16[1024,1024]{1,0:T(8,128)(2,1)}, bf16[1024,1024]{1,0:T(8,128)(2,1)}, u32[]{:S(2)}, u32[]{:S(2)}) collective-permute-start(bf16[1024,1024]{1,0:T(8,128)(2,1)} %multiply_convert_fusion.1), channel_id=1, source_target_pairs={{0,16},{8,24},{16,0},{24,8},{1,17},{9,25},{17,1},{25,9},{2,18},{10... | collective-permute-start | bytes 6291464 | tf_op jit(solution)/shard_map/ppermute | solution.py:65
  399.6 134.2 %collective-permute-start.14 = (bf16[768,1024]{1,0:T(8,128)(2,1)}, bf16[768,1024]{1,0:T(8,128)(2,1)}, u32[]{:S(2)}, u32[]{:S(2)}) collective-permute-start(bf16[768,1024]{1,0:T(8,128)(2,1)} %pad_maximum_fusion.8), channel_id=1, source_target_pairs={{0,16},{8,24},{16,0},{24,8},{1,17},{9,25},{17,1},{25,9},{2,18},{10... | collective-permute-start | bytes 4718600 | tf_op jit(solution)/shard_map/ppermute | solution.py:65
  400.4 133.4 %all-to-all-start.3 = ((bf16[4,64,1024]{2,1,0:T(8,128)(2,1)}), bf16[4,64,1024]{2,1,0:T(8,128)(2,1)}, u32[]{:S(2)}, u32[]{:S(2)}) async-start(bf16[4,64,1024]{2,1,0:T(8,128)(2,1)} %bitcast.706), calls=%async_computation.3 | async-start | bytes 1048576 | tf_op jit(solution)/shard_map/all_to_all | solution.py:185
  534.1 9.6 %collective-permute-start.16 = (bf16[768,1024]{1,0:T(8,128)(2,1)}, bf16[768,1024]{1,0:T(8,128)(2,1)}, u32[]{:S(2)}, u32[]{:S(2)}) collective-permute-start(bf16[768,1024]{1,0:T(8,128)(2,1)} %pad_maximum_fusion.8), channel_id=1, source_target_pairs={{0,8},{8,0},{16,24},{24,16},{1,9},{9,1},{17,25},{25,17},{2,10},{10... | collective-permute-start | bytes 4718600 | tf_op jit(solution)/shard_map/ppermute | solution.py:56
  537.0 16.3 %collective-permute-start.19 = (bf16[1024,1024]{1,0:T(8,128)(2,1)}, bf16[1024,1024]{1,0:T(8,128)(2,1)S(1)}, u32[]{:S(2)}, u32[]{:S(2)}) collective-permute-start(bf16[1024,1024]{1,0:T(8,128)(2,1)} %multiply_convert_fusion.1), channel_id=1, source_target_pairs={{0,8},{8,0},{16,24},{24,16},{1,9},{9,1},{17,25},{25,17},{2,10},{10... | collective-permute-start | bytes 6291464 | tf_op jit(solution)/shard_map/ppermute | solution.py:56
  537.1 18.7 %collective-permute-start.20 = (bf16[1024,1024]{1,0:T(8,128)(2,1)}, bf16[1024,1024]{1,0:T(8,128)(2,1)S(1)}, u32[]{:S(2)}, u32[]{:S(2)}) collective-permute-start(bf16[1024,1024]{1,0:T(8,128)(2,1)} %collective-permute-done.13), channel_id=1, source_target_pairs={{0,8},{8,0},{16,24},{24,16},{1,9},{9,1},{17,25},{25,17},{2,10},{10... | collective-permute-start | bytes 6291464 | tf_op jit(solution)/shard_map/ppermute | solution.py:56
  547.9 50.0 %collective-permute-start.18 = (bf16[4,64,1024]{2,1,0:T(8,128)(2,1)}, bf16[4,64,1024]{2,1,0:T(8,128)(2,1)S(1)}, u32[]{:S(2)}, u32[]{:S(2)}) collective-permute-start(bf16[4,64,1024]{2,1,0:T(8,128)(2,1)} %fusion.160), channel_id=1, source_target_pairs={{0,1},{1,0},{2,3},{3,2},{4,5},{5,4},{6,7},{7,6},{8,9},{9,8},{10,11... | collective-permute-start | bytes 1572872 | tf_op jit(solution)/shard_map/ppermute | solution.py:70
  569.7 14.9 %collective-permute-start.24 = (bf16[4,64,1024]{2,1,0:T(8,128)(2,1)S(1)}, bf16[4,64,1024]{2,1,0:T(8,128)(2,1)S(1)}, u32[]{:S(2)}, u32[]{:S(2)}) collective-permute-start(bf16[4,64,1024]{2,1,0:T(8,128)(2,1)S(1)} %fusion.161), channel_id=1, source_target_pairs={{0,1},{1,0},{2,3},{3,2},{4,5},{5,4},{6,7},{7,6},{8,9},{9,8},{10,11... | collective-permute-start | bytes 1572872 | tf_op jit(solution)/shard_map/ppermute | solution.py:70
  573.4 22.4 %collective-permute-start.25 = (bf16[4,64,1024]{2,1,0:T(8,128)(2,1)S(1)}, bf16[4,64,1024]{2,1,0:T(8,128)(2,1)S(1)}, u32[]{:S(2)}, u32[]{:S(2)}) collective-permute-start(bf16[4,64,1024]{2,1,0:T(8,128)(2,1)S(1)} %fusion.162), channel_id=1, source_target_pairs={{0,1},{1,0},{2,3},{3,2},{4,5},{5,4},{6,7},{7,6},{8,9},{9,8},{10,11... | collective-permute-start | bytes 1572872 | tf_op jit(solution)/shard_map/ppermute | solution.py:70
  577.0 28.7 %collective-permute-start.26 = (bf16[4,64,1024]{2,1,0:T(8,128)(2,1)}, bf16[4,64,1024]{2,1,0:T(8,128)(2,1)}, u32[]{:S(2)}, u32[]{:S(2)}) collective-permute-start(bf16[4,64,1024]{2,1,0:T(8,128)(2,1)} %fusion.163), channel_id=1, source_target_pairs={{0,1},{1,0},{2,3},{3,2},{4,5},{5,4},{6,7},{7,6},{8,9},{9,8},{10,11... | collective-permute-start | bytes 1572872 | tf_op jit(solution)/shard_map/ppermute | solution.py:70
  614.9 254.2 %all-to-all-start.4 = ((bf16[4,4,64,1024]{3,2,1,0:T(8,128)(2,1)}), bf16[4,4,64,1024]{3,2,1,0:T(8,128)(2,1)S(1)}, u32[]{:S(2)}, u32[]{:S(2)}) async-start(bf16[4,4,64,1024]{3,2,1,0:T(8,128)(2,1)} %copy.211), calls=%async_computation.4 | async-start | bytes 4194304 | tf_op jit(solution)/shard_map/all_to_all | solution.py:185
  880.8 21.4 %collective-permute-start.28 = (f32[40,256]{1,0:T(8,128)S(1)}, f32[40,256]{1,0:T(8,128)S(1)}, u32[]{:S(2)}, u32[]{:S(2)}) collective-permute-start(f32[40,256]{1,0:T(8,128)S(1)} %add.733), channel_id=1, source_target_pairs={{0,4},{1,5},{2,6},{3,7},{4,0},{5,1},{6,2},{7,3},{8,12},{9,13},{10,... | collective-permute-start | bytes 122888 | tf_op jit(solution)/shard_map/ppermute | solution.py:70
  898.9 32.4 %all-to-all-start.5 = ((f32[32,32,128]{2,1,0:T(8,128)}), f32[32,32,128]{2,1,0:T(8,128)}, u32[]{:S(2)}, u32[]{:S(2)}) async-start(f32[32,32,128]{2,1,0:T(8,128)} %copy.212), calls=%async_computation.5 | async-start | bytes 1048576 | tf_op jit(solution)/shard_map/all_to_all | solution.py:1258
  903.7 25.8 %collective-permute-start.29 = (f32[40,4,64]{2,1,0:T(4,128)S(1)}, f32[40,4,64]{2,1,0:T(4,128)S(1)}, u32[]{:S(2)}, u32[]{:S(2)}) collective-permute-start(f32[40,4,64]{2,1,0:T(4,128)S(1)} %reshape.1056), channel_id=1, source_target_pairs={{0,1},{1,0},{2,3},{3,2},{4,5},{5,4},{6,7},{7,6},{8,9},{9,8},{10,11... | collective-permute-start | bytes 122888 | tf_op jit(solution)/shard_map/ppermute | solution.py:70
  (91 other events, 1678.5 us)

commit v5 on v4

--- a/solution.py
+++ b/solution.py
@@ -17,7 +17,12 @@
 CHUNK = 1 << 15
 SLACK = 6
 TILE = 128
+LATE_TILE = 256
+SPAN = 256
 VMEM = 52 << 20
+PULL_START = 4
+PULL_GAP = 8
+GRAD_GAP = 5
 
 highest = lax.Precision.HIGHEST
 rope_base = 10000.0
@@ -185,6 +190,131 @@
     return lax.all_to_all(
         values_in, "hid", split_axis=0, concat_axis=0, tiled=True, axis_index_groups=groups
     )
+
+
+def turn_heads(values_in, cosine, sine):
+    half = ROT // 2
+    front, back = values_in[:half], values_in[half:ROT]
+    return jnp.concatenate(
+        [front * cosine - back * sine, back * cosine + front * sine, values_in[ROT:]], axis=0
+    )
+
+
+def across(left, right, left_dim, right_dim):
+    return lax.dot_general(
+        left, right, (((left_dim,), (right_dim,)), ((), ())), preferred_element_type=full
+    )
+
+
+def attend_kernel(
+    products_ref, cosine_ref, sine_ref, start_ref, heads_ref, attended_ref, tops_ref
+):
+    tokens = products_ref.shape[2]
+    for s in range(2):
+        turned = turn_heads(products_ref[s], cosine_ref[...], sine_ref[...])
+        heads_ref[s] = turned.astype(low)
+    heads_ref[2] = products_ref[2].astype(low)
+    for first in range(0, tokens, SPAN):
+        stop = first + SPAN
+        span = slice(first, stop)
+        scores, top = masked_scores(heads_ref, start_ref, first)
+        weights = jnp.exp(scores - top)
+        total = jnp.sum(weights, axis=0, keepdims=True)
+        weights = (weights / total).astype(low)
+        mixed = across(heads_ref[2, :, :stop], weights, 1, 0)
+        attended_ref[:, span] = mixed.astype(low)
+        tops_ref[0, 0:1, span] = top
+        tops_ref[0, 1:2, span] = total
+
+
+def masked_scores(heads_ref, start_ref, first):
+    stop = first + SPAN
+    span = slice(first, stop)
+    scores = across(heads_ref[1, :, :stop], heads_ref[0, :, span], 0, 0) / math.sqrt(HEAD)
+    key = lax.broadcasted_iota(jnp.int32, scores.shape, 0)
+    query = lax.broadcasted_iota(jnp.int32, scores.shape, 1) + first
+    seen = (key >= start_ref[:, span]) & (key <= query)
+    scores = jnp.where(seen, scores, -1e30)
+    return scores, jnp.max(scores, axis=0, keepdims=True)
+
+
+def attend_back_kernel(
+    heads_ref, gradient_ref, cosine_ref, sine_ref, start_ref, tops_ref, lows_ref, key_sum, value_sum
+):
+    tokens = heads_ref.shape[2]
+    cosine, sine = cosine_ref[...], sine_ref[...]
+    scale = 1.0 / math.sqrt(HEAD)
+    key_sum[...] = jnp.zeros_like(key_sum)
+    value_sum[...] = jnp.zeros_like(value_sum)
+    for first in range(0, tokens, SPAN):
+        stop = first + SPAN
+        span = slice(first, stop)
+        scores, _ = masked_scores(heads_ref, start_ref, first)
+        probs = jnp.exp(scores - tops_ref[0, 0:1, span]) / tops_ref[0, 1:2, span]
+        gradient = gradient_ref[:, span]
+        change = across(heads_ref[2, :, :stop], gradient, 0, 0)
+        row_total = jnp.sum(probs * change, axis=0, keepdims=True)
+        change = (probs * (change - row_total)).astype(low)
+        query = across(heads_ref[1, :, :stop], change, 1, 0) * scale
+        lows_ref[0, :, span] = turn_heads(query, cosine[:, span], -sine[:, span]).astype(low)
+        key_sum[:, :stop] = key_sum[:, :stop] + across(heads_ref[0, :, span], change, 1, 1) * scale
+        value_sum[:, :stop] = value_sum[:, :stop] + across(gradient, probs.astype(low), 1, 1)
+    lows_ref[1] = turn_heads(key_sum[...], cosine, -sine).astype(low)
+    lows_ref[2] = value_sum[...].astype(low)
+
+
+def attend(products, cosine, sine, start):
+    _, n_heads, head, tokens = products.shape
+    per_head = pl.BlockSpec((3, None, head, tokens), lambda h: (0, h, 0, 0))
+    table = pl.BlockSpec(cosine.shape, lambda h: (0, 0))
+    return pl.pallas_call(
+        attend_kernel,
+        grid=(n_heads,),
+        out_shape=[
+            jax.ShapeDtypeStruct(products.shape, low),
+            jax.ShapeDtypeStruct((n_heads, head, tokens), low),
+            jax.ShapeDtypeStruct((n_heads, 2, tokens), full),
+        ],
+        in_specs=[per_head, table, table, pl.BlockSpec(start.shape, lambda h: (0, 0))],
+        out_specs=[
+            per_head,
+            pl.BlockSpec((None, head, tokens), lambda h: (h, 0, 0)),
+            pl.BlockSpec((1, 2, tokens), lambda h: (h, 0, 0)),
+        ],
+        compiler_params=pltpu.CompilerParams(vmem_limit_bytes=40 << 20),
+        cost_estimate=pl.CostEstimate(
+            flops=4 * n_heads * head * tokens * tokens,
+            bytes_accessed=10 * products.size,
+            transcendentals=n_heads * tokens * tokens,
+        ),
+    )(products, cosine, sine, start)
+
+
+def attend_back(heads, gradient, cosine, sine, start, tops):
+    _, n_heads, head, tokens = heads.shape
+    per_head = pl.BlockSpec((3, None, head, tokens), lambda h: (0, h, 0, 0))
+    table = pl.BlockSpec(cosine.shape, lambda h: (0, 0))
+    return pl.pallas_call(
+        attend_back_kernel,
+        grid=(n_heads,),
+        out_shape=jax.ShapeDtypeStruct(heads.shape, low),
+        in_specs=[
+            per_head,
+            pl.BlockSpec((None, head, tokens), lambda h: (h, 0, 0)),
+            table,
+            table,
+            pl.BlockSpec(start.shape, lambda h: (0, 0)),
+            pl.BlockSpec((1, 2, tokens), lambda h: (h, 0, 0)),
+        ],
+        out_specs=per_head,
+        scratch_shapes=[pltpu.VMEM((head, tokens), full)] * 2,
+        compiler_params=pltpu.CompilerParams(vmem_limit_bytes=40 << 20),
+        cost_estimate=pl.CostEstimate(
+            flops=10 * n_heads * head * tokens * tokens,
+            bytes_accessed=6 * heads.size,
+            transcendentals=n_heads * tokens * tokens,
+        ),
+    )(heads, gradient, cosine, sine, start, tops)
 
 
 def forward_kernel(dims, *refs):
@@ -236,16 +366,6 @@
     core_peer = {"dp": index + 1 - 2 * core}
     outer_peer = {"dp": (index + 2) % 4}
 
-    def remote(source, target, send, recv, device):
-        return pltpu.make_async_remote_copy(
-            src_ref=source,
-            dst_ref=target,
-            send_sem=send,
-            recv_sem=recv,
-            device_id=device,
-            device_id_type=pl.DeviceIdType.MESH,
-        )
-
     def peer(k):
         return (place + k) % places
 
@@ -274,9 +394,6 @@
             weight_copy(unit, t).start()
 
     barrier = pltpu.get_barrier_semaphore()
-
-    def greet(device):
-        pl.semaphore_signal(barrier, inc=1, device_id=device, device_id_type=pl.DeviceIdType.MESH)
 
     for k in range(1, places):
         greet(z_device(k))
@@ -559,57 +676,141 @@
     )
 
 
-def chain_kernel(ways, places, blocks, n_operands, depth, *refs):
-    operand_refs, refs = refs[:n_operands], refs[n_operands:]
-    out_ref, refs = refs[0], refs[1:]
-    operands, refs = refs[:n_operands], refs[n_operands:]
-    (
-        own,
-        landed,
-        sums,
-        fetched,
-        up_send,
-        up_recv,
-        down_send,
-        down_recv,
-        side_send,
-        side_recv,
-        kept,
-    ) = refs
-    count = sums.shape[0]
-    per_tile = TILE // depth
+def remote(source, target, send, recv, device):
+    return pltpu.make_async_remote_copy(
+        src_ref=source,
+        dst_ref=target,
+        send_sem=send,
+        recv_sem=recv,
+        device_id=device,
+        device_id_type=pl.DeviceIdType.MESH,
+    )
+
+
+def greet(device):
+    pl.semaphore_signal(
+        pltpu.get_barrier_semaphore(),
+        inc=1,
+        device_id=device,
+        device_id_type=pl.DeviceIdType.MESH,
+    )
+
+
+def chain_place(ways, places):
     last = places - 1
     me = lax.axis_index("hid")
     if ways == 2:
         place, way = me // 2, me % 2
-        above, below, beside = me + 2, me - 2, me + 1 - 2 * way
-    else:
-        odd, half = me % 2, places // 2
-        place, way = (1 - odd) * (me // 2) + odd * (last - me // 2), 0
-        turn_up = (place + 1) // half
-        turn_down = (place - 1 + places) // half - 2
-        above = (1 - turn_up) * 2 * (place + 1) + turn_up * (2 * (last - place - 1) + 1)
-        below = (1 - turn_down) * 2 * (place - 1) + turn_down * (2 * (last - place + 1) + 1)
-        beside = me
-
-    def remote(source, target, send, recv, device):
-        return pltpu.make_async_remote_copy(
-            src_ref=source,
-            dst_ref=target,
-            send_sem=send,
-            recv_sem=recv,
-            device_id={"hid": device},
-            device_id_type=pl.DeviceIdType.MESH,
-        )
+        return place, way, me + 2, me - 2, me + 1 - 2 * way
+    odd, half = me % 2, places // 2
+    place = (1 - odd) * (me // 2) + odd * (last - me // 2)
+    turn_up = (place + 1) // half
+    turn_down = (place - 1 + places) // half - 2
+    above = (1 - turn_up) * 2 * (place + 1) + turn_up * (2 * (last - place - 1) + 1)
+    below = (1 - turn_down) * 2 * (place - 1) + turn_down * (2 * (last - place + 1) + 1)
+    return place, 0, above, below, me
+
+
+def chain_semaphores(count):
+    dma = pltpu.SemaphoreType.DMA
+    return [dma, dma((count,)), dma, dma((count,)), dma, dma, dma]
+
+
+def chain_loop(ways, places, out_ref, own, landed, semaphores, compute, hook=None):
+    up_send, up_recv, down_send, down_recv, side_send, side_recv, kept = semaphores
+    count, depth = landed.shape[:2]
+    per_tile = own.shape[0] // depth
+    last = places - 1
+    place, way, above, below, beside = chain_place(ways, places)
 
     def up_copy(i):
-        return remote(sums.at[i], landed.at[i], up_send, up_recv.at[i], above)
+        return remote(landed.at[i], landed.at[i], up_send, up_recv.at[i], {"hid": above})
 
     def down_copy(source, i):
-        return remote(source, out_ref.at[way, i], down_send, down_recv.at[i], below)
+        return remote(source, out_ref.at[way, i], down_send, down_recv.at[i], {"hid": below})
 
     def side_copy(source, i):
-        return remote(source, out_ref.at[way, i], side_send, side_recv, beside)
+        return remote(source, out_ref.at[way, i], side_send, side_recv, {"hid": beside})
+
+    def upward(i):
+        @pl.when(i % per_tile == 0)
+        def _():
+            compute(i // per_tile)
+
+        mine = own[pl.ds(pl.multiple_of(i % per_tile * depth, depth), depth), :]
+
+        @pl.when(place == 0)
+        def _():
+            landed[i] = mine.astype(low)
+            up_copy(i).start()
+
+        @pl.when(place > 0)
+        def _():
+            up_copy(i).wait_recv()
+            landed[i] = (landed[i].astype(full) + mine).astype(low)
+
+            @pl.when(place < last)
+            def _():
+                up_copy(i).start()
+
+            @pl.when(place == last)
+            def _():
+                down_copy(landed.at[i], i).start()
+                if ways == 2:
+                    side_copy(landed.at[i], i).start()
+                pltpu.make_async_copy(landed.at[i], out_ref.at[way, i], kept).start()
+
+    def downward(i):
+        down_copy(landed.at[i], i).wait_recv()
+
+        @pl.when(place > 0)
+        def _():
+            down_copy(out_ref.at[way, i], i).start()
+
+        if ways == 2:
+            side_copy(out_ref.at[way, i], i).start()
+
+    lag = SLACK * (last - place) + 2
+
+    def step(i, carry):
+        @pl.when(i < count)
+        def _():
+            upward(i)
+
+        behind = i - lag
+
+        @pl.when((behind >= 0) & (behind < count) & (place < last))
+        def _():
+            downward(behind)
+
+        if hook is not None:
+            hook(i)
+        return carry
+
+    lax.fori_loop(0, count + SLACK * last + 2, step, 0)
+
+    @pl.when(place < last)
+    def _():
+        remote(landed, landed, up_send, kept, {"hid": above}).wait_send()
+
+    @pl.when(place > 0)
+    def _():
+        remote(landed, out_ref.at[way], down_send, kept, {"hid": below}).wait_send()
+
+    @pl.when(place == last)
+    def _():
+        pltpu.make_async_copy(landed, out_ref.at[way], kept).wait()
+
+    if ways == 2:
+        remote(landed, out_ref.at[way], side_send, kept, {"hid": beside}).wait_send()
+        remote(landed, out_ref.at[1 - way], kept, side_recv, {"hid": beside}).wait_recv()
+
+
+def chain_kernel(ways, places, blocks, n_operands, *refs):
+    operand_refs, out_ref, refs = refs[:n_operands], refs[n_operands], refs[n_operands + 1 :]
+    operands, (own, landed, fetched, *semaphores) = refs[:n_operands], refs[n_operands:]
+    last = places - 1
+    place, way, above, below, beside = chain_place(ways, places)
 
     def fetch(n):
         return pltpu.make_async_copy(operand_refs[n], operands[n], fetched.at[n])
@@ -619,21 +820,16 @@
 
     barrier = pltpu.get_barrier_semaphore()
 
-    def greet(device):
-        pl.semaphore_signal(
-            barrier, inc=1, device_id={"hid": device}, device_id_type=pl.DeviceIdType.MESH
-        )
-
     @pl.when(place > 0)
     def _():
-        greet(below)
+        greet({"hid": below})
 
     @pl.when(place < last)
     def _():
-        greet(above)
+        greet({"hid": above})
 
     if ways == 2:
-        greet(beside)
+        greet({"hid": beside})
     met = jnp.where(place > 0, 1, 0) + jnp.where(place < last, 1, 0) + (ways - 1)
     pl.semaphore_wait(barrier, met)
 
@@ -664,76 +860,7 @@
                     )
                     column += size
 
-    def upward(i):
-        @pl.when(i % per_tile == 0)
-        def _():
-            compute(i // per_tile)
-
-        mine = own[pl.ds(pl.multiple_of(i % per_tile * depth, depth), depth), :]
-
-        @pl.when(place == 0)
-        def _():
-            sums[i] = mine.astype(low)
-            up_copy(i).start()
-
-        @pl.when(place > 0)
-        def _():
-            up_copy(i).wait_recv()
-            sums[i] = (landed[i].astype(full) + mine).astype(low)
-
-            @pl.when(place < last)
-            def _():
-                up_copy(i).start()
-
-            @pl.when(place == last)
-            def _():
-                down_copy(sums.at[i], i).start()
-                if ways == 2:
-                    side_copy(sums.at[i], i).start()
-                pltpu.make_async_copy(sums.at[i], out_ref.at[way, i], kept).start()
-
-    def downward(i):
-        down_copy(sums.at[i], i).wait_recv()
-
-        @pl.when(place > 0)
-        def _():
-            down_copy(out_ref.at[way, i], i).start()
-
-        if ways == 2:
-            side_copy(out_ref.at[way, i], i).start()
-
-    lag = SLACK * (last - place) + 2
-
-    def step(i, carry):
-        @pl.when(i < count)
-        def _():
-            upward(i)
-
-        behind = i - lag
-
-        @pl.when((behind >= 0) & (behind < count) & (place < last))
-        def _():
-            downward(behind)
-
-        return carry
-
-    lax.fori_loop(0, count + SLACK * last + 2, step, 0)
-
-    @pl.when(place < last)
-    def _():
-        remote(sums, landed, up_send, kept, above).wait_send()
-
-    @pl.when(place > 0)
-    def _():
-        remote(sums, out_ref.at[way], down_send, kept, below).wait_send()
-
-    @pl.when(place == last)
-    def _():
-        pltpu.make_async_copy(sums, out_ref.at[way], kept).wait()
-
-    if ways == 2:
-        remote(sums, out_ref.at[way], side_send, kept, beside).wait_send()
-        remote(sums, out_ref.at[1 - way], kept, side_recv, beside).wait_recv()
+    chain_loop(ways, places, out_ref, own, landed, semaphores, compute)
 
 
 def chain_sum(operands, blocks, collective_id):
@@ -744,7 +871,7 @@
     count = rows // depth
     tokens = operands[0].shape[1]
     return pl.pallas_call(
-        functools.partial(chain_kernel, ways, size // ways, blocks, len(operands), depth),
+        functools.partial(chain_kernel, ways, size // ways, blocks, len(operands)),
         out_shape=jax.ShapeDtypeStruct((ways, count, depth, columns), low),
         in_specs=[pl.BlockSpec(memory_space=pl.ANY)] * len(operands),
         out_specs=pl.BlockSpec(memory_space=pl.ANY),
@@ -752,16 +879,9 @@
         + [
             pltpu.VMEM((TILE, columns), full),
             pltpu.VMEM((count, depth, columns), low),
-            pltpu.VMEM((count, depth, columns), low),
             pltpu.SemaphoreType.DMA((len(operands),)),
-            pltpu.SemaphoreType.DMA,
-            pltpu.SemaphoreType.DMA((count,)),
-            pltpu.SemaphoreType.DMA,
-            pltpu.SemaphoreType.DMA((count,)),
-            pltpu.SemaphoreType.DMA,
-            pltpu.SemaphoreType.DMA,
-            pltpu.SemaphoreType.DMA,
-        ],
+        ]
+        + chain_semaphores(count),
         compiler_params=pltpu.CompilerParams(
             collective_id=collective_id, has_side_effects=True, vmem_limit_bytes=60 << 20
         ),
@@ -773,17 +893,357 @@
     )(*operands)
 
 
+def late_kernel(dims, *refs):
+    places, piece, group, n_head, n_units = dims
+    (
+        hidden_ref,
+        hidden_far_ref,
+        lows_ref,
+        lows_far_ref,
+        output_low_ref,
+        attended_ref,
+        normed_ref,
+        turned_ref,
+        turned_up_ref,
+        devs_ref,
+        output_grad_ref,
+        shifts,
+        scales,
+        gains,
+        all_gains,
+    ), refs = refs[:15], refs[15:]
+    (out_ref, split_ref, gain_ref), refs = refs[:3], refs[3:]
+    (
+        hidden,
+        lows,
+        output_low,
+        attended,
+        normed,
+        turned,
+        turned_up,
+        devs,
+        output_grad,
+        kept,
+        given,
+        taken,
+        grads,
+        joins,
+        totals,
+        own,
+        landed,
+        fetched,
+        core_send,
+        core_recv,
+        side_send,
+        side_recv,
+        join_send,
+        join_recv,
+        place_send,
+        place_recv,
+        own_copy,
+        *semaphores,
+    ) = refs
+    index, hid = lax.axis_index("dp"), lax.axis_index("hid")
+    core = index % 2
+    place, way = hid // 2, hid % 2
+    me = index * 2 + way
+    partner = {"hid": hid + 1 - 2 * way}
+    core_peer = {"dp": index + 1 - 2 * core}
+    others = [(i, j) for i in range(4) for j in range(2) if i or j]
+    wide = own.shape[1]
+    feats = normed.shape[1]
+
+    def join_device(i, j):
+        return {"dp": (index + i) % 4, "hid": place * 2 + (way + j) % 2}
+
+    def head_rows(turn):
+        return slice(turn * n_head, (turn + 1) * n_head)
+
+    def unit_rows(turn):
+        return slice(turn * n_units, (turn + 1) * n_units)
+
+    fetches = [
+        [(output_low_ref, output_low), (attended_ref, attended), (normed_ref, normed)],
+        [(hidden_ref, hidden.at[unit_rows(0)])],
+        [
+            (hidden_far_ref, hidden.at[unit_rows(2)]),
+            (turned_ref, turned),
+            (turned_up_ref, turned_up),
+            (devs_ref, devs),
+            (output_grad_ref, output_grad),
+        ]
+        + [
+            (source.at[head_rows(s)], lows.at[s, head_rows(turn)])
+            for s in range(3)
+            for turn, source in ((0, lows_ref), (2, lows_far_ref))
+        ],
+    ]
+
+    def fetch(stage):
+        return [pltpu.make_async_copy(a, b, fetched.at[stage, n]) for n, (a, b) in enumerate(fetches[stage])]
+
+    for stage in range(len(fetches)):
+        for copy in fetch(stage):
+            copy.start()
+
+    for k in range(1, places):
+        greet({"hid": (place + k) % places * 2 + way})
+    for i, j in others:
+        greet(join_device(i, j))
+    pl.semaphore_wait(pltpu.get_barrier_semaphore(), places - 1 + len(others))
+
+    def core_copies(far):
+        source, heads = (hidden_far_ref, lows_far_ref) if far else (hidden_ref, lows_ref)
+        turn = 3 if far else 1
+        yield remote(source, hidden.at[unit_rows(turn)], core_send.at[far], core_recv.at[far], core_peer)
+        for s in range(3):
+            yield remote(
+                heads.at[head_rows(s)],
+                lows.at[s, head_rows(turn)],
+                core_send.at[2 + far],
+                core_recv.at[2 + far],
+                core_peer,
+            )
+
+    for far in range(2):
+        for copy in core_copies(far):
+            copy.start()
+
+    def wait_cores():
+        for far in range(2):
+            remote(hidden_ref, hidden_ref, core_send.at[far], core_recv.at[far], core_peer).wait_recv()
+            remote(lows_ref, lows_ref, core_send.at[2 + far], core_recv.at[2 + far], core_peer).wait_recv()
+
+    per_block = feats // LATE_TILE
+    per_out = n_head // LATE_TILE
+
+    def compute(tile):
+        @pl.when(tile == 0)
+        def _():
+            for copy in fetch(0):
+                copy.wait()
+
+        @pl.when(tile == per_block)
+        def _():
+            for copy in fetch(1):
+                copy.wait()
+
+        inner = tile % per_block
+
+        def product(left, right):
+            own[...] = lax.dot_general(
+                left, right, (((1,), (1,)), ((), ())), preferred_element_type=full
+            )
+
+        def rows(n):
+            return pl.ds(pl.multiple_of(n * LATE_TILE, LATE_TILE), LATE_TILE)
+
+        @pl.when(tile < per_block)
+        def _():
+            half = pl.ds(pl.multiple_of(inner // per_out * wide, wide), wide)
+            product(attended[rows(inner % per_out), :], output_low[half, :])
+
+        block = tile // per_block
+
+        @pl.when((block >= 1) & (block < 5))
+        def _():
+            turn = (block - 1) // 2 + (block - 1) % 2 * 2
+            units = pl.ds(pl.multiple_of(turn * n_units, n_units), n_units)
+            product(normed[3, rows(inner), :], hidden[units, :])
+
+        @pl.when(block >= 5)
+        def _():
+            product(normed[block - 5, rows(inner), :], lows[block - 5])
+
+    totals[...] = jnp.zeros_like(totals)
+
+    def side_copy(s, r):
+        return remote(given.at[s, r], taken.at[s, r], side_send, side_recv.at[s], partner)
+
+    def pull(s):
+        def use(part):
+            for r in range(places):
+                rows = slice(2 * piece * r, 2 * piece * (r + 1))
+                here = part[rows]
+                totals[s, 0:1, :] = totals[s, 0:1, :] + jnp.sum(
+                    here * all_gains[s, r], axis=0, keepdims=True
+                )
+                totals[s, 1:2, :] = totals[s, 1:2, :] + jnp.sum(
+                    here * normed[s, rows, :].astype(full), axis=0, keepdims=True
+                )
+                first = way == 0
+                kept[s, r] = jnp.where(first, here[:piece], here[piece:])
+                given[s, r] = jnp.where(first, here[piece:], here[:piece]).astype(low)
+                side_copy(s, r).start()
+
+        @pl.when(s < 3)
+        def _():
+            use(jnp.dot(turned[s], lows[s], preferred_element_type=full))
+
+        @pl.when(s == 3)
+        def _():
+            use(jnp.dot(turned_up[...], hidden[...], preferred_element_type=full))
+
+    def share_totals():
+        joins[me] = totals[...]
+        for i, j in others:
+            remote(joins.at[me], joins.at[me], join_send, join_recv, join_device(i, j)).start()
+
+    def sum_totals():
+        some = joins.at[pl.ds(0, len(others))]
+        remote(some, some, join_send, join_recv, partner).wait_recv()
+        total = joins[0]
+        for i in range(1, len(others) + 1):
+            total = total + joins[i]
+        totals[...] = total / (feats * 4)
+
+    def stream_grad(s, r):
+        @pl.when(r == 0)
+        def _():
+            remote(given.at[s], taken.at[s], side_send, side_recv.at[s], partner).wait_recv()
+
+        gradient = kept[s, r] + taken[s, r].astype(full)
+        unit = devs[s, r].astype(full) * scales[s] + shifts[s, r]
+        gain_ref[s, r] = jnp.sum(gradient * unit, axis=1, keepdims=True)
+        result = gradient * gains[s, r] - totals[s, 0:1, :] - unit * totals[s, 1:2, :]
+        extra = output_grad[r] * jnp.where(s == 3, 1.0, 0.0)
+        grads[s, r] = (result * scales[s] + extra).astype(low)
+
+        @pl.when(r == place)
+        def _():
+            pltpu.make_async_copy(grads.at[s, r], split_ref.at[s, place], own_copy).start()
+
+        @pl.when(r != place)
+        def _():
+            remote(
+                grads.at[s, r],
+                split_ref.at[s, place],
+                place_send,
+                place_recv,
+                {"hid": r * 2 + way},
+            ).start()
+
+    n_pulls = STREAMS * places
+    middle = PULL_START + PULL_GAP * STREAMS
+    resume = middle + 8
+
+    def hook(i):
+        @pl.when(i == PULL_START)
+        def _():
+            for copy in fetch(2):
+                copy.wait()
+            wait_cores()
+
+        k = (i - PULL_START) // PULL_GAP
+
+        @pl.when((i >= PULL_START) & (i < middle) & ((i - PULL_START) % PULL_GAP == 0))
+        def _():
+            pull(k)
+
+        @pl.when(i == middle)
+        def _():
+            share_totals()
+
+        @pl.when(i == resume)
+        def _():
+            sum_totals()
+
+        n = (i - resume) // GRAD_GAP
+
+        @pl.when((i >= resume) & (n < n_pulls) & ((i - resume) % GRAD_GAP == 0))
+        def _():
+            stream_grad(n // places, n % places)
+
+    chain_loop(2, places, out_ref, own, landed, semaphores, compute, hook)
+
+    def sent(ref, sem):
+        remote(ref, ref, sem, join_recv, partner).wait_send()
+
+    for far in range(2):
+        sent(hidden_ref, core_send.at[far])
+        sent(lows_ref, core_send.at[2 + far])
+    sent(given, side_send)
+    sent(joins.at[pl.ds(0, len(others))], join_send)
+    moved = grads.at[pl.ds(0, places - 1)]
+    sent(moved, place_send)
+    remote(moved, moved, place_send, place_recv, partner).wait_recv()
+    mine = grads.at[0]
+    pltpu.make_async_copy(mine, mine, own_copy).wait()
+
+
+def late_sums(operands, tables, collective_id):
+    hidden, _, lows, _, output_low, attended, normed = operands[:7]
+    _, places, piece, group = operands[9].shape
+    feats = normed.shape[1]
+    n_units, n_head = hidden.shape[0], attended.shape[0]
+    wide = n_units
+    rows = 8 * feats
+    depth = max(16, CHUNK // wide)
+    count = rows // depth
+    vmem, dma = pltpu.VMEM, pltpu.SemaphoreType.DMA
+    block = (STREAMS, places, piece, group)
+    outs = [
+        jax.ShapeDtypeStruct((2, count, depth, wide), low),
+        jax.ShapeDtypeStruct(block, low),
+        jax.ShapeDtypeStruct((STREAMS, places, piece, 1), full),
+    ]
+    any_space, vmem_space = pl.BlockSpec(memory_space=pl.ANY), pl.BlockSpec(memory_space=vmem)
+    total, split, gain_parts = pl.pallas_call(
+        functools.partial(late_kernel, (places, piece, group, n_head, n_units)),
+        out_shape=outs,
+        in_specs=[any_space] * len(operands) + [vmem_space] * len(tables),
+        out_specs=[any_space, any_space, vmem_space],
+        scratch_shapes=[
+            vmem((4 * n_units, group), low),
+            vmem((3, 4 * n_head, group), low),
+            vmem(output_low.shape, low),
+            vmem(attended.shape, low),
+            vmem(normed.shape, low),
+            vmem(operands[7].shape, low),
+            vmem(operands[8].shape, low),
+            vmem(block, low),
+            vmem(block[1:], full),
+            vmem(block, full),
+            vmem(block, low),
+            vmem(block, low),
+            vmem(block, low),
+            vmem((8, STREAMS, 2, group), full),
+            vmem((STREAMS, 2, group), full),
+            vmem((LATE_TILE, wide), full),
+            vmem((count, depth, wide), low),
+            dma((3, 11)),
+            dma((4,)),
+            dma((4,)),
+            dma,
+            dma((STREAMS,)),
+            dma,
+            dma,
+            dma,
+            dma,
+            dma,
+        ]
+        + chain_semaphores(count),
+        compiler_params=pltpu.CompilerParams(
+            collective_id=collective_id, has_side_effects=True, vmem_limit_bytes=63 << 20
+        ),
+        cost_estimate=pl.CostEstimate(
+            flops=4 * rows * wide * group, bytes_accessed=900 << 20, transcendentals=0
+        ),
+    )(*operands, *tables)
+    return total.reshape(2, 8, feats, wide), split, gain_parts
+
+
 def chain_sums(operands, blocks, collective_id):
     groups, held, size = [[]], set(), 0
     for rows, segments in blocks:
         used = {n for seg in segments for n in (seg[0], seg[2])}
         more = sum(2 * operands[n].size for n in used - held)
-        more += 4 * rows * sum(seg[4] for seg in segments)
+        more += 2 * rows * sum(seg[4] for seg in segments)
         if groups[-1] and size + more > VMEM:
             groups.append([])
             held, size = set(), 0
             more = sum(2 * operands[n].size for n in used)
-            more += 4 * rows * sum(seg[4] for seg in segments)
+            more += 2 * rows * sum(seg[4] for seg in segments)
         groups[-1].append((rows, segments))
         held |= used
         size += more
@@ -800,7 +1260,7 @@
     return totals[0] if len(totals) == 1 else jnp.concatenate(totals, axis=1)
 
 
-def assemble_kernel(ways, dp, own_ref, *refs):
+def assemble_kernel(ways, dp, fused, own_ref, *refs):
     halves, (up_ref, *head_refs, out_ref) = refs[:ways], refs[ways:]
     rows, wide = own_ref.shape[2:]
     size = up_ref.shape[1] // dp // ways
@@ -813,11 +1273,12 @@
             start = turn * size
             lanes = pl.ds(pl.multiple_of(start % wide, size), size)
             place = (d * ways + w) * size
-            up_ref[:, place : place + size] = own_ref[w, start // wide, :, lanes].astype(full)
+            up_block = 1 + turn // 2 + turn % 2 * 2 if fused else start // wide
+            up_ref[:, place : place + size] = own_ref[w, up_block, :, lanes].astype(full)
             for s, ref in enumerate(head_refs):
                 lanes = pl.ds(pl.multiple_of(turn * own, own), own)
                 place = (d * ways + w) * own
-                ref[:, place : place + own] = own_ref[w, blocks + s, :, lanes].astype(full)
+                ref[:, place : place + own] = own_ref[w, blocks + s + fused, :, lanes].astype(full)
         start = turn * feats
         lanes = pl.ds(pl.multiple_of(start % wide, feats), feats)
         for w in range(ways):
@@ -827,18 +1288,18 @@
                 out_ref[:, d * feats : (d + 1) * feats] = halves[w][0, 0, :, lanes].astype(full)
 
 
-def assemble(total, w_up):
+def assemble(total, w_up, fused):
     ways, dp = split_ways(), lax.axis_size("dp")
     blocks, rows, wide = total.shape[1:]
     depth = min(64, rows // ways)
     share = rows // ways // depth
 
     def half_map(half):
-        return lambda i: (i // share, blocks - 1, half * share + i % share, 0)
+        return lambda i: (i // share, 0 if fused else blocks - 1, half * share + i % share, 0)
 
     widths = [w_up.shape[1]] + [ways * wide] * 4
     return pl.pallas_call(
-        functools.partial(assemble_kernel, ways, dp),
+        functools.partial(assemble_kernel, ways, dp, int(fused)),
         grid=(rows // depth,),
         out_shape=[jax.ShapeDtypeStruct((rows, n), full) for n in widths],
         in_specs=[pl.BlockSpec((ways, blocks, depth, wide), lambda i: (0, 0, i, 0))]
@@ -1025,8 +1486,9 @@
             (deviations[s].astype(full) * inv_scales[s] + own_shifts[s][:, None]).reshape(mine, group)
             for s in range(STREAMS)
         ]
+        normed_all = normed
         normed = [normed[s] for s in range(STREAMS)]
-        products = [by_head(v) for v in products]
+        products = products.reshape(3, heads, HEAD, group)
         turned_weights = [turned_heads[s] for s in range(3)] + [turned_up]
     else:
         moments = exchange(moments)
@@ -1066,12 +1528,6 @@
         turned_weights = [
             turned(w, ways * n_head, way * n_head, n_head) for w in (w_query, w_key, w_value)
         ] + [turned(w_up, ways * n_units, way * n_units, n_units)]
-    queries = rotate(products[0], cosine, sine).astype(low)
-    keys = rotate(products[1], cosine, sine).astype(low)
-    values = products[2].astype(low)
-    cotangent, queries = lax.optimization_barrier((out_cotangent, queries))
-    upstream = exchange(by_place(cotangent.T)).reshape(mine, group)
-
     out_rows, down_rows = way_rows(w_out), way_rows(w_down)
     turned_weights += [turned(out_rows, feats, 0, feats), turned(down_rows, feats, 0, feats)]
 
@@ -1093,14 +1549,25 @@
             .reshape(heads, HEAD, group)
         )
 
-    q_rows, k_rows, v_rows = by_row(queries), by_row(keys), by_row(values)
-    score_scale = 1.0 / math.sqrt(HEAD)
-    scores = batched(q_rows, k_rows, 1, 1) * score_scale
-    mask = jnp.broadcast_to(visible[None], (heads, rows, row, row)).reshape(scores.shape)
-    scores = jnp.where(mask, scores, -1e30)
-    probs = jax.nn.softmax(scores, axis=-1)
-    probs_low = probs.astype(low)
-    attended = from_row(batched(v_rows, probs_low, 2, 2).astype(low)).reshape(heads * HEAD, group)
+    if fused:
+        starts = doc_start.reshape(1, group)
+        turned_values, attended, tops = attend(products, cosine[0], sine[0], starts)
+        attended = attended.reshape(n_head, group)
+    else:
+        queries = rotate(products[0], cosine, sine).astype(low)
+        keys = rotate(products[1], cosine, sine).astype(low)
+        values = products[2].astype(low)
+        q_rows, k_rows, v_rows = by_row(queries), by_row(keys), by_row(values)
+        score_scale = 1.0 / math.sqrt(HEAD)
+        scores = batched(q_rows, k_rows, 1, 1) * score_scale
+        mask = jnp.broadcast_to(visible[None], (heads, rows, row, row)).reshape(scores.shape)
+        scores = jnp.where(mask, scores, -1e30)
+        probs = jax.nn.softmax(scores, axis=-1)
+        probs_low = probs.astype(low)
+        attended = from_row(batched(v_rows, probs_low, 2, 2).astype(low)).reshape(heads * HEAD, group)
+
+    cotangent, attended = lax.optimization_barrier((out_cotangent, attended))
+    upstream = exchange(by_place(cotangent.T)).reshape(mine, group)
 
     def make_out(index):
         start = index * feats
@@ -1184,18 +1651,23 @@
     hidden_low = (contract(turned_weights[5], output_low, 1, 0) * slope).astype(low)
 
     attended_grad = contract(turned_weights[4], output_low, 1, 0).astype(low)
-    a_rows = by_row(by_head(attended_grad))
-    prob_grad = batched(a_rows, v_rows, 1, 1)
-    row_total = jnp.sum(probs * prob_grad, axis=-1, keepdims=True)
-    score_grad = (probs * (prob_grad - row_total)).astype(low)
-    query_grad = from_row(batched(k_rows, score_grad, 2, 2) * score_scale)
-    key_grad = from_row(batched(q_rows, score_grad, 2, 1) * score_scale)
-    value_grad = from_row(batched(a_rows, probs_low, 2, 1))
-    query_low = rotate(query_grad, cosine, -sine).astype(low).reshape(heads * HEAD, group)
-    key_low = rotate(key_grad, cosine, -sine).astype(low).reshape(heads * HEAD, group)
-    value_low = value_grad.astype(low).reshape(heads * HEAD, group)
-
-    lows_mine = jnp.concatenate([query_low, key_low, value_low], axis=0)
+    if fused:
+        lows_mine = attend_back(
+            turned_values, by_head(attended_grad), cosine[0], sine[0], starts, tops
+        ).reshape(3 * n_head, group)
+    else:
+        a_rows = by_row(by_head(attended_grad))
+        prob_grad = batched(a_rows, v_rows, 1, 1)
+        row_total = jnp.sum(probs * prob_grad, axis=-1, keepdims=True)
+        score_grad = (probs * (prob_grad - row_total)).astype(low)
+        query_grad = from_row(batched(k_rows, score_grad, 2, 2) * score_scale)
+        key_grad = from_row(batched(q_rows, score_grad, 2, 1) * score_scale)
+        value_grad = from_row(batched(a_rows, probs_low, 2, 1))
+        query_low = rotate(query_grad, cosine, -sine).astype(low).reshape(heads * HEAD, group)
+        key_low = rotate(key_grad, cosine, -sine).astype(low).reshape(heads * HEAD, group)
+        value_low = value_grad.astype(low).reshape(heads * HEAD, group)
+
+        lows_mine = jnp.concatenate([query_low, key_low, value_low], axis=0)
     active_kept, hidden_low, lows_mine = lax.optimization_barrier((active, hidden_low, lows_mine))
     hidden_lows, lows = gather_outer(hidden_low), gather_outer(lows_mine)
     blocks = [(active.shape[0], [(0, 0, 1, 0, width)])]
@@ -1204,37 +1676,60 @@
         (branch_sum, block_output, hidden_lows, lows)
     )
     block_output = block_output.transpose(1, 0, 2).reshape(piece, total_tokens).T
-    hidden_lows, lows = gather_cores(hidden_lows), gather_cores(lows)
-
-    normed_grads, alongs, rights = [], [], []
-    for s in range(STREAMS):
-        if s < 3:
-            right = jnp.concatenate([v[s * n_head : (s + 1) * n_head] for v in lows], axis=0)
-        else:
-            right = jnp.concatenate(hidden_lows, axis=0)
-        rights.append(right)
-        part = contract(turned_weights[s], right, 1, 0)
-        alongs.append(jnp.sum(part * all_gains[:, s][:, None], axis=0))
-        alongs.append(jnp.sum(part * normed[s].astype(full), axis=0))
-        part = part.reshape(places, ways, piece, group)
-        kept = lax.dynamic_index_in_dim(part, way, 1, keepdims=False)
-        if ways == 2:
-            given = lax.dynamic_index_in_dim(part, 1 - way, 1, keepdims=False).astype(low)
-            kept = kept + hid_swap(given, 1).astype(full)
-        normed_grads.append(kept.reshape(mine, group))
-    weighted = [normed_grads[s] * gains[s] for s in range(STREAMS)]
-    means_back = sum_features(jnp.stack(alongs, axis=0)) / width
-    gain_parts = [jnp.sum(g * u, axis=1) for g, u in zip(normed_grads, units)]
-    stream_grads = [
-        (weighted[s] - means_back[2 * s] - units[s] * means_back[2 * s + 1]) * inv_scales[s]
-        for s in range(STREAMS)
-    ]
-    stream_grads[3] = stream_grads[3] + output_grad
-    smalls = jnp.concatenate([mixer_grad_part, jnp.stack(gain_parts, axis=0)], axis=0)
-
-    split = jnp.stack([v.astype(low).reshape(places, piece, group) for v in stream_grads], axis=1)
-    attended, split, smalls = lax.optimization_barrier((attended, split, smalls))
-    split = exchange(split)
+
+    if fused:
+        operands = [hidden_lows[0], hidden_lows[1], lows[0], lows[1], output_low, attended]
+        operands += [normed_all, turned_heads, turned_up, deviations]
+        operands.append(output_grad.reshape(places, piece, group))
+        tables = [
+            own_shifts[:, :, None],
+            inv_scales[:, None],
+            own_gains.T.reshape(STREAMS, places, piece, 1),
+            all_gains.T.reshape(STREAMS, places, 2 * piece, 1),
+        ]
+        late_sum, split, gain_parts = late_sums(operands, tables, 1)
+        split = split.swapaxes(0, 1)
+        gain_parts = gain_parts.reshape(STREAMS, mine)
+    else:
+        hidden_lows, lows = gather_cores(hidden_lows), gather_cores(lows)
+
+        normed_grads, alongs, rights = [], [], []
+        for s in range(STREAMS):
+            if s < 3:
+                right = jnp.concatenate([v[s * n_head : (s + 1) * n_head] for v in lows], axis=0)
+            else:
+                right = jnp.concatenate(hidden_lows, axis=0)
+            rights.append(right)
+            part = contract(turned_weights[s], right, 1, 0)
+            alongs.append(jnp.sum(part * all_gains[:, s][:, None], axis=0))
+            alongs.append(jnp.sum(part * normed[s].astype(full), axis=0))
+            part = part.reshape(places, ways, piece, group)
+            kept = lax.dynamic_index_in_dim(part, way, 1, keepdims=False)
+            if ways == 2:
+                given = lax.dynamic_index_in_dim(part, 1 - way, 1, keepdims=False).astype(low)
+                kept = kept + hid_swap(given, 1).astype(full)
+            normed_grads.append(kept.reshape(mine, group))
+        weighted = [normed_grads[s] * gains[s] for s in range(STREAMS)]
+        means_back = sum_features(jnp.stack(alongs, axis=0)) / width
+        gain_parts = [jnp.sum(g * u, axis=1) for g, u in zip(normed_grads, units)]
+        stream_grads = [
+            (weighted[s] - means_back[2 * s] - units[s] * means_back[2 * s + 1]) * inv_scales[s]
+            for s in range(STREAMS)
+        ]
+        stream_grads[3] = stream_grads[3] + output_grad
+        gain_parts = jnp.stack(gain_parts, axis=0)
+
+        split = jnp.stack([v.astype(low).reshape(places, piece, group) for v in stream_grads], axis=1)
+        attended, split = lax.optimization_barrier((attended, split))
+        split = exchange(split)
+        wide = w_query.shape[1] // ways
+        operands = [rights[3]] + rights[:3] + [output_low, normed[3]] + normed[:3] + [attended]
+        blocks = [(feats, [(5, 0, 0, i, wide)]) for i in range(0, rights[3].shape[0], wide)]
+        blocks += [(feats, [(6 + s, 0, 1 + s, 0, wide)]) for s in range(3)]
+        blocks += [(n_head, [(9, 0, 4, i, wide)]) for i in range(0, width, wide)]
+        late_sum = chain_sums(operands, blocks, 1).reshape(ways, -1, feats, wide)
+
+    smalls = jnp.concatenate([mixer_grad_part, gain_parts], axis=0)
     split = jnp.concatenate([split[p] for p in range(places)], axis=-1).astype(full)
     mix_layers = mix_all.reshape(STREAMS, HIST, total_tokens)
     history_grad = sum(mix_layers[s][:, None] * split[s][None] for s in range(STREAMS))
@@ -1244,12 +1739,6 @@
     )
     mix_parts = mix_parts.reshape(n_mix, dp * hid, block).transpose(1, 0, 2)
 
-    wide = w_query.shape[1] // ways
-    operands = [rights[3]] + rights[:3] + [output_low, normed[3]] + normed[:3] + [attended]
-    blocks = [(feats, [(5, 0, 0, i, wide)]) for i in range(0, rights[3].shape[0], wide)]
-    blocks += [(feats, [(6 + s, 0, 1 + s, 0, wide)]) for s in range(3)]
-    blocks += [(n_head, [(9, 0, 4, i, wide)]) for i in range(0, width, wide)]
-    late_sum = chain_sums(operands, blocks, 1)
     late_sum, mix_parts, smalls = lax.optimization_barrier((late_sum, mix_parts, smalls))
     smalls = sum_tokens(smalls)
     smalls = gather_ways(smalls.reshape(-1, places, piece), 2).reshape(-1, feats)
@@ -1258,8 +1747,7 @@
     mix_parts = lax.all_to_all(mix_parts, ("dp", "hid"), split_axis=0, concat_axis=0, tiled=True)
     mix_grad = jnp.sum(mix_parts, axis=0).T
     w_down_grad = unturn(branch_sum.reshape(w_down.shape))
-    late_sum = late_sum.reshape(ways, -1, feats, wide)
-    w_up_grad, w_query_grad, w_key_grad, w_value_grad, w_out_grad = assemble(late_sum, w_up)
+    w_up_grad, w_query_grad, w_key_grad, w_value_grad, w_out_grad = assemble(late_sum, w_up, fused)
 
     return (
         block_output,

time: 941 us -> 850 us (0.903)
  Pallas kernels: 533 us -> 594 us
  matrix products: 80.2 us -> 40.4 us
  local copies, waits for them, and re-layouts: 86.5 us -> 46.9 us
  other arithmetic: 76.2 us -> 44.8 us
  waiting for transfers between devices: 95.6 us -> 68 us
  starting transfers between devices: 60 us -> 47.8 us
    pallas_call x1 -> x4, Pallas kernels: 18.7 us -> 327 us  [the longest x1 298 us: late_sums(): pl.pallas_call(functools.partial(late_kernel, (places, piece, group, n_he...]
    pallas_call x2 -> x1, Pallas kernels: 373 us -> 127 us  [chain_sum(): pl.pallas_call(functools.partial(chain_kernel, ways, size // ways, blocks...]
    ppermute x13 -> x8, waiting for transfers between devices: 53.4 us -> 29.4 us  [hid_swap(): return lax.ppermute(values_in, 'hid', [(i, i ^ bit) for i in range(size)])]
    dot_general x17 -> x13, matrix products: 52.4 us -> 36.2 us  [contract(): lax.dot_general(left, right, (((left_dim,), (right_dim,)), ((), ())), pre...]
    dot_general x5 -> x0, matrix products: 15.3 us -> none  [batched(): lax.dot_general(left, right, (((left_dim,), (right_dim,)), ((0,), (0,))),...]
    unnamed x176 -> x74, local copies, waits for them, and re-layouts: 21.8 us -> 10.6 us
    ppermute x6 -> x5, waiting for transfers between devices: 37.5 us -> 31.7 us  [outer_shift(): return lax.ppermute(values_in, 'dp', pairs)]
    ppermute x13 -> x8, starting transfers between devices: 20.1 us -> 14.9 us  [hid_swap(): return lax.ppermute(values_in, 'hid', [(i, i ^ bit) for i in range(size)])]
  transfers between devices with their start and end apart: 36 -> 24, of which waited for: 17 -> 11; matrix products, arithmetic and copies ran while one was open for 14% -> 10% of each run, Pallas kernels for 57% -> 34%
where the time goes in v5:
time: 850 us; the launch traced here: 844 us
  Pallas kernels  594 us (70%)
  waiting for transfers between devices  68 us (8%)
  starting transfers between devices  47.8 us (6%)
  local copies, waits for them, and re-layouts  46.9 us (6%)
  other arithmetic  44.8 us (5%)
  matrix products  40.4 us (5%)
    pallas_call x1, Pallas kernels, late_sums(): pl.pallas_call(functools.partial(late_kernel, (places, piece, group, n_he...  298 us
    pallas_call x1, Pallas kernels, forward_projections(): pl.pallas_call(functools.partial(forward_kernel, (places, piece, group, n...  130 us
    pallas_call x1, Pallas kernels, chain_sum(): pl.pallas_call(functools.partial(chain_kernel, ways, size // ways, blocks...  127 us
    dot_general x13, matrix products, contract(): lax.dot_general(left, right, (((left_dim,), (right_dim,)), ((), ())), pre...  36.2 us
    ppermute x5, waiting for transfers between devices, outer_shift(): return lax.ppermute(values_in, 'dp', pairs)  31.7 us
    ppermute x8, waiting for transfers between devices, hid_swap(): return lax.ppermute(values_in, 'hid', [(i, i ^ bit) for i in range(size)])  29.4 us
    pallas_call x1, Pallas kernels, assemble(): pl.pallas_call(functools.partial(assemble_kernel, ways, dp, int(fused)),...  18.6 us
  transfers between devices with their start and end apart: 24, of which 11 were waited for; matrix products, arithmetic and copies ran while one was open for 10% of the time, Pallas kernels for 34%

profile of v5, /device:TPU:0, one launch (start us, length us, event | category | flops | bytes accessed | tf_op | source)
XLA Modules:
  0.0 844.0 jit_solution(490398715127732342)
XLA Ops:
  2.2 7.3 all-to-all-start
  13.1 5.4 fusion.161
  20.8 5.1 all-to-all-done
  44.8 129.7 %shard_map.254 = (bf16[4,512,1024]{2,1,0:T(8,128)(2,1)}, bf16[4,4,64,1024]{3,2,1,0:T(8,128)(2,1)}, f32[4,16,1024]{2,1,0:T(8,128)}, bf16[1024,1024]{1,0:T(8,128)(...) custom-call(bf16[4,4,64,1024]{3,2,1,0:T(8,128)(2,1)} %pad_maximum_fu, ...), custom_call_target="tpu_custom_call" | custom-call | flops 7516192768 | bytes 314572800 | tf_op jit(solution)/shard_map/pallas_call | solution.py:629
  174.5 4.7 fusion.107
  182.9 4.8 shard_map.255
  212.9 4.2 fusion.105
  218.0 6.1 all-to-all-start.2
  225.7 6.5 collective-permute-done.1
  237.7 10.5 %collective-permute-done.3 = bf16[4,64,1024]{2,1,0:T(8,128)(2,1)S(1)} collective-permute-done((bf16[4,64,1024]{2,1,0:T(8,128)(2,1)S(1)}, bf16[4,64,1024]{2,1,0:T(8,128)(2,1)S(1)}, u32[]{:S(2)}, u32[]{:S(2)}) %collective-permute-start.3) | collective-permute-done | bytes 524320 | tf_op jit(solution)/shard_map/ppermute | solution.py:75
  252.2 3.9 collective-permute-done.4
  257.4 4.1 collective-permute-done.5
  268.6 3.8 collective-permute-start.7
  284.3 10.7 %collective-permute-done.9 = bf16[4,64,1024]{2,1,0:T(8,128)(2,1)S(1)} collective-permute-done((bf16[4,64,1024]{2,1,0:T(8,128)(2,1)S(1)}, bf16[4,64,1024]{2,1,0:T(8,128)(2,1)S(1)}, u32[]{:S(2)}, u32[]{:S(2)}) %collective-permute-start.9) | collective-permute-done | bytes 524320 | tf_op jit(solution)/shard_map/ppermute | solution.py:75
  296.6 21.1 %collective-permute-done.11 = bf16[512,1024]{1,0:T(8,128)(2,1)} collective-permute-done((bf16[512,1024]{1,0:T(8,128)(2,1)S(1)}, bf16[512,1024]{1,0:T(8,128)(2,1)}, u32[]{:S(2)}, u32[]{:S(2)}) %collective-permute-start.11) | collective-permute-done | bytes 1048608 | tf_op jit(solution)/shard_map/ppermute | solution.py:70
  327.3 5.7 multiply_convert_fusion.refs_0_
  333.0 5.8 shard_map.256
  343.9 4.5 all-to-all-start.3
  350.5 127.3 %shard_map.257 = bf16[2,64,16,2048]{3,2,1,0:T(8,128)(2,1)} custom-call(bf16[1024,1024]{1,0:T(8,128)(2,1)} %get-tuple-element.66.refs_0_, bf16[2048,1024]{1,0:T(8,128)(2,1)} %copy-done.13), custom_call_target="tpu_custom_call" | custom-call | flops 4294967296 | bytes 629145600 | tf_op jit(solution)/shard_map/pallas_call | solution.py:873
  477.9 297.6 %shard_map.258 = (bf16[2,128,32,1024]{3,2,1,0:T(8,128)(2,1)}, bf16[4,4,64,1024]{3,2,1,0:T(8,128)(2,1)}, f32[4,4,64,1]{3,2,1,0:T(8,128)}) custom-call(bf16[1024,1024]{1,0:T(8,128)(2,1)} %multiply_convert_fusion.refs_0_, bf16[1024,1024]{1,0:T(8,128)(2,1)} %collective-permute-done.13.refs_1_, bf16[768,1024]{1,0:T(8,128)(2,1)} %bitcast.505, ...), custom_call_target="tpu_custom_call" | custom-call | flops 17179869184 | bytes 943718400 | tf_op jit(solution)/shard_map/pallas_call | solution.py:1191
  780.3 3.7 fusion
  802.8 5.6 multiply_add_fusion
  809.2 18.6 %shard_map.259 = (f32[512,8192]{1,0:T(8,128)}, f32[512,2048]{1,0:T(8,128)}, f32[512,2048]{1,0:T(8,128)}, f32[512,2048]{1,0:T(8,128)}, f32[512,2048]{1,0:T(8,128)}) custom-call(bf16[2,8,512,1024]{3,2,1,0:T(8,128)(2,1)} %bitcast.516, bf16[2,8,512,1024]{3,2,1,0:T(8,128)(2,1)} %bitcast.517, bf16[2,8,512,1024]{3,2,1,0:T(8,128)(2,1)} %bitcast.518), custom_call_target="tpu_custom_call" | custom-call | bytes 50331648 | tf_op jit(solution)/shard_map/pallas_call | solution.py:1301
  827.8 10.3 %shard_map.260 = f32[2048,2048]{1,0:T(8,128)} custom-call(bf16[2048,2048]{1,0:T(8,128)(2,1)} %bitcast.519), custom_call_target="tpu_custom_call" | custom-call | bytes 25165824 | tf_op jit(solution)/shard_map/pallas_call | solution.py:1325
  (239 shorter events, 135.0 us)
Async XLA Ops:
  2.2 23.7 %all-to-all-start = ((f32[32,32,128]{2,1,0:T(8,128)}), f32[32,32,128]{2,1,0:T(8,128)S(1)}, u32[]{:S(2)}, u32[]{:S(2)}) async-start(f32[32,32,128]{2,1,0:T(8,128)} %broadcast_in_dim.24), calls=%async_computation | async-start | bytes 1048576 | tf_op jit(solution)/shard_map/all_to_all | solution.py:165
  26.8 152.4 %all-to-all-start.1 = ((f32[32,37,128]{2,1,0:T(8,128)}), f32[32,37,128]{2,1,0:T(8,128)S(1)}, u32[]{:S(2)}, u32[]{:S(2)}) async-start(f32[32,37,128]{2,1,0:T(8,128)} %broadcast_in_dim.28), calls=%async_computation.1 | async-start | bytes 1310720 | tf_op jit(solution)/shard_map/all_to_all | solution.py:165
  191.6 11.9 %collective-permute-start = (bf16[512,1024]{1,0:T(8,128)(2,1)}, bf16[512,1024]{1,0:T(8,128)(2,1)}, u32[]{:S(2)}, u32[]{:S(2)}) collective-permute-start(bf16[512,1024]{1,0:T(8,128)(2,1)} %add_convert_fusion.2), channel_id=1, source_target_pairs={{0,8},{8,0},{16,24},{24,16},{1,9},{9,1},{17,25},{25,17},{2,10},{10... | collective-permute-start | bytes 3145736 | tf_op jit(solution)/shard_map/ppermute | solution.py:61
  203.4 22.3 %collective-permute-start.2 = (bf16[512,1024]{1,0:T(8,128)(2,1)}, bf16[512,1024]{1,0:T(8,128)(2,1)}, u32[]{:S(2)}, u32[]{:S(2)}) collective-permute-start(bf16[512,1024]{1,0:T(8,128)(2,1)} %add_convert_fusion), channel_id=1, source_target_pairs={{0,8},{8,0},{16,24},{24,16},{1,9},{9,1},{17,25},{25,17},{2,10},{10... | collective-permute-start | bytes 3145736 | tf_op jit(solution)/shard_map/ppermute | solution.py:61
  206.4 25.9 %collective-permute-start.1 = (bf16[512,1024]{1,0:T(8,128)(2,1)}, bf16[512,1024]{1,0:T(8,128)(2,1)}, u32[]{:S(2)}, u32[]{:S(2)}) collective-permute-start(bf16[512,1024]{1,0:T(8,128)(2,1)} %add_convert_fusion.1), channel_id=1, source_target_pairs={{0,16},{8,24},{16,0},{24,8},{1,17},{9,25},{17,1},{25,9},{2,18},{10... | collective-permute-start | bytes 3145736 | tf_op jit(solution)/shard_map/ppermute | solution.py:70
  218.0 30.6 %all-to-all-start.2 = ((bf16[4,64,1024]{2,1,0:T(8,128)(2,1)}), bf16[4,64,1024]{2,1,0:T(8,128)(2,1)}, u32[]{:S(2)}, u32[]{:S(2)}) async-start(bf16[4,64,1024]{2,1,0:T(8,128)(2,1)} %pad_maximum_fusion.7), calls=%async_computation.2 | async-start | bytes 1048576 | tf_op jit(solution)/shard_map/all_to_all | solution.py:190
  234.6 13.6 %collective-permute-start.3 = (bf16[4,64,1024]{2,1,0:T(8,128)(2,1)S(1)}, bf16[4,64,1024]{2,1,0:T(8,128)(2,1)S(1)}, u32[]{:S(2)}, u32[]{:S(2)}) collective-permute-start(bf16[4,64,1024]{2,1,0:T(8,128)(2,1)S(1)} %fusion.111), channel_id=1, source_target_pairs={{0,1},{1,0},{2,3},{3,2},{4,5},{5,4},{6,7},{7,6},{8,9},{9,8},{10,11... | collective-permute-start | bytes 1572872 | tf_op jit(solution)/shard_map/ppermute | solution.py:75
  250.7 5.4 collective-permute-start.4
  256.1 5.4 collective-permute-start.5
  261.6 1.8 collective-permute-start.6
  268.6 5.5 collective-permute-start.7
  274.1 4.6 collective-permute-start.8
  283.1 11.9 %collective-permute-start.9 = (bf16[4,64,1024]{2,1,0:T(8,128)(2,1)S(1)}, bf16[4,64,1024]{2,1,0:T(8,128)(2,1)S(1)}, u32[]{:S(2)}, u32[]{:S(2)}) collective-permute-start(bf16[4,64,1024]{2,1,0:T(8,128)(2,1)S(1)} %bitcast.531), channel_id=1, source_target_pairs={{0,1},{1,0},{2,3},{3,2},{4,5},{5,4},{6,7},{7,6},{8,9},{9,8},{10,11... | collective-permute-start | bytes 1572872 | tf_op jit(solution)/shard_map/ppermute | solution.py:75
  295.2 22.4 %collective-permute-start.11 = (bf16[512,1024]{1,0:T(8,128)(2,1)S(1)}, bf16[512,1024]{1,0:T(8,128)(2,1)}, u32[]{:S(2)}, u32[]{:S(2)}) collective-permute-start(bf16[512,1024]{1,0:T(8,128)(2,1)S(1)} %bitcast.525), channel_id=1, source_target_pairs={{0,16},{8,24},{16,0},{24,8},{1,17},{9,25},{17,1},{25,9},{2,18},{10... | collective-permute-start | bytes 3145736 | tf_op jit(solution)/shard_map/ppermute | solution.py:70
  296.6 24.3 %collective-permute-start.10 = (bf16[512,1024]{1,0:T(8,128)(2,1)S(1)}, bf16[512,1024]{1,0:T(8,128)(2,1)}, u32[]{:S(2)}, u32[]{:S(2)}) collective-permute-start(bf16[512,1024]{1,0:T(8,128)(2,1)S(1)} %bitcast.526), channel_id=1, source_target_pairs={{0,8},{8,0},{16,24},{24,16},{1,9},{9,1},{17,25},{25,17},{2,10},{10... | collective-permute-start | bytes 3145736 | tf_op jit(solution)/shard_map/ppermute | solution.py:61
  317.7 3.2 collective-permute-start.12
  338.8 139.1 %collective-permute-start.13 = (bf16[1024,1024]{1,0:T(8,128)(2,1)}, bf16[1024,1024]{1,0:T(8,128)(2,1)}, u32[]{:S(2)}, u32[]{:S(2)}) collective-permute-start(bf16[1024,1024]{1,0:T(8,128)(2,1)} %multiply_convert_fusion.refs_0_), channel_id=1, source_target_pairs={{0,16},{8,24},{16,0},{24,8},{1,17},{9,25},{17,1},{25,9},{2,18},{10... | collective-permute-start | bytes 6291464 | tf_op jit(solution)/shard_map/ppermute | solution.py:70
  340.1 137.8 %collective-permute-start.14 = (bf16[768,1024]{1,0:T(8,128)(2,1)S(1)}, bf16[768,1024]{1,0:T(8,128)(2,1)}, u32[]{:S(2)}, u32[]{:S(2)}) collective-permute-start(bf16[768,1024]{1,0:T(8,128)(2,1)S(1)} %bitcast.504), channel_id=1, source_target_pairs={{0,16},{8,24},{16,0},{24,8},{1,17},{9,25},{17,1},{25,9},{2,18},{10... | collective-permute-start | bytes 4718600 | tf_op jit(solution)/shard_map/ppermute | solution.py:70
  343.9 133.9 %all-to-all-start.3 = ((bf16[4,64,1024]{2,1,0:T(8,128)(2,1)}), bf16[4,64,1024]{2,1,0:T(8,128)(2,1)S(1)}, u32[]{:S(2)}, u32[]{:S(2)}) async-start(bf16[4,64,1024]{2,1,0:T(8,128)(2,1)} %bitcast.105), calls=%async_computation.3 | async-start | bytes 1048576 | tf_op jit(solution)/shard_map/all_to_all | solution.py:190
  786.3 4.2 collective-permute-start.16
  787.9 7.6 collective-permute-start.15
  791.2 9.8 %collective-permute-start.17 = (f32[40,256]{1,0:T(8,128)S(1)}, f32[40,256]{1,0:T(8,128)S(1)}, u32[]{:S(2)}, u32[]{:S(2)}) collective-permute-start(f32[40,256]{1,0:T(8,128)S(1)} %add.600), channel_id=1, source_target_pairs={{0,4},{1,5},{2,6},{3,7},{4,0},{5,1},{6,2},{7,3},{8,12},{9,13},{10,... | collective-permute-start | bytes 122888 | tf_op jit(solution)/shard_map/ppermute | solution.py:75
  797.7 43.0 %all-to-all-start.4 = ((f32[32,32,128]{2,1,0:T(8,128)}), f32[32,32,128]{2,1,0:T(8,128)}, u32[]{:S(2)}, u32[]{:S(2)}) async-start(f32[32,32,128]{2,1,0:T(8,128)} %copy.86), calls=%async_computation.4 | async-start | bytes 1048576 | tf_op jit(solution)/shard_map/all_to_all | solution.py:1747
  801.1 37.0 %collective-permute-start.18 = (f32[40,4,64]{2,1,0:T(4,128)S(1)}, f32[40,4,64]{2,1,0:T(4,128)}, u32[]{:S(2)}, u32[]{:S(2)}) collective-permute-start(f32[40,4,64]{2,1,0:T(4,128)S(1)} %reshape.679), channel_id=1, source_target_pairs={{0,1},{1,0},{2,3},{3,2},{4,5},{5,4},{6,7},{7,6},{8,9},{9,8},{10,11... | collective-permute-start | bytes 122888 | tf_op jit(solution)/shard_map/ppermute | solution.py:75
  (34 other events, 1011.6 us)

commit v6 on v5

--- a/solution.py
+++ b/solution.py
@@ -320,6 +320,7 @@
 def forward_kernel(dims, *refs):
     places, piece, group, n_head, n_units = dims
     (send_ref, mom_ref, gains_ref, query_ref, key_ref, value_ref, up_ref), refs = refs[:7], refs[7:]
+    cot_ref, refs = refs[0], refs[1:]
     (
         normed_ref,
         own_ref,
@@ -329,7 +330,8 @@
         heads_ref,
         turned_ref,
         turned_up_ref,
-    ), refs = refs[:8], refs[8:]
+        cot_out,
+    ), refs = refs[:9], refs[9:]
     (
         devs,
         moms,
@@ -355,6 +357,9 @@
         core_recv,
         outer_send,
         outer_recv,
+        cot_send,
+        cot_recv,
+        cot_own,
     ) = refs
     count = weights.shape[0]
     ups = n_units // n_head
@@ -420,6 +425,9 @@
     for s in (3, 0, 1, 2):
         for k in range(1, places):
             dev_copy(s, k, place, peer(k)).start()
+    for k in range(1, places):
+        remote(cot_ref.at[peer(k)], cot_out.at[place], cot_send, cot_recv, z_device(k)).start()
+    pltpu.make_async_copy(cot_ref.at[place], cot_out.at[place], cot_own).start()
     moms[way, place] = mom_ref[place]
     for s in range(STREAMS):
         devs[s, way, place] = send_ref[place, s]
@@ -605,10 +613,14 @@
     sent(joins.at[pl.ds(0, n_others)], join_send)
     sent(core_out, core_send)
     sent(outer_out, outer_send)
+    moved = cot_ref.at[pl.ds(0, places - 1)]
+    sent(moved, cot_send)
+    remote(moved, moved, cot_send, cot_recv, partner).wait_recv()
+    pltpu.make_async_copy(cot_ref.at[0], cot_out.at[0], cot_own).wait()
     pltpu.make_async_copy(weights, weights, turned_sem).wait()
 
 
-def forward_projections(deviations, moments, norm_gains, w_query, w_key, w_value, w_up):
+def forward_projections(deviations, moments, norm_gains, w_query, w_key, w_value, w_up, cotangent):
     places, _, piece, group = deviations.shape
     feats = norm_gains.shape[0]
     n_head = w_query.shape[1] // 8
@@ -624,12 +636,13 @@
         ((3, n_head, group), full),
         ((3, feats, 4 * n_head), low),
         ((feats, 4 * n_units), low),
+        (cotangent.shape, low),
     ]
-    spaces = [vmem] * 6 + [pl.ANY] * 2
+    spaces = [vmem] * 6 + [pl.ANY] * 3
     return pl.pallas_call(
         functools.partial(forward_kernel, (places, piece, group, n_head, n_units)),
         out_shape=[jax.ShapeDtypeStruct(*t) for t in out_types],
-        in_specs=[pl.BlockSpec(memory_space=vmem)] * 3 + [pl.BlockSpec(memory_space=pl.ANY)] * 4,
+        in_specs=[pl.BlockSpec(memory_space=vmem)] * 3 + [pl.BlockSpec(memory_space=pl.ANY)] * 5,
         out_specs=[pl.BlockSpec(memory_space=m) for m in spaces],
         scratch_shapes=[
             vmem((STREAMS, 2, places, piece, group), low),
@@ -656,6 +669,9 @@
             dma((count, 2)),
             dma,
             dma((count,)),
+            dma,
+            dma,
+            dma,
         ],
         compiler_params=pltpu.CompilerParams(
             collective_id=7, has_side_effects=True, vmem_limit_bytes=62 << 20
@@ -673,6 +689,7 @@
         w_key,
         w_value,
         w_up,
+        cotangent,
     )
 
 
@@ -713,24 +730,59 @@
 
 def chain_semaphores(count):
     dma = pltpu.SemaphoreType.DMA
-    return [dma, dma((count,)), dma, dma((count,)), dma, dma, dma]
-
-
-def chain_loop(ways, places, out_ref, own, landed, semaphores, compute, hook=None):
-    up_send, up_recv, down_send, down_recv, side_send, side_recv, kept = semaphores
+    return [dma, dma((count,)), dma, dma((count,)), dma, dma, dma, dma, dma((count,))]
+
+
+def chain_loop(ways, places, out_ref, own, landed, semaphores, compute, hook=None, far=None):
+    (
+        up_send,
+        up_recv,
+        down_send,
+        down_recv,
+        side_send,
+        side_recv,
+        kept,
+        far_send,
+        far_recv,
+    ) = semaphores
     count, depth = landed.shape[:2]
     per_tile = own.shape[0] // depth
     last = places - 1
+    root = last if far is None else places // 2
     place, way, above, below, beside = chain_place(ways, places)
-
-    def up_copy(i):
-        return remote(landed.at[i], landed.at[i], up_send, up_recv.at[i], {"hid": above})
-
-    def down_copy(source, i):
-        return remote(source, out_ref.at[way, i], down_send, down_recv.at[i], {"hid": below})
-
-    def side_copy(source, i):
-        return remote(source, out_ref.at[way, i], side_send, side_recv, {"hid": beside})
+    above, below, beside = {"hid": above}, {"hid": below}, {"hid": beside}
+
+    def send_in(i):
+        @pl.when(place < root)
+        def _():
+            remote(landed.at[i], landed.at[i], up_send, up_recv.at[i], above).start()
+
+        if far is not None:
+
+            @pl.when(place == root + 1)
+            def _():
+                remote(landed.at[i], far.at[i], up_send, far_recv.at[i], below).start()
+
+            @pl.when(place > root + 1)
+            def _():
+                remote(landed.at[i], landed.at[i], up_send, up_recv.at[i], below).start()
+
+    def send_out(source, i):
+        def to(device, send):
+            remote(source, out_ref.at[way, i], send, down_recv.at[i], device).start()
+
+        @pl.when((place <= root) & (place > 0))
+        def _():
+            to(below, down_send)
+
+        if far is not None:
+
+            @pl.when((place >= root) & (place < last))
+            def _():
+                to(above, far_send)
+
+        if ways == 2:
+            remote(source, out_ref.at[way, i], side_send, side_recv, beside).start()
 
     def upward(i):
         @pl.when(i % per_tile == 0)
@@ -738,39 +790,45 @@
             compute(i // per_tile)
 
         mine = own[pl.ds(pl.multiple_of(i % per_tile * depth, depth), depth), :]
-
-        @pl.when(place == 0)
+        ends = place == 0 if far is None else (place == 0) | (place == last)
+
+        @pl.when(ends)
         def _():
             landed[i] = mine.astype(low)
-            up_copy(i).start()
-
-        @pl.when(place > 0)
-        def _():
-            up_copy(i).wait_recv()
-            landed[i] = (landed[i].astype(full) + mine).astype(low)
-
-            @pl.when(place < last)
-            def _():
-                up_copy(i).start()
-
-            @pl.when(place == last)
-            def _():
-                down_copy(landed.at[i], i).start()
-                if ways == 2:
-                    side_copy(landed.at[i], i).start()
-                pltpu.make_async_copy(landed.at[i], out_ref.at[way, i], kept).start()
+
+        @pl.when(jnp.logical_not(ends))
+        def _():
+            remote(landed.at[i], landed.at[i], up_send, up_recv.at[i], above).wait_recv()
+            total = landed[i].astype(full) + mine
+            if far is None:
+                landed[i] = total.astype(low)
+            else:
+
+                @pl.when(place != root)
+                def _():
+                    landed[i] = total.astype(low)
+
+                @pl.when(place == root)
+                def _():
+                    remote(far.at[i], far.at[i], up_send, far_recv.at[i], above).wait_recv()
+                    landed[i] = (total + far[i].astype(full)).astype(low)
+
+        @pl.when(place != root)
+        def _():
+            send_in(i)
+
+        @pl.when(place == root)
+        def _():
+            send_out(landed.at[i], i)
+            pltpu.make_async_copy(landed.at[i], out_ref.at[way, i], kept).start()
 
     def downward(i):
-        down_copy(landed.at[i], i).wait_recv()
-
-        @pl.when(place > 0)
-        def _():
-            down_copy(out_ref.at[way, i], i).start()
-
-        if ways == 2:
-            side_copy(out_ref.at[way, i], i).start()
-
-    lag = SLACK * (last - place) + 2
+        done = out_ref.at[way, i]
+        remote(done, done, down_send, down_recv.at[i], below).wait_recv()
+        send_out(done, i)
+
+    away = root - place if far is None else jnp.where(place < root, root - place, place - root)
+    lag = SLACK * away + 2
 
     def step(i, carry):
         @pl.when(i < count)
@@ -779,7 +837,7 @@
 
         behind = i - lag
 
-        @pl.when((behind >= 0) & (behind < count) & (place < last))
+        @pl.when((behind >= 0) & (behind < count) & (place != root))
         def _():
             downward(behind)
 
@@ -787,28 +845,37 @@
             hook(i)
         return carry
 
-    lax.fori_loop(0, count + SLACK * last + 2, step, 0)
-
-    @pl.when(place < last)
+    lax.fori_loop(0, count + SLACK * root + 2, step, 0)
+
+    def sent(sem):
+        remote(landed, landed, sem, side_recv, beside).wait_send()
+
+    @pl.when(place != root)
     def _():
-        remote(landed, landed, up_send, kept, {"hid": above}).wait_send()
-
-    @pl.when(place > 0)
+        sent(up_send)
+
+    @pl.when((place <= root) & (place > 0))
     def _():
-        remote(landed, out_ref.at[way], down_send, kept, {"hid": below}).wait_send()
-
-    @pl.when(place == last)
+        sent(down_send)
+
+    if far is not None:
+
+        @pl.when((place >= root) & (place < last))
+        def _():
+            sent(far_send)
+
+    @pl.when(place == root)
     def _():
         pltpu.make_async_copy(landed, out_ref.at[way], kept).wait()
 
     if ways == 2:
-        remote(landed, out_ref.at[way], side_send, kept, {"hid": beside}).wait_send()
-        remote(landed, out_ref.at[1 - way], kept, side_recv, {"hid": beside}).wait_recv()
+        sent(side_send)
+        remote(landed, landed, side_send, side_recv, beside).wait_recv()
 
 
 def chain_kernel(ways, places, blocks, n_operands, *refs):
     operand_refs, out_ref, refs = refs[:n_operands], refs[n_operands], refs[n_operands + 1 :]
-    operands, (own, landed, fetched, *semaphores) = refs[:n_operands], refs[n_operands:]
+    operands, (own, landed, far, fetched, *semaphores) = refs[:n_operands], refs[n_operands:]
     last = places - 1
     place, way, above, below, beside = chain_place(ways, places)
 
@@ -860,7 +927,7 @@
                     )
                     column += size
 
-    chain_loop(ways, places, out_ref, own, landed, semaphores, compute)
+    chain_loop(ways, places, out_ref, own, landed, semaphores, compute, far=far)
 
 
 def chain_sum(operands, blocks, collective_id):
@@ -879,6 +946,7 @@
         + [
             pltpu.VMEM((TILE, columns), full),
             pltpu.VMEM((count, depth, columns), low),
+            pltpu.VMEM((count, depth, columns), low),
             pltpu.SemaphoreType.DMA((len(operands),)),
         ]
         + chain_semaphores(count),
@@ -891,6 +959,221 @@
             transcendentals=0,
         ),
     )(*operands)
+
+
+def branch_kernel(dims, *refs):
+    places, piece, group = dims
+    (attended_ref, active_ref, residual_ref, mixer_ref, out_w_ref, down_w_ref), refs = refs[:6], refs[6:]
+    (output_ref, rounded_ref, sums_ref, turned_out_ref, turned_down_ref), refs = refs[:5], refs[5:]
+    (
+        weights,
+        passing,
+        kept,
+        core_out,
+        core_in,
+        outer_out,
+        outer_in,
+        side_out,
+        side_in,
+        parts_out,
+        parts_in,
+        totals,
+        weight_sem,
+        turned_sem,
+        core_send,
+        core_recv,
+        outer_send,
+        outer_recv,
+        side_send,
+        side_recv,
+        part_send,
+        part_recv,
+        total_send,
+        total_recv,
+    ) = refs
+    index, hid = lax.axis_index("dp"), lax.axis_index("hid")
+    outer, core = index // 2, index % 2
+    place, way = hid // 2, hid % 2
+    me = index * 2 + way
+    partner = {"hid": hid + 1 - 2 * way}
+    core_peer = {"dp": index + 1 - 2 * core}
+    outer_peer = {"dp": (index + 2) % 4}
+    others = [(i, j) for i in range(4) for j in range(2) if i or j]
+    n_head, n_units = attended_ref.shape[0], active_ref.shape[0]
+    feats = weights.shape[2]
+    wide = group // 8
+
+    def peer(i, j):
+        there, other = (index + i) % 4, (way + j) % 2
+        return there * 2 + other, {"dp": there, "hid": place * 2 + other}
+
+    def weight_copies(t):
+        there = (1 - outer if t < 2 else outer) * 2 + (core if t % 2 else 1 - core)
+        columns = pl.ds(pl.multiple_of(there * feats, feats), feats)
+        for ref, first, size in ((out_w_ref, 0, n_head), (down_w_ref, n_head, n_units)):
+            rows = pl.ds(pl.multiple_of(way * size, size), size)
+            yield pltpu.make_async_copy(
+                ref.at[rows, columns], weights.at[t, first : first + size], weight_sem.at[t]
+            )
+
+    def turned_copies(t):
+        columns = slice((3 - t) * feats, (4 - t) * feats)
+        for ref, first, size in ((turned_out_ref, 0, n_head), (turned_down_ref, n_head, n_units)):
+            yield pltpu.make_async_copy(
+                weights.at[t, first : first + size], ref.at[:, columns], turned_sem
+            )
+
+    for t in range(4):
+        for copy in weight_copies(t):
+            copy.start()
+    for i, j in others:
+        greet(peer(i, j)[1])
+    pl.semaphore_wait(pltpu.get_barrier_semaphore(), len(others))
+
+    def halves(t, target, kind):
+        pltpu.make_async_copy(weights.at[t], weights.at[t], weight_sem.at[t]).wait()
+        product = across(weights[t, :n_head, :], attended_ref[...], 0, 0)
+        product = product + across(weights[t, n_head:, :], active_ref[...], 0, 0)
+        for q in range(places):
+            first = product[2 * q * piece : (2 * q + 1) * piece]
+            second = product[(2 * q + 1) * piece : (2 * q + 2) * piece]
+            rows = slice(q * piece, (q + 1) * piece)
+            target[0, rows, :] = jnp.where(way == 0, second, first).astype(kind)
+            target[1, rows, :] = jnp.where(way == 0, first, second).astype(kind)
+        for copy in turned_copies(t):
+            copy.start()
+
+    def core_copy(stage, half):
+        return remote(
+            core_out.at[stage, half],
+            core_in.at[stage, half],
+            core_send,
+            core_recv.at[stage, half],
+            core_peer,
+        )
+
+    def outer_copy(half):
+        return remote(
+            outer_out.at[half], outer_in.at[half], outer_send, outer_recv.at[half], outer_peer
+        )
+
+    halves(0, core_out.at[0], low)
+    for half in range(2):
+        core_copy(0, half).start()
+    halves(1, passing, full)
+    for half in range(2):
+        core_copy(0, half).wait_recv()
+        outer_out[half] = (passing[half] + core_in[0, half].astype(full)).astype(low)
+        outer_copy(half).start()
+    halves(2, core_out.at[1], low)
+    for half in range(2):
+        core_copy(1, half).start()
+    halves(3, kept, full)
+    for half in range(2):
+        core_copy(1, half).wait_recv()
+        kept[half] = kept[half] + core_in[1, half].astype(full)
+    kept[1] = kept[1] + residual_ref[...]
+    side = remote(side_out, side_in, side_send, side_recv, partner)
+    outer_copy(0).wait_recv()
+    side_out[...] = (kept[0] + outer_in[0].astype(full)).astype(low)
+    side.start()
+    outer_copy(1).wait_recv()
+    kept[1] = kept[1] + outer_in[1].astype(full)
+    side.wait_recv()
+    output = kept[1] + side_in[...].astype(full)
+    output_ref[...] = output
+    rounded = output.astype(low)
+    rounded_ref[...] = rounded
+
+    mixed = jnp.dot(mixer_ref[...], rounded, preferred_element_type=full)
+    square = jnp.sum(output * output, axis=0, keepdims=True)
+    row = lax.broadcasted_iota(jnp.int32, mixed.shape, 0)
+    mixed = jnp.where(row == mixed.shape[0] - 1, square, mixed)
+    for b in range(8):
+        parts_out[b] = mixed[:, b * wide : (b + 1) * wide]
+    parts_in[me] = parts_out[me]
+    for i, j in others:
+        slot, device = peer(i, j)
+        remote(parts_out.at[slot], parts_in.at[me], part_send, part_recv, device).start()
+    some = pl.ds(0, len(others))
+
+    def whole(ref, send, recv):
+        return remote(ref.at[some], ref.at[some], send, recv, partner)
+
+    whole(parts_in, part_send, part_recv).wait_recv()
+    total = parts_in[0]
+    for b in range(1, 8):
+        total = total + parts_in[b]
+    totals[me] = total
+    for i, j in others:
+        remote(totals.at[me], totals.at[me], total_send, total_recv, peer(i, j)[1]).start()
+    whole(totals, total_send, total_recv).wait_recv()
+    for b in range(8):
+        sums_ref[:, b * wide : (b + 1) * wide] = totals[b]
+
+    whole(parts_out, part_send, part_recv).wait_send()
+    whole(totals, total_send, total_recv).wait_send()
+    remote(core_out, core_out, core_send, side_recv, partner).wait_send()
+    remote(outer_out, outer_out, outer_send, side_recv, partner).wait_send()
+    side.wait_send()
+    pltpu.make_async_copy(weights, weights, turned_sem).wait()
+
+
+def add_branches(places, attended, active, residual, mixer_rows, w_out, w_down):
+    mine, group = residual.shape
+    n_head, n_units = attended.shape[0], active.shape[0]
+    feats = w_out.shape[0]
+    n_sums = 48
+    table = jnp.zeros((n_sums, mine), low).at[: mixer_rows.shape[1]].set(mixer_rows.T)
+    vmem, dma = pltpu.VMEM, pltpu.SemaphoreType.DMA
+    out_types = [
+        ((mine, group), full),
+        ((mine, group), low),
+        ((n_sums, group), full),
+        ((n_head, w_out.shape[1]), low),
+        ((n_units, w_down.shape[1]), low),
+    ]
+    spaces = [vmem] * 3 + [pl.ANY] * 2
+    block = (2, mine, group)
+    slots = (8, n_sums, group // 8)
+    return pl.pallas_call(
+        functools.partial(branch_kernel, (places, mine // places, group)),
+        out_shape=[jax.ShapeDtypeStruct(*t) for t in out_types],
+        in_specs=[pl.BlockSpec(memory_space=vmem)] * 4 + [pl.BlockSpec(memory_space=pl.ANY)] * 2,
+        out_specs=[pl.BlockSpec(memory_space=m) for m in spaces],
+        scratch_shapes=[
+            vmem((4, n_head + n_units, feats), low),
+            vmem(block, full),
+            vmem(block, full),
+            vmem((2,) + block, low),
+            vmem((2,) + block, low),
+            vmem(block, low),
+            vmem(block, low),
+            vmem(block[1:], low),
+            vmem(block[1:], low),
+            vmem(slots, full),
+            vmem(slots, full),
+            vmem(slots, full),
+            dma((4,)),
+            dma,
+            dma,
+            dma((2, 2)),
+            dma,
+            dma((2,)),
+            dma,
+            dma,
+            dma,
+            dma,
+            dma,
+            dma,
+        ],
+        compiler_params=pltpu.CompilerParams(
+            collective_id=8, has_side_effects=True, vmem_limit_bytes=56 << 20
+        ),
+        cost_estimate=pl.CostEstimate(
+            flops=8 * (n_head + n_units) * feats * group, bytes_accessed=100 << 20, transcendentals=0
+        ),
+    )(attended, active, residual, table, w_out, w_down)
 
 
 def late_kernel(dims, *refs):
@@ -1238,12 +1521,12 @@
     for rows, segments in blocks:
         used = {n for seg in segments for n in (seg[0], seg[2])}
         more = sum(2 * operands[n].size for n in used - held)
-        more += 2 * rows * sum(seg[4] for seg in segments)
+        more += 4 * rows * sum(seg[4] for seg in segments)
         if groups[-1] and size + more > VMEM:
             groups.append([])
             held, size = set(), 0
             more = sum(2 * operands[n].size for n in used)
-            more += 2 * rows * sum(seg[4] for seg in segments)
+            more += 4 * rows * sum(seg[4] for seg in segments)
         groups[-1].append((rows, segments))
         held |= used
         size += more
@@ -1332,6 +1615,53 @@
             flops=0, bytes_accessed=6 * total.size, transcendentals=0
         ),
     )(total)
+
+
+def history_kernel(split_ref, stored_ref, mix_ref, grad_ref, parts_ref):
+    streams = [split_ref[s, 0].astype(full) for s in range(STREAMS)]
+    rows = [None] * (STREAMS * HIST)
+    for j in range(HIST):
+        layer = stored_ref[j].astype(full)
+        total = mix_ref[j : j + 1, :] * streams[0]
+        for s in range(1, STREAMS):
+            total = total + mix_ref[s * HIST + j : s * HIST + j + 1, :] * streams[s]
+        grad_ref[j] = total
+        for s in range(STREAMS):
+            rows[s * HIST + j] = jnp.sum(streams[s] * layer, axis=0, keepdims=True)
+    parts = jnp.concatenate(rows, axis=0)
+    block = parts_ref.shape[2]
+    for b in range(parts_ref.shape[0]):
+        parts_ref[b] = parts[:, b * block : (b + 1) * block]
+
+
+def history_gradients(split, stored, mix_all, block):
+    _, places, piece, group = split.shape
+    n_mix, tokens = mix_all.shape
+    wide = min(512, group)
+    per_place = group // wide
+    return pl.pallas_call(
+        history_kernel,
+        grid=(tokens // wide,),
+        out_shape=[
+            jax.ShapeDtypeStruct((HIST, piece, tokens), full),
+            jax.ShapeDtypeStruct((tokens // block, n_mix, block), full),
+        ],
+        in_specs=[
+            pl.BlockSpec((STREAMS, 1, piece, wide), lambda i: (0, i // per_place, 0, i % per_place)),
+            pl.BlockSpec((HIST, piece, wide), lambda i: (0, 0, i)),
+            pl.BlockSpec((n_mix, wide), lambda i: (0, i)),
+        ],
+        out_specs=[
+            pl.BlockSpec((HIST, piece, wide), lambda i: (0, 0, i)),
+            pl.BlockSpec((wide // block, n_mix, block), lambda i: (i, 0, 0)),
+        ],
+        compiler_params=pltpu.CompilerParams(vmem_limit_bytes=40 << 20),
+        cost_estimate=pl.CostEstimate(
+            flops=4 * STREAMS * HIST * piece * tokens,
+            bytes_accessed=6 * HIST * piece * tokens + 2 * split.size,
+            transcendentals=0,
+        ),
+    )(split, stored, mix_all)
 
 
 def to_owner(values_in):
@@ -1474,9 +1804,19 @@
     n_head = heads * HEAD
     n_units = w_up.shape[1] // dp // ways
     if fused:
-        normed, deviations, shifts, active, slope, products, turned_heads, turned_up = (
-            forward_projections(deviations, moments, norm_gains, w_query, w_key, w_value, w_up)
+        normed, deviations, shifts, active, slope, products, turned_heads, turned_up, upstream = (
+            forward_projections(
+                deviations,
+                moments,
+                norm_gains,
+                w_query,
+                w_key,
+                w_value,
+                w_up,
+                by_place(out_cotangent.T),
+            )
         )
+        upstream = upstream.reshape(mine, group)
         inv_scales = shifts[:, 2 * places]
         own_shifts = shifts[:, : 2 * places].reshape(STREAMS, places, ways, group)
         own_shifts = lax.dynamic_index_in_dim(own_shifts, way, 2, keepdims=False)
@@ -1528,8 +1868,6 @@
         turned_weights = [
             turned(w, ways * n_head, way * n_head, n_head) for w in (w_query, w_key, w_value)
         ] + [turned(w_up, ways * n_units, way * n_units, n_units)]
-    out_rows, down_rows = way_rows(w_out), way_rows(w_down)
-    turned_weights += [turned(out_rows, feats, 0, feats), turned(down_rows, feats, 0, feats)]
 
     def by_row(values_in):
         if rows == 1:
@@ -1566,33 +1904,42 @@
         probs_low = probs.astype(low)
         attended = from_row(batched(v_rows, probs_low, 2, 2).astype(low)).reshape(heads * HEAD, group)
 
-    cotangent, attended = lax.optimization_barrier((out_cotangent, attended))
-    upstream = exchange(by_place(cotangent.T)).reshape(mine, group)
-
-    def make_out(index):
-        start = index * feats
-        left = lax.dynamic_slice_in_dim(out_rows, start, feats, 1)
-        other = lax.dynamic_slice_in_dim(down_rows, start, feats, 1)
-        return contract(left, attended, 0, 0) + contract(other, active, 0, 0)
-
-    branches = scatter_dp(make_out).reshape(places, ways, piece, group)
-    kept = lax.dynamic_index_in_dim(branches, way, 1, keepdims=False)
-    if ways == 2:
-        given = lax.dynamic_index_in_dim(branches, 1 - way, 1, keepdims=False).astype(low)
-        kept = kept + hid_swap(given, 1).astype(full)
-    output = residual + kept.reshape(mine, group)
-    output, upstream, turned_weights = lax.optimization_barrier(
-        (output, upstream, turned_weights)
-    )
+        cotangent, attended = lax.optimization_barrier((out_cotangent, attended))
+        upstream = exchange(by_place(cotangent.T)).reshape(mine, group)
+
+    mixer_rows = own_rows(w_mixer)
+    if fused:
+        output, output_rounded, sums, *turned_ends = add_branches(
+            places, attended, active, residual, mixer_rows, w_out, w_down
+        )
+        sums = jnp.concatenate([sums[: mixer_rows.shape[1]], sums[-1:]], axis=0)
+        turned_weights += turned_ends
+    else:
+        out_rows, down_rows = way_rows(w_out), way_rows(w_down)
+        turned_weights += [turned(out_rows, feats, 0, feats), turned(down_rows, feats, 0, feats)]
+        def make_out(index):
+            start = index * feats
+            left = lax.dynamic_slice_in_dim(out_rows, start, feats, 1)
+            other = lax.dynamic_slice_in_dim(down_rows, start, feats, 1)
+            return contract(left, attended, 0, 0) + contract(other, active, 0, 0)
+
+        branches = scatter_dp(make_out).reshape(places, ways, piece, group)
+        kept = lax.dynamic_index_in_dim(branches, way, 1, keepdims=False)
+        if ways == 2:
+            given = lax.dynamic_index_in_dim(branches, 1 - way, 1, keepdims=False).astype(low)
+            kept = kept + hid_swap(given, 1).astype(full)
+        output = residual + kept.reshape(mine, group)
+        output, upstream, turned_weights = lax.optimization_barrier(
+            (output, upstream, turned_weights)
+        )
+        output_rounded = output.astype(low)
+        square = jnp.sum(output * output, axis=0, keepdims=True)
+        mixer_part = contract(mixer_rows, output_rounded, 0, 0)
+        sums = sum_features(jnp.concatenate([mixer_part, square], axis=0))
     upstream = upstream.astype(full)
-    output_rounded = output.astype(low)
 
     block_output = exchange(output_rounded.reshape(places, piece, group))
 
-    square = jnp.sum(output * output, axis=0, keepdims=True)
-    mixer_rows = own_rows(w_mixer)
-    mixer_part = contract(mixer_rows, output_rounded, 0, 0)
-    sums = sum_features(jnp.concatenate([mixer_part, square], axis=0))
     inv_rms = lax.rsqrt(sums[-1] / width + 1e-06)
     inner_raw = sums[:-1]
     inner_pre = inner_raw * inv_rms
@@ -1644,7 +1991,19 @@
     scaled_grad = contract(mixer_rows, inner_low, 1, 0)
     along = jnp.sum(inner_low.astype(full) * inner_raw, axis=0) / width
     output_grad = upstream + inv_rms * scaled_grad - output * (inv_rms * inv_rms * inv_rms) * along
-    output_lows = gather_turns(all_rows(output_grad.astype(low)))
+    if fused:
+        near = output_grad.astype(low)
+        far = outer_shift(near, 1)
+        beside = hid_swap(near, 1)
+        far_beside = outer_shift(beside, 1)
+
+        def interleave(values_in, other):
+            values_in, other = [v.reshape(places, piece, group) for v in (values_in, other)]
+            return ordered(way == 0, values_in, other, 1).reshape(feats, group)
+
+        output_lows = gather_cores([interleave(near, beside), interleave(far, far_beside)])
+    else:
+        output_lows = gather_turns(all_rows(output_grad.astype(low)))
 
     output_low = jnp.concatenate(output_lows, axis=0)
 
@@ -1688,8 +2047,8 @@
             all_gains.T.reshape(STREAMS, places, 2 * piece, 1),
         ]
         late_sum, split, gain_parts = late_sums(operands, tables, 1)
-        split = split.swapaxes(0, 1)
         gain_parts = gain_parts.reshape(STREAMS, mine)
+        history_grad, mix_parts = history_gradients(split, stored, mix_all, block)
     else:
         hidden_lows, lows = gather_cores(hidden_lows), gather_cores(lows)
 
@@ -1728,26 +2087,33 @@
         blocks += [(feats, [(6 + s, 0, 1 + s, 0, wide)]) for s in range(3)]
         blocks += [(n_head, [(9, 0, 4, i, wide)]) for i in range(0, width, wide)]
         late_sum = chain_sums(operands, blocks, 1).reshape(ways, -1, feats, wide)
-
+        split = jnp.concatenate([split[p] for p in range(places)], axis=-1).astype(full)
+        mix_layers = mix_all.reshape(STREAMS, HIST, total_tokens)
+        history_grad = sum(mix_layers[s][:, None] * split[s][None] for s in range(STREAMS))
+        mix_parts = jnp.concatenate(
+            [jnp.sum(split[s][None] * stored.astype(full), axis=1) for s in range(STREAMS)], axis=0
+        )
+        mix_parts = mix_parts.reshape(n_mix, dp * hid, block).transpose(1, 0, 2)
+
+    history_grad = history_grad.swapaxes(1, 2)
     smalls = jnp.concatenate([mixer_grad_part, gain_parts], axis=0)
-    split = jnp.concatenate([split[p] for p in range(places)], axis=-1).astype(full)
-    mix_layers = mix_all.reshape(STREAMS, HIST, total_tokens)
-    history_grad = sum(mix_layers[s][:, None] * split[s][None] for s in range(STREAMS))
-    history_grad = history_grad.swapaxes(1, 2)
-    mix_parts = jnp.concatenate(
-        [jnp.sum(split[s][None] * stored.astype(full), axis=1) for s in range(STREAMS)], axis=0
-    )
-    mix_parts = mix_parts.reshape(n_mix, dp * hid, block).transpose(1, 0, 2)
-
     late_sum, mix_parts, smalls = lax.optimization_barrier((late_sum, mix_parts, smalls))
-    smalls = sum_tokens(smalls)
+    mix_parts = lax.all_to_all(mix_parts, ("dp", "hid"), split_axis=0, concat_axis=0, tiled=True)
+    late_grads = assemble(late_sum, w_up, fused)
+    w_down_grad = unturn(branch_sum.reshape(w_down.shape))
+    bit = ways
+    while bit < hid:
+        smalls = smalls + hid_swap(smalls, bit)
+        if bit == ways:
+            late_grads, smalls = lax.optimization_barrier((late_grads, smalls))
+        else:
+            w_down_grad, smalls = lax.optimization_barrier((w_down_grad, smalls))
+        bit *= 2
+    w_up_grad, w_query_grad, w_key_grad, w_value_grad, w_out_grad = late_grads
     smalls = gather_ways(smalls.reshape(-1, places, piece), 2).reshape(-1, feats)
     w_mixer_grad = smalls[:n_inner].T
     norm_gains_grad = smalls[n_inner:].T
-    mix_parts = lax.all_to_all(mix_parts, ("dp", "hid"), split_axis=0, concat_axis=0, tiled=True)
     mix_grad = jnp.sum(mix_parts, axis=0).T
-    w_down_grad = unturn(branch_sum.reshape(w_down.shape))
-    w_up_grad, w_query_grad, w_key_grad, w_value_grad, w_out_grad = assemble(late_sum, w_up, fused)
 
     return (
         block_output,

time: 850 us -> 803 us (0.945)
  Pallas kernels: 594 us -> 649 us
  waiting for transfers between devices: 68 us -> 40 us
  matrix products: 40.4 us -> 13.5 us
  other arithmetic: 44.8 us -> 23.9 us
  local copies, waits for them, and re-layouts: 46.9 us -> 31.6 us
  starting transfers between devices: 47.8 us -> 37 us
    pallas_call x0 -> x2, Pallas kernels: none -> 49.4 us  [the longest x1 43.3 us: add_branches(): pl.pallas_call(functools.partial(branch_kernel, (places, mine // places,...]
    dot_general x13 -> x4, matrix products: 36.2 us -> 11 us  [contract(): lax.dot_general(left, right, (((left_dim,), (right_dim,)), ((), ())), pre...]
    ppermute x5 -> x4, waiting for transfers between devices: 31.7 us -> 10.7 us  [outer_shift(): return lax.ppermute(values_in, 'dp', pairs)]
    ppermute x8 -> x6, waiting for transfers between devices: 29.4 us -> 17.7 us  [hid_swap(): return lax.ppermute(values_in, 'hid', [(i, i ^ bit) for i in range(size)])]
    pallas_call x1, Pallas kernels: 5.83 us -> 17.4 us  [attend_back(): pl.pallas_call(attend_back_kernel, grid=(n_heads,), out_shape=jax.ShapeDt...]
  transfers between devices with their start and end apart: 24 -> 17, of which waited for: 11 -> 8; matrix products, arithmetic and copies ran while one was open for 10% -> 5% of each run, Pallas kernels for 34% -> 35%
where the time goes in v6:
time: 803 us; the launch traced here: 797 us
  Pallas kernels  649 us (81%)
  waiting for transfers between devices  40 us (5%)
  starting transfers between devices  37 us (5%)
  local copies, waits for them, and re-layouts  31.6 us (4%)
  other arithmetic  23.9 us (3%)
  matrix products  13.5 us (2%)
    pallas_call x1, Pallas kernels, late_sums(): pl.pallas_call(functools.partial(late_kernel, (places, piece, group, n_he...  299 us
    pallas_call x1, Pallas kernels, forward_projections(): pl.pallas_call(functools.partial(forward_kernel, (places, piece, group, n...  130 us
    pallas_call x1, Pallas kernels, chain_sum(): pl.pallas_call(functools.partial(chain_kernel, ways, size // ways, blocks...  119 us
    pallas_call x1, Pallas kernels, add_branches(): pl.pallas_call(functools.partial(branch_kernel, (places, mine // places,...  43.3 us
    pallas_call x1, Pallas kernels, assemble(): pl.pallas_call(functools.partial(assemble_kernel, ways, dp, int(fused)),...  18.7 us
    ppermute x6, waiting for transfers between devices, hid_swap(): return lax.ppermute(values_in, 'hid', [(i, i ^ bit) for i in range(size)])  17.7 us
    pallas_call x1, Pallas kernels, attend_back(): pl.pallas_call(attend_back_kernel, grid=(n_heads,), out_shape=jax.ShapeDt...  17.4 us
  transfers between devices with their start and end apart: 17, of which 8 were waited for; matrix products, arithmetic and copies ran while one was open for 5% of the time, Pallas kernels for 35%

profile of v6, /device:TPU:0, one launch (start us, length us, event | category | flops | bytes accessed | tf_op | source)
XLA Modules:
  0.0 796.7 jit_solution(17192919802837143911)
XLA Ops:
  2.2 7.3 all-to-all-start
  16.9 9.0 %all-to-all-done = f32[32,32,128]{2,1,0:T(8,128)S(1)} async-done(((f32[32,32,128]{2,1,0:T(8,128)}), f32[32,32,128]{2,1,0:T(8,128)S(1)}, u32[]{:S(2)}, u32[]{:S(2)}) %all-to-all-start) | async-done | bytes 524320 | tf_op jit(solution)/shard_map/all_to_all | solution.py:165
  26.8 3.3 all-to-all-start.1
  30.6 3.3 fusion.134
  43.8 130.2 %shard_map.254 = (bf16[4,512,1024]{2,1,0:T(8,128)(2,1)}, bf16[4,4,64,1024]{3,2,1,0:T(8,128)(2,1)}, f32[4,16,1024]{2,1,0:T(8,128)}, bf16[1024,1024]{1,0:T(8,128)(...) custom-call(bf16[4,4,64,1024]{3,2,1,0:T(8,128)(2,1)} %pad_maximum_fu, ...), custom_call_target="tpu_custom_call" | custom-call | flops 7516192768 | bytes 314572800 | tf_op jit(solution)/shard_map/pallas_call | solution.py:642
  181.2 4.8 shard_map.255
  187.9 43.3 %shard_map.256 = (f32[256,1024]{1,0:T(8,128)}, bf16[256,1024]{1,0:T(8,128)(2,1)}, f32[48,1024]{1,0:T(8,128)}, bf16[256,2048]{1,0:T(8,128)(2,1)}, bf16[1024,2048]{1,0:T(8,128)(2,1)}) custom-call(bf16[256,1024]{1,0:T(8,128)(2,1)} %bitcast.430, bf16[1024,1024]{1,0:T(8,128)(2,1)} %get-tuple-element.86.refs_1_.refs_0_, f32[256,1024]{1,0:T(8,128)} %convert_add_fusion.refs_2_, ...), custom_call_target="tpu_custom_call" | custom-call | flops 5368709120 | bytes 104857600 | tf_op jit(solution)/shard_map/pallas_call | solution.py:1139
  235.0 8.5 %collective-permute-start = (f32[2772]{0:T(1024)S(1)}, f32[2772]{0:T(1024)S(1)}, u32[]{:S(2)}, u32[]{:S(2)}) collective-permute-start(f32[2772]{0:T(1024)S(1)} %concatenate.15), channel_id=1, source_target_pairs={{0,2},{1,3},{2,0},{3,1},{4,6},{5,7},{6,4},{7,5},{8,10},{9,11},{10,... | collective-permute-start | bytes 33272 | tf_op jit(solution)/shard_map/ppermute | solution.py:75
  245.2 4.6 collective-permute-done.1
  251.4 2.6 fusion.142
  256.0 9.9 %collective-permute-done.2 = bf16[256,1024]{1,0:T(8,128)(2,1)S(1)} collective-permute-done((bf16[256,1024]{1,0:T(8,128)(2,1)S(1)}, bf16[256,1024]{1,0:T(8,128)(2,1)S(1)}, u32[]{:S(2)}, u32[]{:S(2)}) %collective-permute-start.2) | collective-permute-done | bytes 524320 | tf_op jit(solution)/shard_map/ppermute | solution.py:75
  268.3 10.0 %collective-permute-done.5 = bf16[256,1024]{1,0:T(8,128)(2,1)S(1)} collective-permute-done((bf16[256,1024]{1,0:T(8,128)(2,1)S(1)}, bf16[256,1024]{1,0:T(8,128)(2,1)S(1)}, u32[]{:S(2)}, u32[]{:S(2)}) %collective-permute-start.5) | collective-permute-done | bytes 524320 | tf_op jit(solution)/shard_map/ppermute | solution.py:70
  278.6 2.6 collective-permute-done.6
  286.2 5.7 multiply_convert_fusion.refs_0_
  291.9 17.4 %shard_map.257 = bf16[3,2,128,1024]{3,2,1,0:T(8,128)(2,1)S(1)} custom-call(bf16[3,2,128,1024]{3,2,1,0:T(8,128)(2,1)S(1)} %copy-done.9, bf16[2,128,1024]{2,1,0:T(8,128)(2,1)S(1)} %bitcast.432, f32[16,1024]{1,0:T(8,128)S(1)} %get-tuple-element.197.cosine_ref, f32[16,1024]{1,0:T(8,128)S(1)} %get-tuple-element.196.sine_ref, s32[1,1024]{1,0:T(1,128)S(1)} %bitcast.426, ...), custom_call_target="tpu_custom_call" | custom-call | flops 2684354560 | bytes 4718592 | tf_op jit(solution)/shard_map/pallas_call | solution.py:297
  316.9 3.5 all-to-all-start.2
  322.0 119.3 %shard_map.258 = bf16[2,64,16,2048]{3,2,1,0:T(8,128)(2,1)} custom-call(bf16[1024,1024]{1,0:T(8,128)(2,1)} %get-tuple-element.86.refs_1_.refs_0_, bf16[2048,1024]{1,0:T(8,128)(2,1)} %copy-done.12), custom_call_target="tpu_custom_call" | custom-call | flops 4294967296 | bytes 629145600 | tf_op jit(solution)/shard_map/pallas_call | solution.py:940
  442.1 298.9 %shard_map.259 = (bf16[2,128,32,1024]{3,2,1,0:T(8,128)(2,1)}, bf16[4,4,64,1024]{3,2,1,0:T(8,128)(2,1)}, f32[4,4,64,1]{3,2,1,0:T(8,128)}) custom-call(bf16[1024,1024]{1,0:T(8,128)(2,1)} %multiply_convert_fusion.refs_0_, bf16[1024,1024]{1,0:T(8,128)(2,1)} %collective-permute-done.7.refs_1_, bf16[768,1024]{1,0:T(8,128)(2,1)} %bitcast.428, ...), custom_call_target="tpu_custom_call" | custom-call | flops 17179869184 | bytes 943718400 | tf_op jit(solution)/shard_map/pallas_call | solution.py:1474
  742.4 2.2 copy-done.3
  746.2 6.2 shard_map.260
  752.4 3.8 all-to-all-start.3
  756.3 18.7 %shard_map.262 = (f32[512,8192]{1,0:T(8,128)}, f32[512,2048]{1,0:T(8,128)}, f32[512,2048]{1,0:T(8,128)}, f32[512,2048]{1,0:T(8,128)}, f32[512,2048]{1,0:T(8,128)}) custom-call(bf16[2,8,512,1024]{3,2,1,0:T(8,128)(2,1)} %bitcast.433, bf16[2,8,512,1024]{3,2,1,0:T(8,128)(2,1)} %bitcast.434, bf16[2,8,512,1024]{3,2,1,0:T(8,128)(2,1)} %bitcast.435), custom_call_target="tpu_custom_call" | custom-call | bytes 50331648 | tf_op jit(solution)/shard_map/pallas_call | solution.py:1584
  775.0 2.7 collective-permute-start.11
  778.6 10.3 %shard_map.261 = f32[2048,2048]{1,0:T(8,128)} custom-call(bf16[2048,2048]{1,0:T(8,128)(2,1)} %bitcast.436), custom_call_target="tpu_custom_call" | custom-call | bytes 25165824 | tf_op jit(solution)/shard_map/pallas_call | solution.py:1608
  (179 shorter events, 67.0 us)
Async XLA Ops:
  0.6 233.0 %copy-start = (f32[36,36]{1,0:T(8,128)S(1)}, f32[36,36]{1,0:T(8,128)}, u32[]{:S(2)}) copy-start(f32[36,36]{1,0:T(8,128)} %param.28) | copy-start | bytes 15556
  2.2 23.7 %all-to-all-start = ((f32[32,32,128]{2,1,0:T(8,128)}), f32[32,32,128]{2,1,0:T(8,128)S(1)}, u32[]{:S(2)}, u32[]{:S(2)}) async-start(f32[32,32,128]{2,1,0:T(8,128)} %broadcast_in_dim.18), calls=%async_computation | async-start | bytes 1048576 | tf_op jit(solution)/shard_map/all_to_all | solution.py:165
  26.8 151.5 %all-to-all-start.1 = ((f32[32,37,128]{2,1,0:T(8,128)}), f32[32,37,128]{2,1,0:T(8,128)}, u32[]{:S(2)}, u32[]{:S(2)}) async-start(f32[32,37,128]{2,1,0:T(8,128)} %broadcast_in_dim.26), calls=%async_computation.1 | async-start | bytes 1310720 | tf_op jit(solution)/shard_map/all_to_all | solution.py:165
  180.0 53.7 %copy-start.15 = (f32[5,8,32,128]{3,1,2,0:T(8,128)}, f32[5,8,32,128]{3,1,2,0:T(8,128)S(1)}, u32[]{:S(2)}) copy-start(f32[5,8,32,128]{3,1,2,0:T(8,128)S(1)} %copy.79) | copy-start | bytes 1966084
  187.9 63.5 %copy-start.16 = (bf16[4,64,1024]{2,1,0:T(8,128)(2,1)S(1)}, bf16[4,64,1024]{2,1,0:T(8,128)(2,1)}, u32[]{:S(2)}) copy-start(bf16[4,64,1024]{2,1,0:T(8,128)(2,1)} %get-tuple-element.79) | copy-start | bytes 1572868
  235.0 10.2 %collective-permute-start = (f32[2772]{0:T(1024)S(1)}, f32[2772]{0:T(1024)S(1)}, u32[]{:S(2)}, u32[]{:S(2)}) collective-permute-start(f32[2772]{0:T(1024)S(1)} %concatenate.15), channel_id=1, source_target_pairs={{0,2},{1,3},{2,0},{3,1},{4,6},{5,7},{6,4},{7,5},{8,10},{9,11},{10,... | collective-permute-start | bytes 33272 | tf_op jit(solution)/shard_map/ppermute | solution.py:75
  245.2 4.6 collective-permute-start.1
  254.0 11.9 %collective-permute-start.2 = (bf16[256,1024]{1,0:T(8,128)(2,1)S(1)}, bf16[256,1024]{1,0:T(8,128)(2,1)S(1)}, u32[]{:S(2)}, u32[]{:S(2)}) collective-permute-start(bf16[256,1024]{1,0:T(8,128)(2,1)S(1)} %get-tuple-element.203), channel_id=1, source_target_pairs={{0,1},{1,0},{2,3},{3,2},{4,5},{5,4},{6,7},{7,6},{8,9},{9,8},{10,11... | collective-permute-start | bytes 1572872 | tf_op jit(solution)/shard_map/ppermute | solution.py:75
  255.4 12.9 %collective-permute-start.4 = (bf16[256,1024]{1,0:T(8,128)(2,1)S(1)}, bf16[256,1024]{1,0:T(8,128)(2,1)S(1)}, u32[]{:S(2)}, u32[]{:S(2)}) collective-permute-start(bf16[256,1024]{1,0:T(8,128)(2,1)S(1)} %get-tuple-element.203), channel_id=1, source_target_pairs={{0,16},{8,24},{16,0},{24,8},{1,17},{9,25},{17,1},{25,9},{2,18},{10... | collective-permute-start | bytes 1572872 | tf_op jit(solution)/shard_map/ppermute | solution.py:70
  265.9 12.3 %collective-permute-start.5 = (bf16[256,1024]{1,0:T(8,128)(2,1)S(1)}, bf16[256,1024]{1,0:T(8,128)(2,1)S(1)}, u32[]{:S(2)}, u32[]{:S(2)}) collective-permute-start(bf16[256,1024]{1,0:T(8,128)(2,1)S(1)} %collective-permute-done.2), channel_id=1, source_target_pairs={{0,16},{8,24},{16,0},{24,8},{1,17},{9,25},{17,1},{25,9},{2,18},{10... | collective-permute-start | bytes 1572872 | tf_op jit(solution)/shard_map/ppermute | solution.py:70
  267.5 11.0 %collective-permute-start.3 = (bf16[512,1024]{1,0:T(8,128)(2,1)S(1)}, bf16[512,1024]{1,0:T(8,128)(2,1)S(1)}, u32[]{:S(2)}, u32[]{:S(2)}) collective-permute-start(bf16[512,1024]{1,0:T(8,128)(2,1)S(1)} %bitcast.439), channel_id=1, source_target_pairs={{0,8},{8,0},{16,24},{24,16},{1,9},{9,1},{17,25},{25,17},{2,10},{10... | collective-permute-start | bytes 3145736 | tf_op jit(solution)/shard_map/ppermute | solution.py:61
  278.5 2.7 collective-permute-start.6
  291.8 22.8 %copy-start.18 = (f32[4,4,2,1024]{3,2,1,0:T(2,128)S(1)}, f32[4,4,2,1024]{3,2,1,0:T(2,128)}, u32[]{:S(2)}) copy-start(f32[4,4,2,1024]{3,2,1,0:T(2,128)} %copy-done.17) | copy-start | bytes 393220
  291.9 25.0 %copy-start.11 = (f32[32,32,128]{2,1,0:T(8,128)S(1)}, f32[32,32,128]{2,1,0:T(8,128)}, u32[]{:S(2)}) copy-start(f32[32,32,128]{2,1,0:T(8,128)} %copy-done.10) | copy-start | bytes 1572868
  291.9 28.5 %copy-start.20 = (f32[36]{0:T(128)S(1)}, f32[36]{0:T(128)}, u32[]{:S(2)}) copy-start(f32[36]{0:T(128)} %param.29) | copy-start | bytes 436
  309.3 132.0 %copy-start.5 = (bf16[3,2,128,1024]{3,2,1,0:T(8,128)(2,1)}, bf16[3,2,128,1024]{3,2,1,0:T(8,128)(2,1)S(1)}, u32[]{:S(2)}) copy-start(bf16[3,2,128,1024]{3,2,1,0:T(8,128)(2,1)S(1)} %shard_map.257) | copy-start | bytes 4718596
  309.3 132.8 %collective-permute-start.7 = (bf16[1024,1024]{1,0:T(8,128)(2,1)}, bf16[1024,1024]{1,0:T(8,128)(2,1)}, u32[]{:S(2)}, u32[]{:S(2)}) collective-permute-start(bf16[1024,1024]{1,0:T(8,128)(2,1)} %multiply_convert_fusion.refs_0_), channel_id=1, source_target_pairs={{0,16},{8,24},{16,0},{24,8},{1,17},{9,25},{17,1},{25,9},{2,18},{10... | collective-permute-start | bytes 6291464 | tf_op jit(solution)/shard_map/ppermute | solution.py:70
  315.4 125.9 %collective-permute-start.8 = (bf16[768,1024]{1,0:T(8,128)(2,1)S(1)}, bf16[768,1024]{1,0:T(8,128)(2,1)}, u32[]{:S(2)}, u32[]{:S(2)}) collective-permute-start(bf16[768,1024]{1,0:T(8,128)(2,1)S(1)} %bitcast.427), channel_id=1, source_target_pairs={{0,16},{8,24},{16,0},{24,8},{1,17},{9,25},{17,1},{25,9},{2,18},{10... | collective-permute-start | bytes 4718600 | tf_op jit(solution)/shard_map/ppermute | solution.py:70
  316.9 124.4 %all-to-all-start.2 = ((bf16[4,64,1024]{2,1,0:T(8,128)(2,1)}), bf16[4,64,1024]{2,1,0:T(8,128)(2,1)S(1)}, u32[]{:S(2)}, u32[]{:S(2)}) async-start(bf16[4,64,1024]{2,1,0:T(8,128)(2,1)} %bitcast.458), calls=%async_computation.2 | async-start | bytes 1048576 | tf_op jit(solution)/shard_map/all_to_all | solution.py:190
  752.4 22.6 %collective-permute-start.10 = (f32[40,256]{1,0:T(8,128)S(1)}, f32[40,256]{1,0:T(8,128)S(1)}, u32[]{:S(2)}, u32[]{:S(2)}) collective-permute-start(f32[40,256]{1,0:T(8,128)S(1)} %pad_maximum_fusion.8), channel_id=1, source_target_pairs={{0,2},{1,3},{2,0},{3,1},{4,6},{5,7},{6,4},{7,5},{8,10},{9,11},{10,... | collective-permute-start | bytes 122888 | tf_op jit(solution)/shard_map/ppermute | solution.py:75
  752.4 42.9 %all-to-all-start.3 = ((f32[32,32,128]{2,1,0:T(8,128)}), f32[32,32,128]{2,1,0:T(8,128)S(1)}, u32[]{:S(2)}, u32[]{:S(2)}) async-start(f32[32,32,128]{2,1,0:T(8,128)} %get-tuple-element.103), calls=%async_computation.3 | async-start | bytes 1048576 | tf_op jit(solution)/shard_map/all_to_all | solution.py:2101
  775.0 14.0 %collective-permute-start.11 = (f32[40,256]{1,0:T(8,128)S(1)}, f32[40,256]{1,0:T(8,128)S(1)}, u32[]{:S(2)}, u32[]{:S(2)}) collective-permute-start(f32[40,256]{1,0:T(8,128)S(1)} %add.335), channel_id=1, source_target_pairs={{0,4},{1,5},{2,6},{3,7},{4,0},{5,1},{6,2},{7,3},{8,12},{9,13},{10,... | collective-permute-start | bytes 122888 | tf_op jit(solution)/shard_map/ppermute | solution.py:75
  778.0 13.4 %collective-permute-start.9 = (f32[36,128]{1,0:T(8,128)S(1)}, f32[36,128]{1,0:T(8,128)S(1)}, u32[]{:S(2)}, u32[]{:S(2)}) collective-permute-start(f32[36,128]{1,0:T(8,128)S(1)} %bitcast.540), channel_id=1, source_target_pairs={{0,0},{1,1},{2,8},{3,9},{4,16},{5,17},{6,24},{7,25},{8,2},{9,3},{1... | collective-permute-start | bytes 55304 | tf_op jit(solution)/shard_map/ppermute | solution.py:1677
  789.1 4.5 collective-permute-start.12
  (18 other events, 124.1 us)

commit v7 on v6

--- a/solution.py
+++ b/solution.py
@@ -18,11 +18,13 @@
 SLACK = 6
 TILE = 128
 LATE_TILE = 256
+LATE_CHUNK = 1 << 16
+LATE_SLACK = 4
 SPAN = 256
 VMEM = 52 << 20
-PULL_START = 4
-PULL_GAP = 8
-GRAD_GAP = 5
+PULL_START = 2
+PULL_GAP = 4
+GRAD_GAP = 2
 
 highest = lax.Precision.HIGHEST
 rope_base = 10000.0
@@ -152,11 +154,14 @@
 
 def sum_tokens(values_in):
     size = lax.axis_size("hid")
-    bit = split_ways()
-    while bit < size:
-        values_in = values_in + hid_swap(values_in, bit)
-        bit *= 2
-    return values_in
+    ways = split_ways()
+    places = size // ways
+    mine = lax.axis_index("hid") // ways
+    held = put(jnp.zeros((places,) + values_in.shape, values_in.dtype), values_in, mine)
+    for step in range(1, places):
+        pairs = [(i, (i + step * ways) % size) for i in range(size)]
+        held = put(held, lax.ppermute(values_in, "hid", pairs), (mine + places - step) % places)
+    return jnp.sum(held, axis=0)
 
 
 def gather_all(values_in):
@@ -324,16 +329,19 @@
     (
         normed_ref,
         own_ref,
-        shift_ref,
+        residual_ref,
+        own_shift_ref,
+        scale_ref,
         active_ref,
         slope_ref,
         heads_ref,
         turned_ref,
         turned_up_ref,
         cot_out,
-    ), refs = refs[:9], refs[9:]
+    ), refs = refs[:11], refs[11:]
     (
         devs,
+        shift_ref,
         moms,
         joins,
         weights,
@@ -484,7 +492,10 @@
                 off = moms[w, q, s : s + 1, :] - mean[s : s + 1]
                 shift_ref[s, 2 * q + w : 2 * q + w + 1, :] = off * scale[s : s + 1]
         shift_ref[s, 2 * places : 2 * places + 1, :] = scale[s : s + 1]
-        shift_ref[s, 2 * places + 1 : 2 * places + 2, :] = mean[s : s + 1]
+        scale_ref[s] = scale[s : s + 1]
+        for q in range(places):
+            first, second = [shift_ref[s, 2 * q + w : 2 * q + w + 1, :] for w in range(2)]
+            own_shift_ref[s, q] = jnp.where(way == 0, first, second)
 
     def normalize(s):
         remote(devs.at[s, 1 - way], devs.at[s, 1 - way], way_send, way_recv.at[s], partner).wait_recv()
@@ -576,6 +587,9 @@
         copy.start()
     for s in range(STREAMS):
         own_ref[s] = devs[s, way]
+    for q in range(places):
+        offset = moms[way, q, 3:4, :]
+        residual_ref[q * piece : (q + 1) * piece, :] = devs[3, way, q].astype(full) + offset
 
     step = 32
 
@@ -630,7 +644,9 @@
     out_types = [
         ((STREAMS, feats, group), low),
         ((STREAMS, places, piece, group), low),
-        ((STREAMS, 2 * places + 8, group), full),
+        ((places * piece, group), full),
+        ((STREAMS, places, 1, group), full),
+        ((STREAMS, 1, group), full),
         ((n_units, group), low),
         ((n_units, group), full),
         ((3, n_head, group), full),
@@ -638,7 +654,7 @@
         ((feats, 4 * n_units), low),
         (cotangent.shape, low),
     ]
-    spaces = [vmem] * 6 + [pl.ANY] * 3
+    spaces = [vmem] * 8 + [pl.ANY] * 3
     return pl.pallas_call(
         functools.partial(forward_kernel, (places, piece, group, n_head, n_units)),
         out_shape=[jax.ShapeDtypeStruct(*t) for t in out_types],
@@ -646,6 +662,7 @@
         out_specs=[pl.BlockSpec(memory_space=m) for m in spaces],
         scratch_shapes=[
             vmem((STREAMS, 2, places, piece, group), low),
+            vmem((STREAMS, 2 * places + 8, group), full),
             vmem((2, places, 2 * STREAMS, group), full),
             vmem((8, 2 * STREAMS, group), full),
             vmem((count, 4, feats, n_head), low),
@@ -733,7 +750,7 @@
     return [dma, dma((count,)), dma, dma((count,)), dma, dma, dma, dma, dma((count,))]
 
 
-def chain_loop(ways, places, out_ref, own, landed, semaphores, compute, hook=None, far=None):
+def chain_loop(ways, places, out_ref, own, landed, semaphores, compute, slack, hook=None, far=None):
     (
         up_send,
         up_recv,
@@ -828,7 +845,7 @@
         send_out(done, i)
 
     away = root - place if far is None else jnp.where(place < root, root - place, place - root)
-    lag = SLACK * away + 2
+    lag = slack * away + 2
 
     def step(i, carry):
         @pl.when(i < count)
@@ -845,7 +862,7 @@
             hook(i)
         return carry
 
-    lax.fori_loop(0, count + SLACK * root + 2, step, 0)
+    lax.fori_loop(0, count + slack * root + 2, step, 0)
 
     def sent(sem):
         remote(landed, landed, sem, side_recv, beside).wait_send()
@@ -927,7 +944,7 @@
                     )
                     column += size
 
-    chain_loop(ways, places, out_ref, own, landed, semaphores, compute, far=far)
+    chain_loop(ways, places, out_ref, own, landed, semaphores, compute, SLACK, far=far)
 
 
 def chain_sum(operands, blocks, collective_id):
@@ -967,8 +984,7 @@
     (output_ref, rounded_ref, sums_ref, turned_out_ref, turned_down_ref), refs = refs[:5], refs[5:]
     (
         weights,
-        passing,
-        kept,
+        sums,
         core_out,
         core_in,
         outer_out,
@@ -1017,7 +1033,7 @@
             )
 
     def turned_copies(t):
-        columns = slice((3 - t) * feats, (4 - t) * feats)
+        columns = pl.ds(pl.multiple_of((3 - t) * feats, feats), feats)
         for ref, first, size in ((turned_out_ref, 0, n_head), (turned_down_ref, n_head, n_units)):
             yield pltpu.make_async_copy(
                 weights.at[t, first : first + size], ref.at[:, columns], turned_sem
@@ -1057,21 +1073,24 @@
             outer_out.at[half], outer_in.at[half], outer_send, outer_recv.at[half], outer_peer
         )
 
-    halves(0, core_out.at[0], low)
-    for half in range(2):
-        core_copy(0, half).start()
-    halves(1, passing, full)
-    for half in range(2):
-        core_copy(0, half).wait_recv()
-        outer_out[half] = (passing[half] + core_in[0, half].astype(full)).astype(low)
-        outer_copy(half).start()
-    halves(2, core_out.at[1], low)
-    for half in range(2):
-        core_copy(1, half).start()
-    halves(3, kept, full)
-    for half in range(2):
-        core_copy(1, half).wait_recv()
-        kept[half] = kept[half] + core_in[1, half].astype(full)
+    def stage(k, carry):
+        halves(2 * k, core_out.at[k], low)
+        for half in range(2):
+            core_copy(k, half).start()
+        halves(2 * k + 1, sums.at[k], full)
+        for half in range(2):
+            core_copy(k, half).wait_recv()
+            sums[k, half] = sums[k, half] + core_in[k, half].astype(full)
+
+            @pl.when(k == 0)
+            def _(half=half):
+                outer_out[half] = sums[0, half].astype(low)
+                outer_copy(half).start()
+
+        return carry
+
+    lax.fori_loop(0, 2, stage, 0)
+    kept = sums.at[1]
     kept[1] = kept[1] + residual_ref[...]
     side = remote(side_out, side_in, side_send, side_recv, partner)
     outer_copy(0).wait_recv()
@@ -1143,8 +1162,7 @@
         out_specs=[pl.BlockSpec(memory_space=m) for m in spaces],
         scratch_shapes=[
             vmem((4, n_head + n_units, feats), low),
-            vmem(block, full),
-            vmem(block, full),
+            vmem((2,) + block, full),
             vmem((2,) + block, low),
             vmem((2,) + block, low),
             vmem(block, low),
@@ -1213,6 +1231,7 @@
         joins,
         totals,
         own,
+        pulled,
         landed,
         fetched,
         core_send,
@@ -1344,28 +1363,30 @@
         return remote(given.at[s, r], taken.at[s, r], side_send, side_recv.at[s], partner)
 
     def pull(s):
-        def use(part):
-            for r in range(places):
-                rows = slice(2 * piece * r, 2 * piece * (r + 1))
-                here = part[rows]
-                totals[s, 0:1, :] = totals[s, 0:1, :] + jnp.sum(
-                    here * all_gains[s, r], axis=0, keepdims=True
-                )
-                totals[s, 1:2, :] = totals[s, 1:2, :] + jnp.sum(
-                    here * normed[s, rows, :].astype(full), axis=0, keepdims=True
-                )
-                first = way == 0
-                kept[s, r] = jnp.where(first, here[:piece], here[piece:])
-                given[s, r] = jnp.where(first, here[piece:], here[:piece]).astype(low)
-                side_copy(s, r).start()
-
         @pl.when(s < 3)
         def _():
-            use(jnp.dot(turned[s], lows[s], preferred_element_type=full))
+            pulled[...] = jnp.dot(turned[s], lows[s], preferred_element_type=full)
 
         @pl.when(s == 3)
         def _():
-            use(jnp.dot(turned_up[...], hidden[...], preferred_element_type=full))
+            pulled[...] = jnp.dot(turned_up[...], hidden[...], preferred_element_type=full)
+
+        def use(r, carry):
+            rows = pl.ds(pl.multiple_of(2 * piece * r, 2 * piece), 2 * piece)
+            here = pulled[rows, :]
+            totals[s, 0:1, :] = totals[s, 0:1, :] + jnp.sum(
+                here * all_gains[s, r], axis=0, keepdims=True
+            )
+            totals[s, 1:2, :] = totals[s, 1:2, :] + jnp.sum(
+                here * normed[s, rows, :].astype(full), axis=0, keepdims=True
+            )
+            first = way == 0
+            kept[s, r] = jnp.where(first, here[:piece], here[piece:])
+            given[s, r] = jnp.where(first, here[piece:], here[:piece]).astype(low)
+            side_copy(s, r).start()
+            return carry
+
+        lax.fori_loop(0, places, use, 0)
 
     def share_totals():
         joins[me] = totals[...]
@@ -1437,7 +1458,7 @@
         def _():
             stream_grad(n // places, n % places)
 
-    chain_loop(2, places, out_ref, own, landed, semaphores, compute, hook)
+    chain_loop(2, places, out_ref, own, landed, semaphores, compute, LATE_SLACK, hook)
 
     def sent(ref, sem):
         remote(ref, ref, sem, join_recv, partner).wait_send()
@@ -1461,7 +1482,7 @@
     n_units, n_head = hidden.shape[0], attended.shape[0]
     wide = n_units
     rows = 8 * feats
-    depth = max(16, CHUNK // wide)
+    depth = max(16, LATE_CHUNK // wide)
     count = rows // depth
     vmem, dma = pltpu.VMEM, pltpu.SemaphoreType.DMA
     block = (STREAMS, places, piece, group)
@@ -1493,6 +1514,7 @@
             vmem((8, STREAMS, 2, group), full),
             vmem((STREAMS, 2, group), full),
             vmem((LATE_TILE, wide), full),
+            vmem((feats, group), full),
             vmem((count, depth, wide), low),
             dma((3, 11)),
             dma((4,)),
@@ -1731,6 +1753,14 @@
 
     stored = history.swapaxes(1, 2)
     mix_all = gather_all(mix.T)
+    fused = dp == 4 and ways == 2 and rows == 1
+    if fused:
+        parts = norm_gains.astype(full).T.reshape(STREAMS, places, ways, piece)
+        gain_tables = (
+            lax.dynamic_index_in_dim(parts, way, 2, keepdims=False)[..., None],
+            parts.reshape(STREAMS, places, ways * piece, 1),
+        )
+        mix_all, gain_tables = lax.optimization_barrier((mix_all, gain_tables))
     own_means, own_devs, deviations = [], [], []
     for s in range(STREAMS):
         total = mix_all[s * HIST] * stored[0].astype(full)
@@ -1742,7 +1772,6 @@
         deviations.append(off.astype(low))
     moments = by_place(jnp.stack(own_means + own_devs, axis=0))
     deviations = by_place(jnp.stack(deviations, axis=0))
-    fused = dp == 4 and ways == 2 and rows == 1
 
     table = jnp.concatenate([mix_cotangent.T, segment_ids.astype(full)[None]], axis=0)
     table = lax.dynamic_slice_in_dim(gather_all(table), place * group, group, 1)
@@ -1804,7 +1833,7 @@
     n_head = heads * HEAD
     n_units = w_up.shape[1] // dp // ways
     if fused:
-        normed, deviations, shifts, active, slope, products, turned_heads, turned_up, upstream = (
+        normed, deviations, residual, own_shifts, inv_scales, active, slope, products, *ends = (
             forward_projections(
                 deviations,
                 moments,
@@ -1816,16 +1845,8 @@
                 by_place(out_cotangent.T),
             )
         )
+        turned_heads, turned_up, upstream = ends
         upstream = upstream.reshape(mine, group)
-        inv_scales = shifts[:, 2 * places]
-        own_shifts = shifts[:, : 2 * places].reshape(STREAMS, places, ways, group)
-        own_shifts = lax.dynamic_index_in_dim(own_shifts, way, 2, keepdims=False)
-        offset = own_shifts[3] / inv_scales[3] + shifts[3, 2 * places + 1]
-        residual = (deviations[3].astype(full) + offset[:, None]).reshape(mine, group)
-        units = [
-            (deviations[s].astype(full) * inv_scales[s] + own_shifts[s][:, None]).reshape(mine, group)
-            for s in range(STREAMS)
-        ]
         normed_all = normed
         normed = [normed[s] for s in range(STREAMS)]
         products = products.reshape(3, heads, HEAD, group)
@@ -2041,10 +2062,9 @@
         operands += [normed_all, turned_heads, turned_up, deviations]
         operands.append(output_grad.reshape(places, piece, group))
         tables = [
-            own_shifts[:, :, None],
-            inv_scales[:, None],
-            own_gains.T.reshape(STREAMS, places, piece, 1),
-            all_gains.T.reshape(STREAMS, places, 2 * piece, 1),
+            own_shifts,
+            inv_scales,
+            *gain_tables,
         ]
         late_sum, split, gain_parts = late_sums(operands, tables, 1)
         gain_parts = gain_parts.reshape(STREAMS, mine)

time: 803 us -> 784 us (0.976)
  Pallas kernels: 649 us -> 630 us
    pallas_call x1, Pallas kernels: 17.4 us -> 5.82 us  [attend_back(): pl.pallas_call(attend_back_kernel, grid=(n_heads,), out_shape=jax.ShapeDt...]
    ppermute x0 -> x3, starting transfers between devices: none -> 11 us  [sum_tokens(): lax.ppermute(values_in, 'hid', pairs)]
    ppermute x6 -> x4, starting transfers between devices: 14.2 us -> 5.7 us  [hid_swap(): return lax.ppermute(values_in, 'hid', [(i, i ^ bit) for i in range(size)])]
    ppermute x6 -> x4, waiting for transfers between devices: 17.7 us -> 12.1 us  [hid_swap(): return lax.ppermute(values_in, 'hid', [(i, i ^ bit) for i in range(size)])]
  transfers between devices with their start and end apart: 17 -> 18, of which waited for: 8 -> 6; matrix products, arithmetic and copies ran while one was open for 5% -> 4% of each run, Pallas kernels for 35% -> 36%
where the time goes in v7:
time: 784 us; the launch traced here: 773 us
  Pallas kernels  630 us (80%)
  starting transfers between devices  39.2 us (5%)
  waiting for transfers between devices  35 us (4%)
  other arithmetic  27.9 us (4%)
  local copies, waits for them, and re-layouts  27.3 us (3%)
  matrix products  12.3 us (2%)
    pallas_call x1, Pallas kernels, late_sums(): pl.pallas_call(functools.partial(late_kernel, (places, piece, group, n_he...  291 us
    pallas_call x1, Pallas kernels, forward_projections(): pl.pallas_call(functools.partial(forward_kernel, (places, piece, group, n...  130 us
    pallas_call x1, Pallas kernels, chain_sum(): pl.pallas_call(functools.partial(chain_kernel, ways, size // ways, blocks...  119 us
    pallas_call x1, Pallas kernels, add_branches(): pl.pallas_call(functools.partial(branch_kernel, (places, mine // places,...  43.3 us
    pallas_call x1, Pallas kernels, assemble(): pl.pallas_call(functools.partial(assemble_kernel, ways, dp, int(fused)),...  18.7 us
  transfers between devices with their start and end apart: 18, of which 6 were waited for; matrix products, arithmetic and copies ran while one was open for 4% of the time, Pallas kernels for 36%

profile of v7, /device:TPU:0, one launch (start us, length us, event | category | flops | bytes accessed | tf_op | source)
XLA Modules:
  0.0 773.1 jit_solution(15331711551733377662)
XLA Ops:
  2.2 7.3 all-to-all-start
  17.0 8.9 %all-to-all-done = f32[32,32,128]{2,1,0:T(8,128)S(1)} async-done(((f32[32,32,128]{2,1,0:T(8,128)}), f32[32,32,128]{2,1,0:T(8,128)S(1)}, u32[]{:S(2)}, u32[]{:S(2)}) %all-to-all-start) | async-done | bytes 524320 | tf_op jit(solution)/shard_map/all_to_all | solution.py:170
  26.8 2.6 all-to-all-start.1
  29.9 3.3 fusion.129
  45.8 130.5 %shard_map.254 = (bf16[4,512,1024]{2,1,0:T(8,128)(2,1)}, bf16[4,4,64,1024]{3,2,1,0:T(8,128)(2,1)}, f32[256,1024]{1,0:T(8,128)}, f32[4,4,1,1024]{3,2,1,0:T(1,128)...) custom-call(bf16[4,4,64,1024]{3,2,1,0:T(8,128)(2,1)} %pad_maximum_fu, ...), custom_call_target="tpu_custom_call" | custom-call | flops 7516192768 | bytes 314572800 | tf_op jit(solution)/shard_map/pallas_call | solution.py:658
  179.9 4.8 shard_map.255
  186.7 43.3 %shard_map.256 = (f32[256,1024]{1,0:T(8,128)}, bf16[256,1024]{1,0:T(8,128)(2,1)}, f32[48,1024]{1,0:T(8,128)}, bf16[256,2048]{1,0:T(8,128)(2,1)}, bf16[1024,2048]{1,0:T(8,128)(2,1)}) custom-call(bf16[256,1024]{1,0:T(8,128)(2,1)} %bitcast.417, bf16[1024,1024]{1,0:T(8,128)(2,1)} %get-tuple-element.91.refs_1_.refs_0_, f32[256,1024]{1,0:T(8,128)} %get-tuple-element.82.refs_2_, ...), custom_call_target="tpu_custom_call" | custom-call | flops 5368709120 | bytes 104857600 | tf_op jit(solution)/shard_map/pallas_call | solution.py:1158
  233.8 8.6 %collective-permute-start = (f32[2772]{0:T(1024)S(1)}, f32[2772]{0:T(1024)S(1)}, u32[]{:S(2)}, u32[]{:S(2)}) collective-permute-start(f32[2772]{0:T(1024)S(1)} %concatenate.15), channel_id=1, source_target_pairs={{0,2},{1,3},{2,4},{3,5},{4,6},{5,7},{6,0},{7,1},{8,10},{9,11},{10,... | collective-permute-start | bytes 33272 | tf_op jit(solution)/shard_map/ppermute | solution.py:163
  242.4 2.4 collective-permute-start.2
  252.6 10.7 %collective-permute-done.3 = bf16[256,1024]{1,0:T(8,128)(2,1)} collective-permute-done((bf16[256,1024]{1,0:T(8,128)(2,1)S(1)}, bf16[256,1024]{1,0:T(8,128)(2,1)}, u32[]{:S(2)}, u32[]{:S(2)}) %collective-permute-start.3) | collective-permute-done | bytes 524320 | tf_op jit(solution)/shard_map/ppermute | solution.py:77
  266.0 9.6 %collective-permute-done.6 = bf16[256,1024]{1,0:T(8,128)(2,1)} collective-permute-done((bf16[256,1024]{1,0:T(8,128)(2,1)}, bf16[256,1024]{1,0:T(8,128)(2,1)}, u32[]{:S(2)}, u32[]{:S(2)}) %collective-permute-start.6) | collective-permute-done | bytes 524320 | tf_op jit(solution)/shard_map/ppermute | solution.py:72
  277.0 2.6 collective-permute-done.7
  281.5 1.9 copy-done.20
  284.6 5.7 multiply_convert_fusion.refs_0_
  290.3 5.8 shard_map.257
  300.6 4.4 all-to-all-start.2
  306.7 119.1 %shard_map.258 = bf16[2,64,16,2048]{3,2,1,0:T(8,128)(2,1)} custom-call(bf16[1024,1024]{1,0:T(8,128)(2,1)} %get-tuple-element.91.refs_1_.refs_0_, bf16[2048,1024]{1,0:T(8,128)(2,1)} %copy-done.11), custom_call_target="tpu_custom_call" | custom-call | flops 4294967296 | bytes 629145600 | tf_op jit(solution)/shard_map/pallas_call | solution.py:957
  426.6 291.0 %shard_map.259 = (bf16[2,64,64,1024]{3,2,1,0:T(8,128)(2,1)}, bf16[4,4,64,1024]{3,2,1,0:T(8,128)(2,1)}, f32[4,4,64,1]{3,2,1,0:T(8,128)}) custom-call(bf16[1024,1024]{1,0:T(8,128)(2,1)} %multiply_convert_fusion.refs_0_, bf16[1024,1024]{1,0:T(8,128)(2,1)} %collective-permute-done.8.refs_1_, bf16[768,1024]{1,0:T(8,128)(2,1)} %bitcast.415, ...), custom_call_target="tpu_custom_call" | custom-call | flops 17179869184 | bytes 943718400 | tf_op jit(solution)/shard_map/pallas_call | solution.py:1495
  719.0 2.2 copy-done.3
  722.7 6.2 shard_map.260
  729.0 3.3 all-to-all-start.3
  732.4 18.7 %shard_map.262 = (f32[512,8192]{1,0:T(8,128)}, f32[512,2048]{1,0:T(8,128)}, f32[512,2048]{1,0:T(8,128)}, f32[512,2048]{1,0:T(8,128)}, f32[512,2048]{1,0:T(8,128)}) custom-call(bf16[2,8,512,1024]{3,2,1,0:T(8,128)(2,1)} %bitcast.420, bf16[2,8,512,1024]{3,2,1,0:T(8,128)(2,1)} %bitcast.421, bf16[2,8,512,1024]{3,2,1,0:T(8,128)(2,1)} %bitcast.422), custom_call_target="tpu_custom_call" | custom-call | bytes 50331648 | tf_op jit(solution)/shard_map/pallas_call | solution.py:1606
  751.1 2.7 collective-permute-start.12
  754.8 10.3 %shard_map.261 = f32[2048,2048]{1,0:T(8,128)} custom-call(bf16[2048,2048]{1,0:T(8,128)(2,1)} %bitcast.423), custom_call_target="tpu_custom_call" | custom-call | bytes 25165824 | tf_op jit(solution)/shard_map/pallas_call | solution.py:1630
  (172 shorter events, 65.4 us)
Async XLA Ops:
  0.6 231.9 %copy-start = (f32[36,36]{1,0:T(8,128)S(1)}, f32[36,36]{1,0:T(8,128)}, u32[]{:S(2)}) copy-start(f32[36,36]{1,0:T(8,128)} %param.28) | copy-start | bytes 15556
  2.2 23.7 %all-to-all-start = ((f32[32,32,128]{2,1,0:T(8,128)}), f32[32,32,128]{2,1,0:T(8,128)S(1)}, u32[]{:S(2)}, u32[]{:S(2)}) async-start(f32[32,32,128]{2,1,0:T(8,128)} %broadcast_in_dim.39), calls=%async_computation | async-start | bytes 1048576 | tf_op jit(solution)/shard_map/all_to_all | solution.py:170
  26.8 149.5 %all-to-all-start.1 = ((f32[32,37,128]{2,1,0:T(8,128)}), f32[32,37,128]{2,1,0:T(8,128)S(1)}, u32[]{:S(2)}, u32[]{:S(2)}) async-start(f32[32,37,128]{2,1,0:T(8,128)} %broadcast_in_dim.44), calls=%async_computation.1 | async-start | bytes 1310720 | tf_op jit(solution)/shard_map/all_to_all | solution.py:170
  176.8 55.7 %copy-start.14 = (f32[5,8,32,128]{3,1,2,0:T(8,128)}, f32[5,8,32,128]{3,1,2,0:T(8,128)S(1)}, u32[]{:S(2)}) copy-start(f32[5,8,32,128]{3,1,2,0:T(8,128)S(1)} %copy.83) | copy-start | bytes 1966084
  186.7 62.6 %copy-start.15 = (bf16[4,64,1024]{2,1,0:T(8,128)(2,1)S(1)}, bf16[4,64,1024]{2,1,0:T(8,128)(2,1)}, u32[]{:S(2)}) copy-start(bf16[4,64,1024]{2,1,0:T(8,128)(2,1)} %get-tuple-element.84) | copy-start | bytes 1572868
  229.9 19.3 %copy-start.10 = (f32[256,1024]{1,0:T(8,128)S(1)}, f32[256,1024]{1,0:T(8,128)}, u32[]{:S(2)}) copy-start(f32[256,1024]{1,0:T(8,128)} %get-tuple-element.86) | copy-start | bytes 3145732
  233.8 11.2 %collective-permute-start = (f32[2772]{0:T(1024)S(1)}, f32[2772]{0:T(1024)S(1)}, u32[]{:S(2)}, u32[]{:S(2)}) collective-permute-start(f32[2772]{0:T(1024)S(1)} %concatenate.15), channel_id=1, source_target_pairs={{0,2},{1,3},{2,4},{3,5},{4,6},{5,7},{6,0},{7,1},{8,10},{9,11},{10,... | collective-permute-start | bytes 33272 | tf_op jit(solution)/shard_map/ppermute | solution.py:163
  242.4 4.6 collective-permute-start.1
  242.4 4.8 collective-permute-start.2
  247.7 18.2 %copy-start.17 = (f32[36]{0:T(128)}, f32[36]{0:T(128)S(1)}, u32[]{:S(2)}) copy-start(f32[36]{0:T(128)S(1)} %get-tuple-element.240) | copy-start | bytes 436
  250.6 12.6 %collective-permute-start.3 = (bf16[256,1024]{1,0:T(8,128)(2,1)S(1)}, bf16[256,1024]{1,0:T(8,128)(2,1)}, u32[]{:S(2)}, u32[]{:S(2)}) collective-permute-start(bf16[256,1024]{1,0:T(8,128)(2,1)S(1)} %get-tuple-element.211), channel_id=1, source_target_pairs={{0,1},{1,0},{2,3},{3,2},{4,5},{5,4},{6,7},{7,6},{8,9},{9,8},{10,11... | collective-permute-start | bytes 1572872 | tf_op jit(solution)/shard_map/ppermute | solution.py:77
  252.0 14.0 %collective-permute-start.5 = (bf16[256,1024]{1,0:T(8,128)(2,1)S(1)}, bf16[256,1024]{1,0:T(8,128)(2,1)}, u32[]{:S(2)}, u32[]{:S(2)}) collective-permute-start(bf16[256,1024]{1,0:T(8,128)(2,1)S(1)} %get-tuple-element.211), channel_id=1, source_target_pairs={{0,16},{8,24},{16,0},{24,8},{1,17},{9,25},{17,1},{25,9},{2,18},{10... | collective-permute-start | bytes 1572872 | tf_op jit(solution)/shard_map/ppermute | solution.py:72
  263.2 12.3 %collective-permute-start.6 = (bf16[256,1024]{1,0:T(8,128)(2,1)}, bf16[256,1024]{1,0:T(8,128)(2,1)}, u32[]{:S(2)}, u32[]{:S(2)}) collective-permute-start(bf16[256,1024]{1,0:T(8,128)(2,1)} %collective-permute-done.3), channel_id=1, source_target_pairs={{0,16},{8,24},{16,0},{24,8},{1,17},{9,25},{17,1},{25,9},{2,18},{10... | collective-permute-start | bytes 1572872 | tf_op jit(solution)/shard_map/ppermute | solution.py:72
  265.9 11.2 %collective-permute-start.4 = (bf16[512,1024]{1,0:T(8,128)(2,1)S(1)}, bf16[512,1024]{1,0:T(8,128)(2,1)S(1)}, u32[]{:S(2)}, u32[]{:S(2)}) collective-permute-start(bf16[512,1024]{1,0:T(8,128)(2,1)S(1)} %bitcast.424), channel_id=1, source_target_pairs={{0,8},{8,0},{16,24},{24,16},{1,9},{9,1},{17,25},{25,17},{2,10},{10... | collective-permute-start | bytes 3145736 | tf_op jit(solution)/shard_map/ppermute | solution.py:63
  276.9 2.7 collective-permute-start.7
  296.2 129.6 %copy-start.5 = (bf16[3,2,128,1024]{3,2,1,0:T(8,128)(2,1)}, bf16[3,2,128,1024]{3,2,1,0:T(8,128)(2,1)S(1)}, u32[]{:S(2)}) copy-start(bf16[3,2,128,1024]{3,2,1,0:T(8,128)(2,1)S(1)} %shard_map.257) | copy-start | bytes 4718596
  296.2 130.4 %collective-permute-start.8 = (bf16[1024,1024]{1,0:T(8,128)(2,1)}, bf16[1024,1024]{1,0:T(8,128)(2,1)}, u32[]{:S(2)}, u32[]{:S(2)}) collective-permute-start(bf16[1024,1024]{1,0:T(8,128)(2,1)} %multiply_convert_fusion.refs_0_), channel_id=1, source_target_pairs={{0,16},{8,24},{16,0},{24,8},{1,17},{9,25},{17,1},{25,9},{2,18},{10... | collective-permute-start | bytes 6291464 | tf_op jit(solution)/shard_map/ppermute | solution.py:72
  297.2 128.6 %collective-permute-start.9 = (bf16[768,1024]{1,0:T(8,128)(2,1)S(1)}, bf16[768,1024]{1,0:T(8,128)(2,1)}, u32[]{:S(2)}, u32[]{:S(2)}) collective-permute-start(bf16[768,1024]{1,0:T(8,128)(2,1)S(1)} %bitcast.414), channel_id=1, source_target_pairs={{0,16},{8,24},{16,0},{24,8},{1,17},{9,25},{17,1},{25,9},{2,18},{10... | collective-permute-start | bytes 4718600 | tf_op jit(solution)/shard_map/ppermute | solution.py:72
  300.6 125.2 %all-to-all-start.2 = ((bf16[4,64,1024]{2,1,0:T(8,128)(2,1)}), bf16[4,64,1024]{2,1,0:T(8,128)(2,1)S(1)}, u32[]{:S(2)}, u32[]{:S(2)}) async-start(bf16[4,64,1024]{2,1,0:T(8,128)(2,1)} %bitcast.444), calls=%async_computation.2 | async-start | bytes 1048576 | tf_op jit(solution)/shard_map/all_to_all | solution.py:195
  728.9 22.2 %collective-permute-start.11 = (f32[40,256]{1,0:T(8,128)S(1)}, f32[40,256]{1,0:T(8,128)S(1)}, u32[]{:S(2)}, u32[]{:S(2)}) collective-permute-start(f32[40,256]{1,0:T(8,128)S(1)} %pad_maximum_fusion.8), channel_id=1, source_target_pairs={{0,2},{1,3},{2,0},{3,1},{4,6},{5,7},{6,4},{7,5},{8,10},{9,11},{10,... | collective-permute-start | bytes 122888 | tf_op jit(solution)/shard_map/ppermute | solution.py:77
  729.0 42.4 %all-to-all-start.3 = ((f32[32,32,128]{2,1,0:T(8,128)}), f32[32,32,128]{2,1,0:T(8,128)S(1)}, u32[]{:S(2)}, u32[]{:S(2)}) async-start(f32[32,32,128]{2,1,0:T(8,128)} %get-tuple-element.113), calls=%async_computation.3 | async-start | bytes 1048576 | tf_op jit(solution)/shard_map/all_to_all | solution.py:2121
  751.1 14.0 %collective-permute-start.12 = (f32[40,256]{1,0:T(8,128)S(1)}, f32[40,256]{1,0:T(8,128)S(1)}, u32[]{:S(2)}, u32[]{:S(2)}) collective-permute-start(f32[40,256]{1,0:T(8,128)S(1)} %add.335), channel_id=1, source_target_pairs={{0,4},{1,5},{2,6},{3,7},{4,0},{5,1},{6,2},{7,3},{8,12},{9,13},{10,... | collective-permute-start | bytes 122888 | tf_op jit(solution)/shard_map/ppermute | solution.py:77
  754.1 13.4 %collective-permute-start.10 = (f32[36,128]{1,0:T(8,128)S(1)}, f32[36,128]{1,0:T(8,128)S(1)}, u32[]{:S(2)}, u32[]{:S(2)}) collective-permute-start(f32[36,128]{1,0:T(8,128)S(1)} %bitcast.527), channel_id=1, source_target_pairs={{0,0},{1,1},{2,8},{3,9},{4,16},{5,17},{6,24},{7,25},{8,2},{9,3},{1... | collective-permute-start | bytes 55304 | tf_op jit(solution)/shard_map/ppermute | solution.py:1699
  765.2 4.5 collective-permute-start.13
  (15 other events, 84.8 us)

commit v8 on v7

--- a/solution.py
+++ b/solution.py
@@ -548,26 +548,29 @@
                 preferred_element_type=full,
             )
 
-        core_out[unit, 0] = product(0).astype(low)
-        core_copy(unit, 0).start()
-        passing = product(1)
-        core_out[unit, 1] = product(2).astype(low)
-        core_copy(unit, 1).start()
-        core_copy(unit, 0).wait_recv()
-        outer_out[unit] = (passing + core_in[unit, 0].astype(full)).astype(low)
-        outer_copy(unit).start()
-        kept = product(3)
-        core_copy(unit, 1).wait_recv()
-        kept = kept + core_in[unit, 1].astype(full)
-
-        @pl.when(unit < ups)
-        def _():
-            slope_ref[pl.ds(pl.multiple_of(unit * n_head, n_head), n_head), :] = kept
-
-        @pl.when(unit >= ups)
-        def _():
-            heads_ref[unit - ups] = kept
-
+        def stage(k, carry):
+            core_out[unit, k] = product(2 * k).astype(low)
+            core_copy(unit, k).start()
+            kept = product(2 * k + 1)
+            core_copy(unit, k).wait_recv()
+            kept = kept + core_in[unit, k].astype(full)
+
+            @pl.when(k == 0)
+            def _():
+                outer_out[unit] = kept.astype(low)
+                outer_copy(unit).start()
+
+            @pl.when((k == 1) & (unit < ups))
+            def _():
+                slope_ref[pl.ds(pl.multiple_of(unit * n_head, n_head), n_head), :] = kept
+
+            @pl.when((k == 1) & (unit >= ups))
+            def _():
+                heads_ref[unit - ups] = kept
+
+            return carry
+
+        lax.fori_loop(0, 2, stage, 0)
         return carry
 
     lax.fori_loop(0, count, project, 0)
@@ -1369,7 +1372,16 @@
 
         @pl.when(s == 3)
         def _():
-            pulled[...] = jnp.dot(turned_up[...], hidden[...], preferred_element_type=full)
+            pulled[...] = jnp.zeros_like(pulled)
+
+            def add_turn(turn, carry):
+                units = pl.ds(pl.multiple_of(turn * n_units, n_units), n_units)
+                pulled[...] += jnp.dot(
+                    turned_up[:, units], hidden[units, :], preferred_element_type=full
+                )
+                return carry
+
+            lax.fori_loop(0, 4, add_turn, 0)
 
         def use(r, carry):
             rows = pl.ds(pl.multiple_of(2 * piece * r, 2 * piece), 2 * piece)
@@ -1639,6 +1651,50 @@
     )(total)
 
 
+def stream_kernel(stored_ref, mix_ref, deviations_ref, moments_ref):
+    means, spreads = [], []
+    for s in range(STREAMS):
+        total = mix_ref[s * HIST : s * HIST + 1, :] * stored_ref[0].astype(full)
+        for j in range(1, HIST):
+            row = s * HIST + j
+            total = total + mix_ref[row : row + 1, :] * stored_ref[j].astype(full)
+        mean = jnp.mean(total, axis=0, keepdims=True)
+        off = total - mean
+        deviations_ref[0, s] = off.astype(low)
+        means.append(mean)
+        spreads.append(jnp.sum(off * off, axis=0, keepdims=True))
+    moments_ref[0] = jnp.concatenate(means + spreads, axis=0)
+
+
+def mix_streams(stored, mix_all, places):
+    _, piece, tokens = stored.shape
+    group = tokens // places
+    wide = min(512, group)
+    per_place = group // wide
+    return pl.pallas_call(
+        stream_kernel,
+        grid=(tokens // wide,),
+        out_shape=[
+            jax.ShapeDtypeStruct((places, STREAMS, piece, group), low),
+            jax.ShapeDtypeStruct((places, 2 * STREAMS, group), full),
+        ],
+        in_specs=[
+            pl.BlockSpec((HIST, piece, wide), lambda i: (0, 0, i)),
+            pl.BlockSpec((mix_all.shape[0], wide), lambda i: (0, i)),
+        ],
+        out_specs=[
+            pl.BlockSpec((1, STREAMS, piece, wide), lambda i: (i // per_place, 0, 0, i % per_place)),
+            pl.BlockSpec((1, 2 * STREAMS, wide), lambda i: (i // per_place, 0, i % per_place)),
+        ],
+        compiler_params=pltpu.CompilerParams(vmem_limit_bytes=40 << 20),
+        cost_estimate=pl.CostEstimate(
+            flops=2 * STREAMS * HIST * piece * tokens,
+            bytes_accessed=4 * HIST * piece * tokens,
+            transcendentals=0,
+        ),
+    )(stored, mix_all)
+
+
 def history_kernel(split_ref, stored_ref, mix_ref, grad_ref, parts_ref):
     streams = [split_ref[s, 0].astype(full) for s in range(STREAMS)]
     rows = [None] * (STREAMS * HIST)
@@ -1761,17 +1817,7 @@
             parts.reshape(STREAMS, places, ways * piece, 1),
         )
         mix_all, gain_tables = lax.optimization_barrier((mix_all, gain_tables))
-    own_means, own_devs, deviations = [], [], []
-    for s in range(STREAMS):
-        total = mix_all[s * HIST] * stored[0].astype(full)
-        for j in range(1, HIST):
-            total = total + mix_all[s * HIST + j] * stored[j].astype(full)
-        own_means.append(jnp.mean(total, axis=0))
-        off = total - own_means[s]
-        own_devs.append(jnp.sum(off * off, axis=0))
-        deviations.append(off.astype(low))
-    moments = by_place(jnp.stack(own_means + own_devs, axis=0))
-    deviations = by_place(jnp.stack(deviations, axis=0))
+    deviations, moments = mix_streams(stored, mix_all, places)
 
     table = jnp.concatenate([mix_cotangent.T, segment_ids.astype(full)[None]], axis=0)
     table = lax.dynamic_slice_in_dim(gather_all(table), place * group, group, 1)

time: 784 us -> 770 us (0.982)
  other arithmetic: 27.9 us -> 12 us
    unnamed x47 -> x53, local copies, waits for them, and re-layouts: 12.7 us -> 16.5 us
  transfers between devices with their start and end apart: 18 -> 18, of which waited for: 6 -> 7; matrix products, arithmetic and copies ran while one was open for 4% -> 2% of each run, Pallas kernels for 36% -> 37%
where the time goes in v8:
time: 770 us; the launch traced here: 766 us
  Pallas kernels  636 us (83%)
  starting transfers between devices  39.2 us (5%)
  waiting for transfers between devices  35.3 us (5%)
  local copies, waits for them, and re-layouts  31 us (4%)
  other arithmetic  12 us (2%)
  matrix products  11.9 us (2%)
    pallas_call x1, Pallas kernels, late_sums(): pl.pallas_call(functools.partial(late_kernel, (places, piece, group, n_he...  291 us
    pallas_call x1, Pallas kernels, forward_projections(): pl.pallas_call(functools.partial(forward_kernel, (places, piece, group, n...  132 us
    pallas_call x1, Pallas kernels, chain_sum(): pl.pallas_call(functools.partial(chain_kernel, ways, size // ways, blocks...  118 us
    pallas_call x1, Pallas kernels, add_branches(): pl.pallas_call(functools.partial(branch_kernel, (places, mine // places,...  43.2 us
    pallas_call x1, Pallas kernels, assemble(): pl.pallas_call(functools.partial(assemble_kernel, ways, dp, int(fused)),...  18.7 us
    unnamed x53, local copies, waits for them, and re-layouts  16.5 us
  transfers between devices with their start and end apart: 18, of which 7 were waited for; matrix products, arithmetic and copies ran while one was open for 2% of the time, Pallas kernels for 37%

profile of v8, /device:TPU:0, one launch (start us, length us, event | category | flops | bytes accessed | tf_op | source)
XLA Modules:
  0.0 766.4 jit_solution(18139418000306319453)
XLA Ops:
  2.2 7.3 all-to-all-start
  17.0 8.9 %all-to-all-done = f32[32,32,128]{2,1,0:T(8,128)S(1)} async-done(((f32[32,32,128]{2,1,0:T(8,128)}), f32[32,32,128]{2,1,0:T(8,128)S(1)}, u32[]{:S(2)}, u32[]{:S(2)}) %all-to-all-start) | async-done | bytes 524320 | tf_op jit(solution)/shard_map/all_to_all | solution.py:170
  26.8 2.6 all-to-all-start.1
  29.5 2.2 copy-done.2
  31.6 4.6 shard_map.254
  38.2 132.3 %shard_map.255 = (bf16[4,512,1024]{2,1,0:T(8,128)(2,1)}, bf16[4,4,64,1024]{3,2,1,0:T(8,128)(2,1)}, f32[256,1024]{1,0:T(8,128)}, f32[4,4,1,1024]{3,2,1,0:T(1,128)...) custom-call(bf16[4,4,64,1024]{3,2,1,0:T(8,128)(2,1)} %copy-done.5, ...), custom_call_target="tpu_custom_call" | custom-call | flops 7516192768 | bytes 314572800 | tf_op jit(solution)/shard_map/pallas_call | solution.py:661
  174.2 4.8 shard_map.256
  180.9 43.2 %shard_map.257 = (f32[256,1024]{1,0:T(8,128)}, bf16[256,1024]{1,0:T(8,128)(2,1)}, f32[48,1024]{1,0:T(8,128)}, bf16[256,2048]{1,0:T(8,128)(2,1)}, bf16[1024,2048]{1,0:T(8,128)(2,1)}) custom-call(bf16[256,1024]{1,0:T(8,128)(2,1)} %bitcast.130, bf16[1024,1024]{1,0:T(8,128)(2,1)} %get-tuple-element.95.refs_1_.refs_0_, f32[256,1024]{1,0:T(8,128)} %get-tuple-element.86.refs_2_, ...), custom_call_target="tpu_custom_call" | custom-call | flops 5368709120 | bytes 104857600 | tf_op jit(solution)/shard_map/pallas_call | solution.py:1161
  228.0 9.0 %collective-permute-start = (f32[2772]{0:T(1024)S(1)}, f32[2772]{0:T(1024)S(1)}, u32[]{:S(2)}, u32[]{:S(2)}) collective-permute-start(f32[2772]{0:T(1024)S(1)} %concatenate.15), channel_id=1, source_target_pairs={{0,2},{1,3},{2,4},{3,5},{4,6},{5,7},{6,0},{7,1},{8,10},{9,11},{10,... | collective-permute-start | bytes 33272 | tf_op jit(solution)/shard_map/ppermute | solution.py:163
  237.0 2.4 collective-permute-start.2
  247.5 10.5 %collective-permute-done.3 = bf16[256,1024]{1,0:T(8,128)(2,1)S(1)} collective-permute-done((bf16[256,1024]{1,0:T(8,128)(2,1)S(1)}, bf16[256,1024]{1,0:T(8,128)(2,1)S(1)}, u32[]{:S(2)}, u32[]{:S(2)}) %collective-permute-start.3) | collective-permute-done | bytes 524320 | tf_op jit(solution)/shard_map/ppermute | solution.py:77
  259.9 10.6 %collective-permute-done.6 = bf16[256,1024]{1,0:T(8,128)(2,1)} collective-permute-done((bf16[256,1024]{1,0:T(8,128)(2,1)S(1)}, bf16[256,1024]{1,0:T(8,128)(2,1)}, u32[]{:S(2)}, u32[]{:S(2)}) %collective-permute-start.6) | collective-permute-done | bytes 524320 | tf_op jit(solution)/shard_map/ppermute | solution.py:72
  271.8 2.6 collective-permute-done.7
  279.4 5.7 multiply_convert_fusion.refs_0_
  285.1 5.8 shard_map.258
  295.4 4.4 all-to-all-start.2
  301.8 118.5 %shard_map.259 = bf16[2,64,16,2048]{3,2,1,0:T(8,128)(2,1)} custom-call(bf16[1024,1024]{1,0:T(8,128)(2,1)} %get-tuple-element.95.refs_1_.refs_0_, bf16[2048,1024]{1,0:T(8,128)(2,1)} %copy-done.13), custom_call_target="tpu_custom_call" | custom-call | flops 4294967296 | bytes 629145600 | tf_op jit(solution)/shard_map/pallas_call | solution.py:960
  420.3 291.3 %shard_map.260 = (bf16[2,64,64,1024]{3,2,1,0:T(8,128)(2,1)}, bf16[4,4,64,1024]{3,2,1,0:T(8,128)(2,1)}, f32[4,4,64,1]{3,2,1,0:T(8,128)}) custom-call(bf16[1024,1024]{1,0:T(8,128)(2,1)} %multiply_convert_fusion.refs_0_, bf16[1024,1024]{1,0:T(8,128)(2,1)} %collective-permute-done.8.refs_1_, bf16[768,1024]{1,0:T(8,128)(2,1)} %bitcast.128, ...), custom_call_target="tpu_custom_call" | custom-call | flops 17179869184 | bytes 943718400 | tf_op jit(solution)/shard_map/pallas_call | solution.py:1507
  713.0 2.2 copy-done.3
  716.8 6.2 shard_map.261
  723.1 3.0 all-to-all-start.3
  726.2 18.7 %shard_map.263 = (f32[512,8192]{1,0:T(8,128)}, f32[512,2048]{1,0:T(8,128)}, f32[512,2048]{1,0:T(8,128)}, f32[512,2048]{1,0:T(8,128)}, f32[512,2048]{1,0:T(8,128)}) custom-call(bf16[2,8,512,1024]{3,2,1,0:T(8,128)(2,1)} %bitcast.133, bf16[2,8,512,1024]{3,2,1,0:T(8,128)(2,1)} %bitcast.134, bf16[2,8,512,1024]{3,2,1,0:T(8,128)(2,1)} %bitcast.135), custom_call_target="tpu_custom_call" | custom-call | bytes 50331648 | tf_op jit(solution)/shard_map/pallas_call | solution.py:1618
  744.9 2.7 collective-permute-start.12
  748.6 10.3 %shard_map.262 = f32[2048,2048]{1,0:T(8,128)} custom-call(bf16[2048,2048]{1,0:T(8,128)(2,1)} %bitcast.136), custom_call_target="tpu_custom_call" | custom-call | bytes 25165824 | tf_op jit(solution)/shard_map/pallas_call | solution.py:1642
  (155 shorter events, 55.3 us)
Async XLA Ops:
  0.6 226.0 %copy-start = (f32[36,36]{1,0:T(8,128)S(1)}, f32[36,36]{1,0:T(8,128)}, u32[]{:S(2)}) copy-start(f32[36,36]{1,0:T(8,128)} %param.28) | copy-start | bytes 15556
  2.2 23.7 %all-to-all-start = ((f32[32,32,128]{2,1,0:T(8,128)}), f32[32,32,128]{2,1,0:T(8,128)S(1)}, u32[]{:S(2)}, u32[]{:S(2)}) async-start(f32[32,32,128]{2,1,0:T(8,128)} %broadcast_in_dim.39), calls=%async_computation | async-start | bytes 1048576 | tf_op jit(solution)/shard_map/all_to_all | solution.py:170
  26.8 143.7 %all-to-all-start.1 = ((f32[32,37,128]{2,1,0:T(8,128)}), f32[32,37,128]{2,1,0:T(8,128)S(1)}, u32[]{:S(2)}, u32[]{:S(2)}) async-start(f32[32,37,128]{2,1,0:T(8,128)} %broadcast_in_dim.78), calls=%async_computation.1 | async-start | bytes 1310720 | tf_op jit(solution)/shard_map/all_to_all | solution.py:170
  180.9 63.1 %copy-start.15 = (bf16[4,64,1024]{2,1,0:T(8,128)(2,1)S(1)}, bf16[4,64,1024]{2,1,0:T(8,128)(2,1)}, u32[]{:S(2)}) copy-start(bf16[4,64,1024]{2,1,0:T(8,128)(2,1)} %get-tuple-element.88) | copy-start | bytes 1572868
  224.1 19.9 %copy-start.12 = (f32[256,1024]{1,0:T(8,128)S(1)}, f32[256,1024]{1,0:T(8,128)}, u32[]{:S(2)}) copy-start(f32[256,1024]{1,0:T(8,128)} %get-tuple-element.90) | copy-start | bytes 3145732
  228.0 11.7 %collective-permute-start = (f32[2772]{0:T(1024)S(1)}, f32[2772]{0:T(1024)S(1)}, u32[]{:S(2)}, u32[]{:S(2)}) collective-permute-start(f32[2772]{0:T(1024)S(1)} %concatenate.15), channel_id=1, source_target_pairs={{0,2},{1,3},{2,4},{3,5},{4,6},{5,7},{6,0},{7,1},{8,10},{9,11},{10,... | collective-permute-start | bytes 33272 | tf_op jit(solution)/shard_map/ppermute | solution.py:163
  237.0 4.6 collective-permute-start.1
  237.0 4.8 collective-permute-start.2
  245.5 12.5 %collective-permute-start.3 = (bf16[256,1024]{1,0:T(8,128)(2,1)S(1)}, bf16[256,1024]{1,0:T(8,128)(2,1)S(1)}, u32[]{:S(2)}, u32[]{:S(2)}) collective-permute-start(bf16[256,1024]{1,0:T(8,128)(2,1)S(1)} %get-tuple-element.167), channel_id=1, source_target_pairs={{0,1},{1,0},{2,3},{3,2},{4,5},{5,4},{6,7},{7,6},{8,9},{9,8},{10,11... | collective-permute-start | bytes 1572872 | tf_op jit(solution)/shard_map/ppermute | solution.py:77
  246.9 13.0 %collective-permute-start.5 = (bf16[256,1024]{1,0:T(8,128)(2,1)S(1)}, bf16[256,1024]{1,0:T(8,128)(2,1)S(1)}, u32[]{:S(2)}, u32[]{:S(2)}) collective-permute-start(bf16[256,1024]{1,0:T(8,128)(2,1)S(1)} %get-tuple-element.167), channel_id=1, source_target_pairs={{0,16},{8,24},{16,0},{24,8},{1,17},{9,25},{17,1},{25,9},{2,18},{10... | collective-permute-start | bytes 1572872 | tf_op jit(solution)/shard_map/ppermute | solution.py:72
  258.0 12.5 %collective-permute-start.6 = (bf16[256,1024]{1,0:T(8,128)(2,1)S(1)}, bf16[256,1024]{1,0:T(8,128)(2,1)}, u32[]{:S(2)}, u32[]{:S(2)}) collective-permute-start(bf16[256,1024]{1,0:T(8,128)(2,1)S(1)} %collective-permute-done.3), channel_id=1, source_target_pairs={{0,16},{8,24},{16,0},{24,8},{1,17},{9,25},{17,1},{25,9},{2,18},{10... | collective-permute-start | bytes 1572872 | tf_op jit(solution)/shard_map/ppermute | solution.py:72
  259.3 12.5 %collective-permute-start.4 = (bf16[512,1024]{1,0:T(8,128)(2,1)S(1)}, bf16[512,1024]{1,0:T(8,128)(2,1)S(1)}, u32[]{:S(2)}, u32[]{:S(2)}) collective-permute-start(bf16[512,1024]{1,0:T(8,128)(2,1)S(1)} %bitcast.137), channel_id=1, source_target_pairs={{0,8},{8,0},{16,24},{24,16},{1,9},{9,1},{17,25},{25,17},{2,10},{10... | collective-permute-start | bytes 3145736 | tf_op jit(solution)/shard_map/ppermute | solution.py:63
  271.7 2.7 collective-permute-start.7
  285.1 14.7 %copy-start.17 = (f32[36]{0:T(128)S(1)}, f32[36]{0:T(128)}, u32[]{:S(2)}) copy-start(f32[36]{0:T(128)} %param.29) | copy-start | bytes 436
  290.9 129.3 %copy-start.6 = (bf16[3,2,128,1024]{3,2,1,0:T(8,128)(2,1)}, bf16[3,2,128,1024]{3,2,1,0:T(8,128)(2,1)S(1)}, u32[]{:S(2)}) copy-start(bf16[3,2,128,1024]{3,2,1,0:T(8,128)(2,1)S(1)} %shard_map.258) | copy-start | bytes 4718596
  291.0 129.3 %collective-permute-start.8 = (bf16[1024,1024]{1,0:T(8,128)(2,1)}, bf16[1024,1024]{1,0:T(8,128)(2,1)}, u32[]{:S(2)}, u32[]{:S(2)}) collective-permute-start(bf16[1024,1024]{1,0:T(8,128)(2,1)} %multiply_convert_fusion.refs_0_), channel_id=1, source_target_pairs={{0,16},{8,24},{16,0},{24,8},{1,17},{9,25},{17,1},{25,9},{2,18},{10... | collective-permute-start | bytes 6291464 | tf_op jit(solution)/shard_map/ppermute | solution.py:72
  291.6 128.7 %collective-permute-start.9 = (bf16[768,1024]{1,0:T(8,128)(2,1)S(1)}, bf16[768,1024]{1,0:T(8,128)(2,1)}, u32[]{:S(2)}, u32[]{:S(2)}) collective-permute-start(bf16[768,1024]{1,0:T(8,128)(2,1)S(1)} %bitcast.127), channel_id=1, source_target_pairs={{0,16},{8,24},{16,0},{24,8},{1,17},{9,25},{17,1},{25,9},{2,18},{10... | collective-permute-start | bytes 4718600 | tf_op jit(solution)/shard_map/ppermute | solution.py:72
  295.4 124.8 %all-to-all-start.2 = ((bf16[4,64,1024]{2,1,0:T(8,128)(2,1)}), bf16[4,64,1024]{2,1,0:T(8,128)(2,1)}, u32[]{:S(2)}, u32[]{:S(2)}) async-start(bf16[4,64,1024]{2,1,0:T(8,128)(2,1)} %bitcast.156), calls=%async_computation.2 | async-start | bytes 1048576 | tf_op jit(solution)/shard_map/all_to_all | solution.py:195
  723.0 21.9 %collective-permute-start.11 = (f32[40,256]{1,0:T(8,128)S(1)}, f32[40,256]{1,0:T(8,128)S(1)}, u32[]{:S(2)}, u32[]{:S(2)}) collective-permute-start(f32[40,256]{1,0:T(8,128)S(1)} %pad_maximum_fusion.5), channel_id=1, source_target_pairs={{0,2},{1,3},{2,0},{3,1},{4,6},{5,7},{6,4},{7,5},{8,10},{9,11},{10,... | collective-permute-start | bytes 122888 | tf_op jit(solution)/shard_map/ppermute | solution.py:77
  723.1 42.1 %all-to-all-start.3 = ((f32[32,32,128]{2,1,0:T(8,128)}), f32[32,32,128]{2,1,0:T(8,128)S(1)}, u32[]{:S(2)}, u32[]{:S(2)}) async-start(f32[32,32,128]{2,1,0:T(8,128)} %get-tuple-element.117), calls=%async_computation.3 | async-start | bytes 1048576 | tf_op jit(solution)/shard_map/all_to_all | solution.py:2167
  744.9 13.9 %collective-permute-start.12 = (f32[40,256]{1,0:T(8,128)S(1)}, f32[40,256]{1,0:T(8,128)S(1)}, u32[]{:S(2)}, u32[]{:S(2)}) collective-permute-start(f32[40,256]{1,0:T(8,128)S(1)} %add.111), channel_id=1, source_target_pairs={{0,4},{1,5},{2,6},{3,7},{4,0},{5,1},{6,2},{7,3},{8,12},{9,13},{10,... | collective-permute-start | bytes 122888 | tf_op jit(solution)/shard_map/ppermute | solution.py:77
  747.9 13.3 %collective-permute-start.10 = (f32[36,128]{1,0:T(8,128)S(1)}, f32[36,128]{1,0:T(8,128)S(1)}, u32[]{:S(2)}, u32[]{:S(2)}) collective-permute-start(f32[36,128]{1,0:T(8,128)S(1)} %bitcast.167), channel_id=1, source_target_pairs={{0,0},{1,1},{2,8},{3,9},{4,16},{5,17},{6,24},{7,25},{8,2},{9,3},{1... | collective-permute-start | bytes 55304 | tf_op jit(solution)/shard_map/ppermute | solution.py:1755
  748.6 17.9 %copy-start.1 = (f32[36,36]{1,0:T(8,128)S(1)}, f32[36,36]{1,0:T(8,128)}, u32[]{:S(2)}) copy-start(f32[36,36]{1,0:T(8,128)} %param.28) | copy-start | bytes 15556
  759.0 4.5 collective-permute-start.13
  (18 other events, 81.8 us)

commit v9 on v8

--- a/solution.py
+++ b/solution.py
@@ -637,9 +637,9 @@
     pltpu.make_async_copy(weights, weights, turned_sem).wait()
 
 
-def forward_projections(deviations, moments, norm_gains, w_query, w_key, w_value, w_up, cotangent):
+def forward_projections(deviations, moments, gains, w_query, w_key, w_value, w_up, cotangent):
     places, _, piece, group = deviations.shape
-    feats = norm_gains.shape[0]
+    feats = gains.shape[1]
     n_head = w_query.shape[1] // 8
     n_units = w_up.shape[1] // 8
     count = n_units // n_head + 3
@@ -704,7 +704,7 @@
     )(
         deviations,
         moments,
-        norm_gains.T.astype(full)[:, :, None],
+        gains,
         w_query,
         w_key,
         w_value,
@@ -1214,8 +1214,7 @@
         shifts,
         scales,
         gains,
-        all_gains,
-    ), refs = refs[:15], refs[15:]
+    ), refs = refs[:14], refs[14:]
     (out_ref, split_ref, gain_ref), refs = refs[:3], refs[3:]
     (
         hidden,
@@ -1387,7 +1386,7 @@
             rows = pl.ds(pl.multiple_of(2 * piece * r, 2 * piece), 2 * piece)
             here = pulled[rows, :]
             totals[s, 0:1, :] = totals[s, 0:1, :] + jnp.sum(
-                here * all_gains[s, r], axis=0, keepdims=True
+                here * gains[s, rows, :], axis=0, keepdims=True
             )
             totals[s, 1:2, :] = totals[s, 1:2, :] + jnp.sum(
                 here * normed[s, rows, :].astype(full), axis=0, keepdims=True
@@ -1421,7 +1420,8 @@
         gradient = kept[s, r] + taken[s, r].astype(full)
         unit = devs[s, r].astype(full) * scales[s] + shifts[s, r]
         gain_ref[s, r] = jnp.sum(gradient * unit, axis=1, keepdims=True)
-        result = gradient * gains[s, r] - totals[s, 0:1, :] - unit * totals[s, 1:2, :]
+        rows = pl.ds(pl.multiple_of((2 * r + way) * piece, piece), piece)
+        result = gradient * gains[s, rows, :] - totals[s, 0:1, :] - unit * totals[s, 1:2, :]
         extra = output_grad[r] * jnp.where(s == 3, 1.0, 0.0)
         grads[s, r] = (result * scales[s] + extra).astype(low)
 
@@ -1811,12 +1811,8 @@
     mix_all = gather_all(mix.T)
     fused = dp == 4 and ways == 2 and rows == 1
     if fused:
-        parts = norm_gains.astype(full).T.reshape(STREAMS, places, ways, piece)
-        gain_tables = (
-            lax.dynamic_index_in_dim(parts, way, 2, keepdims=False)[..., None],
-            parts.reshape(STREAMS, places, ways * piece, 1),
-        )
-        mix_all, gain_tables = lax.optimization_barrier((mix_all, gain_tables))
+        gain_columns = norm_gains.T.astype(full)[:, :, None]
+        mix_all, gain_columns = lax.optimization_barrier((mix_all, gain_columns))
     deviations, moments = mix_streams(stored, mix_all, places)
 
     table = jnp.concatenate([mix_cotangent.T, segment_ids.astype(full)[None]], axis=0)
@@ -1883,7 +1879,7 @@
             forward_projections(
                 deviations,
                 moments,
-                norm_gains,
+                gain_columns,
                 w_query,
                 w_key,
                 w_value,
@@ -2110,7 +2106,7 @@
         tables = [
             own_shifts,
             inv_scales,
-            *gain_tables,
+            gain_columns,
         ]
         late_sum, split, gain_parts = late_sums(operands, tables, 1)
         gain_parts = gain_parts.reshape(STREAMS, mine)

time: 770 us -> 767 us (level)
  no operation moved by 1% of the time
where the time goes in v9:
time: 767 us; the launch traced here: 764 us
  Pallas kernels  634 us (83%)
  starting transfers between devices  39.2 us (5%)
  waiting for transfers between devices  36.7 us (5%)
  local copies, waits for them, and re-layouts  28.5 us (4%)
  other arithmetic  12 us (2%)
  matrix products  11.9 us (2%)
    pallas_call x1, Pallas kernels, late_sums(): pl.pallas_call(functools.partial(late_kernel, (places, piece, group, n_he...  291 us
    pallas_call x1, Pallas kernels, forward_projections(): pl.pallas_call(functools.partial(forward_kernel, (places, piece, group, n...  131 us
    pallas_call x1, Pallas kernels, chain_sum(): pl.pallas_call(functools.partial(chain_kernel, ways, size // ways, blocks...  119 us
    pallas_call x1, Pallas kernels, add_branches(): pl.pallas_call(functools.partial(branch_kernel, (places, mine // places,...  43.1 us
    pallas_call x1, Pallas kernels, assemble(): pl.pallas_call(functools.partial(assemble_kernel, ways, dp, int(fused)),...  18.7 us
    unnamed x53, local copies, waits for them, and re-layouts  16.5 us
  transfers between devices with their start and end apart: 18, of which 7 were waited for; matrix products, arithmetic and copies ran while one was open for 2% of the time, Pallas kernels for 37%

profile of v9, /device:TPU:0, one launch (start us, length us, event | category | flops | bytes accessed | tf_op | source)
XLA Modules:
  0.0 764.1 jit_solution(2802054572702652214)
XLA Ops:
  2.2 7.3 all-to-all-start
  15.5 10.4 %all-to-all-done = f32[32,32,128]{2,1,0:T(8,128)S(1)} async-done(((f32[32,32,128]{2,1,0:T(8,128)}), f32[32,32,128]{2,1,0:T(8,128)S(1)}, u32[]{:S(2)}, u32[]{:S(2)}) %all-to-all-start) | async-done | bytes 524320 | tf_op jit(solution)/shard_map/all_to_all | solution.py:170
  26.8 2.6 all-to-all-start.1
  30.8 2.2 copy-done.2
  33.0 4.6 shard_map.254
  39.6 131.2 %shard_map.255 = (bf16[4,512,1024]{2,1,0:T(8,128)(2,1)}, bf16[4,4,64,1024]{3,2,1,0:T(8,128)(2,1)}, f32[256,1024]{1,0:T(8,128)}, f32[4,4,1,1024]{3,2,1,0:T(1,128)...) custom-call(bf16[4,4,64,1024]{3,2,1,0:T(8,128)(2,1)} %copy-done.5, ...), custom_call_target="tpu_custom_call" | custom-call | flops 7516192768 | bytes 314572800 | tf_op jit(solution)/shard_map/pallas_call | solution.py:661
  174.5 4.8 shard_map.256
  181.2 43.1 %shard_map.257 = (f32[256,1024]{1,0:T(8,128)}, bf16[256,1024]{1,0:T(8,128)(2,1)}, f32[48,1024]{1,0:T(8,128)}, bf16[256,2048]{1,0:T(8,128)(2,1)}, bf16[1024,2048]{1,0:T(8,128)(2,1)}) custom-call(bf16[256,1024]{1,0:T(8,128)(2,1)} %bitcast.126, bf16[1024,1024]{1,0:T(8,128)(2,1)} %get-tuple-element.95.refs_1_.refs_0_, f32[256,1024]{1,0:T(8,128)} %get-tuple-element.86.refs_2_, ...), custom_call_target="tpu_custom_call" | custom-call | flops 5368709120 | bytes 104857600 | tf_op jit(solution)/shard_map/pallas_call | solution.py:1161
  228.2 9.1 %collective-permute-start = (f32[2772]{0:T(1024)S(1)}, f32[2772]{0:T(1024)S(1)}, u32[]{:S(2)}, u32[]{:S(2)}) collective-permute-start(f32[2772]{0:T(1024)S(1)} %concatenate.15), channel_id=1, source_target_pairs={{0,2},{1,3},{2,4},{3,5},{4,6},{5,7},{6,0},{7,1},{8,10},{9,11},{10,... | collective-permute-start | bytes 33272 | tf_op jit(solution)/shard_map/ppermute | solution.py:163
  237.3 2.4 collective-permute-start.2
  247.7 10.5 %collective-permute-done.3 = bf16[256,1024]{1,0:T(8,128)(2,1)S(1)} collective-permute-done((bf16[256,1024]{1,0:T(8,128)(2,1)S(1)}, bf16[256,1024]{1,0:T(8,128)(2,1)S(1)}, u32[]{:S(2)}, u32[]{:S(2)}) %collective-permute-start.3) | collective-permute-done | bytes 524320 | tf_op jit(solution)/shard_map/ppermute | solution.py:77
  260.2 10.6 %collective-permute-done.6 = bf16[256,1024]{1,0:T(8,128)(2,1)} collective-permute-done((bf16[256,1024]{1,0:T(8,128)(2,1)S(1)}, bf16[256,1024]{1,0:T(8,128)(2,1)}, u32[]{:S(2)}, u32[]{:S(2)}) %collective-permute-start.6) | collective-permute-done | bytes 524320 | tf_op jit(solution)/shard_map/ppermute | solution.py:72
  272.1 2.6 collective-permute-done.7
  279.7 5.7 multiply_convert_fusion.refs_0_
  285.4 5.8 shard_map.258
  293.3 4.4 all-to-all-start.2
  299.6 118.5 %shard_map.259 = bf16[2,64,16,2048]{3,2,1,0:T(8,128)(2,1)} custom-call(bf16[1024,1024]{1,0:T(8,128)(2,1)} %get-tuple-element.95.refs_1_.refs_0_, bf16[2048,1024]{1,0:T(8,128)(2,1)} %copy-done.13), custom_call_target="tpu_custom_call" | custom-call | flops 4294967296 | bytes 629145600 | tf_op jit(solution)/shard_map/pallas_call | solution.py:960
  418.2 291.1 %shard_map.260 = (bf16[2,64,64,1024]{3,2,1,0:T(8,128)(2,1)}, bf16[4,4,64,1024]{3,2,1,0:T(8,128)(2,1)}, f32[4,4,64,1]{3,2,1,0:T(8,128)}) custom-call(bf16[1024,1024]{1,0:T(8,128)(2,1)} %multiply_convert_fusion.refs_0_, bf16[1024,1024]{1,0:T(8,128)(2,1)} %collective-permute-done.8.refs_1_, bf16[768,1024]{1,0:T(8,128)(2,1)} %bitcast.124, ...), custom_call_target="tpu_custom_call" | custom-call | flops 17179869184 | bytes 943718400 | tf_op jit(solution)/shard_map/pallas_call | solution.py:1507
  710.7 2.2 copy-done.3
  714.5 6.2 shard_map.261
  720.8 3.0 all-to-all-start.3
  723.9 18.7 %shard_map.263 = (f32[512,8192]{1,0:T(8,128)}, f32[512,2048]{1,0:T(8,128)}, f32[512,2048]{1,0:T(8,128)}, f32[512,2048]{1,0:T(8,128)}, f32[512,2048]{1,0:T(8,128)}) custom-call(bf16[2,8,512,1024]{3,2,1,0:T(8,128)(2,1)} %bitcast.129, bf16[2,8,512,1024]{3,2,1,0:T(8,128)(2,1)} %bitcast.130, bf16[2,8,512,1024]{3,2,1,0:T(8,128)(2,1)} %bitcast.131), custom_call_target="tpu_custom_call" | custom-call | bytes 50331648 | tf_op jit(solution)/shard_map/pallas_call | solution.py:1618
  742.5 2.7 collective-permute-start.12
  746.2 10.3 %shard_map.262 = f32[2048,2048]{1,0:T(8,128)} custom-call(bf16[2048,2048]{1,0:T(8,128)(2,1)} %bitcast.132), custom_call_target="tpu_custom_call" | custom-call | bytes 25165824 | tf_op jit(solution)/shard_map/pallas_call | solution.py:1642
  (150 shorter events, 52.8 us)
Async XLA Ops:
  0.6 226.3 %copy-start = (f32[36,36]{1,0:T(8,128)S(1)}, f32[36,36]{1,0:T(8,128)}, u32[]{:S(2)}) copy-start(f32[36,36]{1,0:T(8,128)} %param.28) | copy-start | bytes 15556
  2.2 23.7 %all-to-all-start = ((f32[32,32,128]{2,1,0:T(8,128)}), f32[32,32,128]{2,1,0:T(8,128)S(1)}, u32[]{:S(2)}, u32[]{:S(2)}) async-start(f32[32,32,128]{2,1,0:T(8,128)} %broadcast_in_dim.38), calls=%async_computation | async-start | bytes 1048576 | tf_op jit(solution)/shard_map/all_to_all | solution.py:170
  26.8 144.0 %all-to-all-start.1 = ((f32[32,37,128]{2,1,0:T(8,128)}), f32[32,37,128]{2,1,0:T(8,128)S(1)}, u32[]{:S(2)}, u32[]{:S(2)}) async-start(f32[32,37,128]{2,1,0:T(8,128)} %broadcast_in_dim.42), calls=%async_computation.1 | async-start | bytes 1310720 | tf_op jit(solution)/shard_map/all_to_all | solution.py:170
  181.2 63.1 %copy-start.15 = (bf16[4,64,1024]{2,1,0:T(8,128)(2,1)S(1)}, bf16[4,64,1024]{2,1,0:T(8,128)(2,1)}, u32[]{:S(2)}) copy-start(bf16[4,64,1024]{2,1,0:T(8,128)(2,1)} %get-tuple-element.88) | copy-start | bytes 1572868
  224.4 19.9 %copy-start.12 = (f32[256,1024]{1,0:T(8,128)S(1)}, f32[256,1024]{1,0:T(8,128)}, u32[]{:S(2)}) copy-start(f32[256,1024]{1,0:T(8,128)} %get-tuple-element.90) | copy-start | bytes 3145732
  228.2 11.7 %collective-permute-start = (f32[2772]{0:T(1024)S(1)}, f32[2772]{0:T(1024)S(1)}, u32[]{:S(2)}, u32[]{:S(2)}) collective-permute-start(f32[2772]{0:T(1024)S(1)} %concatenate.15), channel_id=1, source_target_pairs={{0,2},{1,3},{2,4},{3,5},{4,6},{5,7},{6,0},{7,1},{8,10},{9,11},{10,... | collective-permute-start | bytes 33272 | tf_op jit(solution)/shard_map/ppermute | solution.py:163
  237.3 4.6 collective-permute-start.1
  237.3 4.8 collective-permute-start.2
  245.7 12.5 %collective-permute-start.3 = (bf16[256,1024]{1,0:T(8,128)(2,1)S(1)}, bf16[256,1024]{1,0:T(8,128)(2,1)S(1)}, u32[]{:S(2)}, u32[]{:S(2)}) collective-permute-start(bf16[256,1024]{1,0:T(8,128)(2,1)S(1)} %get-tuple-element.163), channel_id=1, source_target_pairs={{0,1},{1,0},{2,3},{3,2},{4,5},{5,4},{6,7},{7,6},{8,9},{9,8},{10,11... | collective-permute-start | bytes 1572872 | tf_op jit(solution)/shard_map/ppermute | solution.py:77
  247.2 13.0 %collective-permute-start.5 = (bf16[256,1024]{1,0:T(8,128)(2,1)S(1)}, bf16[256,1024]{1,0:T(8,128)(2,1)S(1)}, u32[]{:S(2)}, u32[]{:S(2)}) collective-permute-start(bf16[256,1024]{1,0:T(8,128)(2,1)S(1)} %get-tuple-element.163), channel_id=1, source_target_pairs={{0,16},{8,24},{16,0},{24,8},{1,17},{9,25},{17,1},{25,9},{2,18},{10... | collective-permute-start | bytes 1572872 | tf_op jit(solution)/shard_map/ppermute | solution.py:72
  258.2 12.5 %collective-permute-start.6 = (bf16[256,1024]{1,0:T(8,128)(2,1)S(1)}, bf16[256,1024]{1,0:T(8,128)(2,1)}, u32[]{:S(2)}, u32[]{:S(2)}) collective-permute-start(bf16[256,1024]{1,0:T(8,128)(2,1)S(1)} %collective-permute-done.3), channel_id=1, source_target_pairs={{0,16},{8,24},{16,0},{24,8},{1,17},{9,25},{17,1},{25,9},{2,18},{10... | collective-permute-start | bytes 1572872 | tf_op jit(solution)/shard_map/ppermute | solution.py:72
  259.6 12.5 %collective-permute-start.4 = (bf16[512,1024]{1,0:T(8,128)(2,1)S(1)}, bf16[512,1024]{1,0:T(8,128)(2,1)S(1)}, u32[]{:S(2)}, u32[]{:S(2)}) collective-permute-start(bf16[512,1024]{1,0:T(8,128)(2,1)S(1)} %bitcast.133), channel_id=1, source_target_pairs={{0,8},{8,0},{16,24},{24,16},{1,9},{9,1},{17,25},{25,17},{2,10},{10... | collective-permute-start | bytes 3145736 | tf_op jit(solution)/shard_map/ppermute | solution.py:63
  272.0 2.7 collective-permute-start.7
  291.2 127.0 %copy-start.6 = (bf16[3,2,128,1024]{3,2,1,0:T(8,128)(2,1)}, bf16[3,2,128,1024]{3,2,1,0:T(8,128)(2,1)S(1)}, u32[]{:S(2)}) copy-start(bf16[3,2,128,1024]{3,2,1,0:T(8,128)(2,1)S(1)} %shard_map.258) | copy-start | bytes 4718596
  291.2 127.0 %collective-permute-start.8 = (bf16[1024,1024]{1,0:T(8,128)(2,1)}, bf16[1024,1024]{1,0:T(8,128)(2,1)}, u32[]{:S(2)}, u32[]{:S(2)}) collective-permute-start(bf16[1024,1024]{1,0:T(8,128)(2,1)} %multiply_convert_fusion.refs_0_), channel_id=1, source_target_pairs={{0,16},{8,24},{16,0},{24,8},{1,17},{9,25},{17,1},{25,9},{2,18},{10... | collective-permute-start | bytes 6291464 | tf_op jit(solution)/shard_map/ppermute | solution.py:72
  291.9 126.3 %collective-permute-start.9 = (bf16[768,1024]{1,0:T(8,128)(2,1)S(1)}, bf16[768,1024]{1,0:T(8,128)(2,1)}, u32[]{:S(2)}, u32[]{:S(2)}) collective-permute-start(bf16[768,1024]{1,0:T(8,128)(2,1)S(1)} %bitcast.123), channel_id=1, source_target_pairs={{0,16},{8,24},{16,0},{24,8},{1,17},{9,25},{17,1},{25,9},{2,18},{10... | collective-permute-start | bytes 4718600 | tf_op jit(solution)/shard_map/ppermute | solution.py:72
  293.3 124.9 %all-to-all-start.2 = ((bf16[4,64,1024]{2,1,0:T(8,128)(2,1)}), bf16[4,64,1024]{2,1,0:T(8,128)(2,1)}, u32[]{:S(2)}, u32[]{:S(2)}) async-start(bf16[4,64,1024]{2,1,0:T(8,128)(2,1)} %bitcast.152), calls=%async_computation.2 | async-start | bytes 1048576 | tf_op jit(solution)/shard_map/all_to_all | solution.py:195
  709.3 14.5 %copy-start.14 = (f32[36,1024]{1,0:T(8,128)S(1)}, f32[36,1024]{1,0:T(8,128)}, u32[]{:S(2)}) copy-start(f32[36,1024]{1,0:T(8,128)} %fusion.17) | copy-start | bytes 442372
  720.7 21.8 %collective-permute-start.11 = (f32[40,256]{1,0:T(8,128)S(1)}, f32[40,256]{1,0:T(8,128)S(1)}, u32[]{:S(2)}, u32[]{:S(2)}) collective-permute-start(f32[40,256]{1,0:T(8,128)S(1)} %pad_maximum_fusion.5), channel_id=1, source_target_pairs={{0,2},{1,3},{2,0},{3,1},{4,6},{5,7},{6,4},{7,5},{8,10},{9,11},{10,... | collective-permute-start | bytes 122888 | tf_op jit(solution)/shard_map/ppermute | solution.py:77
  720.8 42.0 %all-to-all-start.3 = ((f32[32,32,128]{2,1,0:T(8,128)}), f32[32,32,128]{2,1,0:T(8,128)S(1)}, u32[]{:S(2)}, u32[]{:S(2)}) async-start(f32[32,32,128]{2,1,0:T(8,128)} %get-tuple-element.115), calls=%async_computation.3 | async-start | bytes 1048576 | tf_op jit(solution)/shard_map/all_to_all | solution.py:2163
  742.5 13.9 %collective-permute-start.12 = (f32[40,256]{1,0:T(8,128)S(1)}, f32[40,256]{1,0:T(8,128)S(1)}, u32[]{:S(2)}, u32[]{:S(2)}) collective-permute-start(f32[40,256]{1,0:T(8,128)S(1)} %add.109), channel_id=1, source_target_pairs={{0,4},{1,5},{2,6},{3,7},{4,0},{5,1},{6,2},{7,3},{8,12},{9,13},{10,... | collective-permute-start | bytes 122888 | tf_op jit(solution)/shard_map/ppermute | solution.py:77
  745.5 13.3 %collective-permute-start.10 = (f32[36,128]{1,0:T(8,128)S(1)}, f32[36,128]{1,0:T(8,128)S(1)}, u32[]{:S(2)}, u32[]{:S(2)}) collective-permute-start(f32[36,128]{1,0:T(8,128)S(1)} %bitcast.162), channel_id=1, source_target_pairs={{0,0},{1,1},{2,8},{3,9},{4,16},{5,17},{6,24},{7,25},{8,2},{9,3},{1... | collective-permute-start | bytes 55304 | tf_op jit(solution)/shard_map/ppermute | solution.py:1755
  746.2 17.9 %copy-start.1 = (f32[36,36]{1,0:T(8,128)S(1)}, f32[36,36]{1,0:T(8,128)}, u32[]{:S(2)}) copy-start(f32[36,36]{1,0:T(8,128)} %param.28) | copy-start | bytes 15556
  756.6 4.5 collective-permute-start.13
  (18 other events, 81.1 us)
